TPU v7x, 32 devices: a whole 2x2x4 slice. The times are simulated.
32 devices in a mesh: tok: 4 (over z), head: 8 (over y, x, core).
Axes of the slice: x: 2, y: 2, z: 4, core: 2. Of those that a mesh axis runs over, the one named last changes fastest.
Arguments:
- block_input: bfloat16 [4, 1536, 2048], P('tok', 'head'), may hold values from -6 to 6
- segment_ids: int32 [4, 1536], P('tok'), may hold values from 0 to 3, as said below
- positions: int32 [4, 1536], P('tok'), may hold values from 0 to 1023, as said below
- attention_gain: float32 [2048], replicated, may hold values from 0.5 to 1.5
- query_down: bfloat16 [2048, 1024], replicated, may hold values from -0.125 to 0.125
- query_gain: float32 [1024], replicated, may hold values from 0.5 to 1.5
- query_up: bfloat16 [1024, 4096], P(None, 'head'), may hold values from -0.1875 to 0.1875
- key_proj: bfloat16 [2048, 256], replicated, may hold values from -0.125 to 0.125
- value_proj: bfloat16 [2048, 256], replicated, may hold values from -0.125 to 0.125
- out_proj: bfloat16 [4096, 2048], P('head'), may hold values from -0.375 to 0.375
- feed_gain: float32 [2048], replicated, may hold values from 0.5 to 1.5
- gate_weight: bfloat16 [2048, 5632], P(None, 'head'), may hold values from -0.125 to 0.125
- up_weight: bfloat16 [2048, 5632], P(None, 'head'), may hold values from -0.125 to 0.125
- down_weight: bfloat16 [5632, 2048], P('head'), may hold values from -0.078125 to 0.078125
- out_grad: bfloat16 [4, 1536, 2048], P('tok', 'head'), may hold values from -6 to 6
Outputs:
- block_output: bfloat16 [4, 1536, 2048], P('tok', 'head')
- input_gradient: float32 [4, 1536, 2048], P('tok', 'head')
- attention_gain_gradient: float32 [2048], replicated
- query_down_gradient: float32 [2048, 1024], replicated
- query_gain_gradient: float32 [1024], replicated
- query_up_gradient: float32 [1024, 4096], P(None, 'head')
- key_proj_gradient: float32 [2048, 256], replicated
- value_proj_gradient: float32 [2048, 256], replicated
- out_proj_gradient: float32 [4096, 2048], P('head')
- feed_gain_gradient: float32 [2048], replicated
- gate_weight_gradient: float32 [2048, 5632], P(None, 'head')
- up_weight_gradient: float32 [2048, 5632], P(None, 'head')
- down_weight_gradient: float32 [5632, 2048], P('head')
Inputs may be any that keep to these rules, and one draw needn't show every extreme that they name: `segment_ids`: within each pack the ids start at 0 and never fall; the first document of every pack has min(1536, max(1024, 768)) tokens, and every pack has the same number of documents. Within a document the positions rise by one from token to token; the first document of every pack starts at 0.
All inputs are finite; a program needn't handle non-finite values.
Results may differ from a plain program's by a relative error of at most 0.023.
Values may be sent and summed in bfloat16 or wider, within the bound.
No kernel may reach another device: no remote copies, remote signals or barrier semaphores. Data moves between devices by JAX's collectives and lax.ppermute only.
A program may use at most 256 MiB of HBM per device.

v0:
```python
import math

import jax
import jax.numpy as jnp
from jax import lax
from jax.sharding import PartitionSpec as P

norm_epsilon = 1e-05
rope_base = 10000.0


def normalize(value, gain):
    scale = lax.rsqrt(jnp.mean(value * value, axis=-1, keepdims=True) + norm_epsilon)
    return value * scale * gain


def norm_backward(value, gain, upper):
    scale = lax.rsqrt(jnp.mean(value * value, axis=-1, keepdims=True) + norm_epsilon)
    scaled = upper * gain
    lower = scale * scaled - value * (scale * scale * scale) * jnp.mean(
        scaled * value, axis=-1, keepdims=True
    )
    return (lower, jnp.sum(upper * value * scale, axis=0))


def rotation(places, head_width):
    half = head_width // 2
    steps = jnp.arange(half).astype(jnp.float32) * (2.0 / head_width)
    inverse = jnp.exp(steps * -math.log(rope_base))
    angles = places.astype(jnp.float32)[:, None] * inverse[None, :]
    return (jnp.cos(angles), jnp.sin(angles))


def rotate(value, cosine, sine):
    half = value.shape[-1] // 2
    first = value[..., :half]
    second = value[..., half:]
    return jnp.concatenate(
        [first * cosine - second * sine, second * cosine + first * sine], axis=-1
    )


def right_transposed(left, right):
    return lax.dot_general(
        left, right, (((1,), (1,)), ((), ())), preferred_element_type=jnp.float32
    )


def left_transposed(left, right):
    return lax.dot_general(
        left, right, (((0,), (0,)), ((), ())), preferred_element_type=jnp.float32
    )


def allowed_block(segments, start, block, key_order):
    query_order = start + jnp.arange(block)
    own_segments = lax.dynamic_slice_in_dim(segments, start, block, 0)
    return (key_order[None, :] <= query_order[:, None]) & (
        segments[None, :] == own_segments[:, None]
    )


def block_scores(queries, keys, segments, start, block, key_order, scale):
    query_block = lax.dynamic_slice_in_dim(queries, start, block, 0)
    scores = (
        jnp.einsum("bhd,kd->hbk", query_block, keys, preferred_element_type=jnp.float32) * scale
    )
    allowed = allowed_block(segments, start, block, key_order)
    return (query_block, jnp.where(allowed[None], scores, -1e30))


def attend_forward(queries, keys, values, segments, block, scale):
    length = queries.shape[0]
    key_order = jnp.arange(length)

    def one_block(index):
        query_block, scores = block_scores(
            queries, keys, segments, index * block, block, key_order, scale
        )
        top = jnp.max(scores, axis=-1, keepdims=True)
        weights = jnp.exp(scores - top)
        total = jnp.sum(weights, axis=-1, keepdims=True)
        probs = (weights / total).astype(jnp.bfloat16)
        result = jnp.einsum("hbk,kd->bhd", probs, values, preferred_element_type=jnp.float32)
        return (result.astype(jnp.bfloat16), (top + jnp.log(total))[..., 0])

    outputs, log_totals = lax.map(one_block, jnp.arange(length // block))
    return (outputs.reshape(length, -1), log_totals)


def attend_backward(queries, keys, values, segments, log_totals, outer_grad, block, scale):
    length = queries.shape[0]
    key_order = jnp.arange(length)

    def one_block(carry, index):
        keys_total, values_total = carry
        start = index * block
        query_block, scores = block_scores(queries, keys, segments, start, block, key_order, scale)
        grad_block = lax.dynamic_slice_in_dim(outer_grad, start, block, 0)
        probs = jnp.exp(scores - log_totals[index][..., None])
        prob_grad = jnp.einsum(
            "bhd,kd->hbk", grad_block, values, preferred_element_type=jnp.float32
        )
        centre = jnp.sum(probs * prob_grad, axis=-1, keepdims=True)
        score_grad = (probs * (prob_grad - centre)).astype(jnp.bfloat16)
        query_grad = (
            jnp.einsum("hbk,kd->bhd", score_grad, keys, preferred_element_type=jnp.float32) * scale
        )
        keys_total = (
            keys_total
            + jnp.einsum("hbk,bhd->kd", score_grad, query_block, preferred_element_type=jnp.float32)
            * scale
        )
        values_total = values_total + jnp.einsum(
            "hbk,bhd->kd",
            probs.astype(jnp.bfloat16),
            grad_block,
            preferred_element_type=jnp.float32,
        )
        return ((keys_total, values_total), query_grad)

    initial = (jnp.zeros(keys.shape, jnp.float32), jnp.zeros(values.shape, jnp.float32))
    (keys_total, values_total), query_grads = lax.scan(
        one_block, initial, jnp.arange(length // block)
    )
    return (query_grads.reshape(queries.shape), keys_total, values_total)


def body(
    block_input,
    segment_ids,
    positions,
    attention_gain,
    query_down,
    query_gain,
    query_up,
    key_proj,
    value_proj,
    out_proj,
    feed_gain,
    gate_weight,
    up_weight,
    down_weight,
    out_grad,
):
    rows = block_input.shape[1]
    segments = segment_ids[0]
    places = positions[0]
    length = segments.shape[0]
    head_width = key_proj.shape[1]
    heads_here = query_up.shape[1] // head_width
    block = min(512, length)
    scale = 1.0 / math.sqrt(head_width)
    first_row = lax.axis_index("head") * rows
    rows_in = block_input[0].astype(jnp.float32)
    normed_rows = normalize(rows_in, attention_gain).astype(jnp.bfloat16)
    normed_in = lax.all_gather(normed_rows, "head", axis=0, tiled=True)
    latent = jnp.dot(normed_in, query_down, preferred_element_type=jnp.float32)
    latent_normed = normalize(latent, query_gain).astype(jnp.bfloat16)
    cosine, sine = rotation(places, head_width)
    query_pre = jnp.dot(latent_normed, query_up, preferred_element_type=jnp.float32).reshape(
        length, heads_here, head_width
    )
    queries = rotate(query_pre, cosine[:, None], sine[:, None]).astype(jnp.bfloat16)
    keys = rotate(
        jnp.dot(normed_in, key_proj, preferred_element_type=jnp.float32), cosine, sine
    ).astype(jnp.bfloat16)
    values = jnp.dot(normed_in, value_proj, preferred_element_type=jnp.float32).astype(jnp.bfloat16)
    mixed, log_totals = attend_forward(queries, keys, values, segments, block, scale)
    attention = lax.psum_scatter(
        jnp.dot(mixed, out_proj, preferred_element_type=jnp.float32).astype(jnp.bfloat16),
        "head",
        scatter_dimension=0,
        tiled=True,
    ).astype(jnp.float32)
    middle = rows_in + attention
    normed_mid_rows = normalize(middle, feed_gain).astype(jnp.bfloat16)
    normed_mid = lax.all_gather(normed_mid_rows, "head", axis=0, tiled=True)
    gate = jnp.dot(normed_mid, gate_weight, preferred_element_type=jnp.float32)
    upward = jnp.dot(normed_mid, up_weight, preferred_element_type=jnp.float32)
    sigmoid_gate = jax.nn.sigmoid(gate)
    swish = gate * sigmoid_gate
    hidden = (swish * upward).astype(jnp.bfloat16)
    feed_rows = lax.psum_scatter(
        jnp.dot(hidden, down_weight, preferred_element_type=jnp.float32).astype(jnp.bfloat16),
        "head",
        scatter_dimension=0,
        tiled=True,
    ).astype(jnp.float32)
    block_output = (middle + feed_rows).astype(jnp.bfloat16)
    cotangent_rows = out_grad[0]
    cotangent = lax.all_gather(cotangent_rows, "head", axis=0, tiled=True)
    hidden_grad = right_transposed(cotangent, down_weight)
    down_gradient = left_transposed(hidden, cotangent)
    gate_grad = (hidden_grad * upward * sigmoid_gate * (1.0 + gate * (1.0 - sigmoid_gate))).astype(
        jnp.bfloat16
    )
    upward_grad = (hidden_grad * swish).astype(jnp.bfloat16)
    gate_gradient = left_transposed(normed_mid, gate_grad)
    up_gradient = left_transposed(normed_mid, upward_grad)
    mid_partial = right_transposed(gate_grad, gate_weight) + right_transposed(
        upward_grad, up_weight
    )
    mid_grad = lax.psum_scatter(
        mid_partial.astype(jnp.bfloat16), "head", scatter_dimension=0, tiled=True
    ).astype(jnp.float32)
    middle_norm_grad, feed_gain_partial = norm_backward(middle, feed_gain, mid_grad)
    middle_grad = cotangent_rows.astype(jnp.float32) + middle_norm_grad
    attention_grad = middle_grad.astype(jnp.bfloat16)
    attention_grad_all = lax.all_gather(attention_grad, "head", axis=0, tiled=True)
    mixed_grad = right_transposed(attention_grad_all, out_proj).astype(jnp.bfloat16)
    proj_gradient = left_transposed(mixed, attention_grad_all)
    query_grad, key_grad, value_grad = attend_backward(
        queries,
        keys,
        values,
        segments,
        log_totals,
        mixed_grad.reshape(length, heads_here, head_width),
        block,
        scale,
    )
    query_pre_grad = (
        rotate(query_grad, cosine[:, None], -sine[:, None]).reshape(length, -1).astype(jnp.bfloat16)
    )
    query_up_gradient = left_transposed(latent_normed, query_pre_grad)
    latent_partial = right_transposed(query_pre_grad, query_up)
    latent_rows, key_rows, value_rows = (
        lax.psum_scatter(
            latent_partial.astype(jnp.bfloat16), "head", scatter_dimension=0, tiled=True
        ).astype(jnp.float32),
        lax.psum_scatter(
            key_grad.astype(jnp.bfloat16), "head", scatter_dimension=0, tiled=True
        ).astype(jnp.float32),
        lax.psum_scatter(
            value_grad.astype(jnp.bfloat16), "head", scatter_dimension=0, tiled=True
        ).astype(jnp.float32),
    )
    own_latent = lax.dynamic_slice_in_dim(latent, first_row, rows, 0)
    latent_grad_full, query_gain_partial = norm_backward(own_latent, query_gain, latent_rows)
    latent_grad = latent_grad_full.astype(jnp.bfloat16)
    own_cosine = lax.dynamic_slice_in_dim(cosine, first_row, rows, 0)
    own_sine = lax.dynamic_slice_in_dim(sine, first_row, rows, 0)
    key_pre_grad = rotate(key_rows, own_cosine, -own_sine).astype(jnp.bfloat16)
    value_low_grad = value_rows.astype(jnp.bfloat16)
    in_grad = (
        right_transposed(latent_grad, query_down)
        + right_transposed(key_pre_grad, key_proj)
        + right_transposed(value_low_grad, value_proj)
    )
    query_down_partial = left_transposed(normed_rows, latent_grad)
    key_proj_partial = left_transposed(normed_rows, key_pre_grad)
    value_proj_partial = left_transposed(normed_rows, value_low_grad)
    input_norm_grad, attention_gain_partial = norm_backward(rows_in, attention_gain, in_grad)
    input_gradient = middle_grad + input_norm_grad
    shared = lax.psum(
        (
            query_down_partial,
            key_proj_partial,
            value_proj_partial,
            attention_gain_partial,
            query_gain_partial,
            feed_gain_partial,
        ),
        ("tok", "head"),
    )
    local = (
        lax.psum(query_up_gradient.astype(jnp.bfloat16), "tok").astype(jnp.float32),
        lax.psum(proj_gradient.astype(jnp.bfloat16), "tok").astype(jnp.float32),
        lax.psum(gate_gradient.astype(jnp.bfloat16), "tok").astype(jnp.float32),
        lax.psum(up_gradient.astype(jnp.bfloat16), "tok").astype(jnp.float32),
        lax.psum(down_gradient.astype(jnp.bfloat16), "tok").astype(jnp.float32),
    )
    return (
        block_output[None],
        input_gradient[None],
        shared[3],
        shared[0],
        shared[4],
        local[0],
        shared[1],
        shared[2],
        local[1],
        shared[5],
        local[2],
        local[3],
        local[4],
    )


def solution(mesh):
    in_specs = (
        P("tok", "head", None),
        P("tok", None),
        P("tok", None),
        P(),
        P(),
        P(),
        P(None, "head"),
        P(),
        P(),
        P("head", None),
        P(),
        P(None, "head"),
        P(None, "head"),
        P("head", None),
        P("tok", "head", None),
    )
    out_specs = (
        P("tok", "head", None),
        P("tok", "head", None),
        P(),
        P(),
        P(),
        P(None, "head"),
        P(),
        P(),
        P("head", None),
        P(),
        P(None, "head"),
        P(None, "head"),
        P("head", None),
    )
    return jax.shard_map(body, mesh=mesh, in_specs=in_specs, out_specs=out_specs, check_vma=False)
```

profile of v0, /device:TPU:0, one launch (start us, length us, event | category | flops | bytes accessed | tf_op | source)
XLA Modules:
  0.0 1390.5 jit_solution(3441061401580680849)
XLA Ops:
  12.9 47.6 %all-gather.6.cloned.1.call-done = bf16[1536,2048]{1,0:T(8,128)(2,1)} async-done(((bf16[192,2048]{1,0:T(8,128)(2,1)}), bf16[1536,2048]{1,0:T(8,128)(2,1)}) %all-gather.6.cloned.1.call-update) | async-done | bytes 6291472 | tf_op jit(solution)/shard_map/all_gather | solution.py:157
  60.6 11.9 multiply_reduce_fusion
  74.4 4.2 fusion.73
  87.4 5.1 fusion.90
  94.4 3.0 copy.77
  97.4 3.0 copy.76
  104.7 5.5 convolution_convert_fusion.7
  110.2 35.3 %while.28 = (s32[]{:T(128)}, bf16[3,512,2,256]{3,2,1,0:T(2,128)(2,1)}, f32[3,2,512]{2,1,0:T(2,128)}, s32[3]{0:T(128)S(1)}, s32[1,1536]{1,0:T(1,128)S(1)}, /*inde...) while((s32[]{:T(128)}, ...), condition=%wide.region_5.6_spmd.clone, body=%wide.region_2.5_spmd.clone.sunk | while | flops 1632108032 | bytes 28897524 | solution.py:87
  148.5 5.3 convolution_convert_fusion.1
  153.9 61.9 %reduce-scatter.9.cloned.1.call-done = bf16[192,2048]{1,0:T(8,128)(2,1)} async-done(((bf16[1536,2048]{1,0:T(8,128)(2,1)}), bf16[192,2048]{1,0:T(8,128)(2,1)}) %reduce-scatter.9.cloned.1.call-update) | async-done | bytes 786448 | tf_op jit(solution)/shard_map/reduce_scatter | solution.py:170
  220.7 45.0 %all-gather.8.cloned.1.call-done = bf16[1536,2048]{1,0:T(8,128)(2,1)} async-done(((bf16[192,2048]{1,0:T(8,128)(2,1)}), bf16[1536,2048]{1,0:T(8,128)(2,1)}) %all-gather.8.cloned.1.call-update) | async-done | bytes 6291472 | tf_op jit(solution)/shard_map/all_gather | solution.py:178
  265.7 10.5 fusion.98
  276.2 6.6 fusion.97
  282.9 30.3 %all-gather.12.cloned.1.call-done = bf16[1,1536,2048]{2,1,0:T(8,128)(2,1)} async-done(((bf16[1,192,2048]{2,1,0:T(8,128)(2,1)}), bf16[1,1536,2048]{2,1,0:T(8,128)(2,1)}) %all-gather.12.cloned.1.call-update) | async-done | bytes 6291472 | tf_op jit(solution)/shard_map/all_gather | solution.py:192
  313.2 11.9 multiply_convert_fusion.1
  325.2 5.1 fusion.99
  330.3 8.8 add_convert_fusion
  339.1 61.9 %reduce-scatter.13.cloned.1.call-done = bf16[192,2048]{1,0:T(8,128)(2,1)} async-done(((bf16[1536,2048]{1,0:T(8,128)(2,1)}), bf16[192,2048]{1,0:T(8,128)(2,1)}) %reduce-scatter.13.cloned.1.call-update) | async-done | bytes 786448 | tf_op jit(solution)/shard_map/reduce_scatter | solution.py:204
  406.8 45.6 %all-gather.10.cloned.1.call-done = bf16[1536,2048]{1,0:T(8,128)(2,1)} async-done(((bf16[192,2048]{1,0:T(8,128)(2,1)}), bf16[1536,2048]{1,0:T(8,128)(2,1)}) %all-gather.10.cloned.1.call-update) | async-done | bytes 6291472 | tf_op jit(solution)/shard_map/all_gather | solution.py:210
  452.3 8.0 convolution_convert_fusion.6
  460.9 70.3 %while.29 = (s32[]{:T(128)}, f32[1536,256]{1,0:T(8,128)}, f32[1536,256]{1,0:T(8,128)}, f32[3,512,2,256]{3,1,0,2:T(8,128)}, s32[3]{0:T(128)}, /*index=5*/s32[1,15...) while((s32[]{:T(128)}, f32[1536,256]{1,0:T(8,128)}, ...), condition=%wide.region_14.15_spmd.clone, body=%wide.region_12.14_spmd.clone.sunk | while | flops 4045274624 | bytes 101515776 | solution.py:123
  470.0 3.7 fusion.176
  479.0 3.2 fusion.178
  493.4 3.7 fusion.176
  502.5 3.2 fusion.178
  516.8 3.7 fusion.176
  525.9 3.2 fusion.178
  547.5 5.2 convolution_convert_fusion.2
  552.8 9.1 convolution_convert_fusion
  562.0 9.8 fusion.51
  571.8 9.1 convolution_convert_fusion.3
  581.0 5.9 convolution_convert_fusion.4
  586.9 3.2 convolution_convert_fusion.8
  590.2 4.7 convolution_convert_fusion.5
  601.4 8.5 reduce-scatter.17.cloned.1.call-done
  612.9 47.3 %reduce-scatter.15.cloned.1.call-done = bf16[192,1024]{1,0:T(8,128)(2,1)} async-done(((bf16[1536,1024]{1,0:T(8,128)(2,1)}), bf16[192,1024]{1,0:T(8,128)(2,1)}) %reduce-scatter.15.cloned.1.call-update) | async-done | bytes 393232 | tf_op jit(solution)/shard_map/reduce_scatter | solution.py:229
  661.7 6.3 fusion.91
  669.0 4.3 fusion.93
  677.0 40.4 %all-reduce = (f32[2048]{0:T(1024)}, f32[1024]{0:T(1024)}, f32[2048]{0:T(1024)}) all-reduce(f32[2048]{0:T(1024)S(1)} %get-tuple-element.268, f32[1024]{0:T(1024)S(1)} %get-tuple-element.264, f32[2048]{0:T(1024)S(1)} %copy-done.34), channel_id=1, replica_groups=mesh['tok'=4,'head'=8] {'tok','head'}, use_global_device_ids=true, to_apply=%region_21.22 | all-reduce | flops 5120 | bytes 40960 | tf_op jit(solution)/shard_map/psum | solution.py:256
  717.4 8.5 reduce-scatter.11.cloned.1.call-done
  725.9 5.2 fusion.67
  731.1 402.6 %all-reduce.8.cloned.1.call-done = (bf16[1024,512]{1,0:T(8,128)(2,1)}, bf16[512,2048]{1,0:T(8,128)(2,1)}, bf16[2048,704]{0,1:T(8,128)(2,1)}, bf16[2048,704]{0,1:T(8,128)(2,1)}, bf16[704,2048]{1,0:T(8,128)(2,1)}) async-done(((bf16[1024,512]{1,0:T(8,128)(2,1)}, bf16[512,2048]{1,0:T(8,128)(2,1)}, bf16[2048,704]{0,1:T(8,128)(2,1)}, bf16[2048,704]{0,1:T(8,128)(2,1)}, bf16[704,2048]{1,0:T(8,128)(2,1)}), ...) | async-done | bytes 11796496 | tf_op jit(solution)/shard_map/psum | solution.py:268
  1133.7 3.0 convert_element_type.176
  1139.3 3.3 convert_element_type.180
  1142.6 3.7 convert_element_type.182
  1146.2 3.3 convert_element_type.184
  1149.6 221.7 %all-reduce.6.cloned.1.call-done = (f32[2048,1024]{1,0:T(8,128)}, f32[2048,256]{1,0:T(8,128)}, f32[2048,256]{1,0:T(8,128)}) async-done(((f32[2048,1024]{1,0:T(8,128)}, f32[2048,256]{1,0:T(8,128)}, f32[2048,256]{1,0:T(8,128)}), (f32[2048,1024]{1,0:T(8,128)}, f32[2048,256]{1,0:T(8,128)}, f32[2048,256]{1,0:T(8,128)})) %all-reduce.6.cloned.1.call-update) | async-done | bytes 12582928 | tf_op jit(solution)/shard_map/psum | solution.py:256
  1371.2 8.6 copy.124
  (295 shorter events, 149.3 us)
Async XLA Ops:
  7.2 306.0 %copy-start = (bf16[704,2048]{1,0:T(8,128)(2,1)S(1)}, bf16[704,2048]{1,0:T(8,128)(2,1)}, u32[]{:S(2)}) copy-start(bf16[704,2048]{1,0:T(8,128)(2,1)} %param.32) | copy-start | bytes 8650756
  7.2 5.1 copy-start.26
  7.2 5.7 copy-start.45
  7.2 53.4 %all-gather.6.cloned.1.call-start = ((), (), s32[]{:S(2)}) async-start(), calls=%async_computation.6 | async-start | bytes 7077888 | tf_op jit(solution)/shard_map/all_gather | solution.py:157
  12.2 203.5 %reduce-scatter.9.cloned.1.call-start = ((), (), s32[]{:S(2)}) async-start(), calls=%async_computation.7 | async-start | bytes 7077888 | tf_op jit(solution)/shard_map/reduce_scatter | solution.py:170
  60.6 11.9 copy-start.21
  60.6 11.9 copy-start.48
  72.5 14.9 %copy-start.35 = (f32[1536]{0:T(1024)}, f32[1536]{0:T(1024)S(1)}, u32[]{:S(2)}) copy-start(f32[1536]{0:T(1024)S(1)} %add_rsqrt_fusion) | copy-start | bytes 18436
  80.9 6.5 copy-start.32
  153.8 63.7 %copy-start.28 = (f32[2048]{0:T(1024)S(1)}, f32[2048]{0:T(1024)}, u32[]{:S(2)}) copy-start(f32[2048]{0:T(1024)} %param.29) | copy-start | bytes 24580
  153.8 111.9 %all-gather.8.cloned.1.call-start = ((), (), s32[]{:S(2)}) async-start(), calls=%async_computation.8 | async-start | bytes 7077888 | tf_op jit(solution)/shard_map/all_gather | solution.py:178
  217.5 186.5 %copy-start.37 = (f32[192]{0:T(256)}, f32[192]{0:T(256)S(1)}, u32[]{:S(2)}) copy-start(f32[192]{0:T(256)S(1)} %get-tuple-element.352) | copy-start | bytes 2308
  217.5 186.5 %copy-start.41 = (f32[192]{0:T(256)}, f32[192]{0:T(256)S(1)}, u32[]{:S(2)}) copy-start(f32[192]{0:T(256)S(1)} %get-tuple-element.351) | copy-start | bytes 2308
  220.1 93.1 %all-gather.12.cloned.1.call-start = ((), (), s32[]{:S(2)}) async-start(), calls=%async_computation.14 | async-start | bytes 7077888 | tf_op jit(solution)/shard_map/all_gather | solution.py:192
  220.6 180.4 %reduce-scatter.13.cloned.1.call-start = ((), (), s32[]{:S(2)}) async-start(), calls=%async_computation.10 | async-start | bytes 7077888 | tf_op jit(solution)/shard_map/reduce_scatter | solution.py:204
  265.7 10.5 copy-start.47
  265.7 10.5 copy-start.49
  313.2 11.9 copy-start.50
  325.1 5.1 copy-start.53
  325.1 5.1 copy-start.51
  339.1 113.2 %all-gather.10.cloned.1.call-start = ((), (), s32[]{:S(2)}) async-start(), calls=%async_computation.11 | async-start | bytes 7077888 | tf_op jit(solution)/shard_map/all_gather | solution.py:210
  406.7 189.6 %reduce-scatter.19.cloned.1.call-start = ((), (), s32[]{:S(2)}) async-start(), calls=%async_computation.15 | async-start | bytes 884736
  479.0 3.3 copy-start.2
  536.0 73.9 %reduce-scatter.17.cloned.1.call-start = ((), (), s32[]{:S(2)}) async-start(), calls=%async_computation.13 | async-start | bytes 884736 | tf_op jit(solution)/shard_map/reduce_scatter | solution.py:235
  540.7 119.4 %reduce-scatter.15.cloned.1.call-start = ((), (), s32[]{:S(2)}) async-start(), calls=%async_computation.12 | async-start | bytes 3538944 | tf_op jit(solution)/shard_map/reduce_scatter | solution.py:229
  552.7 173.2 %reduce-scatter.11.cloned.1.call-start = ((), (), s32[]{:S(2)}) async-start(), calls=%async_computation.9 | async-start | bytes 7077888 | tf_op jit(solution)/shard_map/reduce_scatter | solution.py:184
  561.9 571.8 %all-reduce.8.cloned.1.call-start = ((), (), s32[]{:S(2)}) async-start(), calls=%async_computation.17 | async-start | bytes 23592960 | tf_op jit(solution)/shard_map/psum | solution.py:268
  561.9 9.8 copy-start.55
  562.0 18.9 %slice-start.2 = ((s8[6291456]{0:T(1024)(128)(4,1)}), s8[4194304]{0:T(1024)(128)(4,1)S(1)}, s32[]{:S(2)}) async-start(s8[6291456]{0:T(1024)(128)(4,1)} %bitcast.210), calls=%async_computation.20 | async-start | bytes 8388608
  571.8 9.1 slice-start.3
  571.8 9.1 copy-start.54
  571.8 15.1 %slice-start = ((s8[6291456]{0:T(1024)(128)(4,1)}), s8[4194304]{0:T(1024)(128)(4,1)S(1)}, s32[]{:S(2)}) async-start(s8[6291456]{0:T(1024)(128)(4,1)} %bitcast.201), calls=%async_computation.18 | async-start | bytes 8388608
  571.8 18.4 %slice-start.4 = ((s8[6291456]{0:T(1024)(128)(4,1)}), s8[4194304]{0:T(1024)(128)(4,1)S(1)}, s32[]{:S(2)}) async-start(s8[6291456]{0:T(1024)(128)(4,1)} %bitcast.212), calls=%async_computation.22 | async-start | bytes 8388608
  580.9 6.0 slice-start.1
  580.9 6.0 copy-start.18
  580.9 6.0 copy-start.33
  580.9 6.0 copy-start.36
  581.0 9.2 slice-start.5
  594.9 776.3 %all-reduce.6.cloned.1.call-start = ((), (), s32[]{:S(2)}) async-start(), calls=%async_computation.16 | async-start | bytes 25165824 | tf_op jit(solution)/shard_map/psum | solution.py:256
  669.0 4.3 copy-start.22
  675.1 50.8 %copy-start.29 = (f32[2048]{0:T(1024)S(1)}, f32[2048]{0:T(1024)}, u32[]{:S(2)}) copy-start(f32[2048]{0:T(1024)} %param.29) | copy-start | bytes 24580
  675.1 50.8 %copy-start.38 = (f32[192]{0:T(256)S(1)}, f32[192]{0:T(256)}, u32[]{:S(2)}) copy-start(f32[192]{0:T(256)} %copy-done.37) | copy-start | bytes 2308
  675.1 50.8 %copy-start.42 = (f32[192]{0:T(256)S(1)}, f32[192]{0:T(256)}, u32[]{:S(2)}) copy-start(f32[192]{0:T(256)} %copy-done.41) | copy-start | bytes 2308
  675.1 50.8 %copy-start.44 = (f32[192]{0:T(256)S(1)}, f32[192]{0:T(256)}, u32[]{:S(2)}) copy-start(f32[192]{0:T(256)} %copy-done.43) | copy-start | bytes 2308
  675.1 50.8 %copy-start.46 = (f32[192]{0:T(256)S(1)}, f32[192]{0:T(256)}, u32[]{:S(2)}) copy-start(f32[192]{0:T(256)} %get-tuple-element.347) | copy-start | bytes 2308
  1139.3 3.3 copy-start.11
  1142.6 3.7 copy-start.10
  1371.2 8.6 copy-start.15
  (42 other events, 97.6 us)
Sparse Core Ops, SparseCore 0:
  12.3 48.2 all-gather.5
  153.9 61.7 reduce-scatter.8
  220.2 45.5 all-gather.7
  267.6 45.5 all-gather.11
  339.2 61.7 reduce-scatter.12
  406.8 45.5 all-gather.9
  536.1 35.0 reduce-scatter.18
  574.9 34.9 reduce-scatter.16
  613.9 46.2 reduce-scatter.14
  663.8 62.1 reduce-scatter.10
  730.2 403.4 all-reduce.7
  1140.5 230.6 all-reduce.5
where the time goes:
time: 1400 us; the launch traced here: 1390 us
  waiting for transfers between devices  982 us (70%)
  matrix products  205 us (15%)
  other arithmetic  75.6 us (5%)
  local copies, waits for them, and re-layouts  62.5 us (4%)
  blocking collectives  40.4 us (3%)
  between operations  15 us (1%)
    psum x1, waiting for transfers between devices, body(): lax.psum(query_up_gradient.astype(jnp.bfloat16), 'tok').astype(jnp.float32)  403 us
    psum x1, waiting for transfers between devices, body(): lax.psum((query_down_partial, key_proj_partial, value_proj_partial, atten...  222 us
    reduce_scatter x1, waiting for transfers between devices, body(): lax.psum_scatter(jnp.dot(mixed, out_proj, preferred_element_type=jnp.floa...  61.9 us
    reduce_scatter x1, waiting for transfers between devices, body(): lax.psum_scatter(mid_partial.astype(jnp.bfloat16), 'head', scatter_dimens...  61.9 us
    all_gather x1, waiting for transfers between devices, body(): normed_in = lax.all_gather(normed_rows, 'head', axis=0, tiled=True)  47.6 us
    reduce_scatter x1, waiting for transfers between devices, body(): lax.psum_scatter(latent_partial.astype(jnp.bfloat16), 'head', scatter_dim...  47.3 us
    dot_general x8, matrix products, right_transposed(): lax.dot_general(left, right, (((1,), (1,)), ((), ())), preferred_element_...  45.8 us
    all_gather x1, waiting for transfers between devices, body(): lax.all_gather(attention_grad, 'head', axis=0, tiled=True)  45.6 us
  transfers between devices with their start and end apart: 12, of which 11 were waited for; matrix products, arithmetic and copies ran while one was open for 9% of the time, Pallas kernels for 0%

commit v1 on v0

v1 whole, which is shorter than its diff:
```python
import functools
import math

import jax
import jax.numpy as jnp
from jax import lax
from jax.experimental import pallas as pl
from jax.experimental.pallas import tpu as pltpu
from jax.sharding import PartitionSpec as P

norm_epsilon = 1e-05
rope_base = 10000.0
first_document = 1024
bf16 = jnp.bfloat16
f32 = jnp.float32


def inverse_rms(value):
    return lax.rsqrt(jnp.mean(value * value, axis=-1, keepdims=True) + norm_epsilon)


def norm_backward(value, gain, upper):
    scale = inverse_rms(value)
    scaled = upper * gain
    lower = scale * scaled - value * (scale * scale * scale) * jnp.mean(
        scaled * value, axis=-1, keepdims=True
    )
    return (lower, jnp.sum(upper * value * scale, axis=0))


def rotation(places, head_width):
    half = head_width // 2
    steps = jnp.arange(half).astype(f32) * (2.0 / head_width)
    inverse = jnp.exp(steps * -math.log(rope_base))
    angles = places.astype(f32)[:, None] * inverse[None, :]
    return (jnp.cos(angles), jnp.sin(angles))


def rotate(value, cosine, sine):
    half = value.shape[-1] // 2
    first = value[..., :half]
    second = value[..., half:]
    return jnp.concatenate(
        [first * cosine - second * sine, second * cosine + first * sine], axis=-1
    )


def dot(left, right):
    return jnp.dot(left, right, preferred_element_type=f32)


def right_transposed(left, right):
    return lax.dot_general(left, right, (((1,), (1,)), ((), ())), preferred_element_type=f32)


def left_transposed(left, right):
    return lax.dot_general(left, right, (((0,), (0,)), ((), ())), preferred_element_type=f32)


def add_low(left, right):
    return (left.astype(f32) + right.astype(f32)).astype(bf16)


class Clock:
    def __init__(self):
        self.last = ()

    def __call__(self, *values):
        held = lax.optimization_barrier(values + self.last)
        self.last = (held[0],)
        return held[0] if len(values) == 1 else held[: len(values)]


class Plane:
    def __init__(self, size):
        self.size = size
        self.fast = size == 8 and lax.axis_size("tok") == 4
        self.me = lax.axis_index("head")
        if self.fast:
            even = [index % 2 == 0 for index in range(size)]
            self.hop_a = [(i, i ^ (2 if even[i] else 4)) for i in range(size)]
            self.hop_b = [(i, i ^ (4 if even[i] else 2)) for i in range(size)]
            self.hop_c = [(i, i ^ 1) for i in range(size)]
            mask_a = jnp.where(self.me % 2 == 0, 2, 4)
            other = self.me ^ 1
            order = [
                self.me,
                other,
                self.me ^ mask_a,
                other ^ (6 - mask_a),
                self.me ^ (6 - mask_a),
                other ^ mask_a,
                self.me ^ 6,
                other ^ 6,
            ]
            self.table = jnp.stack(order).astype(jnp.int32)
            self.groups = [(0, 2), (2, 6), (6, 8)]
        else:
            self.table = jnp.arange(size, dtype=jnp.int32)
            self.groups = [(0, size)]

    def move(self, value, hop):
        return lax.ppermute(value, "head", hop)

    def gather(self, rows):
        whole = lax.all_gather(rows, "head", axis=0, tiled=True)
        return list(jnp.split(whole, self.size, axis=0))

    def scatter(self, pieces):
        whole = jnp.concatenate(pieces, axis=0)
        return lax.psum_scatter(whole, "head", scatter_dimension=0, tiled=True).astype(f32)

    def total(self, value):
        if not self.fast:
            return lax.psum(value, "head")
        for bit in (1, 2, 4):
            value = value + self.move(value, [(i, i ^ bit) for i in range(8)])
        return value


class Line:
    def __init__(self, size):
        self.size = size
        self.me = lax.axis_index("tok")
        half = size // 2
        self.stages = [([(k, k + 1), (size - 1 - k, size - 2 - k)], None) for k in range(half - 1)]
        self.stages.append(([(half - 1, half), (half, half - 1)], None))
        for k in reversed(range(half - 1)):
            self.stages.append(([(k + 1, k), (size - 2 - k, size - 1 - k)], k))

    def start(self, stage, value):
        return lax.ppermute(value, "tok", self.stages[stage][0])

    def finish(self, stage, value, came, plus=add_low):
        outward = self.stages[stage][1]
        if outward is None:
            return plus(value, came)
        mine = (self.me == outward) | (self.me == self.size - 1 - outward)
        return jnp.where(mine, came, value)

    def total(self, value, plus=add_low):
        for stage in range(len(self.stages)):
            value = self.finish(stage, value, self.start(stage, value), plus)
        return value


class Belt:
    inward = [(0, 1), (3, 2)]
    middle = [(1, 2), (2, 1)]
    outward = [(1, 0), (2, 3)]

    def __init__(self, line, clock):
        self.clock = clock
        self.inner = jnp.where((line.me == 1) | (line.me == 2), 1, 0).astype(jnp.int32).reshape(1)

    def move(self, value, pairs):
        return lax.ppermute(value, "tok", pairs)

    def begin(self, value):
        value = self.clock(value)
        return {"own": value, "came": self.move(value, self.inward)}

    def cross(self, item):
        item["came"] = self.clock(item["came"])
        item["own"] = self.clock(add_rows(item["own"], item["came"]))
        item["came"] = self.move(item["own"], self.middle)

    def back(self, item, value=None):
        item["came"] = self.clock(item["came"])
        if value is None:
            item["own"] = self.clock(add_rows(item["own"], item["came"]))
            item["came"] = self.move(item["own"], self.outward)
            return None
        both = self.clock(add_or_begin(self.inner, item["own"], item["came"], value))
        came = self.move(both, self.inward + self.outward)
        item["own"], item["came"] = both, came
        return {"own": value, "came": came}

    def end(self, item, size, at=0, past=None):
        item["came"] = self.clock(item["came"])
        return self.clock(settle(self.inner, item["own"], item["came"], size, at, past))


def query_blocks(length):
    first = min(length, max(first_document, length // 2))
    block = 256
    return [
        (start, min(block, length - start), 0 if start < first else first)
        for start in range(0, length, block)
    ]


def allowed(seg_column, seg_row, start, rows, low, high):
    query_order = start + lax.broadcasted_iota(jnp.int32, (rows, high - low), 0)
    key_order = low + lax.broadcasted_iota(jnp.int32, (rows, high - low), 1)
    same = seg_column[start : start + rows, :] == seg_row[:, low:high]
    return (key_order <= query_order) & same


def weights_of(stacked, keys, permit, heads, scale):
    scores = right_transposed(stacked, keys) * scale
    scores = jnp.where(jnp.concatenate([permit] * heads, axis=0), scores, -1e30)
    top = jnp.max(scores, axis=-1, keepdims=True)
    weights = jnp.exp(scores - top)
    return weights, jnp.sum(weights, axis=-1, keepdims=True)


def stack_heads(ref, start, rows, heads, width):
    return jnp.concatenate(
        [ref[start : start + rows, h * width : (h + 1) * width] for h in range(heads)], axis=0
    )


def attend_forward_kernel(count, heads, width, rank, scale, *refs):
    table = refs[0]
    pieces = refs[1 : 1 + count]
    weight, cosine, sine, seg_column, seg_row = refs[1 + count : 6 + count]
    queries, keys, values, mixed, mixed_there = refs[6 + count :]
    length = queries.shape[0]
    rows = length // count
    half = width // 2
    for r in range(count):
        there = pl.ds(pl.multiple_of(table[r] * rows, rows), rows)
        keys[there, :] = pieces[r][:, rank : rank + width]
        values[there, :] = pieces[r][:, rank + width :]
        flat = dot(pieces[r][:, :rank], weight[...])
        cos = cosine[there, :]
        sin = sine[there, :]
        for h in range(heads):
            first = flat[:, h * width : h * width + half]
            second = flat[:, h * width + half : (h + 1) * width]
            queries[there, h * width : h * width + half] = (first * cos - second * sin).astype(bf16)
            queries[there, h * width + half : (h + 1) * width] = (
                second * cos + first * sin
            ).astype(bf16)
    for start, size, low in query_blocks(length):
        high = start + size
        stacked = stack_heads(queries, start, size, heads, width)
        permit = allowed(seg_column, seg_row, start, size, low, high)
        weights, total = weights_of(stacked, keys[low:high, :], permit, heads, scale)
        probs = (weights / total).astype(bf16)
        result = dot(probs, values[low:high, :]).astype(bf16)
        for h in range(heads):
            mixed[start:high, h * width : (h + 1) * width] = result[h * size : (h + 1) * size]
    for r in range(count):
        there = pl.ds(pl.multiple_of(table[r] * rows, rows), rows)
        mixed_there[r * rows : (r + 1) * rows, :] = mixed[there, :]


def brief():
    return pl.CostEstimate(flops=1024, bytes_accessed=1024, transcendentals=0)


def vmem():
    return pl.BlockSpec(memory_space=pltpu.VMEM)


def smem():
    return pl.BlockSpec(memory_space=pltpu.SMEM)


def attend_forward(table, pieces, weight, cosine, sine, segments, heads, width, scale):
    count = len(pieces)
    length = cosine.shape[0]
    rank = weight.shape[0]
    shapes = [
        jax.ShapeDtypeStruct((length, heads * width), bf16),
        jax.ShapeDtypeStruct((length, width), bf16),
        jax.ShapeDtypeStruct((length, width), bf16),
        jax.ShapeDtypeStruct((length, heads * width), bf16),
        jax.ShapeDtypeStruct((length, heads * width), bf16),
    ]
    return pl.pallas_call(
        functools.partial(attend_forward_kernel, count, heads, width, rank, scale),
        out_shape=shapes,
        in_specs=[smem()] + [vmem()] * (count + 5),
        out_specs=[vmem()] * 5,
        compiler_params=pltpu.CompilerParams(vmem_limit_bytes=48 << 20),
        cost_estimate=brief(),
        name="attend_forward",
    )(table, *pieces, weight, cosine, sine, segments[:, None], segments[None, :])


def attend_backward_kernel(parts, heads, width, scale, *refs):
    table = refs[0]
    grads_in = refs[1 : 1 + parts]
    queries, keys, values, cosine, sine, seg_column, seg_row = refs[1 + parts : 8 + parts]
    query_there, pair_there, outer, query_out, key_total, value_total = refs[8 + parts :]
    length = queries.shape[0]
    count = table.shape[0]
    rows = length // count
    half = width // 2

    def there(r):
        return pl.ds(pl.multiple_of(table[r] * rows, rows), rows)

    r = 0
    for part in grads_in:
        for k in range(part.shape[0] // rows):
            outer[there(r), :] = part[k * rows : (k + 1) * rows, :]
            r += 1
    key_total[...] = jnp.zeros_like(key_total)
    value_total[...] = jnp.zeros_like(value_total)
    for start, size, low in query_blocks(length):
        high = start + size
        stacked = stack_heads(queries, start, size, heads, width)
        grads = stack_heads(outer, start, size, heads, width)
        permit = allowed(seg_column, seg_row, start, size, low, high)
        weights, total = weights_of(stacked, keys[low:high, :], permit, heads, scale)
        probs = weights / total
        prob_grad = right_transposed(grads, values[low:high, :])
        centre = jnp.sum(probs * prob_grad, axis=-1, keepdims=True)
        score_grad = (probs * (prob_grad - centre)).astype(bf16)
        query_grad = dot(score_grad, keys[low:high, :]) * scale
        key_total[low:high, :] += left_transposed(score_grad, stacked) * scale
        value_total[low:high, :] += left_transposed(probs.astype(bf16), grads)
        cos = cosine[start:high, :]
        sin = sine[start:high, :]
        for h in range(heads):
            first = query_grad[h * size : (h + 1) * size, :half]
            second = query_grad[h * size : (h + 1) * size, half:]
            query_out[start:high, h * width : h * width + half] = (
                first * cos + second * sin
            ).astype(bf16)
            query_out[start:high, h * width + half : (h + 1) * width] = (
                second * cos - first * sin
            ).astype(bf16)
    for r in range(count):
        here = slice(r * rows, (r + 1) * rows)
        query_there[here, :] = query_out[there(r), :]
        pair_there[here, :width] = key_total[there(r), :].astype(bf16)
        pair_there[here, width:] = value_total[there(r), :].astype(bf16)


def attend_backward(table, grads, queries, keys, values, cosine, sine, segments, heads, scale):
    parts = len(grads)
    length, width = keys.shape
    shapes = [
        jax.ShapeDtypeStruct((length, heads * width), bf16),
        jax.ShapeDtypeStruct((length, 2 * width), bf16),
    ]
    return pl.pallas_call(
        functools.partial(attend_backward_kernel, parts, heads, width, scale),
        out_shape=shapes,
        in_specs=[smem()] + [vmem()] * (parts + 7),
        out_specs=[vmem()] * 2,
        scratch_shapes=[
            pltpu.VMEM((length, heads * width), bf16),
            pltpu.VMEM((length, heads * width), bf16),
            pltpu.VMEM((length, width), f32),
            pltpu.VMEM((length, width), f32),
        ],
        compiler_params=pltpu.CompilerParams(vmem_limit_bytes=44 << 20),
        cost_estimate=brief(),
        name="attend_backward",
    )(
        table,
        *grads,
        queries,
        keys,
        values,
        cosine,
        sine,
        segments[:, None],
        segments[None, :],
    )


def rows_product_kernel(*refs):
    pieces, weight, out = refs[:-2], refs[-2], refs[-1]
    rows = pieces[0].shape[0]
    for p in range(0, len(pieces), 2):
        here = jnp.concatenate([pieces[p][...], pieces[p + 1][...]], axis=0)
        out[p * rows : (p + 2) * rows, :] = right_transposed(here, weight[...]).astype(out.dtype)


def rows_product(pieces, weight, kind):
    return pl.pallas_call(
        rows_product_kernel,
        out_shape=jax.ShapeDtypeStruct(
            (len(pieces) * pieces[0].shape[0], weight.shape[0]), kind
        ),
        in_specs=[vmem()] * (len(pieces) + 1),
        out_specs=vmem(),
        compiler_params=pltpu.CompilerParams(vmem_limit_bytes=32 << 20),
        cost_estimate=brief(),
        name="rows_product",
    )(*pieces, weight)


def latent_share_kernel(low, size, query_grads, pairs, weight, *refs):
    outs = refs[:-3]
    held, beside, sems = refs[-3:]
    rows = outs[0].shape[0]
    rank = weight.shape[0]
    here = pl.ds(low * rows, size)
    copies = [
        pltpu.make_async_copy(query_grads.at[here, :], held, sems.at[0]),
        pltpu.make_async_copy(pairs.at[here, :], beside, sems.at[1]),
    ]
    for copy in copies:
        copy.start()
    for copy in copies:
        copy.wait()
    for p in range(0, size // rows, 2):
        total = right_transposed(held[p * rows : (p + 2) * rows, :], weight[...])
        for k in range(2):
            outs[p + k][:, :rank] = total[k * rows : (k + 1) * rows].astype(bf16)
            outs[p + k][:, rank:] = beside[(p + k) * rows : (p + k + 1) * rows, :]


def latent_shares(clock, query_grads, pairs, weight, count):
    rows = query_grads.shape[0] // count
    rank, inner = weight.shape
    extra = pairs.shape[1]

    def share(low, high):
        size = (high - low) * rows
        return pl.pallas_call(
            functools.partial(latent_share_kernel, low, size),
            out_shape=[jax.ShapeDtypeStruct((rows, rank + extra), bf16)] * (high - low),
            in_specs=[any_space(), any_space(), vmem()],
            out_specs=[vmem()] * (high - low),
            scratch_shapes=[
                pltpu.VMEM((size, inner), bf16),
                pltpu.VMEM((size, extra), bf16),
                pltpu.SemaphoreType.DMA((2,)),
            ],
            compiler_params=pltpu.CompilerParams(vmem_limit_bytes=32 << 20),
            cost_estimate=brief(),
            name="latent_share",
        )(*clock(query_grads, pairs), weight)

    return share


def join_kernel(count, *refs):
    pieces, whole = refs[:count], refs[count]
    rows = pieces[0].shape[0]
    for r in range(count):
        whole[r * rows : (r + 1) * rows, :] = pieces[r][...]


def join(pieces):
    count = len(pieces)
    rows, columns = pieces[0].shape
    step = min(columns, 512)
    return pl.pallas_call(
        functools.partial(join_kernel, count),
        grid=(columns // step,),
        out_shape=jax.ShapeDtypeStruct((count * rows, columns), bf16),
        in_specs=[pl.BlockSpec((rows, step), lambda j: (0, j))] * count,
        out_specs=pl.BlockSpec((count * rows, step), lambda j: (0, j)),
        compiler_params=pltpu.CompilerParams(vmem_limit_bytes=17 << 20),
        cost_estimate=brief(),
        name="join",
    )(*pieces)


def any_space():
    return pl.BlockSpec(memory_space=pl.ANY)


def share_kernel(low, size, terms, transposed, *refs):
    lefts = refs[:terms]
    weights = refs[terms : 2 * terms]
    outs = refs[2 * terms : -terms - 1]
    held, sems = refs[-terms - 1 : -1], refs[-1]
    rows = outs[0].shape[0]
    copies = []
    for t in range(terms):
        copy = pltpu.make_async_copy(lefts[t].at[pl.ds(low * rows, size), :], held[t], sems.at[t])
        copy.start()
        copies.append(copy)
    for copy in copies:
        copy.wait()
    product = right_transposed if transposed else dot
    for p in range(size // (2 * rows)):
        here = pl.ds(2 * p * rows, 2 * rows)
        total = product(held[0][here, :], weights[0][...])
        for t in range(1, terms):
            total = total + product(held[t][here, :], weights[t][...])
        outs[2 * p][...] = total[:rows].astype(bf16)
        outs[2 * p + 1][...] = total[rows:].astype(bf16)


def shares(clock, lefts, weights, count, transposed):
    rows = lefts[0].shape[0] // count
    inner = lefts[0].shape[1]
    columns = weights[0].shape[0] if transposed else weights[0].shape[1]
    terms = len(lefts)

    def share(low, high):
        size = (high - low) * rows
        return pl.pallas_call(
            functools.partial(share_kernel, low, size, terms, transposed),
            out_shape=[jax.ShapeDtypeStruct((rows, columns), bf16)] * (high - low),
            in_specs=[any_space()] * terms + [vmem()] * terms,
            out_specs=[vmem()] * (high - low),
            scratch_shapes=[pltpu.VMEM((size, inner), bf16)] * terms
            + [pltpu.SemaphoreType.DMA((terms,))],
            compiler_params=pltpu.CompilerParams(vmem_limit_bytes=40 << 20),
            cost_estimate=brief(),
            name="share",
        )(*clock(*lefts, lefts[0])[:terms], *weights)

    return share


def feed_kernel(pairs, first, *refs):
    pieces = refs[: 2 * pairs]
    upper, gate_weight, up_weight = refs[2 * pairs : 2 * pairs + 3]
    rest = refs[2 * pairs + 3 :]
    outs, held, buffers, sems = rest[-8:-5], rest[-5], rest[-4:-1], rest[-1]
    rows = pieces[0].shape[0]

    def rows_of(p):
        return pl.ds((first + p) * 2 * rows, 2 * rows)

    loads = []
    for p in range(pairs):
        load = pltpu.make_async_copy(upper.at[rows_of(p), :], held.at[p], sems.at[3, p])
        load.start()
        loads.append(load)
    copies = []
    for p in range(pairs):
        here = jnp.concatenate([pieces[2 * p][...], pieces[2 * p + 1][...]], axis=0)
        gate = right_transposed(here, gate_weight[...])
        upward = right_transposed(here, up_weight[...])
        loads[p].wait()
        hidden_grad = held[p]
        sigmoid = jax.nn.sigmoid(gate)
        swish = gate * sigmoid
        results = (
            swish * upward,
            hidden_grad * upward * sigmoid * (1.0 + gate * (1.0 - sigmoid)),
            hidden_grad * swish,
        )
        for k, result in enumerate(results):
            buffers[k][p] = result.astype(bf16)
            copy = pltpu.make_async_copy(buffers[k].at[p], outs[k].at[rows_of(p), :], sems.at[k, p])
            copy.start()
            copies.append(copy)
    for copy in copies:
        copy.wait()


def feed(pieces, low, high, upper, gate_weight, up_weight, count, past):
    rows, dim = pieces[0].shape
    units = gate_weight.shape[0]
    pairs = (high - low) // 2
    operands = list(pieces[low:high]) + [upper, gate_weight, up_weight]
    specs = [vmem()] * (high - low) + [any_space()] + [vmem()] * 2
    aliases = {}
    if past is not None:
        aliases = {len(operands) + k: k for k in range(3)}
        operands += list(past)
        specs += [any_space()] * 3
    size = (high - low) * rows
    return pl.pallas_call(
        functools.partial(feed_kernel, pairs, low // 2),
        out_shape=[jax.ShapeDtypeStruct((count * rows, units), bf16)] * 3,
        in_specs=specs,
        out_specs=[any_space()] * 3,
        scratch_shapes=[pltpu.VMEM((pairs, 2 * rows, units), f32)]
        + [pltpu.VMEM((pairs, 2 * rows, units), bf16)] * 3
        + [pltpu.SemaphoreType.DMA((4, pairs))],
        input_output_aliases=aliases,
        compiler_params=pltpu.CompilerParams(vmem_limit_bytes=28 << 20),
        cost_estimate=brief(),
        name="feed",
    )(*operands)


def sum_kernel(*refs):
    total = refs[0][...].astype(f32)
    for ref in refs[1:-1]:
        total = total + ref[...].astype(f32)
    refs[-1][...] = total.astype(bf16)


def call(kernel, shapes, operands, name, scalars=0, limit=24, scratch=()):
    single = not isinstance(shapes, list)
    return pl.pallas_call(
        kernel,
        out_shape=shapes,
        in_specs=[smem()] * scalars + [vmem()] * (len(operands) - scalars),
        out_specs=vmem() if single else [vmem()] * len(shapes),
        scratch_shapes=list(scratch),
        compiler_params=pltpu.CompilerParams(vmem_limit_bytes=limit << 20),
        cost_estimate=brief(),
        name=name,
    )(*operands)


def shaped(shape, kind):
    return jax.ShapeDtypeStruct(shape, kind)


def add_rows(*values):
    return call(sum_kernel, shaped(values[0].shape, bf16), values, "add_rows")


def add_or_begin_kernel(inner, own, came, value, out):
    @pl.when(inner[0] == 1)
    def _():
        out[...] = (own[...].astype(f32) + came[...].astype(f32)).astype(bf16)

    @pl.when(inner[0] == 0)
    def _():
        out[...] = value[...]


def add_or_begin(inner, own, came, value):
    return call(
        add_or_begin_kernel,
        shaped(own.shape, bf16),
        [inner, own, came, value],
        "add_or_begin",
        scalars=1,
    )


def settle_kernel(at, *refs):
    inner, own, came = refs[:3]
    out, buffer, sem = refs[-3:]
    rows = own.shape[0]

    @pl.when(inner[0] == 1)
    def _():
        buffer[...] = own[...].astype(f32)

    @pl.when(inner[0] == 0)
    def _():
        buffer[...] = came[...].astype(f32)

    copy = pltpu.make_async_copy(buffer, out.at[pl.ds(at, rows), :], sem)
    copy.start()
    copy.wait()


def settle(inner, own, came, size, at, past):
    rows, columns = own.shape
    operands = [inner, own, came]
    specs = [smem(), vmem(), vmem()]
    aliases = {}
    if past is not None:
        aliases = {3: 0}
        operands.append(past)
        specs.append(any_space())
    return pl.pallas_call(
        functools.partial(settle_kernel, at),
        out_shape=shaped((size, columns), f32),
        in_specs=specs,
        out_specs=any_space(),
        scratch_shapes=[pltpu.VMEM((rows, columns), f32), pltpu.SemaphoreType.DMA],
        input_output_aliases=aliases,
        compiler_params=pltpu.CompilerParams(vmem_limit_bytes=24 << 20),
        cost_estimate=brief(),
        name="settle",
    )(*operands)


def product_kernel(left, right, *outs):
    total = left_transposed(left[...], right[...]).astype(bf16)
    rows = outs[0].shape[0]
    for k, out in enumerate(outs):
        out[...] = total[k * rows : (k + 1) * rows]


def weight_product(left, right, parts, step=512):
    tokens, units = left.shape
    columns = right.shape[1]
    step = min(step, columns)
    rows = units // parts
    return pl.pallas_call(
        product_kernel,
        grid=(columns // step,),
        out_shape=[shaped((rows, columns), bf16)] * parts,
        in_specs=[
            pl.BlockSpec((tokens, units), lambda j: (0, 0)),
            pl.BlockSpec((tokens, step), lambda j: (0, j)),
        ],
        out_specs=[pl.BlockSpec((rows, step), lambda j: (0, j))] * parts,
        compiler_params=pltpu.CompilerParams(vmem_limit_bytes=26 << 20),
        cost_estimate=brief(),
        name="weight_product",
    )(left, right)


def rotated(first, second, cosine, sine):
    return first * cosine - second * sine, second * cosine + first * sine


def enter_kernel(rank, width, x, gain, down, latent_gain, key, value, cosine, sine, *outs):
    normed, latent, packed = outs
    half = width // 2
    rows = x[...].astype(f32)
    low = (rows * inverse_rms(rows) * gain[...]).astype(bf16)
    normed[...] = low
    inner = dot(low, down[...])
    latent[...] = inner
    packed[:, :rank] = (inner * inverse_rms(inner) * latent_gain[...]).astype(bf16)
    keys = dot(low, key[...])
    first, second = rotated(keys[:, :half], keys[:, half:], cosine[...], sine[...])
    packed[:, rank : rank + half] = first.astype(bf16)
    packed[:, rank + half : rank + width] = second.astype(bf16)
    packed[:, rank + width :] = dot(low, value[...]).astype(bf16)


def enter(x, gain, down, latent_gain, key, value, cosine, sine):
    rows, dim = x.shape
    rank, width = down.shape[1], key.shape[1]
    return call(
        functools.partial(enter_kernel, rank, width),
        [shaped((rows, dim), bf16), shaped((rows, rank), f32), shaped((rows, rank + 2 * width), bf16)],
        [x, gain[None], down, latent_gain[None], key, value, cosine, sine],
        "enter",
    )


def summed(parts):
    total = parts[0][...].astype(f32)
    for part in parts[1:]:
        total = total + part[...].astype(f32)
    return total


def middle_kernel(x, gain, *refs):
    parts, (middle, normed) = refs[:-2], refs[-2:]
    total = x[...].astype(f32) + summed(parts)
    middle[...] = total
    normed[...] = (total * inverse_rms(total) * gain[...]).astype(bf16)


def middle_rows(x, gain, parts):
    shape = x.shape
    return call(
        middle_kernel,
        [shaped(shape, f32), shaped(shape, bf16)],
        [x, gain[None], *parts],
        "middle_rows",
    )


def lower_norm(value, gain, upper):
    scale = inverse_rms(value)
    scaled = upper * gain
    lower = scale * scaled - value * (scale * scale * scale) * jnp.mean(
        scaled * value, axis=-1, keepdims=True
    )
    return lower, jnp.sum(upper * value * scale, axis=0, keepdims=True)


def middle_back_kernel(middle, gain, cotangent, *refs):
    parts, (total, low, gain_part) = refs[:-3], refs[-3:]
    lower, gain_part[...] = lower_norm(middle[...], gain[...], summed(parts))
    result = cotangent[...].astype(f32) + lower
    total[...] = result
    low[...] = result.astype(bf16)


def middle_back(middle, gain, cotangent, parts):
    shape = middle.shape
    return call(
        middle_back_kernel,
        [shaped(shape, f32), shaped(shape, bf16), shaped((1, shape[1]), f32)],
        [middle, gain[None], cotangent, *parts],
        "middle_back",
    )


def latent_back_kernel(latent, gain, cosine, sine, *refs):
    parts, (packed, gain_part) = refs[:-2], refs[-2:]
    rank = latent.shape[1]
    total = summed(parts)
    lower, gain_part[...] = lower_norm(latent[...], gain[...], total[:, :rank])
    width = (total.shape[1] - rank) // 2
    half = width // 2
    packed[:, :rank] = lower.astype(bf16)
    first, second = rotated(
        total[:, rank : rank + half], total[:, rank + half : rank + width], cosine[...], -sine[...]
    )
    packed[:, rank : rank + half] = first.astype(bf16)
    packed[:, rank + half : rank + width] = second.astype(bf16)
    packed[:, rank + width :] = total[:, rank + width :].astype(bf16)


def latent_back(latent, gain, cosine, sine, parts):
    shape = parts[0].shape
    return call(
        latent_back_kernel,
        [shaped(shape, bf16), shaped((1, latent.shape[1]), f32)],
        [latent, gain[None], cosine, sine, *parts],
        "latent_back",
    )


def leave_kernel(packed, down, key, value, x, gain, upper, result, gain_part):
    rank, width = down.shape[1], key.shape[1]
    total = right_transposed(packed[:, :rank], down[...])
    total = total + right_transposed(packed[:, rank : rank + width], key[...])
    total = total + right_transposed(packed[:, rank + width :], value[...])
    lower, gain_part[...] = lower_norm(x[...].astype(f32), gain[...], total)
    result[...] = upper[...] + lower


def leave(packed, down, key, value, x, gain, upper):
    return call(
        leave_kernel,
        [shaped(x.shape, f32), shaped((1, x.shape[1]), f32)],
        [packed, down, key, value, x, gain[None], upper],
        "leave",
    )


def shared_kernel(count, table, normed, grads, *outs):
    rows = outs[0].shape[0]
    for r in range(count):
        there = pl.ds(pl.multiple_of(table[r] * rows, rows), rows)
        outs[r][...] = left_transposed(normed[:, there], grads[...]).astype(bf16)


def shared_shares(table, normed, grads):
    count = table.shape[0]
    rows = normed.shape[1] // count
    columns = grads.shape[1]
    return list(
        pl.pallas_call(
            functools.partial(shared_kernel, count),
            out_shape=[jax.ShapeDtypeStruct((rows, columns), bf16)] * count,
            in_specs=[smem(), vmem(), vmem()],
            out_specs=[vmem()] * count,
            compiler_params=pltpu.CompilerParams(vmem_limit_bytes=40 << 20),
            cost_estimate=brief(),
            name="shared_shares",
        )(table, normed, grads)
    )


def unpack_kernel(count, parts, table, *refs):
    pieces = refs[:count]
    outs = refs[count : count + len(parts)]
    buffers = refs[count + len(parts) : -1]
    sems = refs[-1]
    rows = pieces[0].shape[0]
    flying = []
    for r in range(count):
        slot = r % 2
        if r >= 2:
            for copy in flying[r - 2]:
                copy.wait()
        there = pl.ds(pl.multiple_of(table[r] * rows, rows), rows)
        copies = []
        for k, (low, high) in enumerate(parts):
            buffers[k][slot] = pieces[r][:, low:high].astype(f32)
            copy = pltpu.make_async_copy(
                buffers[k].at[slot], outs[k].at[there, :], sems.at[k, slot]
            )
            copy.start()
            copies.append(copy)
        flying.append(copies)
    for copies in flying[-2:]:
        for copy in copies:
            copy.wait()


def unpack(table, pieces, parts):
    count = len(pieces)
    rows = pieces[0].shape[0]
    return pl.pallas_call(
        functools.partial(unpack_kernel, count, parts),
        out_shape=[jax.ShapeDtypeStruct((count * rows, high - low), f32) for low, high in parts],
        in_specs=[smem()] + [vmem()] * count,
        out_specs=[any_space()] * len(parts),
        scratch_shapes=[pltpu.VMEM((2, rows, high - low), f32) for low, high in parts]
        + [pltpu.SemaphoreType.DMA((len(parts), 2))],
        compiler_params=pltpu.CompilerParams(vmem_limit_bytes=40 << 20),
        cost_estimate=brief(),
        name="unpack",
    )(table, *pieces)


def body(
    packs,
    group,
    block_input,
    segment_ids,
    positions,
    attention_gain,
    query_down,
    query_gain,
    query_up,
    key_proj,
    value_proj,
    out_proj,
    feed_gain,
    gate_weight,
    up_weight,
    down_weight,
    out_grad,
):
    plane = Plane(group)
    line = Line(packs)
    rows = block_input.shape[1]
    segments = segment_ids[0]
    places = positions[0]
    width = key_proj.shape[1]
    rank = query_down.shape[1]
    heads = query_up.shape[1] // width
    scale = 1.0 / math.sqrt(width)
    first_row = plane.me * rows

    gate_rows, up_rows = gate_weight.T, up_weight.T
    clock = Clock()
    belt = Belt(line, clock)
    fast = plane.fast
    move = plane.move
    hop_a, hop_b, hop_c = (plane.hop_a, plane.hop_b, plane.hop_c) if fast else (None,) * 3
    cotangent_rows = out_grad[0]

    x = block_input[0]
    if fast:
        cot_a = move(cotangent_rows, hop_a)
        cot_o = move(cotangent_rows, hop_c)
    own_places = lax.dynamic_slice_in_dim(places, first_row, rows, 0)
    own_cosine, own_sine = rotation(own_places, width)
    normed_rows, latent, packed = enter(
        x, attention_gain, query_down, query_gain, key_proj, value_proj, own_cosine, own_sine
    )
    cosine, sine = rotation(places, width)
    if fast:
        packed = clock(packed)
        a, b, s_o = move(packed, hop_a), move(packed, hop_b), move(packed, hop_c)
        cosine, sine = clock(cosine, sine)
        a, cot_a = clock(a, cot_a)
        c, a_o = move(a, hop_b), move(a, hop_c)
        cot_ao = move(cot_a, hop_c)
        b = clock(b)
        b_o = move(b, hop_c)
        c = clock(c)
        c_o = move(c, hop_c)
        cotangent_rows, cot_a = clock(cotangent_rows, cot_a)
        cot_b = move(cotangent_rows, hop_b)
        cot_c = move(cot_a, hop_b)
        pieces = [packed, s_o, a, a_o, b, b_o, c, c_o]
    else:
        pieces = plane.gather(packed)
    queries, keys, values, mixed, mixed_there = attend_forward(
        plane.table, pieces, query_up, cosine, sine, segments, heads, width, scale
    )

    def first_part(share):
        c, c_send = clock(*share(6, 8))
        c_came = move(c_send, hop_c)
        return c, c_came

    def second_part(share, c, c_came):
        c = clock(add_rows(c, clock(c_came)))
        c_in = move(c, hop_b)
        a, a_send, b, b_send = clock(*share(2, 6))
        b_came, a_came = move(b_send, hop_c), move(a_send, hop_c)
        b = clock(add_rows(b, clock(b_came)))
        b_in = move(b, hop_b)
        own, own_send = clock(*share(0, 2))
        own_came = move(own_send, hop_c)
        return c_in, a, a_came, b_in, own, own_came

    def third_part(c_in, a, a_came, b_in, own, own_came):
        c_in, a_came = clock(c_in, a_came)
        a = clock(add_rows(a, a_came, c_in))
        a_in = move(a, hop_a)
        return [own, own_came, b_in, a_in]

    share = shares(clock, [mixed_there], [out_proj], group, False)
    if fast:
        state = second_part(share, *first_part(share))
        cot_b, cot_c = clock(cot_b, cot_c)
        cot_bo, cot_co = move(cot_b, hop_c), move(cot_c, hop_c)
        parts = third_part(*state)
        cot_bo, cot_co = clock(cot_bo, cot_co)
        cot_pieces = [cotangent_rows, cot_o, cot_a, cot_ao, cot_b, cot_bo, cot_c, cot_co]
        hidden_grad = clock(rows_product(cot_pieces, down_weight, f32))
        parts = clock(*parts)
    else:
        cot_pieces = plane.gather(cotangent_rows)
        hidden_grad = rows_product(cot_pieces, down_weight, f32)
        parts = [plane.scatter(share(0, group))]
    middle, normed_mid_rows = middle_rows(x, feed_gain, parts)

    def feed_group(pieces, low, high, past):
        return clock(*feed(pieces, low, high, hidden_grad, gate_rows, up_rows, group, past))

    if fast:
        normed_mid_rows = clock(normed_mid_rows)
        a, b = move(normed_mid_rows, hop_a), move(normed_mid_rows, hop_b)
        s_o = move(normed_mid_rows, hop_c)
        cot_pieces[1] = clock(cot_pieces[1])
        cotangent = clock(join(cot_pieces))
        s_o = clock(s_o)
        mid_pieces = [normed_mid_rows, s_o]
        past = feed_group(mid_pieces, 0, 2, None)
        a, b = clock(a, b)
        c = move(a, hop_b)
        a_o, b_o = move(a, hop_c), move(b, hop_c)
        a_o, b_o = clock(a_o, b_o)
        mid_pieces += [a, a_o, b, b_o]
        past = feed_group(mid_pieces, 2, 6, past)
        c = clock(c)
        c_o = clock(move(c, hop_c))
        mid_pieces += [c, c_o]
        past = feed_group(mid_pieces, 6, 8, past)
    else:
        cotangent = join(cot_pieces)
        mid_pieces = plane.gather(normed_mid_rows)
        past = feed_group(mid_pieces, 0, group, None)
    hidden, gate_grad, upward_grad = past
    units = hidden.shape[1]
    dim = x.shape[1]

    share = shares(clock, [gate_grad, upward_grad], [gate_rows, up_rows], group, False)
    if fast:
        c, c_came = first_part(share)
        down_one, down_two = clock(*weight_product(clock(hidden), cotangent, 2))
        down_one, down_two = belt.begin(down_one), belt.begin(down_two)
        state = second_part(share, c, c_came)
        normed_mid = clock(join(mid_pieces))
        parts = third_part(*state)
        gate_one, gate_two = clock(*weight_product(clock(gate_grad), normed_mid, 2))
        parts = clock(*parts)
    else:
        normed_mid = join(mid_pieces)
        parts = [plane.scatter(share(0, group))]
    middle_grad, attention_grad, feed_gain_part = middle_back(
        middle, feed_gain, cotangent_rows, parts
    )
    if fast:
        attention_grad = clock(attention_grad)
        a, b = move(attention_grad, hop_a), move(attention_grad, hop_b)
        s_o = move(attention_grad, hop_c)
        up_one, up_two = clock(*weight_product(clock(upward_grad), normed_mid, 2))
        outer = [clock(rows_product([attention_grad, clock(s_o)], out_proj, bf16))]
        belt.cross(down_one)
        a, b = clock(a, b)
        c = move(a, hop_b)
        a_o, b_o = move(a, hop_c), move(b, hop_c)
        a_o, b_o = clock(a_o, b_o)
        outer.append(clock(rows_product([a, a_o, b, b_o], out_proj, bf16)))
        c = clock(c)
        c_o = clock(move(c, hop_c))
        outer.append(rows_product([c, c_o], out_proj, bf16))
        grad_pieces = [attention_grad, s_o, a, a_o, b, b_o, c, c_o]
    else:
        grad_pieces = plane.gather(attention_grad)
        outer = [rows_product(grad_pieces, out_proj, bf16)]

    query_pre_grad, pair_grads = clock(
        *attend_backward(
            plane.table, outer, queries, keys, values, cosine, sine, segments, heads, scale
        )
    )

    def out_proj_sum(number):
        return weight_product(clock(mixed_there), join(grad_pieces), number)

    def query_up_sum():
        return weight_product(join(pieces)[:, :rank], clock(query_pre_grad), 1)[0]

    share = latent_shares(clock, query_pre_grad, pair_grads, query_up, group)
    if fast:
        c, c_came = first_part(share)
        state = second_part(share, c, c_came)
        gate_one = belt.back(down_one, gate_one)
        belt.cross(down_two)
        parts = third_part(*state)
        out_one, out_two = clock(*out_proj_sum(2))
        parts = clock(*parts)
    else:
        parts = [plane.scatter(share(0, group))]

    packed_grad, query_gain_part = clock(
        *latent_back(latent, query_gain, own_cosine, own_sine, parts)
    )

    shared_pieces = shared_shares(plane.table, normed_rows, packed_grad)
    feed_share = shares(clock, [hidden], [down_weight], group, False)
    if fast:
        shared_pieces = clock(*shared_pieces)

        def share(low, high):
            return shared_pieces[low:high]

        state = second_part(share, *first_part(share))
        gate_two = belt.back(down_two, gate_two)
        down_gradient = belt.end(down_one, units)
        belt.cross(gate_one)
        parts = third_part(*state)
        query_sum = clock(query_up_sum())
        input_gradient, attention_gain_part = clock(
            *leave(
                clock(packed_grad),
                query_down,
                key_proj,
                value_proj,
                x,
                attention_gain,
                middle_grad,
            )
        )
        parts = clock(*parts)
        shared = belt.begin(clock(add_rows(*parts)))
        up_one = belt.back(gate_one, up_one)
        down_gradient = belt.end(down_two, units, units // 2, down_gradient)
        belt.cross(gate_two)
        belt.cross(shared)
        state = second_part(feed_share, *first_part(feed_share))
        parts = third_part(*state)
        up_two = belt.back(gate_two, up_two)
        gate_gradient = belt.end(gate_one, units)
        belt.cross(up_one)
        belt.back(shared)
        parts = clock(*parts)
        out_one = belt.begin(out_one)
        block_output = clock(add_rows(middle, *parts))
        gains = jnp.concatenate([attention_gain_part, query_gain_part, feed_gain_part], axis=1)
        gains = line.total(plane.total(gains), lambda left, right: left + right)[0]
        belt.back(up_one)
        gate_gradient = belt.end(gate_two, units, units // 2, gate_gradient)
        belt.cross(up_two)
        own = clock(jnp.where(belt.inner[0] == 1, shared["own"], clock(shared["came"])))
        a, b, s_o = move(own, hop_a), move(own, hop_b), move(own, hop_c)
        out_two = belt.begin(out_two)
        query_sum = belt.begin(query_sum)
        belt.cross(out_one)
        a, b = clock(a, b)
        c, a_o, b_o = move(a, hop_b), move(a, hop_c), move(b, hop_c)
        belt.back(up_two)
        up_gradient = belt.end(up_one, units)
        belt.cross(out_two)
        c = clock(c)
        c_o = clock(move(c, hop_c))
        belt.back(out_one)
        belt.cross(query_sum)
        up_gradient = belt.end(up_two, units, units // 2, up_gradient)
        belt.back(out_two)
        size = heads * width
        proj_gradient = belt.end(out_one, size)
        belt.back(query_sum)
        proj_gradient = belt.end(out_two, size, size // 2, proj_gradient)
        query_up_gradient = belt.end(query_sum, rank)
        shared_all = [own, s_o, a, a_o, b, b_o, c, c_o]
    else:
        input_gradient, attention_gain_part = leave(
            packed_grad, query_down, key_proj, value_proj, x, attention_gain, middle_grad
        )
        block_output = add_rows(middle, plane.scatter(feed_share(0, group)))
        gains = jnp.concatenate([attention_gain_part, query_gain_part, feed_gain_part], axis=1)
        gains = line.total(plane.total(gains), lambda left, right: left + right)[0]
        shared = line.total(plane.scatter(list(shared_pieces)).astype(bf16))
        shared_all = plane.gather(shared)
        down_gradient, gate_gradient, up_gradient, proj_gradient, query_up_gradient = (
            line.total(value).astype(f32)
            for value in (
                weight_product(hidden, cotangent, 1)[0],
                weight_product(gate_grad, normed_mid, 1)[0],
                weight_product(upward_grad, normed_mid, 1)[0],
                out_proj_sum(1)[0],
                query_up_sum(),
            )
        )
    query_down_gradient, key_proj_gradient, value_proj_gradient = unpack(
        plane.table,
        shared_all,
        ((0, rank), (rank, rank + width), (rank + width, rank + 2 * width)),
    )
    return (
        block_output[None],
        input_gradient[None],
        gains[:dim],
        query_down_gradient,
        gains[dim : dim + rank],
        query_up_gradient,
        key_proj_gradient,
        value_proj_gradient,
        proj_gradient,
        gains[dim + rank :],
        gate_gradient.T,
        up_gradient.T,
        down_gradient,
    )


def solution(mesh):
    in_specs = (
        P("tok", "head", None),
        P("tok", None),
        P("tok", None),
        P(),
        P(),
        P(),
        P(None, "head"),
        P(),
        P(),
        P("head", None),
        P(),
        P(None, "head"),
        P(None, "head"),
        P("head", None),
        P("tok", "head", None),
    )
    out_specs = (
        P("tok", "head", None),
        P("tok", "head", None),
        P(),
        P(),
        P(),
        P(None, "head"),
        P(),
        P(),
        P("head", None),
        P(),
        P(None, "head"),
        P(None, "head"),
        P("head", None),
    )
    sizes = dict(mesh.shape)
    return jax.shard_map(
        functools.partial(body, sizes["tok"], sizes["head"]),
        mesh=mesh,
        in_specs=in_specs,
        out_specs=out_specs,
        check_vma=False,
    )
```

time: 1400 us -> 655 us (0.47)
  waiting for transfers between devices: 982 us -> 302 us
  matrix products: 205 us -> 0 us
  Pallas kernels: 0 us -> 174 us
  starting transfers between devices: 0.5 us -> 121 us
  other arithmetic: 75.6 us -> 8.18 us
  blocking collectives: 40.4 us -> 0 us
  local copies, waits for them, and re-layouts: 62.5 us -> 36.5 us
    psum x2 -> x0, waiting for transfers between devices: 624 us -> none  [the longest x1 403 us: body(): lax.psum(query_up_gradient.astype(jnp.bfloat16), 'tok').astype(jnp.float32)]
    ppermute x0 -> x102, waiting for transfers between devices: none -> 302 us  [the longest x26 171 us: move(): return lax.ppermute(value, 'tok', pairs)]
    dot_general x45 -> x0, matrix products: 205 us -> none  [the longest x8 45.8 us: right_transposed(): lax.dot_general(left, right, (((1,), (1,)), ((), ())), preferred_element_...]
    reduce_scatter x5 -> x0, waiting for transfers between devices: 188 us -> none  [the longest x1 61.9 us: body(): lax.psum_scatter(jnp.dot(mixed, out_proj, preferred_element_type=jnp.floa...]
    pallas_call x0 -> x83, Pallas kernels: none -> 174 us  [the longest x42 42.2 us: call(): pl.pallas_call(kernel, out_shape=shapes, in_specs=[smem()] * scalars + [v...]
    all_gather x4 -> x0, waiting for transfers between devices: 169 us -> none  [the longest x1 47.6 us: body(): normed_in = lax.all_gather(normed_rows, 'head', axis=0, tiled=True)]
    ppermute x0 -> x102, starting transfers between devices: none -> 121 us  [the longest x26 75.4 us: move(): return lax.ppermute(value, 'tok', pairs)]
    psum x1 -> x0, blocking collectives: 40.4 us -> none  [body(): lax.psum((query_down_partial, key_proj_partial, value_proj_partial, atten...]
  transfers between devices with their start and end apart: 12 -> 102, of which waited for: 11 -> 44; matrix products, arithmetic and copies ran while one was open for 9% -> 2% of each run, Pallas kernels for 0% -> 22%
where the time goes in v1:
time: 655 us; the launch traced here: 645 us
  waiting for transfers between devices  302 us (46%)
  Pallas kernels  174 us (27%)
  starting transfers between devices  121 us (18%)
  local copies, waits for them, and re-layouts  36.5 us (6%)
  other arithmetic  8.18 us (1%)
    ppermute x26, waiting for transfers between devices, move(): return lax.ppermute(value, 'tok', pairs)  171 us
    ppermute x73, waiting for transfers between devices, move(): return lax.ppermute(value, 'head', hop)  128 us
    ppermute x26, starting transfers between devices, move(): return lax.ppermute(value, 'tok', pairs)  75.4 us
    pallas_call x42, Pallas kernels, call(): pl.pallas_call(kernel, out_shape=shapes, in_specs=[smem()] * scalars + [v...  42.2 us
    ppermute x73, starting transfers between devices, move(): return lax.ppermute(value, 'head', hop)  37.6 us
    unnamed x252, local copies, waits for them, and re-layouts  33.5 us
    pallas_call x5, Pallas kernels, weight_product(): pl.pallas_call(product_kernel, grid=(columns // step,), out_shape=[shaped...  24.9 us
    pallas_call x9, Pallas kernels, share(): pl.pallas_call(functools.partial(share_kernel, low, size, terms, transpos...  24.4 us
  transfers between devices with their start and end apart: 102, of which 44 were waited for; matrix products, arithmetic and copies ran while one was open for 2% of the time, Pallas kernels for 22%

profile of v1, /device:TPU:0, one launch (start us, length us, event | category | flops | bytes accessed | tf_op | source)
XLA Modules:
  0.0 644.6 jit_solution(3465504107918513077)
XLA Ops:
  16.6 4.3 multiply_sine_fusion
  20.9 8.4 %collective-permute-done.1.refs_3_.refs_2_ = bf16[192,1536]{1,0:T(8,128)(2,1)S(1)} collective-permute-done((bf16[192,1536]{1,0:T(8,128)(2,1)S(1)}, bf16[192,1536]{1,0:T(8,128)(2,1)S(1)}, u32[]{:S(2)}, u32[]{:S(2)}) %collective-permute-start.1) | collective-permute-done | bytes 589856 | tf_op jit(solution)/shard_map/ppermute | solution.py:103
  31.1 8.1 %collective-permute-done.6.refs_7_.refs_6_ = bf16[192,1536]{1,0:T(8,128)(2,1)S(1)} collective-permute-done((bf16[192,1536]{1,0:T(8,128)(2,1)S(1)}, bf16[192,1536]{1,0:T(8,128)(2,1)S(1)}, u32[]{:S(2)}, u32[]{:S(2)}) %collective-permute-start.6) | collective-permute-done | bytes 589856 | tf_op jit(solution)/shard_map/ppermute | solution.py:103
  41.4 10.2 %attend_forward.1 = (bf16[1536,512]{1,0:T(8,128)(2,1)}, bf16[1536,256]{1,0:T(8,128)(2,1)S(1)}, bf16[1536,256]{1,0:T(8,128)(2,1)}, bf16[1536,512]{1,0:T(8,128)(2,1)}, bf16[1536,512]{1,0:T(8,128)(2,1)}) custom-call(s32[8]{0:T(128)S(1)} %stack.35.refs_0_.table, bf16[192,1536]{1,0:T(8,128)(2,1)S(1)} %get-tuple-element.346.refs_1_.refs_0_, ...), custom_call_target="tpu_custom_call" | custom-call | flops 1024 | bytes 1024 | tf_op jit(solution)/shard_map/attend_forward/pallas_call | solution.py:273
  63.7 7.5 %collective-permute-done.15.refs_6_ = bf16[192,2048]{1,0:T(8,128)(2,1)S(1)} collective-permute-done((bf16[192,2048]{1,0:T(8,128)(2,1)S(1)}, bf16[192,2048]{1,0:T(8,128)(2,1)S(1)}, u32[]{:S(2)}, u32[]{:S(2)}) %collective-permute-start.15) | collective-permute-done | bytes 786464 | tf_op jit(solution)/shard_map/ppermute | solution.py:103
  71.2 8.4 %collective-permute-done.14.refs_4_ = bf16[192,2048]{1,0:T(8,128)(2,1)S(1)} collective-permute-done((bf16[192,2048]{1,0:T(8,128)(2,1)S(1)}, bf16[192,2048]{1,0:T(8,128)(2,1)S(1)}, u32[]{:S(2)}, u32[]{:S(2)}) %collective-permute-start.14) | collective-permute-done | bytes 786464 | tf_op jit(solution)/shard_map/ppermute | solution.py:103
  80.2 7.9 %collective-permute-done.12.refs_2_ = bf16[192,2048]{1,0:T(8,128)(2,1)S(1)} collective-permute-done((bf16[192,2048]{1,0:T(8,128)(2,1)S(1)}, bf16[192,2048]{1,0:T(8,128)(2,1)S(1)}, u32[]{:S(2)}, u32[]{:S(2)}) %collective-permute-start.12) | collective-permute-done | bytes 786464 | tf_op jit(solution)/shard_map/ppermute | solution.py:103
  90.5 5.1 rows_product.4.refs_2_.refs_4_
  95.6 11.8 %collective-permute-done.11.refs_2_ = bf16[192,2048]{1,0:T(8,128)(2,1)S(1)} collective-permute-done((bf16[192,2048]{1,0:T(8,128)(2,1)S(1)}, bf16[192,2048]{1,0:T(8,128)(2,1)S(1)}, u32[]{:S(2)}, u32[]{:S(2)}) %collective-permute-start.11) | collective-permute-done | bytes 786464 | tf_op jit(solution)/shard_map/ppermute | solution.py:103
  115.8 3.9 feed.3
  119.7 9.3 %collective-permute-done.22.refs_2_.refs_4_ = bf16[192,2048]{1,0:T(8,128)(2,1)S(1)} collective-permute-done((bf16[192,2048]{1,0:T(8,128)(2,1)S(1)}, bf16[192,2048]{1,0:T(8,128)(2,1)S(1)}, u32[]{:S(2)}, u32[]{:S(2)}) %collective-permute-start.22) | collective-permute-done | bytes 786464 | tf_op jit(solution)/shard_map/ppermute | solution.py:103
  135.0 8.2 %feed.4 = (bf16[1536,704]{1,0:T(8,128)(2,1)S(1)}, bf16[1536,704]{1,0:T(8,128)(2,1)S(1)}, bf16[1536,704]{1,0:T(8,128)(2,1)S(1)}) custom-call(bf16[192,2048]{1,0:T(8,128)(2,1)S(1)} %collective-permute-done.21.refs_0_.refs_2_, bf16[192,2048]{1,0:T(8,128)(2,1)S(1)} %collective-permute-done.25.refs_1_.refs_3_, ...), custom_call_target="tpu_custom_call", output_to_operand_aliasing={{0}: (7, {}), {1}: (8, {}), {2}: (9, {})} | custom-call | flops 1024 | bytes 1024 | tf_op jit(solution)/shard_map/feed/pallas_call | solution.py:560
  145.5 3.9 feed.5
  155.5 6.5 %weight_product.5 = (bf16[352,2048]{1,0:T(8,128)(2,1)}, bf16[352,2048]{1,0:T(8,128)(2,1)}) custom-call(bf16[1536,704]{1,0:T(8,128)(2,1)S(1)} %get-tuple-element.610.left.refs_0_, bf16[1536,2048]{1,0:T(8,128)(2,1)S(1)} %copy-done.11), custom_call_target="tpu_custom_call" | custom-call | flops 1024 | bytes 1024 | tf_op jit(solution)/shard_map/weight_product/pallas_call | solution.py:676
  162.3 6.6 %share.13 = (bf16[192,2048]{1,0:T(8,128)(2,1)S(1)}, bf16[192,2048]{1,0:T(8,128)(2,1)}, bf16[192,2048]{1,0:T(8,128)(2,1)S(1)}, bf16[192,2048]{1,0:T(8,128)(2,1)}) custom-call(bf16[1536,704]{1,0:T(8,128)(2,1)S(1)} %get-tuple-element.459.refs_0_.left, bf16[1536,704]{1,0:T(8,128)(2,1)S(1)} %get-tuple-element.469.refs_1_.left, bf16[704,2048]{1,0:T(8,128)(2,1)S(1)} %bitcast.29, ...), custom_call_target="tpu_custom_call" | custom-call | flops 1024 | bytes 1024 | tf_op jit(solution)/shard_map/share/pallas_call | solution.py:495
  175.9 3.7 share.14
  185.5 3.7 collective-permute-start.38
  189.2 5.9 weight_product.6
  204.9 5.9 weight_product.7
  214.1 6.7 %collective-permute-done.38.refs_1_ = bf16[352,2048]{1,0:T(8,128)(2,1)S(1)} collective-permute-done((bf16[352,2048]{1,0:T(8,128)(2,1)}, bf16[352,2048]{1,0:T(8,128)(2,1)S(1)}, u32[]{:S(2)}, u32[]{:S(2)}) %collective-permute-start.38) | collective-permute-done | bytes 1441824 | tf_op jit(solution)/shard_map/ppermute | solution.py:157
  229.0 7.2 %collective-permute-done.41.refs_0_.refs_6_ = bf16[192,2048]{1,0:T(8,128)(2,1)S(1)} collective-permute-done((bf16[192,2048]{1,0:T(8,128)(2,1)S(1)}, bf16[192,2048]{1,0:T(8,128)(2,1)S(1)}, u32[]{:S(2)}, u32[]{:S(2)}) %collective-permute-start.41) | collective-permute-done | bytes 786464 | tf_op jit(solution)/shard_map/ppermute | solution.py:103
  238.0 7.6 %collective-permute-start.49 = (bf16[352,2048]{1,0:T(8,128)(2,1)}, bf16[352,2048]{1,0:T(8,128)(2,1)}, u32[]{:S(2)}, u32[]{:S(2)}) collective-permute-start(bf16[352,2048]{1,0:T(8,128)(2,1)} %get-tuple-element.434.refs_0_), channel_id=1, source_target_pairs={{0,8},{24,16},{1,9},{25,17},{2,10},{26,18},{3,11},{27,19},{4,12},{... | collective-permute-start | bytes 4325384 | tf_op jit(solution)/shard_map/ppermute | solution.py:157
  246.7 8.4 %attend_backward.1 = (bf16[1536,512]{1,0:T(8,128)(2,1)S(1)}, bf16[1536,512]{1,0:T(8,128)(2,1)S(1)}) custom-call(s32[8]{0:T(128)S(1)} %stack.35.refs_0_.table, bf16[384,512]{1,0:T(8,128)(2,1)S(1)} %rows_product.5.refs_1_, bf16[768,512]{1,0:T(8,128)(2,1)S(1)} %rows_product.6.refs_2_, bf16[384,512]{1,0:T(8,128)(2,1)S(1)} %rows_product.7.refs_3_, ...), custom_call_target="tpu_custom_call" | custom-call | flops 1024 | bytes 1024 | tf_op jit(solution)/shard_map/attend_backward/pallas_call | solution.py:342
  271.3 4.2 collective-permute-done.49.refs_1_
  281.5 4.7 weight_product.8
  293.8 4.4 collective-permute-start.58
  301.7 28.5 %collective-permute-done.58.refs_2_.refs_1_ = bf16[352,2048]{1,0:T(8,128)(2,1)S(1)} collective-permute-done((bf16[352,2048]{1,0:T(8,128)(2,1)S(1)}, bf16[352,2048]{1,0:T(8,128)(2,1)S(1)}, u32[]{:S(2)}, u32[]{:S(2)}) %collective-permute-start.58) | collective-permute-done | bytes 1441824 | tf_op jit(solution)/shard_map/ppermute | solution.py:157
  333.9 4.3 collective-permute-start.62
  345.0 3.7 leave.1
  351.6 18.5 %collective-permute-done.62.refs_2_.refs_1_ = bf16[352,2048]{1,0:T(8,128)(2,1)S(1)} collective-permute-done((bf16[352,2048]{1,0:T(8,128)(2,1)S(1)}, bf16[352,2048]{1,0:T(8,128)(2,1)S(1)}, u32[]{:S(2)}, u32[]{:S(2)}) %collective-permute-start.62) | collective-permute-done | bytes 1441824 | tf_op jit(solution)/shard_map/ppermute | solution.py:157
  372.3 14.0 %collective-permute-done.61.refs_1_ = bf16[256,1536]{1,0:T(8,128)(2,1)S(1)} collective-permute-done((bf16[256,1536]{1,0:T(8,128)(2,1)S(1)}, bf16[256,1536]{1,0:T(8,128)(2,1)S(1)}, u32[]{:S(2)}, u32[]{:S(2)}) %collective-permute-start.61) | collective-permute-done | bytes 786464 | tf_op jit(solution)/shard_map/ppermute | solution.py:157
  388.8 4.4 collective-permute-start.72
  399.5 8.9 %collective-permute-done.68.refs_2_ = bf16[192,2048]{1,0:T(8,128)(2,1)S(1)} collective-permute-done((bf16[192,2048]{1,0:T(8,128)(2,1)S(1)}, bf16[192,2048]{1,0:T(8,128)(2,1)S(1)}, u32[]{:S(2)}, u32[]{:S(2)}) %collective-permute-start.68) | collective-permute-done | bytes 786464 | tf_op jit(solution)/shard_map/ppermute | solution.py:103
  415.1 10.1 %collective-permute-done.72.refs_2_.refs_1_ = bf16[352,2048]{1,0:T(8,128)(2,1)S(1)} collective-permute-done((bf16[352,2048]{1,0:T(8,128)(2,1)S(1)}, bf16[352,2048]{1,0:T(8,128)(2,1)S(1)}, u32[]{:S(2)}, u32[]{:S(2)}) %collective-permute-start.72) | collective-permute-done | bytes 1441824 | tf_op jit(solution)/shard_map/ppermute | solution.py:157
  429.2 4.0 collective-permute-start.81
  436.8 8.7 %collective-permute-done.70.refs_4_ = bf16[192,2048]{1,0:T(8,128)(2,1)} collective-permute-done((bf16[192,2048]{1,0:T(8,128)(2,1)}, bf16[192,2048]{1,0:T(8,128)(2,1)}, u32[]{:S(2)}, u32[]{:S(2)}) %collective-permute-start.70) | collective-permute-done | bytes 786464 | tf_op jit(solution)/shard_map/ppermute | solution.py:103
  445.5 4.2 collective-permute-start.86
  456.4 9.6 %collective-permute-done.81.refs_2_.refs_1_ = bf16[352,2048]{1,0:T(8,128)(2,1)} collective-permute-done((bf16[352,2048]{1,0:T(8,128)(2,1)}, bf16[352,2048]{1,0:T(8,128)(2,1)}, u32[]{:S(2)}, u32[]{:S(2)}) %collective-permute-start.81) | collective-permute-done | bytes 1441824 | tf_op jit(solution)/shard_map/ppermute | solution.py:157
  472.2 8.9 %collective-permute-done.80 = bf16[256,1536]{1,0:T(8,128)(2,1)} collective-permute-done((bf16[256,1536]{1,0:T(8,128)(2,1)}, bf16[256,1536]{1,0:T(8,128)(2,1)}, u32[]{:S(2)}, u32[]{:S(2)}) %collective-permute-start.80) | collective-permute-done | bytes 786464 | tf_op jit(solution)/shard_map/ppermute | solution.py:157
  486.0 4.6 collective-permute-start.90
  490.9 9.5 %collective-permute-done.85.refs_4_ = bf16[256,1536]{1,0:T(8,128)(2,1)S(1)} collective-permute-done((bf16[256,1536]{1,0:T(8,128)(2,1)S(1)}, bf16[256,1536]{1,0:T(8,128)(2,1)S(1)}, u32[]{:S(2)}, u32[]{:S(2)}) %collective-permute-start.85) | collective-permute-done | bytes 786464 | tf_op jit(solution)/shard_map/ppermute | solution.py:103
  503.4 16.8 %collective-permute-start.94 = (bf16[1024,512]{1,0:T(8,128)(2,1)S(1)}, bf16[1024,512]{1,0:T(8,128)(2,1)S(1)}, u32[]{:S(2)}, u32[]{:S(2)}) collective-permute-start(bf16[1024,512]{1,0:T(8,128)(2,1)S(1)} %copy-done.39), channel_id=1, source_target_pairs={{0,8},{24,16},{1,9},{25,17},{2,10},{26,18},{3,11},{27,19},{4,12},{... | collective-permute-start | bytes 3145736 | tf_op jit(solution)/shard_map/ppermute | solution.py:157
  528.0 11.9 %collective-permute-done.94.refs_1_ = bf16[1024,512]{1,0:T(8,128)(2,1)S(1)} collective-permute-done((bf16[1024,512]{1,0:T(8,128)(2,1)S(1)}, bf16[1024,512]{1,0:T(8,128)(2,1)S(1)}, u32[]{:S(2)}, u32[]{:S(2)}) %collective-permute-start.94) | collective-permute-done | bytes 1048608 | tf_op jit(solution)/shard_map/ppermute | solution.py:157
  551.8 6.1 collective-permute-start.77
  567.2 13.9 %collective-permute-done.97.refs_2_ = bf16[256,2048]{1,0:T(8,128)(2,1)} collective-permute-done((bf16[256,2048]{1,0:T(8,128)(2,1)S(1)}, bf16[256,2048]{1,0:T(8,128)(2,1)}, u32[]{:S(2)}, u32[]{:S(2)}) %collective-permute-start.97) | collective-permute-done | bytes 1048608 | tf_op jit(solution)/shard_map/ppermute | solution.py:157
  591.7 5.8 unpack.1
  597.5 23.0 %collective-permute-done.101.refs_2_ = bf16[256,2048]{1,0:T(8,128)(2,1)S(1)} collective-permute-done((bf16[256,2048]{1,0:T(8,128)(2,1)S(1)}, bf16[256,2048]{1,0:T(8,128)(2,1)S(1)}, u32[]{:S(2)}, u32[]{:S(2)}) %collective-permute-start.101) | collective-permute-done | bytes 1048608 | tf_op jit(solution)/shard_map/ppermute | solution.py:157
  622.0 20.7 %collective-permute-done.100.refs_2_ = bf16[1024,512]{1,0:T(8,128)(2,1)S(1)} collective-permute-done((bf16[1024,512]{1,0:T(8,128)(2,1)S(1)}, bf16[1024,512]{1,0:T(8,128)(2,1)S(1)}, u32[]{:S(2)}, u32[]{:S(2)}) %collective-permute-start.100) | collective-permute-done | bytes 1048608 | tf_op jit(solution)/shard_map/ppermute | solution.py:157
  (509 shorter events, 228.9 us)
Async XLA Ops:
  0.6 28.7 %collective-permute-start.2 = (bf16[192,2048]{1,0:T(8,128)(2,1)}, bf16[192,2048]{1,0:T(8,128)(2,1)S(1)}, u32[]{:S(2)}, u32[]{:S(2)}) collective-permute-start(bf16[192,2048]{1,0:T(8,128)(2,1)} %bitcast.37), channel_id=1, source_target_pairs={{0,2},{1,5},{2,0},{3,7},{4,6},{5,1},{6,4},{7,3},{8,10},{9,13},{10,... | collective-permute-start | bytes 2359304 | tf_op jit(solution)/shard_map/ppermute | solution.py:103
  59.6 20.1 %collective-permute-start.14 = (bf16[192,2048]{1,0:T(8,128)(2,1)S(1)}, bf16[192,2048]{1,0:T(8,128)(2,1)S(1)}, u32[]{:S(2)}, u32[]{:S(2)}) collective-permute-start(bf16[192,2048]{1,0:T(8,128)(2,1)S(1)} %bitcast.38), channel_id=1, source_target_pairs={{0,4},{1,3},{2,6},{3,1},{4,0},{5,7},{6,2},{7,5},{8,12},{9,11},{10,... | collective-permute-start | bytes 2359304 | tf_op jit(solution)/shard_map/ppermute | solution.py:103
  61.3 26.8 %collective-permute-start.12 = (bf16[192,2048]{1,0:T(8,128)(2,1)S(1)}, bf16[192,2048]{1,0:T(8,128)(2,1)S(1)}, u32[]{:S(2)}, u32[]{:S(2)}) collective-permute-start(bf16[192,2048]{1,0:T(8,128)(2,1)S(1)} %add_rows.33), channel_id=1, source_target_pairs={{0,4},{1,3},{2,6},{3,1},{4,0},{5,7},{6,2},{7,5},{8,12},{9,11},{10,... | collective-permute-start | bytes 2359304 | tf_op jit(solution)/shard_map/ppermute | solution.py:103
  61.6 26.5 %collective-permute-start.13 = (bf16[192,2048]{1,0:T(8,128)(2,1)S(1)}, bf16[192,2048]{1,0:T(8,128)(2,1)S(1)}, u32[]{:S(2)}, u32[]{:S(2)}) collective-permute-start(bf16[192,2048]{1,0:T(8,128)(2,1)S(1)} %get-tuple-element.377), channel_id=1, source_target_pairs={{0,1},{1,0},{2,3},{3,2},{4,5},{5,4},{6,7},{7,6},{8,9},{9,8},{10,11... | collective-permute-start | bytes 2359304 | tf_op jit(solution)/shard_map/ppermute | solution.py:103
  88.1 19.3 %collective-permute-start.11 = (bf16[192,2048]{1,0:T(8,128)(2,1)S(1)}, bf16[192,2048]{1,0:T(8,128)(2,1)S(1)}, u32[]{:S(2)}, u32[]{:S(2)}) collective-permute-start(bf16[192,2048]{1,0:T(8,128)(2,1)S(1)} %add_rows.34), channel_id=1, source_target_pairs={{0,4},{1,3},{2,6},{3,1},{4,0},{5,7},{6,2},{7,5},{8,12},{9,11},{10,... | collective-permute-start | bytes 2359304 | tf_op jit(solution)/shard_map/ppermute | solution.py:103
  88.7 19.3 %collective-permute-start.16 = (bf16[192,2048]{1,0:T(8,128)(2,1)S(1)}, bf16[192,2048]{1,0:T(8,128)(2,1)S(1)}, u32[]{:S(2)}, u32[]{:S(2)}) collective-permute-start(bf16[192,2048]{1,0:T(8,128)(2,1)S(1)} %add_rows.35), channel_id=1, source_target_pairs={{0,2},{1,5},{2,0},{3,7},{4,6},{5,1},{6,4},{7,3},{8,10},{9,13},{10,... | collective-permute-start | bytes 2359304 | tf_op jit(solution)/shard_map/ppermute | solution.py:103
  90.5 17.6 %collective-permute-start.10 = (bf16[192,2048]{1,0:T(8,128)(2,1)S(1)}, bf16[192,2048]{1,0:T(8,128)(2,1)S(1)}, u32[]{:S(2)}, u32[]{:S(2)}) collective-permute-start(bf16[192,2048]{1,0:T(8,128)(2,1)S(1)} %get-tuple-element.376), channel_id=1, source_target_pairs={{0,1},{1,0},{2,3},{3,2},{4,5},{5,4},{6,7},{7,6},{8,9},{9,8},{10,11... | collective-permute-start | bytes 2359304 | tf_op jit(solution)/shard_map/ppermute | solution.py:103
  109.4 19.7 %collective-permute-start.22 = (bf16[192,2048]{1,0:T(8,128)(2,1)S(1)}, bf16[192,2048]{1,0:T(8,128)(2,1)S(1)}, u32[]{:S(2)}, u32[]{:S(2)}) collective-permute-start(bf16[192,2048]{1,0:T(8,128)(2,1)S(1)} %get-tuple-element.393.refs_0_), channel_id=1, source_target_pairs={{0,4},{1,3},{2,6},{3,1},{4,0},{5,7},{6,2},{7,5},{8,12},{9,11},{10,... | collective-permute-start | bytes 2359304 | tf_op jit(solution)/shard_map/ppermute | solution.py:103
  109.7 19.4 %collective-permute-start.21 = (bf16[192,2048]{1,0:T(8,128)(2,1)S(1)}, bf16[192,2048]{1,0:T(8,128)(2,1)S(1)}, u32[]{:S(2)}, u32[]{:S(2)}) collective-permute-start(bf16[192,2048]{1,0:T(8,128)(2,1)S(1)} %get-tuple-element.393.refs_0_), channel_id=1, source_target_pairs={{0,2},{1,5},{2,0},{3,7},{4,6},{5,1},{6,4},{7,3},{8,10},{9,13},{10,... | collective-permute-start | bytes 2359304 | tf_op jit(solution)/shard_map/ppermute | solution.py:103
  175.2 20.0 %collective-permute-start.31 = (bf16[192,2048]{1,0:T(8,128)(2,1)}, bf16[192,2048]{1,0:T(8,128)(2,1)}, u32[]{:S(2)}, u32[]{:S(2)}) collective-permute-start(bf16[192,2048]{1,0:T(8,128)(2,1)} %add_rows.37), channel_id=1, source_target_pairs={{0,4},{1,3},{2,6},{3,1},{4,0},{5,7},{6,2},{7,5},{8,12},{9,11},{10,... | collective-permute-start | bytes 2359304 | tf_op jit(solution)/shard_map/ppermute | solution.py:103
  185.5 35.3 %collective-permute-start.38 = (bf16[352,2048]{1,0:T(8,128)(2,1)}, bf16[352,2048]{1,0:T(8,128)(2,1)S(1)}, u32[]{:S(2)}, u32[]{:S(2)}) collective-permute-start(bf16[352,2048]{1,0:T(8,128)(2,1)} %get-tuple-element.433.refs_0_), channel_id=1, source_target_pairs={{0,8},{24,16},{1,9},{25,17},{2,10},{26,18},{3,11},{27,19},{4,12},{... | collective-permute-start | bytes 4325384 | tf_op jit(solution)/shard_map/ppermute | solution.py:157
  202.6 21.0 %collective-permute-start.37 = (bf16[192,2048]{1,0:T(8,128)(2,1)S(1)}, bf16[192,2048]{1,0:T(8,128)(2,1)S(1)}, u32[]{:S(2)}, u32[]{:S(2)}) collective-permute-start(bf16[192,2048]{1,0:T(8,128)(2,1)S(1)} %get-tuple-element.468.refs_0_), channel_id=1, source_target_pairs={{0,4},{1,3},{2,6},{3,1},{4,0},{5,7},{6,2},{7,5},{8,12},{9,11},{10,... | collective-permute-start | bytes 2359304 | tf_op jit(solution)/shard_map/ppermute | solution.py:103
  203.1 20.5 %collective-permute-start.36 = (bf16[192,2048]{1,0:T(8,128)(2,1)S(1)}, bf16[192,2048]{1,0:T(8,128)(2,1)S(1)}, u32[]{:S(2)}, u32[]{:S(2)}) collective-permute-start(bf16[192,2048]{1,0:T(8,128)(2,1)S(1)} %get-tuple-element.468.refs_0_), channel_id=1, source_target_pairs={{0,2},{1,5},{2,0},{3,7},{4,6},{5,1},{6,4},{7,3},{8,10},{9,13},{10,... | collective-permute-start | bytes 2359304 | tf_op jit(solution)/shard_map/ppermute | solution.py:103
  236.2 33.0 %collective-permute-start.50 = (bf16[352,2048]{1,0:T(8,128)(2,1)}, bf16[352,2048]{1,0:T(8,128)(2,1)}, u32[]{:S(2)}, u32[]{:S(2)}) collective-permute-start(bf16[352,2048]{1,0:T(8,128)(2,1)} %add_rows.39.own), channel_id=1, source_target_pairs={{8,16},{16,8},{9,17},{17,9},{10,18},{18,10},{11,19},{19,11},{12,20... | collective-permute-start | bytes 4325384 | tf_op jit(solution)/shard_map/ppermute | solution.py:157
  238.0 37.5 %collective-permute-start.49 = (bf16[352,2048]{1,0:T(8,128)(2,1)}, bf16[352,2048]{1,0:T(8,128)(2,1)}, u32[]{:S(2)}, u32[]{:S(2)}) collective-permute-start(bf16[352,2048]{1,0:T(8,128)(2,1)} %get-tuple-element.434.refs_0_), channel_id=1, source_target_pairs={{0,8},{24,16},{1,9},{25,17},{2,10},{26,18},{3,11},{27,19},{4,12},{... | collective-permute-start | bytes 4325384 | tf_op jit(solution)/shard_map/ppermute | solution.py:157
  267.6 18.6 %collective-permute-start.46 = (bf16[192,1536]{1,0:T(8,128)(2,1)S(1)}, bf16[192,1536]{1,0:T(8,128)(2,1)S(1)}, u32[]{:S(2)}, u32[]{:S(2)}) collective-permute-start(bf16[192,1536]{1,0:T(8,128)(2,1)S(1)} %add_rows.41), channel_id=1, source_target_pairs={{0,4},{1,3},{2,6},{3,1},{4,0},{5,7},{6,2},{7,5},{8,12},{9,11},{10,... | collective-permute-start | bytes 1769480 | tf_op jit(solution)/shard_map/ppermute | solution.py:103
  293.8 36.4 %collective-permute-start.58 = (bf16[352,2048]{1,0:T(8,128)(2,1)S(1)}, bf16[352,2048]{1,0:T(8,128)(2,1)S(1)}, u32[]{:S(2)}, u32[]{:S(2)}) collective-permute-start(bf16[352,2048]{1,0:T(8,128)(2,1)S(1)} %add_or_begin.4.refs_1_), channel_id=1, source_target_pairs={{0,8},{24,16},{8,0},{16,24},{1,9},{25,17},{9,1},{17,25},{2,10},{26... | collective-permute-start | bytes 4325384 | tf_op jit(solution)/shard_map/ppermute | solution.py:157
  298.5 33.8 %collective-permute-start.57 = (bf16[256,1536]{1,0:T(8,128)(2,1)S(1)}, bf16[256,1536]{1,0:T(8,128)(2,1)S(1)}, u32[]{:S(2)}, u32[]{:S(2)}) collective-permute-start(bf16[256,1536]{1,0:T(8,128)(2,1)S(1)} %get-tuple-element.562), channel_id=1, source_target_pairs={{0,1},{1,0},{2,3},{3,2},{4,5},{5,4},{6,7},{7,6},{8,9},{9,8},{10,11... | collective-permute-start | bytes 2359304 | tf_op jit(solution)/shard_map/ppermute | solution.py:103
  299.0 33.4 %collective-permute-start.56 = (bf16[256,1536]{1,0:T(8,128)(2,1)S(1)}, bf16[256,1536]{1,0:T(8,128)(2,1)S(1)}, u32[]{:S(2)}, u32[]{:S(2)}) collective-permute-start(bf16[256,1536]{1,0:T(8,128)(2,1)S(1)} %add_rows.44), channel_id=1, source_target_pairs={{0,4},{1,3},{2,6},{3,1},{4,0},{5,7},{6,2},{7,5},{8,12},{9,11},{10,... | collective-permute-start | bytes 2359304 | tf_op jit(solution)/shard_map/ppermute | solution.py:103
  301.0 47.7 %collective-permute-start.55 = (bf16[256,1536]{1,0:T(8,128)(2,1)S(1)}, bf16[256,1536]{1,0:T(8,128)(2,1)S(1)}, u32[]{:S(2)}, u32[]{:S(2)}) collective-permute-start(bf16[256,1536]{1,0:T(8,128)(2,1)S(1)} %add_rows.45), channel_id=1, source_target_pairs={{0,4},{1,3},{2,6},{3,1},{4,0},{5,7},{6,2},{7,5},{8,12},{9,11},{10,... | collective-permute-start | bytes 2359304 | tf_op jit(solution)/shard_map/ppermute | solution.py:103
  330.2 18.5 %collective-permute-start.54 = (bf16[256,1536]{1,0:T(8,128)(2,1)S(1)}, bf16[256,1536]{1,0:T(8,128)(2,1)S(1)}, u32[]{:S(2)}, u32[]{:S(2)}) collective-permute-start(bf16[256,1536]{1,0:T(8,128)(2,1)S(1)} %get-tuple-element.561), channel_id=1, source_target_pairs={{0,1},{1,0},{2,3},{3,2},{4,5},{5,4},{6,7},{7,6},{8,9},{9,8},{10,11... | collective-permute-start | bytes 2359304 | tf_op jit(solution)/shard_map/ppermute | solution.py:103
  333.1 18.2 %collective-permute-start.63 = (bf16[352,2048]{1,0:T(8,128)(2,1)S(1)}, bf16[352,2048]{1,0:T(8,128)(2,1)S(1)}, u32[]{:S(2)}, u32[]{:S(2)}) collective-permute-start(bf16[352,2048]{1,0:T(8,128)(2,1)S(1)} %add_rows.46.own), channel_id=1, source_target_pairs={{8,16},{16,8},{9,17},{17,9},{10,18},{18,10},{11,19},{19,11},{12,20... | collective-permute-start | bytes 4325384 | tf_op jit(solution)/shard_map/ppermute | solution.py:157
  333.9 36.3 %collective-permute-start.62 = (bf16[352,2048]{1,0:T(8,128)(2,1)S(1)}, bf16[352,2048]{1,0:T(8,128)(2,1)S(1)}, u32[]{:S(2)}, u32[]{:S(2)}) collective-permute-start(bf16[352,2048]{1,0:T(8,128)(2,1)S(1)} %add_or_begin.5.refs_1_), channel_id=1, source_target_pairs={{0,8},{24,16},{8,0},{16,24},{1,9},{25,17},{9,1},{17,25},{2,10},{26... | collective-permute-start | bytes 4325384 | tf_op jit(solution)/shard_map/ppermute | solution.py:157
  349.3 36.9 %collective-permute-start.61 = (bf16[256,1536]{1,0:T(8,128)(2,1)S(1)}, bf16[256,1536]{1,0:T(8,128)(2,1)S(1)}, u32[]{:S(2)}, u32[]{:S(2)}) collective-permute-start(bf16[256,1536]{1,0:T(8,128)(2,1)S(1)} %add_rows.48.refs_0_), channel_id=1, source_target_pairs={{0,8},{24,16},{1,9},{25,17},{2,10},{26,18},{3,11},{27,19},{4,12},{... | collective-permute-start | bytes 2359304 | tf_op jit(solution)/shard_map/ppermute | solution.py:157
  388.0 25.2 %collective-permute-start.73 = (bf16[352,2048]{1,0:T(8,128)(2,1)S(1)}, bf16[352,2048]{1,0:T(8,128)(2,1)S(1)}, u32[]{:S(2)}, u32[]{:S(2)}) collective-permute-start(bf16[352,2048]{1,0:T(8,128)(2,1)S(1)} %add_rows.49.own), channel_id=1, source_target_pairs={{8,16},{16,8},{9,17},{17,9},{10,18},{18,10},{11,19},{19,11},{12,20... | collective-permute-start | bytes 4325384 | tf_op jit(solution)/shard_map/ppermute | solution.py:157
  388.8 36.4 %collective-permute-start.72 = (bf16[352,2048]{1,0:T(8,128)(2,1)S(1)}, bf16[352,2048]{1,0:T(8,128)(2,1)S(1)}, u32[]{:S(2)}, u32[]{:S(2)}) collective-permute-start(bf16[352,2048]{1,0:T(8,128)(2,1)S(1)} %add_or_begin.6.refs_1_), channel_id=1, source_target_pairs={{0,8},{24,16},{8,0},{16,24},{1,9},{25,17},{9,1},{17,25},{2,10},{26... | collective-permute-start | bytes 4325384 | tf_op jit(solution)/shard_map/ppermute | solution.py:157
  398.6 34.9 %collective-permute-start.71 = (bf16[256,1536]{1,0:T(8,128)(2,1)S(1)}, bf16[256,1536]{1,0:T(8,128)(2,1)S(1)}, u32[]{:S(2)}, u32[]{:S(2)}) collective-permute-start(bf16[256,1536]{1,0:T(8,128)(2,1)S(1)} %add_rows.50.refs_0_), channel_id=1, source_target_pairs={{8,16},{16,8},{9,17},{17,9},{10,18},{18,10},{11,19},{19,11},{12,20... | collective-permute-start | bytes 2359304 | tf_op jit(solution)/shard_map/ppermute | solution.py:157
  408.4 26.2 %collective-permute-start.67 = (bf16[192,2048]{1,0:T(8,128)(2,1)S(1)}, bf16[192,2048]{1,0:T(8,128)(2,1)S(1)}, u32[]{:S(2)}, u32[]{:S(2)}) collective-permute-start(bf16[192,2048]{1,0:T(8,128)(2,1)S(1)} %add_rows.52), channel_id=1, source_target_pairs={{0,4},{1,3},{2,6},{3,1},{4,0},{5,7},{6,2},{7,5},{8,12},{9,11},{10,... | collective-permute-start | bytes 2359304 | tf_op jit(solution)/shard_map/ppermute | solution.py:103
  427.3 27.4 %collective-permute-start.82 = (bf16[352,2048]{1,0:T(8,128)(2,1)S(1)}, bf16[352,2048]{1,0:T(8,128)(2,1)}, u32[]{:S(2)}, u32[]{:S(2)}) collective-permute-start(bf16[352,2048]{1,0:T(8,128)(2,1)S(1)} %add_rows.54.refs_0_), channel_id=1, source_target_pairs={{8,16},{16,8},{9,17},{17,9},{10,18},{18,10},{11,19},{19,11},{12,20... | collective-permute-start | bytes 4325384 | tf_op jit(solution)/shard_map/ppermute | solution.py:157
  429.2 36.8 %collective-permute-start.81 = (bf16[352,2048]{1,0:T(8,128)(2,1)}, bf16[352,2048]{1,0:T(8,128)(2,1)}, u32[]{:S(2)}, u32[]{:S(2)}) collective-permute-start(bf16[352,2048]{1,0:T(8,128)(2,1)} %add_or_begin.7.refs_1_), channel_id=1, source_target_pairs={{0,8},{24,16},{8,0},{16,24},{1,9},{25,17},{9,1},{17,25},{2,10},{26... | collective-permute-start | bytes 4325384 | tf_op jit(solution)/shard_map/ppermute | solution.py:157
  435.5 45.6 %collective-permute-start.80 = (bf16[256,1536]{1,0:T(8,128)(2,1)}, bf16[256,1536]{1,0:T(8,128)(2,1)}, u32[]{:S(2)}, u32[]{:S(2)}) collective-permute-start(bf16[256,1536]{1,0:T(8,128)(2,1)} %add_rows.55), channel_id=1, source_target_pairs={{8,0},{16,24},{9,1},{17,25},{10,2},{18,26},{11,3},{19,27},{12,4},{... | collective-permute-start | bytes 2359304 | tf_op jit(solution)/shard_map/ppermute | solution.py:157
  445.5 40.5 %collective-permute-start.86 = (bf16[256,2048]{1,0:T(8,128)(2,1)}, bf16[256,2048]{1,0:T(8,128)(2,1)S(1)}, u32[]{:S(2)}, u32[]{:S(2)}) collective-permute-start(bf16[256,2048]{1,0:T(8,128)(2,1)} %copy-done.85), channel_id=1, source_target_pairs={{0,8},{24,16},{1,9},{25,17},{2,10},{26,18},{3,11},{27,19},{4,12},{... | collective-permute-start | bytes 3145736 | tf_op jit(solution)/shard_map/ppermute | solution.py:157
  471.3 32.0 %collective-permute-start.92 = (bf16[352,2048]{1,0:T(8,128)(2,1)S(1)}, bf16[352,2048]{1,0:T(8,128)(2,1)S(1)}, u32[]{:S(2)}, u32[]{:S(2)}) collective-permute-start(bf16[352,2048]{1,0:T(8,128)(2,1)S(1)} %add_rows.58.refs_0_), channel_id=1, source_target_pairs={{8,16},{16,8},{9,17},{17,9},{10,18},{18,10},{11,19},{19,11},{12,20... | collective-permute-start | bytes 4325384 | tf_op jit(solution)/shard_map/ppermute | solution.py:157
  482.4 18.0 %collective-permute-start.85 = (bf16[256,1536]{1,0:T(8,128)(2,1)S(1)}, bf16[256,1536]{1,0:T(8,128)(2,1)S(1)}, u32[]{:S(2)}, u32[]{:S(2)}) collective-permute-start(bf16[256,1536]{1,0:T(8,128)(2,1)S(1)} %broadcast_select_fusion.refs_0_), channel_id=1, source_target_pairs={{0,4},{1,3},{2,6},{3,1},{4,0},{5,7},{6,2},{7,5},{8,12},{9,11},{10,... | collective-permute-start | bytes 2359304 | tf_op jit(solution)/shard_map/ppermute | solution.py:103
  484.2 36.3 %collective-permute-start.91 = (bf16[352,2048]{1,0:T(8,128)(2,1)S(1)}, bf16[352,2048]{1,0:T(8,128)(2,1)S(1)}, u32[]{:S(2)}, u32[]{:S(2)}) collective-permute-start(bf16[352,2048]{1,0:T(8,128)(2,1)S(1)} %add_rows.57.refs_1_), channel_id=1, source_target_pairs={{8,0},{16,24},{9,1},{17,25},{10,2},{18,26},{11,3},{19,27},{12,4},{... | collective-permute-start | bytes 4325384 | tf_op jit(solution)/shard_map/ppermute | solution.py:157
  486.0 36.2 %collective-permute-start.90 = (bf16[256,2048]{1,0:T(8,128)(2,1)S(1)}, bf16[256,2048]{1,0:T(8,128)(2,1)S(1)}, u32[]{:S(2)}, u32[]{:S(2)}) collective-permute-start(bf16[256,2048]{1,0:T(8,128)(2,1)S(1)} %copy-done.84), channel_id=1, source_target_pairs={{0,8},{24,16},{1,9},{25,17},{2,10},{26,18},{3,11},{27,19},{4,12},{... | collective-permute-start | bytes 3145736 | tf_op jit(solution)/shard_map/ppermute | solution.py:157
  501.2 21.3 %collective-permute-start.89 = (bf16[256,1536]{1,0:T(8,128)(2,1)S(1)}, bf16[256,1536]{1,0:T(8,128)(2,1)S(1)}, u32[]{:S(2)}, u32[]{:S(2)}) collective-permute-start(bf16[256,1536]{1,0:T(8,128)(2,1)S(1)} %collective-permute-done.84.refs_2_), channel_id=1, source_target_pairs={{0,4},{1,3},{2,6},{3,1},{4,0},{5,7},{6,2},{7,5},{8,12},{9,11},{10,... | collective-permute-start | bytes 2359304 | tf_op jit(solution)/shard_map/ppermute | solution.py:103
  502.6 23.0 %collective-permute-start.95 = (bf16[256,2048]{1,0:T(8,128)(2,1)S(1)}, bf16[256,2048]{1,0:T(8,128)(2,1)S(1)}, u32[]{:S(2)}, u32[]{:S(2)}) collective-permute-start(bf16[256,2048]{1,0:T(8,128)(2,1)S(1)} %add_rows.59.refs_0_), channel_id=1, source_target_pairs={{8,16},{16,8},{9,17},{17,9},{10,18},{18,10},{11,19},{19,11},{12,20... | collective-permute-start | bytes 3145736 | tf_op jit(solution)/shard_map/ppermute | solution.py:157
  503.4 36.5 %collective-permute-start.94 = (bf16[1024,512]{1,0:T(8,128)(2,1)S(1)}, bf16[1024,512]{1,0:T(8,128)(2,1)S(1)}, u32[]{:S(2)}, u32[]{:S(2)}) collective-permute-start(bf16[1024,512]{1,0:T(8,128)(2,1)S(1)} %copy-done.39), channel_id=1, source_target_pairs={{0,8},{24,16},{1,9},{25,17},{2,10},{26,18},{3,11},{27,19},{4,12},{... | collective-permute-start | bytes 3145736 | tf_op jit(solution)/shard_map/ppermute | solution.py:157
  522.6 39.3 %collective-permute-start.99 = (bf16[352,2048]{1,0:T(8,128)(2,1)S(1)}, bf16[352,2048]{1,0:T(8,128)(2,1)}, u32[]{:S(2)}, u32[]{:S(2)}) collective-permute-start(bf16[352,2048]{1,0:T(8,128)(2,1)S(1)} %add_rows.60.refs_1_), channel_id=1, source_target_pairs={{8,0},{16,24},{9,1},{17,25},{10,2},{18,26},{11,3},{19,27},{12,4},{... | collective-permute-start | bytes 4325384 | tf_op jit(solution)/shard_map/ppermute | solution.py:157
  523.9 41.3 %collective-permute-start.98 = (bf16[256,2048]{1,0:T(8,128)(2,1)S(1)}, bf16[256,2048]{1,0:T(8,128)(2,1)}, u32[]{:S(2)}, u32[]{:S(2)}) collective-permute-start(bf16[256,2048]{1,0:T(8,128)(2,1)S(1)} %add_rows.61.refs_0_), channel_id=1, source_target_pairs={{8,16},{16,8},{9,17},{17,9},{10,18},{18,10},{11,19},{19,11},{12,20... | collective-permute-start | bytes 3145736 | tf_op jit(solution)/shard_map/ppermute | solution.py:157
  526.5 54.5 %collective-permute-start.97 = (bf16[256,2048]{1,0:T(8,128)(2,1)S(1)}, bf16[256,2048]{1,0:T(8,128)(2,1)}, u32[]{:S(2)}, u32[]{:S(2)}) collective-permute-start(bf16[256,2048]{1,0:T(8,128)(2,1)S(1)} %add_rows.62.refs_1_), channel_id=1, source_target_pairs={{8,0},{16,24},{9,1},{17,25},{10,2},{18,26},{11,3},{19,27},{12,4},{... | collective-permute-start | bytes 3145736 | tf_op jit(solution)/shard_map/ppermute | solution.py:157
  541.1 42.7 %collective-permute-start.96 = (bf16[1024,512]{1,0:T(8,128)(2,1)}, bf16[1024,512]{1,0:T(8,128)(2,1)}, u32[]{:S(2)}, u32[]{:S(2)}) collective-permute-start(bf16[1024,512]{1,0:T(8,128)(2,1)} %add_rows.63.refs_0_), channel_id=1, source_target_pairs={{8,16},{16,8},{9,17},{17,9},{10,18},{18,10},{11,19},{19,11},{12,20... | collective-permute-start | bytes 3145736 | tf_op jit(solution)/shard_map/ppermute | solution.py:157
  560.6 27.8 %collective-permute-start.79 = (f32[1,5120]{1,0:T(1,128)}, f32[1,5120]{1,0:T(1,128)}, u32[]{:S(2)}, u32[]{:S(2)}) collective-permute-start(f32[1,5120]{1,0:T(1,128)} %add.28), channel_id=1, source_target_pairs={{8,0},{16,24},{9,1},{17,25},{10,2},{18,26},{11,3},{19,27},{12,4},{... | collective-permute-start | bytes 61448 | tf_op jit(solution)/shard_map/ppermute | solution.py:132
  561.9 29.7 %collective-permute-start.83 = (bf16[256,1536]{1,0:T(8,128)(2,1)}, bf16[256,1536]{1,0:T(8,128)(2,1)S(1)}, u32[]{:S(2)}, u32[]{:S(2)}) collective-permute-start(bf16[256,1536]{1,0:T(8,128)(2,1)} %copy-done.56), channel_id=1, source_target_pairs={{0,1},{1,0},{2,3},{3,2},{4,5},{5,4},{6,7},{7,6},{8,9},{9,8},{10,11... | collective-permute-start | bytes 2359304 | tf_op jit(solution)/shard_map/ppermute | solution.py:103
  565.2 26.4 %collective-permute-start.87 = (bf16[256,1536]{1,0:T(8,128)(2,1)S(1)}, bf16[256,1536]{1,0:T(8,128)(2,1)S(1)}, u32[]{:S(2)}, u32[]{:S(2)}) collective-permute-start(bf16[256,1536]{1,0:T(8,128)(2,1)S(1)} %copy-done.92), channel_id=1, source_target_pairs={{0,1},{1,0},{2,3},{3,2},{4,5},{5,4},{6,7},{7,6},{8,9},{9,8},{10,11... | collective-permute-start | bytes 2359304 | tf_op jit(solution)/shard_map/ppermute | solution.py:103
  583.8 36.7 %collective-permute-start.101 = (bf16[256,2048]{1,0:T(8,128)(2,1)S(1)}, bf16[256,2048]{1,0:T(8,128)(2,1)S(1)}, u32[]{:S(2)}, u32[]{:S(2)}) collective-permute-start(bf16[256,2048]{1,0:T(8,128)(2,1)S(1)} %add_rows.64.refs_1_), channel_id=1, source_target_pairs={{8,0},{16,24},{9,1},{17,25},{10,2},{18,26},{11,3},{19,27},{12,4},{... | collective-permute-start | bytes 3145736 | tf_op jit(solution)/shard_map/ppermute | solution.py:157
  588.4 54.3 %collective-permute-start.100 = (bf16[1024,512]{1,0:T(8,128)(2,1)S(1)}, bf16[1024,512]{1,0:T(8,128)(2,1)S(1)}, u32[]{:S(2)}, u32[]{:S(2)}) collective-permute-start(bf16[1024,512]{1,0:T(8,128)(2,1)S(1)} %add_rows.65.refs_1_), channel_id=1, source_target_pairs={{8,0},{16,24},{9,1},{17,25},{10,2},{18,26},{11,3},{19,27},{12,4},{... | collective-permute-start | bytes 3145736 | tf_op jit(solution)/shard_map/ppermute | solution.py:157
  (179 other events, 1393.2 us)

commit v2 on v1

--- a/solution.py
+++ b/solution.py
@@ -65,10 +65,14 @@
     def __init__(self):
         self.last = ()
 
-    def __call__(self, *values):
+    def all(self, *values):
         held = lax.optimization_barrier(values + self.last)
         self.last = (held[0],)
-        return held[0] if len(values) == 1 else held[: len(values)]
+        return held[: len(values)]
+
+    def __call__(self, *values):
+        held = self.all(*values)
+        return held[0] if len(values) == 1 else held
 
 
 class Plane:
@@ -176,9 +180,11 @@
         item["own"], item["came"] = both, came
         return {"own": value, "came": came}
 
-    def end(self, item, size, at=0, past=None):
+    def land(self, item):
         item["came"] = self.clock(item["came"])
-        return self.clock(settle(self.inner, item["own"], item["came"], size, at, past))
+
+    def end(self, item, size, at=0, past=None, low=0, high=None):
+        return settle(self.inner, item["own"], item["came"], size, at, past, low, high)
 
 
 def query_blocks(length):
@@ -215,12 +221,13 @@
     table = refs[0]
     pieces = refs[1 : 1 + count]
     weight, cosine, sine, seg_column, seg_row = refs[1 + count : 6 + count]
-    queries, keys, values, mixed, mixed_there = refs[6 + count :]
+    latents, queries, keys, values, mixed_there, mixed = refs[6 + count :]
     length = queries.shape[0]
     rows = length // count
     half = width // 2
     for r in range(count):
         there = pl.ds(pl.multiple_of(table[r] * rows, rows), rows)
+        latents[there, :] = pieces[r][:, :rank]
         keys[there, :] = pieces[r][:, rank : rank + width]
         values[there, :] = pieces[r][:, rank + width :]
         flat = dot(pieces[r][:, :rank], weight[...])
@@ -264,10 +271,10 @@
     length = cosine.shape[0]
     rank = weight.shape[0]
     shapes = [
+        jax.ShapeDtypeStruct((length, rank), bf16),
         jax.ShapeDtypeStruct((length, heads * width), bf16),
         jax.ShapeDtypeStruct((length, width), bf16),
         jax.ShapeDtypeStruct((length, width), bf16),
-        jax.ShapeDtypeStruct((length, heads * width), bf16),
         jax.ShapeDtypeStruct((length, heads * width), bf16),
     ]
     return pl.pallas_call(
@@ -275,6 +282,7 @@
         out_shape=shapes,
         in_specs=[smem()] + [vmem()] * (count + 5),
         out_specs=[vmem()] * 5,
+        scratch_shapes=[pltpu.VMEM((length, heads * width), bf16)],
         compiler_params=pltpu.CompilerParams(vmem_limit_bytes=48 << 20),
         cost_estimate=brief(),
         name="attend_forward",
@@ -285,7 +293,7 @@
     table = refs[0]
     grads_in = refs[1 : 1 + parts]
     queries, keys, values, cosine, sine, seg_column, seg_row = refs[1 + parts : 8 + parts]
-    query_there, pair_there, outer, query_out, key_total, value_total = refs[8 + parts :]
+    query_out, pair_out, outer, key_total, value_total = refs[8 + parts :]
     length = queries.shape[0]
     count = table.shape[0]
     rows = length // count
@@ -325,11 +333,8 @@
             query_out[start:high, h * width + half : (h + 1) * width] = (
                 second * cos - first * sin
             ).astype(bf16)
-    for r in range(count):
-        here = slice(r * rows, (r + 1) * rows)
-        query_there[here, :] = query_out[there(r), :]
-        pair_there[here, :width] = key_total[there(r), :].astype(bf16)
-        pair_there[here, width:] = value_total[there(r), :].astype(bf16)
+    pair_out[:, :width] = key_total[...].astype(bf16)
+    pair_out[:, width:] = value_total[...].astype(bf16)
 
 
 def attend_backward(table, grads, queries, keys, values, cosine, sine, segments, heads, scale):
@@ -345,7 +350,6 @@
         in_specs=[smem()] + [vmem()] * (parts + 7),
         out_specs=[vmem()] * 2,
         scratch_shapes=[
-            pltpu.VMEM((length, heads * width), bf16),
             pltpu.VMEM((length, heads * width), bf16),
             pltpu.VMEM((length, width), f32),
             pltpu.VMEM((length, width), f32),
@@ -382,22 +386,25 @@
         ),
         in_specs=[vmem()] * (len(pieces) + 1),
         out_specs=vmem(),
-        compiler_params=pltpu.CompilerParams(vmem_limit_bytes=32 << 20),
+        compiler_params=pltpu.CompilerParams(vmem_limit_bytes=36 << 20),
         cost_estimate=brief(),
         name="rows_product",
     )(*pieces, weight)
 
 
-def latent_share_kernel(low, size, query_grads, pairs, weight, *refs):
+def latent_share_kernel(low, size, table, query_grads, pairs, weight, *refs):
     outs = refs[:-3]
     held, beside, sems = refs[-3:]
     rows = outs[0].shape[0]
     rank = weight.shape[0]
-    here = pl.ds(low * rows, size)
-    copies = [
-        pltpu.make_async_copy(query_grads.at[here, :], held, sems.at[0]),
-        pltpu.make_async_copy(pairs.at[here, :], beside, sems.at[1]),
-    ]
+    copies = []
+    for k in range(size // rows):
+        there = pl.ds(pl.multiple_of(table[low + k] * rows, rows), rows)
+        here = pl.ds(k * rows, rows)
+        copies += [
+            pltpu.make_async_copy(query_grads.at[there, :], held.at[here, :], sems.at[0, k]),
+            pltpu.make_async_copy(pairs.at[there, :], beside.at[here, :], sems.at[1, k]),
+        ]
     for copy in copies:
         copy.start()
     for copy in copies:
@@ -409,27 +416,28 @@
             outs[p + k][:, rank:] = beside[(p + k) * rows : (p + k + 1) * rows, :]
 
 
-def latent_shares(clock, query_grads, pairs, weight, count):
+def latent_shares(table, query_grads, pairs, weight):
+    count = table.shape[0]
     rows = query_grads.shape[0] // count
     rank, inner = weight.shape
     extra = pairs.shape[1]
 
-    def share(low, high):
+    def share(clock, low, high):
         size = (high - low) * rows
         return pl.pallas_call(
             functools.partial(latent_share_kernel, low, size),
             out_shape=[jax.ShapeDtypeStruct((rows, rank + extra), bf16)] * (high - low),
-            in_specs=[any_space(), any_space(), vmem()],
+            in_specs=[smem(), any_space(), any_space(), vmem()],
             out_specs=[vmem()] * (high - low),
             scratch_shapes=[
                 pltpu.VMEM((size, inner), bf16),
                 pltpu.VMEM((size, extra), bf16),
-                pltpu.SemaphoreType.DMA((2,)),
+                pltpu.SemaphoreType.DMA((2, high - low)),
             ],
-            compiler_params=pltpu.CompilerParams(vmem_limit_bytes=32 << 20),
+            compiler_params=pltpu.CompilerParams(vmem_limit_bytes=36 << 20),
             cost_estimate=brief(),
             name="latent_share",
-        )(*clock(query_grads, pairs), weight)
+        )(table, *clock(query_grads, pairs), weight)
 
     return share
 
@@ -461,7 +469,7 @@
     return pl.BlockSpec(memory_space=pl.ANY)
 
 
-def share_kernel(low, size, terms, transposed, *refs):
+def share_kernel(low, size, terms, *refs):
     lefts = refs[:terms]
     weights = refs[terms : 2 * terms]
     outs = refs[2 * terms : -terms - 1]
@@ -474,35 +482,34 @@
         copies.append(copy)
     for copy in copies:
         copy.wait()
-    product = right_transposed if transposed else dot
     for p in range(size // (2 * rows)):
         here = pl.ds(2 * p * rows, 2 * rows)
-        total = product(held[0][here, :], weights[0][...])
+        total = dot(held[0][here, :], weights[0][...])
         for t in range(1, terms):
-            total = total + product(held[t][here, :], weights[t][...])
+            total = total + dot(held[t][here, :], weights[t][...])
         outs[2 * p][...] = total[:rows].astype(bf16)
         outs[2 * p + 1][...] = total[rows:].astype(bf16)
 
 
-def shares(clock, lefts, weights, count, transposed):
+def shares(lefts, weights, count):
     rows = lefts[0].shape[0] // count
     inner = lefts[0].shape[1]
-    columns = weights[0].shape[0] if transposed else weights[0].shape[1]
+    columns = weights[0].shape[1]
     terms = len(lefts)
 
-    def share(low, high):
+    def share(clock, low, high):
         size = (high - low) * rows
         return pl.pallas_call(
-            functools.partial(share_kernel, low, size, terms, transposed),
+            functools.partial(share_kernel, low, size, terms),
             out_shape=[jax.ShapeDtypeStruct((rows, columns), bf16)] * (high - low),
             in_specs=[any_space()] * terms + [vmem()] * terms,
             out_specs=[vmem()] * (high - low),
             scratch_shapes=[pltpu.VMEM((size, inner), bf16)] * terms
             + [pltpu.SemaphoreType.DMA((terms,))],
-            compiler_params=pltpu.CompilerParams(vmem_limit_bytes=40 << 20),
+            compiler_params=pltpu.CompilerParams(vmem_limit_bytes=36 << 20),
             cost_estimate=brief(),
             name="share",
-        )(*clock(*lefts, lefts[0])[:terms], *weights)
+        )(*clock.all(*lefts), *weights)
 
     return share
 
@@ -546,7 +553,7 @@
 
 
 def feed(pieces, low, high, upper, gate_weight, up_weight, count, past):
-    rows, dim = pieces[0].shape
+    rows, dim = pieces[low].shape
     units = gate_weight.shape[0]
     pairs = (high - low) // 2
     operands = list(pieces[low:high]) + [upper, gate_weight, up_weight]
@@ -621,26 +628,27 @@
     )
 
 
-def settle_kernel(at, *refs):
+def settle_kernel(low, at, *refs):
     inner, own, came = refs[:3]
     out, buffer, sem = refs[-3:]
-    rows = own.shape[0]
+    rows = buffer.shape[0]
 
     @pl.when(inner[0] == 1)
     def _():
-        buffer[...] = own[...].astype(f32)
+        buffer[...] = own[low : low + rows, :].astype(f32)
 
     @pl.when(inner[0] == 0)
     def _():
-        buffer[...] = came[...].astype(f32)
+        buffer[...] = came[low : low + rows, :].astype(f32)
 
     copy = pltpu.make_async_copy(buffer, out.at[pl.ds(at, rows), :], sem)
     copy.start()
     copy.wait()
 
 
-def settle(inner, own, came, size, at, past):
-    rows, columns = own.shape
+def settle(inner, own, came, size, at=0, past=None, low=0, high=None):
+    columns = own.shape[1]
+    rows = (high or own.shape[0]) - low
     operands = [inner, own, came]
     specs = [smem(), vmem(), vmem()]
     aliases = {}
@@ -649,43 +657,199 @@
         operands.append(past)
         specs.append(any_space())
     return pl.pallas_call(
-        functools.partial(settle_kernel, at),
+        functools.partial(settle_kernel, low, at),
         out_shape=shaped((size, columns), f32),
         in_specs=specs,
         out_specs=any_space(),
         scratch_shapes=[pltpu.VMEM((rows, columns), f32), pltpu.SemaphoreType.DMA],
         input_output_aliases=aliases,
-        compiler_params=pltpu.CompilerParams(vmem_limit_bytes=24 << 20),
+        compiler_params=pltpu.CompilerParams(vmem_limit_bytes=16 << 20),
         cost_estimate=brief(),
         name="settle",
     )(*operands)
 
 
-def product_kernel(left, right, *outs):
+def product_kernel(first, left, right, *refs):
+    outs = refs[first:]
     total = left_transposed(left[...], right[...]).astype(bf16)
-    rows = outs[0].shape[0]
-    for k, out in enumerate(outs):
-        out[...] = total[k * rows : (k + 1) * rows]
-
-
-def weight_product(left, right, parts, step=512):
+    if first:
+        total = jnp.concatenate([refs[0][...], total], axis=0)
+    low = 0
+    for out in outs:
+        rows = out.shape[0]
+        out[...] = total[low : low + rows]
+        low += rows
+
+
+def weight_product(left, right, rows, above=None, step=512):
     tokens, units = left.shape
     columns = right.shape[1]
     step = min(step, columns)
-    rows = units // parts
+    operands = [left, right]
+    specs = [
+        pl.BlockSpec((tokens, units), lambda j: (0, 0)),
+        pl.BlockSpec((tokens, step), lambda j: (0, j)),
+    ]
+    if above is not None:
+        operands.append(above)
+        specs.append(pl.BlockSpec((above.shape[0], step), lambda j: (0, j)))
     return pl.pallas_call(
-        product_kernel,
+        functools.partial(product_kernel, len(operands) - 2),
         grid=(columns // step,),
-        out_shape=[shaped((rows, columns), bf16)] * parts,
-        in_specs=[
-            pl.BlockSpec((tokens, units), lambda j: (0, 0)),
-            pl.BlockSpec((tokens, step), lambda j: (0, j)),
-        ],
-        out_specs=[pl.BlockSpec((rows, step), lambda j: (0, j))] * parts,
-        compiler_params=pltpu.CompilerParams(vmem_limit_bytes=26 << 20),
+        out_shape=[shaped((one, columns), bf16) for one in rows],
+        in_specs=specs,
+        out_specs=[pl.BlockSpec((one, step), lambda j: (0, j)) for one in rows],
+        compiler_params=pltpu.CompilerParams(vmem_limit_bytes=30 << 20),
         cost_estimate=brief(),
         name="weight_product",
-    )(left, right)
+    )(*operands)
+
+
+def pack_last_kernel(above, wide, below, out):
+    top = above.shape[0]
+    rows, columns = wide.shape
+    parts = out.shape[1] // columns
+    step = rows // parts
+    out[:top, :] = above[...]
+    for j in range(parts):
+        out[top : top + step, j * columns : (j + 1) * columns] = wide[j * step : (j + 1) * step, :]
+    out[top + step :, :] = below[...]
+
+
+def pack_last(above, wide, below):
+    columns = above.shape[1]
+    rows = above.shape[0] + wide.size // columns + below.shape[0]
+    return call(
+        pack_last_kernel, shaped((rows, columns), bf16), [above, wide, below], "pack_last"
+    )
+
+
+def settle_last_kernel(top, inner, own, came, wide, below):
+    rows, columns = wide.shape
+    parts = own.shape[1] // columns
+    step = rows // parts
+
+    def write(source):
+        for j in range(parts):
+            wide[j * step : (j + 1) * step, :] = source[
+                top : top + step, j * columns : (j + 1) * columns
+            ].astype(f32)
+        below[...] = source[top + step :, :].astype(f32)
+
+    @pl.when(inner[0] == 1)
+    def _():
+        write(own)
+
+    @pl.when(inner[0] == 0)
+    def _():
+        write(came)
+
+
+def settle_last(inner, own, came, top, rows, columns):
+    total, dim = own.shape
+    left = total - top - rows * columns // dim
+    return call(
+        functools.partial(settle_last_kernel, top),
+        [shaped((rows, columns), f32), shaped((left, dim), f32)],
+        [inner, own, came],
+        "settle_last",
+        scalars=1,
+    )
+
+
+def pack_kernel(count, *refs):
+    total = summed(refs[:count]).astype(bf16)
+    beside, out = refs[count:]
+    rows, columns = total.shape
+    tall = rows * 3 // 4
+    out[:tall, :columns] = total[:tall]
+    third = columns // 3
+    for j in range(3):
+        low = j * (rows - tall)
+        out[low : low + rows - tall, columns:] = total[tall:, j * third : (j + 1) * third]
+    out[tall:, :] = beside[...]
+
+
+def pack(parts, beside):
+    rows, columns = parts[0].shape
+    tall = rows * 3 // 4
+    return call(
+        functools.partial(pack_kernel, len(parts)),
+        shaped((tall + beside.shape[0], beside.shape[1]), bf16),
+        [*parts, beside],
+        "pack",
+    )
+
+
+def pick_kernel(inner, own, came, out):
+    rows = out.shape[0]
+
+    @pl.when(inner[0] == 1)
+    def _():
+        out[...] = own[:rows, :]
+
+    @pl.when(inner[0] == 0)
+    def _():
+        out[...] = came[:rows, :]
+
+
+def pick(inner, own, came, rows):
+    return call(
+        pick_kernel,
+        shaped((rows, own.shape[1]), bf16),
+        [inner, own, came],
+        "pick",
+        scalars=1,
+    )
+
+
+def widen_kernel(*refs):
+    out = refs[-1]
+    low = 0
+    for x in refs[:-1]:
+        rows = x.shape[0]
+        out[low : low + rows, :] = x[...].astype(f32)
+        low += rows
+
+
+def widen(parts, step=512):
+    rows = sum(part.shape[0] for part in parts)
+    columns = parts[0].shape[1]
+    return pl.pallas_call(
+        widen_kernel,
+        grid=(columns // step,),
+        out_shape=shaped((rows, columns), f32),
+        in_specs=[pl.BlockSpec((part.shape[0], step), lambda j: (0, j)) for part in parts],
+        out_specs=pl.BlockSpec((rows, step), lambda j: (0, j)),
+        compiler_params=pltpu.CompilerParams(vmem_limit_bytes=16 << 20),
+        cost_estimate=brief(),
+        name="widen",
+    )(*parts)
+
+
+def settle_two_kernel(inner, own, came, above, below):
+    rows = above.shape[0]
+
+    @pl.when(inner[0] == 1)
+    def _():
+        above[...] = own[:rows, :].astype(f32)
+        below[...] = own[rows:, :].astype(f32)
+
+    @pl.when(inner[0] == 0)
+    def _():
+        above[...] = came[:rows, :].astype(f32)
+        below[...] = came[rows:, :].astype(f32)
+
+
+def settle_two(inner, own, came, rows):
+    total, columns = own.shape
+    return call(
+        settle_two_kernel,
+        [shaped((rows, columns), f32), shaped((total - rows, columns), f32)],
+        [inner, own, came],
+        "settle_two",
+        scalars=1,
+    )
 
 
 def rotated(first, second, cosine, sine):
@@ -716,6 +880,7 @@
         [shaped((rows, dim), bf16), shaped((rows, rank), f32), shaped((rows, rank + 2 * width), bf16)],
         [x, gain[None], down, latent_gain[None], key, value, cosine, sine],
         "enter",
+        limit=60,
     )
 
 
@@ -831,19 +996,22 @@
             out_shape=[jax.ShapeDtypeStruct((rows, columns), bf16)] * count,
             in_specs=[smem(), vmem(), vmem()],
             out_specs=[vmem()] * count,
-            compiler_params=pltpu.CompilerParams(vmem_limit_bytes=40 << 20),
+            compiler_params=pltpu.CompilerParams(vmem_limit_bytes=36 << 20),
             cost_estimate=brief(),
             name="shared_shares",
         )(table, normed, grads)
     )
 
 
-def unpack_kernel(count, parts, table, *refs):
+def unpack_kernel(count, parts, packed, table, *refs):
     pieces = refs[:count]
     outs = refs[count : count + len(parts)]
     buffers = refs[count + len(parts) : -1]
     sems = refs[-1]
-    rows = pieces[0].shape[0]
+    rows = buffers[0].shape[1]
+    tall = rows * 3 // 4
+    columns = parts[-1][1]
+    third = columns // 3
     flying = []
     for r in range(count):
         slot = r % 2
@@ -853,7 +1021,18 @@
         there = pl.ds(pl.multiple_of(table[r] * rows, rows), rows)
         copies = []
         for k, (low, high) in enumerate(parts):
-            buffers[k][slot] = pieces[r][:, low:high].astype(f32)
+            if packed:
+                buffers[k][slot, :tall, :] = pieces[r][:, low:high].astype(f32)
+                for j in range(3):
+                    first, last = max(low, j * third), min(high, (j + 1) * third)
+                    if first < last:
+                        start = columns - j * third
+                        buffers[k][slot, tall:, first - low : last - low] = pieces[r][
+                            j * (rows - tall) : (j + 1) * (rows - tall),
+                            start + first : start + last,
+                        ].astype(f32)
+            else:
+                buffers[k][slot] = pieces[r][:, low:high].astype(f32)
             copy = pltpu.make_async_copy(
                 buffers[k].at[slot], outs[k].at[there, :], sems.at[k, slot]
             )
@@ -865,17 +1044,19 @@
             copy.wait()
 
 
-def unpack(table, pieces, parts):
+def unpack(table, pieces, parts, packed):
     count = len(pieces)
     rows = pieces[0].shape[0]
+    if packed:
+        rows = rows * 4 // 3
     return pl.pallas_call(
-        functools.partial(unpack_kernel, count, parts),
+        functools.partial(unpack_kernel, count, parts, packed),
         out_shape=[jax.ShapeDtypeStruct((count * rows, high - low), f32) for low, high in parts],
         in_specs=[smem()] + [vmem()] * count,
         out_specs=[any_space()] * len(parts),
         scratch_shapes=[pltpu.VMEM((2, rows, high - low), f32) for low, high in parts]
         + [pltpu.SemaphoreType.DMA((len(parts), 2))],
-        compiler_params=pltpu.CompilerParams(vmem_limit_bytes=40 << 20),
+        compiler_params=pltpu.CompilerParams(vmem_limit_bytes=36 << 20),
         cost_estimate=brief(),
         name="unpack",
     )(table, *pieces)
@@ -920,259 +1101,321 @@
     cotangent_rows = out_grad[0]
 
     x = block_input[0]
-    if fast:
-        cot_a = move(cotangent_rows, hop_a)
-        cot_o = move(cotangent_rows, hop_c)
+    dim = x.shape[1]
+    always = (segments[0] & 1) <= 1
+
+    def stage(run):
+        def inside():
+            inner = Clock()
+            inner.last = clock.last
+            return tuple(run(inner))
+
+        if not fast:
+            return inside()
+        shapes = jax.eval_shape(inside)
+        result = lax.cond(
+            always, inside, lambda: tuple(jnp.zeros(one.shape, one.dtype) for one in shapes)
+        )
+        return clock.all(*result)
+
+    def hops(values, ways, filler=None, apart=False):
+        def run(clock):
+            held = clock.all(*values)
+            came = [move(value, way) for value, way in zip(held, ways)]
+            more = list(filler(clock, *came)) if filler else []
+            return [*clock.all(*came), *more]
+
+        result = stage(run) if apart else run(clock)
+        return list(result[: len(values)]), list(result[len(values) :])
+
+    def gather(rows, first=None, second=None, apart=False, between=None, last=False):
+        def beside(clock, a, b, s_o):
+            return first(clock, [rows, clock(s_o)]) if first else []
+
+        (a, b, s_o), more = hops([rows, rows, rows], [hop_a, hop_b, hop_c], beside, apart)
+        if between:
+            between()
+
+        def beside(clock, c, a_o, b_o):
+            if not second:
+                return []
+            a_o, b_o = clock(a_o, b_o)
+            return second(clock, [a, a_o, b, b_o], more)
+
+        (c, a_o, b_o), later = hops([a, a, b], [hop_b, hop_c, hop_c], beside, apart)
+        (c_o,), _ = hops([c], [hop_c], None, apart or last)
+        return [rows, s_o, a, a_o, b, b_o, c, c_o], more, later
+
+    def scatter(share, filler=None, apart=False, between=None):
+        c, c_send = clock(*share(clock, 6, 8))
+        (c_came,), near = hops(
+            [c_send], [hop_c], lambda clock, came: clock(*share(clock, 2, 6)), apart
+        )
+        a, a_send, b, b_send = near
+        c = clock(add_rows(c, c_came))
+        (c_in, a_came, b_came), (own, own_send) = hops(
+            [c, a_send, b_send],
+            [hop_b, hop_c, hop_c],
+            lambda clock, *came: clock(*share(clock, 0, 2)),
+            apart,
+        )
+        a, b = clock(add_rows(a, a_came, c_in), add_rows(b, b_came))
+        if between:
+            between()
+        (a_in, b_in, own_came), more = hops(
+            [a, b, own_send],
+            [hop_a, hop_b, hop_c],
+            (lambda clock, *came: filler(clock)) if filler else None,
+            apart,
+        )
+        return [own, own_came, b_in, a_in], more
+
     own_places = lax.dynamic_slice_in_dim(places, first_row, rows, 0)
     own_cosine, own_sine = rotation(own_places, width)
-    normed_rows, latent, packed = enter(
-        x, attention_gain, query_down, query_gain, key_proj, value_proj, own_cosine, own_sine
-    )
-    cosine, sine = rotation(places, width)
-    if fast:
-        packed = clock(packed)
-        a, b, s_o = move(packed, hop_a), move(packed, hop_b), move(packed, hop_c)
-        cosine, sine = clock(cosine, sine)
-        a, cot_a = clock(a, cot_a)
-        c, a_o = move(a, hop_b), move(a, hop_c)
-        cot_ao = move(cot_a, hop_c)
-        b = clock(b)
-        b_o = move(b, hop_c)
-        c = clock(c)
-        c_o = move(c, hop_c)
-        cotangent_rows, cot_a = clock(cotangent_rows, cot_a)
-        cot_b = move(cotangent_rows, hop_b)
-        cot_c = move(cot_a, hop_b)
-        pieces = [packed, s_o, a, a_o, b, b_o, c, c_o]
-    else:
+
+    def enter_rows():
+        return enter(
+            x, attention_gain, query_down, query_gain, key_proj, value_proj, own_cosine, own_sine
+        )
+
+    def attend(pieces, cosine, sine):
+        return attend_forward(
+            plane.table, pieces, query_up, cosine, sine, segments, heads, width, scale
+        )
+
+    def attend_back(outer):
+        return attend_backward(
+            plane.table, outer, queries, keys, values, cosine, sine, segments, heads, scale
+        )
+
+    def leave_rows(packed_grad):
+        return leave(
+            packed_grad, query_down, key_proj, value_proj, x, attention_gain, middle_grad
+        )
+
+    def sum_gains(parts, total):
+        return total(jnp.concatenate(parts, axis=1))
+
+    units = gate_rows.shape[0]
+    size = heads * width
+    columns = ((0, rank), (rank, rank + width), (rank + width, rank + 2 * width))
+    add = lambda left, right: left + right
+
+    if not fast:
+        normed_rows, latent, packed = enter_rows()
+        cosine, sine = rotation(places, width)
         pieces = plane.gather(packed)
-    queries, keys, values, mixed, mixed_there = attend_forward(
-        plane.table, pieces, query_up, cosine, sine, segments, heads, width, scale
-    )
-
-    def first_part(share):
-        c, c_send = clock(*share(6, 8))
-        c_came = move(c_send, hop_c)
-        return c, c_came
-
-    def second_part(share, c, c_came):
-        c = clock(add_rows(c, clock(c_came)))
-        c_in = move(c, hop_b)
-        a, a_send, b, b_send = clock(*share(2, 6))
-        b_came, a_came = move(b_send, hop_c), move(a_send, hop_c)
-        b = clock(add_rows(b, clock(b_came)))
-        b_in = move(b, hop_b)
-        own, own_send = clock(*share(0, 2))
-        own_came = move(own_send, hop_c)
-        return c_in, a, a_came, b_in, own, own_came
-
-    def third_part(c_in, a, a_came, b_in, own, own_came):
-        c_in, a_came = clock(c_in, a_came)
-        a = clock(add_rows(a, a_came, c_in))
-        a_in = move(a, hop_a)
-        return [own, own_came, b_in, a_in]
-
-    share = shares(clock, [mixed_there], [out_proj], group, False)
-    if fast:
-        state = second_part(share, *first_part(share))
-        cot_b, cot_c = clock(cot_b, cot_c)
-        cot_bo, cot_co = move(cot_b, hop_c), move(cot_c, hop_c)
-        parts = third_part(*state)
-        cot_bo, cot_co = clock(cot_bo, cot_co)
-        cot_pieces = [cotangent_rows, cot_o, cot_a, cot_ao, cot_b, cot_bo, cot_c, cot_co]
-        hidden_grad = clock(rows_product(cot_pieces, down_weight, f32))
-        parts = clock(*parts)
-    else:
+        latents, queries, keys, values, mixed_there = attend(pieces, cosine, sine)
+        share = shares([mixed_there], [out_proj], group)
+        parts = [plane.scatter(share(clock, 0, group))]
+        middle, normed_mid_rows = middle_rows(x, feed_gain, parts)
         cot_pieces = plane.gather(cotangent_rows)
         hidden_grad = rows_product(cot_pieces, down_weight, f32)
-        parts = [plane.scatter(share(0, group))]
-    middle, normed_mid_rows = middle_rows(x, feed_gain, parts)
-
-    def feed_group(pieces, low, high, past):
-        return clock(*feed(pieces, low, high, hidden_grad, gate_rows, up_rows, group, past))
-
-    if fast:
-        normed_mid_rows = clock(normed_mid_rows)
-        a, b = move(normed_mid_rows, hop_a), move(normed_mid_rows, hop_b)
-        s_o = move(normed_mid_rows, hop_c)
-        cot_pieces[1] = clock(cot_pieces[1])
-        cotangent = clock(join(cot_pieces))
-        s_o = clock(s_o)
-        mid_pieces = [normed_mid_rows, s_o]
-        past = feed_group(mid_pieces, 0, 2, None)
-        a, b = clock(a, b)
-        c = move(a, hop_b)
-        a_o, b_o = move(a, hop_c), move(b, hop_c)
-        a_o, b_o = clock(a_o, b_o)
-        mid_pieces += [a, a_o, b, b_o]
-        past = feed_group(mid_pieces, 2, 6, past)
-        c = clock(c)
-        c_o = clock(move(c, hop_c))
-        mid_pieces += [c, c_o]
-        past = feed_group(mid_pieces, 6, 8, past)
-    else:
-        cotangent = join(cot_pieces)
         mid_pieces = plane.gather(normed_mid_rows)
-        past = feed_group(mid_pieces, 0, group, None)
-    hidden, gate_grad, upward_grad = past
-    units = hidden.shape[1]
-    dim = x.shape[1]
-
-    share = shares(clock, [gate_grad, upward_grad], [gate_rows, up_rows], group, False)
-    if fast:
-        c, c_came = first_part(share)
-        down_one, down_two = clock(*weight_product(clock(hidden), cotangent, 2))
-        down_one, down_two = belt.begin(down_one), belt.begin(down_two)
-        state = second_part(share, c, c_came)
-        normed_mid = clock(join(mid_pieces))
-        parts = third_part(*state)
-        gate_one, gate_two = clock(*weight_product(clock(gate_grad), normed_mid, 2))
-        parts = clock(*parts)
-    else:
-        normed_mid = join(mid_pieces)
-        parts = [plane.scatter(share(0, group))]
-    middle_grad, attention_grad, feed_gain_part = middle_back(
-        middle, feed_gain, cotangent_rows, parts
-    )
-    if fast:
-        attention_grad = clock(attention_grad)
-        a, b = move(attention_grad, hop_a), move(attention_grad, hop_b)
-        s_o = move(attention_grad, hop_c)
-        up_one, up_two = clock(*weight_product(clock(upward_grad), normed_mid, 2))
-        outer = [clock(rows_product([attention_grad, clock(s_o)], out_proj, bf16))]
-        belt.cross(down_one)
-        a, b = clock(a, b)
-        c = move(a, hop_b)
-        a_o, b_o = move(a, hop_c), move(b, hop_c)
-        a_o, b_o = clock(a_o, b_o)
-        outer.append(clock(rows_product([a, a_o, b, b_o], out_proj, bf16)))
-        c = clock(c)
-        c_o = clock(move(c, hop_c))
-        outer.append(rows_product([c, c_o], out_proj, bf16))
-        grad_pieces = [attention_grad, s_o, a, a_o, b, b_o, c, c_o]
-    else:
+        hidden, gate_grad, upward_grad = feed(
+            mid_pieces, 0, group, hidden_grad, gate_rows, up_rows, group, None
+        )
+        cotangent, normed_mid = join(cot_pieces), join(mid_pieces)
+        share = shares([gate_grad, upward_grad], [gate_rows, up_rows], group)
+        parts = [plane.scatter(share(clock, 0, group))]
+        middle_grad, attention_grad, feed_gain_part = middle_back(
+            middle, feed_gain, cotangent_rows, parts
+        )
         grad_pieces = plane.gather(attention_grad)
         outer = [rows_product(grad_pieces, out_proj, bf16)]
-
-    query_pre_grad, pair_grads = clock(
-        *attend_backward(
-            plane.table, outer, queries, keys, values, cosine, sine, segments, heads, scale
-        )
-    )
-
-    def out_proj_sum(number):
-        return weight_product(clock(mixed_there), join(grad_pieces), number)
-
-    def query_up_sum():
-        return weight_product(join(pieces)[:, :rank], clock(query_pre_grad), 1)[0]
-
-    share = latent_shares(clock, query_pre_grad, pair_grads, query_up, group)
-    if fast:
-        c, c_came = first_part(share)
-        state = second_part(share, c, c_came)
-        gate_one = belt.back(down_one, gate_one)
-        belt.cross(down_two)
-        parts = third_part(*state)
-        out_one, out_two = clock(*out_proj_sum(2))
-        parts = clock(*parts)
+        query_pre_grad, pair_grads = attend_back(outer)
+        share = latent_shares(plane.table, query_pre_grad, pair_grads, query_up)
+        parts = [plane.scatter(share(clock, 0, group))]
+        packed_grad, query_gain_part = latent_back(latent, query_gain, own_cosine, own_sine, parts)
+        shared_pieces = shared_shares(plane.table, normed_rows, packed_grad)
+        shared = line.total(plane.scatter(list(shared_pieces)).astype(bf16))
+        query_down_gradient, key_proj_gradient, value_proj_gradient = unpack(
+            plane.table, plane.gather(shared), columns, False
+        )
+        input_gradient, attention_gain_part = leave_rows(packed_grad)
+        share = shares([hidden], [down_weight], group)
+        block_output = add_rows(middle, plane.scatter(share(clock, 0, group)))
+        gains = sum_gains([attention_gain_part, query_gain_part, feed_gain_part], plane.total)
+        gains = line.total(gains, add)[0]
+        down_gradient, gate_gradient, up_gradient, proj_gradient, query_up_gradient = (
+            line.total(weight_product(left, right, [left.shape[1]])[0]).astype(f32)
+            for left, right in (
+                (hidden, cotangent),
+                (gate_grad, normed_mid),
+                (upward_grad, normed_mid),
+                (mixed_there, join(grad_pieces)),
+                (latents, query_pre_grad),
+            )
+        )
     else:
-        parts = [plane.scatter(share(0, group))]
-
-    packed_grad, query_gain_part = clock(
-        *latent_back(latent, query_gain, own_cosine, own_sine, parts)
-    )
-
-    shared_pieces = shared_shares(plane.table, normed_rows, packed_grad)
-    feed_share = shares(clock, [hidden], [down_weight], group, False)
-    if fast:
-        shared_pieces = clock(*shared_pieces)
-
-        def share(low, high):
-            return shared_pieces[low:high]
-
-        state = second_part(share, *first_part(share))
-        gate_two = belt.back(down_two, gate_two)
-        down_gradient = belt.end(down_one, units)
-        belt.cross(gate_one)
-        parts = third_part(*state)
-        query_sum = clock(query_up_sum())
-        input_gradient, attention_gain_part = clock(
-            *leave(
-                clock(packed_grad),
-                query_down,
-                key_proj,
-                value_proj,
-                x,
-                attention_gain,
-                middle_grad,
+        half = units // 2
+        cot_a = move(cotangent_rows, hop_a)
+        normed_rows, latent, packed = enter_rows()
+        packed = clock(packed)
+
+        def angles(clock, own):
+            return clock(*rotation(clock(places), width))
+
+        pieces, (cosine, sine), _ = gather(packed, angles, apart=True)
+        cot_now, cot_a = clock(cotangent_rows, cot_a)
+        cot_b, cot_c = move(cot_now, hop_b), move(cot_a, hop_b)
+        cot_o, cot_ao = move(cot_now, hop_c), move(cot_a, hop_c)
+        pieces[0] = clock(packed)
+
+        latents, queries, keys, values, mixed_there = clock(*attend(pieces, cosine, sine))
+        share = shares([mixed_there], [out_proj], group)
+        c, c_send = clock(*share(clock, 6, 8))
+        a, a_send, b, b_send = clock(*share(clock, 2, 6))
+        own, own_send = clock(*share(clock, 0, 2))
+        cot_b, cot_c, cot_o, cot_ao = clock(cot_b, cot_c, cot_o, cot_ao)
+        (c_came,), _ = hops([c_send], [hop_c])
+        c = clock(add_rows(c, c_came))
+        (c_in, a_came, b_came), _ = hops([c, a_send, b_send], [hop_b, hop_c, hop_c])
+        a, b = clock(add_rows(a, a_came, c_in), add_rows(b, b_came))
+
+        def beside_last(clock, a_in, b_in, own_came, cot_bo, cot_co):
+            cot_bo, cot_co = clock(cot_bo, cot_co)
+            cot_pieces = [cotangent_rows, cot_o, cot_a, cot_ao, cot_b, cot_bo, cot_c, cot_co]
+            hidden_grad = clock(rows_product(cot_pieces, down_weight, f32))
+            return [hidden_grad]
+
+        (a_in, b_in, own_came, cot_bo, cot_co), (hidden_grad,) = hops(
+            [a, b, own_send, cot_b, cot_c], [hop_a, hop_b, hop_c, hop_c, hop_c], beside_last
+        )
+        cot_pieces = [cotangent_rows, cot_o, cot_a, cot_ao, cot_b, cot_bo, cot_c, cot_co]
+        middle, normed_mid_rows = clock(*middle_rows(x, feed_gain, [own, own_came, b_in, a_in]))
+
+        def feed_group(clock, pieces, low, high, past):
+            pieces = [None] * low + [clock(pieces[0]), *pieces[1:]]
+            return clock(
+                *feed(pieces, low, high, hidden_grad, gate_rows, up_rows, group, past)
             )
-        )
-        parts = clock(*parts)
-        shared = belt.begin(clock(add_rows(*parts)))
-        up_one = belt.back(gate_one, up_one)
-        down_gradient = belt.end(down_two, units, units // 2, down_gradient)
-        belt.cross(gate_two)
-        belt.cross(shared)
-        state = second_part(feed_share, *first_part(feed_share))
-        parts = third_part(*state)
-        up_two = belt.back(gate_two, up_two)
-        gate_gradient = belt.end(gate_one, units)
-        belt.cross(up_one)
-        belt.back(shared)
-        parts = clock(*parts)
-        out_one = belt.begin(out_one)
+
+        def near_feed(clock, near):
+            cotangent = clock(join([clock(cot_pieces[0]), *cot_pieces[1:]]))
+            return [cotangent, *feed_group(clock, near, 0, 2, None)]
+
+        def next_feed(clock, near, more):
+            return feed_group(clock, near, 2, 6, more[1:])
+
+        mid_pieces, (cotangent, *_), past = gather(normed_mid_rows, near_feed, next_feed)
+        hidden, gate_grad, upward_grad = feed_group(clock, mid_pieces[6:], 6, 8, past)
+        chunk = units * 3 // 4
+        tall = dim * 3 // (4 * group)
+        beside = chunk - tall
+        one, tail = clock(*weight_product(clock(hidden), cotangent, [chunk, units - chunk]))
+        one = belt.begin(one)
+        two = []
+
+        def middle_filler(clock):
+            normed_mid = clock(join([clock(mid_pieces[0]), *mid_pieces[1:]]))
+            part, rest = clock(*weight_product(gate_grad, normed_mid, [chunk, units - half], tail))
+            two.append(belt.begin(part))
+            return [normed_mid, rest]
+
+        share = shares([gate_grad, upward_grad], [gate_rows, up_rows], group)
+        parts, (normed_mid, tail) = scatter(share, middle_filler)
+        two = two[0]
+        belt.cross(one)
+        middle_grad, attention_grad, feed_gain_part = clock(
+            *middle_back(middle, feed_gain, cotangent_rows, parts)
+        )
+
+        def near_grad(clock, near):
+            outer = clock(rows_product([clock(near[0]), near[1]], out_proj, bf16))
+            pair = clock(*weight_product(clock(upward_grad), normed_mid, [chunk, chunk], tail))
+            return [outer, *pair]
+
+        def next_grad(clock, near, more):
+            return [clock(rows_product([clock(near[0]), *near[1:]], out_proj, bf16))]
+
+        grad_pieces, (outer_near, three, four), (outer_next,) = gather(
+            attention_grad, near_grad, next_grad, last=True
+        )
+        outer_last = clock(rows_product([clock(grad_pieces[6]), grad_pieces[7]], out_proj, bf16))
+        three = belt.back(one, three)
+        belt.cross(two)
+
+        query_pre_grad, pair_grads = clock(*attend_back([outer_near, outer_next, clock(outer_last)]))
+
+        def latent_filler(clock):
+            whole = clock(join([clock(grad_pieces[0]), *grad_pieces[1:]]))
+            return clock(*weight_product(mixed_there, whole, [beside, size - beside]))
+
+        share = latent_shares(plane.table, query_pre_grad, pair_grads, query_up)
+        parts, (five, six) = scatter(share, latent_filler)
+        packed_grad, query_gain_part = clock(
+            *latent_back(latent, query_gain, own_cosine, own_sine, parts)
+        )
+        belt.cross(three)
+        four = belt.back(two, four)
+
+        shared_pieces = clock(*shared_shares(plane.table, normed_rows, packed_grad))
+
+        def shared_filler(clock):
+            leaving = clock(*leave_rows(clock(packed_grad)))
+            product = clock(weight_product(clock(latents), query_pre_grad, [rank])[0])
+            belt.land(one)
+            return [*leaving, product, clock(belt.end(one, units))]
+
+        parts, (input_gradient, attention_gain_part, query_sum, down_gradient) = scatter(
+            lambda clock, low, high: shared_pieces[low:high], shared_filler
+        )
+        five = clock(pack(parts, five))
+        belt.cross(four)
+        five = belt.back(three, five)
+        fill = -(2 * dim + rank) % (16 * dim)
+
+        def gain_rows(clock):
+            gains = sum_gains(
+                [clock(attention_gain_part), query_gain_part, feed_gain_part], plane.total
+            )
+            gains = jnp.concatenate([gains[0], jnp.zeros((fill,), f32)]).reshape(-1, dim)
+            return [pack_last(six, query_sum, gains.astype(bf16))]
+
+        (six,) = stage(gain_rows)
+
+        settled = []
+
+        def turn():
+            belt.back(four)
+            belt.cross(five)
+            begun = belt.begin(six)
+            belt.land(two)
+            down = clock(belt.end(two, units, chunk, down_gradient, 0, units - chunk))
+            gate = clock(belt.end(two, units, 0, None, units - chunk))
+            belt.land(three)
+            gate = clock(belt.end(three, units, half, gate, 0, half))
+            up = clock(belt.end(three, units, 0, None, half))
+            belt.land(four)
+            belt.back(five)
+            belt.cross(begun)
+            settled.extend([begun, down, gate, up])
+
+        share = shares([hidden], [down_weight], group)
+        parts, _ = scatter(share, None, True, turn)
         block_output = clock(add_rows(middle, *parts))
-        gains = jnp.concatenate([attention_gain_part, query_gain_part, feed_gain_part], axis=1)
-        gains = line.total(plane.total(gains), lambda left, right: left + right)[0]
-        belt.back(up_one)
-        gate_gradient = belt.end(gate_two, units, units // 2, gate_gradient)
-        belt.cross(up_two)
-        own = clock(jnp.where(belt.inner[0] == 1, shared["own"], clock(shared["came"])))
-        a, b, s_o = move(own, hop_a), move(own, hop_b), move(own, hop_c)
-        out_two = belt.begin(out_two)
-        query_sum = belt.begin(query_sum)
-        belt.cross(out_one)
-        a, b = clock(a, b)
-        c, a_o, b_o = move(a, hop_b), move(a, hop_c), move(b, hop_c)
-        belt.back(up_two)
-        up_gradient = belt.end(up_one, units)
-        belt.cross(out_two)
-        c = clock(c)
-        c_o = clock(move(c, hop_c))
-        belt.back(out_one)
-        belt.cross(query_sum)
-        up_gradient = belt.end(up_two, units, units // 2, up_gradient)
-        belt.back(out_two)
-        size = heads * width
-        proj_gradient = belt.end(out_one, size)
-        belt.back(query_sum)
-        proj_gradient = belt.end(out_two, size, size // 2, proj_gradient)
-        query_up_gradient = belt.end(query_sum, rank)
-        shared_all = [own, s_o, a, a_o, b, b_o, c, c_o]
-    else:
-        input_gradient, attention_gain_part = leave(
-            packed_grad, query_down, key_proj, value_proj, x, attention_gain, middle_grad
-        )
-        block_output = add_rows(middle, plane.scatter(feed_share(0, group)))
-        gains = jnp.concatenate([attention_gain_part, query_gain_part, feed_gain_part], axis=1)
-        gains = line.total(plane.total(gains), lambda left, right: left + right)[0]
-        shared = line.total(plane.scatter(list(shared_pieces)).astype(bf16))
-        shared_all = plane.gather(shared)
-        down_gradient, gate_gradient, up_gradient, proj_gradient, query_up_gradient = (
-            line.total(value).astype(f32)
-            for value in (
-                weight_product(hidden, cotangent, 1)[0],
-                weight_product(gate_grad, normed_mid, 1)[0],
-                weight_product(upward_grad, normed_mid, 1)[0],
-                out_proj_sum(1)[0],
-                query_up_sum(),
-            )
-        )
-    query_down_gradient, key_proj_gradient, value_proj_gradient = unpack(
-        plane.table,
-        shared_all,
-        ((0, rank), (rank, rank + width), (rank + width, rank + 2 * width)),
-    )
+        six, down_gradient, gate_gradient, up_gradient = settled
+        up_gradient = clock(belt.end(four, units, chunk - half, up_gradient))
+        belt.land(five)
+        shared_rows = clock(pick(belt.inner, five["own"], five["came"], tall))
+
+        def between():
+            belt.back(six)
+
+        shared_all, _, _ = gather(shared_rows, apart=True, between=between)
+        query_down_gradient, key_proj_gradient, value_proj_gradient = clock(
+            *unpack(plane.table, shared_all, columns, True)
+        )
+        proj_gradient = clock(belt.end(five, size, 0, None, tall))
+        belt.land(six)
+        proj_gradient = clock(
+            belt.end(six, size, beside, proj_gradient, 0, size - beside)
+        )
+        query_up_gradient, gains = settle_last(
+            belt.inner, six["own"], six["came"], size - beside, rank, size
+        )
+        gains = gains.reshape(-1)
     return (
         block_output[None],
         input_gradient[None],
@@ -1183,7 +1426,7 @@
         key_proj_gradient,
         value_proj_gradient,
         proj_gradient,
-        gains[dim + rank :],
+        gains[dim + rank : dim + rank + dim],
         gate_gradient.T,
         up_gradient.T,
         down_gradient,

time: 655 us -> 609 us (0.930)
  waiting for transfers between devices: 302 us -> 252 us
  Pallas kernels: 174 us -> 215 us
  starting transfers between devices: 121 us -> 96.7 us
  local copies, waits for them, and re-layouts: 36.5 us -> 26.8 us
    ppermute x26 -> x15, waiting for transfers between devices: 171 us -> 86.4 us  [move(): return lax.ppermute(value, 'tok', pairs)]
    ppermute x73, waiting for transfers between devices: 128 us -> 166 us  [move(): return lax.ppermute(value, 'head', hop)]
    ppermute x26 -> x15, starting transfers between devices: 75.4 us -> 42.3 us  [move(): return lax.ppermute(value, 'tok', pairs)]
    ppermute x73, starting transfers between devices: 37.6 us -> 54.3 us  [move(): return lax.ppermute(value, 'head', hop)]
    pallas_call x42 -> x37, Pallas kernels: 42.2 us -> 58.1 us  [call(): pl.pallas_call(kernel, out_shape=shapes, in_specs=[smem()] * scalars + [v...]
    pallas_call x24 -> x23, Pallas kernels: 74.6 us -> 85.9 us  [the longest x9 30.2 us: share(): pl.pallas_call(functools.partial(share_kernel, low, size, terms), out_sha...]
    unnamed x252 -> x151, local copies, waits for them, and re-layouts: 33.5 us -> 23.1 us
    ppermute x3 -> x0, starting transfers between devices: 8 us -> none  [start(): return lax.ppermute(value, 'tok', self.stages[stage][0])]
  transfers between devices with their start and end apart: 102 -> 88, of which waited for: 44 -> 35; matrix products, arithmetic and copies ran while one was open for 2% -> 1% of each run, Pallas kernels for 22% -> 31%
where the time goes in v2:
time: 609 us; the launch traced here: 600 us
  waiting for transfers between devices  252 us (41%)
  Pallas kernels  215 us (35%)
  starting transfers between devices  96.7 us (16%)
  local copies, waits for them, and re-layouts  26.8 us (4%)
  other arithmetic  6.42 us (1%)
    ppermute x73, waiting for transfers between devices, move(): return lax.ppermute(value, 'head', hop)  166 us
    ppermute x15, waiting for transfers between devices, move(): return lax.ppermute(value, 'tok', pairs)  86.4 us
    pallas_call x37, Pallas kernels, call(): pl.pallas_call(kernel, out_shape=shapes, in_specs=[smem()] * scalars + [v...  58.1 us
    ppermute x73, starting transfers between devices, move(): return lax.ppermute(value, 'head', hop)  54.3 us
    ppermute x15, starting transfers between devices, move(): return lax.ppermute(value, 'tok', pairs)  42.3 us
    pallas_call x9, Pallas kernels, share(): pl.pallas_call(functools.partial(share_kernel, low, size, terms), out_sha...  30.2 us
    pallas_call x5, Pallas kernels, weight_product(): pl.pallas_call(functools.partial(product_kernel, len(operands) - 2), grid...  26.1 us
    unnamed x151, local copies, waits for them, and re-layouts  23.1 us
  transfers between devices with their start and end apart: 88, of which 35 were waited for; matrix products, arithmetic and copies ran while one was open for 1% of the time, Pallas kernels for 31%

profile of v2, /device:TPU:0, one launch (start us, length us, event | category | flops | bytes accessed | tf_op | source)
XLA Modules:
  0.0 599.8 jit_solution(14463727001397250061)
XLA Ops:
  5.6 5.5 enter.1
  12.2 15.3 %conditional.11 = (bf16[192,1536]{1,0:T(8,128)(2,1)}, bf16[192,1536]{1,0:T(8,128)(2,1)}, bf16[192,1536]{1,0:T(8,128)(2,1)}, f32[1536,128]{1,0:T(8,128)}, f32[1536,128]{1,0:T(8,128)}) conditional(s32[]{:T(128)} %bitcast.14, () %tuple.297, (bf16[192,1536]{1,0:T(8,128)(2,1)}, s32[1,1536]{1,0:T(1,128)S(1)}) %tuple.508), branch_computations={%region_0.1_spmd, %region_1.2_spmd} | conditional | flops 198400 | bytes 8682660 | solution.py:1116
  14.4 4.3 multiply_sine_fusion
  18.7 8.8 %collective-permute-done.19 = bf16[192,1536]{1,0:T(8,128)(2,1)} collective-permute-done((bf16[192,1536]{1,0:T(8,128)(2,1)}, bf16[192,1536]{1,0:T(8,128)(2,1)}, u32[]{:S(2)}, u32[]{:S(2)}) %collective-permute-start.19) | collective-permute-done | bytes 589856 | tf_op jit(solution)/shard_map/cond/branch_1_fun/ppermute | solution.py:107
  27.5 10.3 %conditional.12 = (bf16[192,1536]{1,0:T(8,128)(2,1)}, bf16[192,1536]{1,0:T(8,128)(2,1)}, bf16[192,1536]{1,0:T(8,128)(2,1)}) conditional(s32[]{:T(128)} %bitcast.14, () %tuple.296, (bf16[192,1536]{1,0:T(8,128)(2,1)}, bf16[192,1536]{1,0:T(8,128)(2,1)}) %tuple.300), branch_computations={%region_2.3_spmd, %region_3.4_spmd} | conditional | bytes 7078032 | solution.py:1116
  29.7 8.0 %collective-permute-done = bf16[192,1536]{1,0:T(8,128)(2,1)} collective-permute-done((bf16[192,1536]{1,0:T(8,128)(2,1)}, bf16[192,1536]{1,0:T(8,128)(2,1)}, u32[]{:S(2)}, u32[]{:S(2)}) %collective-permute-start) | collective-permute-done | bytes 589856 | tf_op jit(solution)/shard_map/cond/branch_1_fun/ppermute | solution.py:107
  45.1 11.3 %attend_forward.1 = (bf16[1536,1024]{1,0:T(8,128)(2,1)}, bf16[1536,512]{1,0:T(8,128)(2,1)S(1)}, bf16[1536,256]{1,0:T(8,128)(2,1)S(1)}, bf16[1536,256]{1,0:T(8,128)(2,1)S(1)}, bf16[1536,512]{1,0:T(8,128)(2,1)}) custom-call(s32[8]{0:T(128)S(1)} %stack.35.refs_0_.table, bf16[192,1536]{1,0:T(8,128)(2,1)} %get-tuple-element.577.refs_1_, ...), custom_call_target="tpu_custom_call" | custom-call | flops 1024 | bytes 1024 | tf_op jit(solution)/shard_map/attend_forward/pallas_call | solution.py:280
  68.3 9.8 %collective-permute-done.31.refs_2_ = bf16[192,2048]{1,0:T(8,128)(2,1)S(1)} collective-permute-done((bf16[192,2048]{1,0:T(8,128)(2,1)S(1)}, bf16[192,2048]{1,0:T(8,128)(2,1)S(1)}, u32[]{:S(2)}, u32[]{:S(2)}) %collective-permute-start.31) | collective-permute-done | bytes 786464 | tf_op jit(solution)/shard_map/ppermute | solution.py:107
  82.4 7.4 %rows_product.4.refs_2_.refs_4_ = f32[1536,704]{1,0:T(8,128)S(1)} custom-call(bf16[192,2048]{1,0:T(8,128)(2,1)} %bitcast.13.refs_0_.cotangent, bf16[192,2048]{1,0:T(8,128)(2,1)} %collective-permute-done.28.refs_1_, bf16[192,2048]{1,0:T(8,128)(2,1)} %collective-permute-done.25.refs_2_, bf16[192,2048]{1,0:T(8,128)(2,1)} %collective-permute-done.29.refs_3_, ...), custom_call_target="tpu_custom_call" | custom-call | flops 1024 | bytes 1024 | tf_op jit(solution)/shard_map/rows_product/pallas_call | solution.py:382
  89.9 9.4 %collective-permute-done.34.refs_3_ = bf16[192,2048]{1,0:T(8,128)(2,1)S(1)} collective-permute-done((bf16[192,2048]{1,0:T(8,128)(2,1)S(1)}, bf16[192,2048]{1,0:T(8,128)(2,1)S(1)}, u32[]{:S(2)}, u32[]{:S(2)}) %collective-permute-start.34) | collective-permute-done | bytes 786464 | tf_op jit(solution)/shard_map/ppermute | solution.py:107
  109.6 3.9 feed.3
  113.5 7.1 %collective-permute-done.39.refs_0_.refs_2_ = bf16[192,2048]{1,0:T(8,128)(2,1)S(1)} collective-permute-done((bf16[192,2048]{1,0:T(8,128)(2,1)S(1)}, bf16[192,2048]{1,0:T(8,128)(2,1)S(1)}, u32[]{:S(2)}, u32[]{:S(2)}) %collective-permute-start.39) | collective-permute-done | bytes 786464 | tf_op jit(solution)/shard_map/ppermute | solution.py:107
  126.4 8.0 %feed.4 = (bf16[1536,704]{1,0:T(8,128)(2,1)S(1)}, bf16[1536,704]{1,0:T(8,128)(2,1)S(1)}, bf16[1536,704]{1,0:T(8,128)(2,1)S(1)}) custom-call(bf16[192,2048]{1,0:T(8,128)(2,1)S(1)} %collective-permute-done.39.refs_0_.refs_2_, bf16[192,2048]{1,0:T(8,128)(2,1)S(1)} %collective-permute-done.43.refs_1_.refs_3_, ...), custom_call_target="tpu_custom_call", output_to_operand_aliasing={{0}: (7, {}), {1}: (8, {}), {2}: (9, {})} | custom-call | flops 1024 | bytes 1024 | tf_op jit(solution)/shard_map/feed/pallas_call | solution.py:567
  144.3 5.9 weight_product.5
  153.3 5.1 collective-permute-start.53
  158.4 6.0 share.15
  170.3 6.4 %collective-permute-done.47.refs_2_ = bf16[192,2048]{1,0:T(8,128)(2,1)S(1)} collective-permute-done((bf16[192,2048]{1,0:T(8,128)(2,1)S(1)}, bf16[192,2048]{1,0:T(8,128)(2,1)S(1)}, u32[]{:S(2)}, u32[]{:S(2)}) %collective-permute-start.47) | collective-permute-done | bytes 786464 | tf_op jit(solution)/shard_map/ppermute | solution.py:107
  181.6 6.6 %weight_product.6 = (bf16[528,2048]{1,0:T(8,128)(2,1)}, bf16[352,2048]{1,0:T(8,128)(2,1)S(1)}) custom-call(bf16[1536,704]{1,0:T(8,128)(2,1)S(1)} %get-tuple-element.703.refs_0_.left, bf16[1536,2048]{1,0:T(8,128)(2,1)S(1)} %join.4.right, bf16[176,2048]{1,0:T(8,128)(2,1)S(1)} %get-tuple-element.725.refs_0_), custom_call_target="tpu_custom_call" | custom-call | flops 1024 | bytes 1024 | tf_op jit(solution)/shard_map/weight_product/pallas_call | solution.py:696
  188.2 8.7 %collective-permute-done.50.refs_3_ = bf16[192,2048]{1,0:T(8,128)(2,1)S(1)} collective-permute-done((bf16[192,2048]{1,0:T(8,128)(2,1)S(1)}, bf16[192,2048]{1,0:T(8,128)(2,1)S(1)}, u32[]{:S(2)}, u32[]{:S(2)}) %collective-permute-start.50) | collective-permute-done | bytes 786464 | tf_op jit(solution)/shard_map/ppermute | solution.py:107
  196.9 6.9 %collective-permute-done.53.refs_1_ = bf16[528,2048]{1,0:T(8,128)(2,1)} collective-permute-done((bf16[528,2048]{1,0:T(8,128)(2,1)S(1)}, bf16[528,2048]{1,0:T(8,128)(2,1)}, u32[]{:S(2)}, u32[]{:S(2)}) %collective-permute-start.53) | collective-permute-done | bytes 2162720 | tf_op jit(solution)/shard_map/ppermute | solution.py:161
  209.3 7.4 %collective-permute-start.60 = (bf16[528,2048]{1,0:T(8,128)(2,1)}, bf16[528,2048]{1,0:T(8,128)(2,1)}, u32[]{:S(2)}, u32[]{:S(2)}) collective-permute-start(bf16[528,2048]{1,0:T(8,128)(2,1)} %get-tuple-element.728.refs_0_), channel_id=1, source_target_pairs={{0,8},{24,16},{1,9},{25,17},{2,10},{26,18},{3,11},{27,19},{4,12},{... | collective-permute-start | bytes 6488072 | tf_op jit(solution)/shard_map/ppermute | solution.py:161
  224.8 6.3 %weight_product.7 = (bf16[528,2048]{1,0:T(8,128)(2,1)S(1)}, bf16[528,2048]{1,0:T(8,128)(2,1)S(1)}) custom-call(bf16[1536,704]{1,0:T(8,128)(2,1)S(1)} %get-tuple-element.745.refs_1_.left, bf16[1536,2048]{1,0:T(8,128)(2,1)S(1)} %join.4.right, bf16[352,2048]{1,0:T(8,128)(2,1)S(1)} %get-tuple-element.746.refs_0_), custom_call_target="tpu_custom_call" | custom-call | flops 1024 | bytes 1024 | tf_op jit(solution)/shard_map/weight_product/pallas_call | solution.py:696
  233.9 7.2 %collective-permute-done.55.refs_0_.refs_2_ = bf16[192,2048]{1,0:T(8,128)(2,1)} collective-permute-done((bf16[192,2048]{1,0:T(8,128)(2,1)S(1)}, bf16[192,2048]{1,0:T(8,128)(2,1)}, u32[]{:S(2)}, u32[]{:S(2)}) %collective-permute-start.55) | collective-permute-done | bytes 786464 | tf_op jit(solution)/shard_map/ppermute | solution.py:107
  249.4 4.5 collective-permute-done.59.refs_0_.refs_6_
  268.5 9.2 %attend_backward.1 = (bf16[1536,512]{1,0:T(8,128)(2,1)S(1)}, bf16[1536,512]{1,0:T(8,128)(2,1)S(1)}) custom-call(s32[8]{0:T(128)S(1)} %stack.35.refs_0_.table, bf16[384,512]{1,0:T(8,128)(2,1)S(1)} %rows_product.5.refs_1_, bf16[768,512]{1,0:T(8,128)(2,1)S(1)} %copy-done.42, bf16[384,512]{1,0:T(8,128)(2,1)S(1)} %rows_product.7.refs_3_, ...), custom_call_target="tpu_custom_call" | custom-call | flops 1024 | bytes 1024 | tf_op jit(solution)/shard_map/attend_backward/pallas_call | solution.py:347
  288.7 5.4 collective-permute-done.63.refs_2_
  301.5 5.3 weight_product.8
  323.8 10.2 %collective-permute-done.72.refs_2_ = bf16[256,1536]{1,0:T(8,128)(2,1)S(1)} collective-permute-done((bf16[256,1536]{1,0:T(8,128)(2,1)S(1)}, bf16[256,1536]{1,0:T(8,128)(2,1)S(1)}, u32[]{:S(2)}, u32[]{:S(2)}) %collective-permute-start.72) | collective-permute-done | bytes 786464 | tf_op jit(solution)/shard_map/ppermute | solution.py:107
  345.5 8.8 %collective-permute-done.77.refs_3_ = bf16[256,1536]{1,0:T(8,128)(2,1)S(1)} collective-permute-done((bf16[256,1536]{1,0:T(8,128)(2,1)S(1)}, bf16[256,1536]{1,0:T(8,128)(2,1)S(1)}, u32[]{:S(2)}, u32[]{:S(2)}) %collective-permute-start.77) | collective-permute-done | bytes 786464 | tf_op jit(solution)/shard_map/ppermute | solution.py:107
  354.7 13.4 %collective-permute-done.76.refs_1_.refs_2_ = bf16[528,2048]{1,0:T(8,128)(2,1)S(1)} collective-permute-done((bf16[528,2048]{1,0:T(8,128)(2,1)S(1)}, bf16[528,2048]{1,0:T(8,128)(2,1)S(1)}, u32[]{:S(2)}, u32[]{:S(2)}) %collective-permute-start.76) | collective-permute-done | bytes 2162720 | tf_op jit(solution)/shard_map/ppermute | solution.py:161
  376.5 11.6 %conditional.15 = (bf16[448,2048]{1,0:T(8,128)(2,1)}) conditional(s32[]{:T(128)} %bitcast.14, () %tuple.341, (f32[1,2048]{1,0:T(1,128)S(1)}, f32[1,1024]{1,0:T(1,128)S(1)}, f32[1,2048]{1,0:T(1,128)S(1)}, bf16[176,2048]{1,0:T(8,128)(2,1)}, bf16[1024,512]{1,0:T(8,128)(2,1)S(1)}) %tuple.507), branch_computations={%region_8.9_spmd, %region_9.10_spmd} | conditional | flops 41984 | bytes 1835018 | solution.py:1116
  388.2 4.9 share.17
  398.8 12.1 %conditional.17 = (bf16[192,2048]{1,0:T(8,128)(2,1)}, bf16[192,2048]{1,0:T(8,128)(2,1)}, bf16[192,2048]{1,0:T(8,128)(2,1)}, bf16[192,2048]{1,0:T(8,128)(2,1)}, bf16[192,2048]{1,0:T(8,128)(2,1)}) conditional(s32[]{:T(128)} %bitcast.14, () %tuple.324, (bf16[192,2048]{1,0:T(8,128)(2,1)S(1)}, bf16[192,2048]{1,0:T(8,128)(2,1)S(1)}, ...), branch_computations={%region_12.13_spmd, %region_13.14_spmd} | conditional | flops 1024 | bytes 9438368 | solution.py:1116
  401.1 4.5 share.10
  405.6 5.3 collective-permute-done.6
  418.6 4.7 collective-permute-done.80.refs_1_.refs_2_
  426.5 7.8 %collective-permute-start.82 = (bf16[448,2048]{1,0:T(8,128)(2,1)S(1)}, bf16[448,2048]{1,0:T(8,128)(2,1)S(1)}, u32[]{:S(2)}, u32[]{:S(2)}) collective-permute-start(bf16[448,2048]{1,0:T(8,128)(2,1)S(1)} %copy-done.68), channel_id=1, source_target_pairs={{0,8},{24,16},{1,9},{25,17},{2,10},{26,18},{3,11},{27,19},{4,12},{... | collective-permute-start | bytes 5505032 | tf_op jit(solution)/shard_map/ppermute | solution.py:161
  437.3 4.0 settle.12
  444.9 28.1 %collective-permute-done.84.refs_2_ = bf16[528,2048]{1,0:T(8,128)(2,1)S(1)} collective-permute-done((bf16[528,2048]{1,0:T(8,128)(2,1)S(1)}, bf16[528,2048]{1,0:T(8,128)(2,1)S(1)}, u32[]{:S(2)}, u32[]{:S(2)}) %collective-permute-start.84) | collective-permute-done | bytes 2162720 | tf_op jit(solution)/shard_map/ppermute | solution.py:161
  479.3 18.7 %conditional.18 = (bf16[192,2048]{1,0:T(8,128)(2,1)}, bf16[192,2048]{1,0:T(8,128)(2,1)}, bf16[192,2048]{1,0:T(8,128)(2,1)}) conditional(s32[]{:T(128)} %bitcast.14, () %tuple.441, (bf16[192,2048]{1,0:T(8,128)(2,1)S(1)}, bf16[192,2048]{1,0:T(8,128)(2,1)S(1)}, bf16[192,2048]{1,0:T(8,128)(2,1)S(1)}) %tuple.506), branch_computations={%region_14.15_spmd, %region_15.16_spmd} | conditional | bytes 9437328 | solution.py:1116
  482.2 15.8 %collective-permute-done.9 = bf16[192,2048]{1,0:T(8,128)(2,1)} collective-permute-done((bf16[192,2048]{1,0:T(8,128)(2,1)S(1)}, bf16[192,2048]{1,0:T(8,128)(2,1)}, u32[]{:S(2)}, u32[]{:S(2)}) %collective-permute-start.9) | collective-permute-done | bytes 786464 | tf_op jit(solution)/shard_map/cond/branch_1_fun/ppermute | solution.py:107
  506.9 19.5 %collective-permute-done.86.came.refs_2_ = bf16[528,2048]{1,0:T(8,128)(2,1)} collective-permute-done((bf16[528,2048]{1,0:T(8,128)(2,1)S(1)}, bf16[528,2048]{1,0:T(8,128)(2,1)}, u32[]{:S(2)}, u32[]{:S(2)}) %collective-permute-start.86) | collective-permute-done | bytes 2162720 | tf_op jit(solution)/shard_map/ppermute | solution.py:161
  528.0 17.8 %conditional.19 = (bf16[192,2048]{1,0:T(8,128)(2,1)}, bf16[192,2048]{1,0:T(8,128)(2,1)}, bf16[192,2048]{1,0:T(8,128)(2,1)}) conditional(s32[]{:T(128)} %bitcast.14, () %tuple.462, bf16[192,2048]{1,0:T(8,128)(2,1)S(1)} %pick.1.refs_0_), branch_computations={%region_16.17_spmd, %region_17.18_spmd} | conditional | bytes 9437328 | solution.py:1116
  531.0 14.9 %collective-permute-done.12 = bf16[192,2048]{1,0:T(8,128)(2,1)} collective-permute-done((bf16[192,2048]{1,0:T(8,128)(2,1)S(1)}, bf16[192,2048]{1,0:T(8,128)(2,1)}, u32[]{:S(2)}, u32[]{:S(2)}) %collective-permute-start.12) | collective-permute-done | bytes 786464 | tf_op jit(solution)/shard_map/cond/branch_1_fun/ppermute | solution.py:107
  554.2 12.4 %conditional.20 = (bf16[192,2048]{1,0:T(8,128)(2,1)}, bf16[192,2048]{1,0:T(8,128)(2,1)}, bf16[192,2048]{1,0:T(8,128)(2,1)}) conditional(s32[]{:T(128)} %bitcast.14, () %tuple.469, (bf16[192,2048]{1,0:T(8,128)(2,1)}, bf16[192,2048]{1,0:T(8,128)(2,1)}) %tuple.470), branch_computations={%region_18.19_spmd, %region_19.20_spmd} | conditional | bytes 9437328 | solution.py:1116
  555.6 11.0 %collective-permute-done.15 = bf16[192,2048]{1,0:T(8,128)(2,1)} collective-permute-done((bf16[192,2048]{1,0:T(8,128)(2,1)}, bf16[192,2048]{1,0:T(8,128)(2,1)}, u32[]{:S(2)}, u32[]{:S(2)}) %collective-permute-start.15) | collective-permute-done | bytes 786464 | tf_op jit(solution)/shard_map/cond/branch_1_fun/ppermute | solution.py:107
  569.3 7.8 %unpack.1 = (f32[2048,1024]{1,0:T(8,128)}, f32[2048,256]{1,0:T(8,128)}, f32[2048,256]{1,0:T(8,128)}) custom-call(s32[8]{0:T(128)S(1)} %stack.35.refs_0_.table, bf16[192,2048]{1,0:T(8,128)(2,1)S(1)} %pick.1.refs_0_, bf16[192,2048]{1,0:T(8,128)(2,1)} %get-tuple-element.950.refs_1_, bf16[192,2048]{1,0:T(8,128)(2,1)} %get-tuple-element.947.refs_2_, ...), custom_call_target="tpu_custom_call" | custom-call | flops 1024 | bytes 1024 | tf_op jit(solution)/shard_map/unpack/pallas_call | solution.py:1052
  577.2 13.8 %collective-permute-done.87.came.refs_2_ = bf16[448,2048]{1,0:T(8,128)(2,1)} collective-permute-done((bf16[448,2048]{1,0:T(8,128)(2,1)}, bf16[448,2048]{1,0:T(8,128)(2,1)}, u32[]{:S(2)}, u32[]{:S(2)}) %collective-permute-start.87) | collective-permute-done | bytes 1835040 | tf_op jit(solution)/shard_map/ppermute | solution.py:161
  (385 shorter events, 259.2 us)
Async XLA Ops:
  0.6 39.5 %collective-permute-start.25 = (bf16[192,2048]{1,0:T(8,128)(2,1)}, bf16[192,2048]{1,0:T(8,128)(2,1)}, u32[]{:S(2)}, u32[]{:S(2)}) collective-permute-start(bf16[192,2048]{1,0:T(8,128)(2,1)} %bitcast.13.refs_0_.cotangent), channel_id=1, source_target_pairs={{0,2},{1,5},{2,0},{3,7},{4,6},{5,1},{6,4},{7,3},{8,10},{9,13},{10,... | collective-permute-start | bytes 2359304 | tf_op jit(solution)/shard_map/ppermute | solution.py:107
  12.2 15.3 %collective-permute-start.19 = (bf16[192,1536]{1,0:T(8,128)(2,1)}, bf16[192,1536]{1,0:T(8,128)(2,1)}, u32[]{:S(2)}, u32[]{:S(2)}) collective-permute-start(bf16[192,1536]{1,0:T(8,128)(2,1)} %get-tuple-element.71), channel_id=1, source_target_pairs={{0,2},{1,5},{2,0},{3,7},{4,6},{5,1},{6,4},{7,3},{8,10},{9,13},{10,... | collective-permute-start | bytes 1769480 | tf_op jit(solution)/shard_map/cond/branch_1_fun/ppermute | solution.py:107
  12.3 15.2 %collective-permute-start.20 = (bf16[192,1536]{1,0:T(8,128)(2,1)}, bf16[192,1536]{1,0:T(8,128)(2,1)}, u32[]{:S(2)}, u32[]{:S(2)}) collective-permute-start(bf16[192,1536]{1,0:T(8,128)(2,1)} %get-tuple-element.71), channel_id=1, source_target_pairs={{0,4},{1,3},{2,6},{3,1},{4,0},{5,7},{6,2},{7,5},{8,12},{9,11},{10,... | collective-permute-start | bytes 1769480 | tf_op jit(solution)/shard_map/cond/branch_1_fun/ppermute | solution.py:107
  14.3 13.2 %collective-permute-start.21 = (bf16[192,1536]{1,0:T(8,128)(2,1)}, bf16[192,1536]{1,0:T(8,128)(2,1)}, u32[]{:S(2)}, u32[]{:S(2)}) collective-permute-start(bf16[192,1536]{1,0:T(8,128)(2,1)} %get-tuple-element.71), channel_id=1, source_target_pairs={{0,1},{1,0},{2,3},{3,2},{4,5},{5,4},{6,7},{7,6},{8,9},{9,8},{10,11... | collective-permute-start | bytes 1769480 | tf_op jit(solution)/shard_map/cond/branch_1_fun/ppermute | solution.py:107
  40.2 23.4 %collective-permute-start.26 = (bf16[192,2048]{1,0:T(8,128)(2,1)}, bf16[192,2048]{1,0:T(8,128)(2,1)}, u32[]{:S(2)}, u32[]{:S(2)}) collective-permute-start(bf16[192,2048]{1,0:T(8,128)(2,1)} %bitcast.13.refs_0_.cotangent), channel_id=1, source_target_pairs={{0,4},{1,3},{2,6},{3,1},{4,0},{5,7},{6,2},{7,5},{8,12},{9,11},{10,... | collective-permute-start | bytes 2359304 | tf_op jit(solution)/shard_map/ppermute | solution.py:107
  41.8 21.7 %collective-permute-start.27 = (bf16[192,2048]{1,0:T(8,128)(2,1)}, bf16[192,2048]{1,0:T(8,128)(2,1)}, u32[]{:S(2)}, u32[]{:S(2)}) collective-permute-start(bf16[192,2048]{1,0:T(8,128)(2,1)} %collective-permute-done.25.refs_2_), channel_id=1, source_target_pairs={{0,4},{1,3},{2,6},{3,1},{4,0},{5,7},{6,2},{7,5},{8,12},{9,11},{10,... | collective-permute-start | bytes 2359304 | tf_op jit(solution)/shard_map/ppermute | solution.py:107
  42.2 21.3 %collective-permute-start.28 = (bf16[192,2048]{1,0:T(8,128)(2,1)}, bf16[192,2048]{1,0:T(8,128)(2,1)}, u32[]{:S(2)}, u32[]{:S(2)}) collective-permute-start(bf16[192,2048]{1,0:T(8,128)(2,1)} %bitcast.13.refs_0_.cotangent), channel_id=1, source_target_pairs={{0,1},{1,0},{2,3},{3,2},{4,5},{5,4},{6,7},{7,6},{8,9},{9,8},{10,11... | collective-permute-start | bytes 2359304 | tf_op jit(solution)/shard_map/ppermute | solution.py:107
  42.2 21.4 %collective-permute-start.29 = (bf16[192,2048]{1,0:T(8,128)(2,1)}, bf16[192,2048]{1,0:T(8,128)(2,1)}, u32[]{:S(2)}, u32[]{:S(2)}) collective-permute-start(bf16[192,2048]{1,0:T(8,128)(2,1)} %collective-permute-done.25.refs_2_), channel_id=1, source_target_pairs={{0,1},{1,0},{2,3},{3,2},{4,5},{5,4},{6,7},{7,6},{8,9},{9,8},{10,11... | collective-permute-start | bytes 2359304 | tf_op jit(solution)/shard_map/ppermute | solution.py:107
  79.3 20.0 %collective-permute-start.34 = (bf16[192,2048]{1,0:T(8,128)(2,1)S(1)}, bf16[192,2048]{1,0:T(8,128)(2,1)S(1)}, u32[]{:S(2)}, u32[]{:S(2)}) collective-permute-start(bf16[192,2048]{1,0:T(8,128)(2,1)S(1)} %add_rows.26), channel_id=1, source_target_pairs={{0,2},{1,5},{2,0},{3,7},{4,6},{5,1},{6,4},{7,3},{8,10},{9,13},{10,... | collective-permute-start | bytes 2359304 | tf_op jit(solution)/shard_map/ppermute | solution.py:107
  80.6 18.7 %collective-permute-start.35 = (bf16[192,2048]{1,0:T(8,128)(2,1)S(1)}, bf16[192,2048]{1,0:T(8,128)(2,1)S(1)}, u32[]{:S(2)}, u32[]{:S(2)}) collective-permute-start(bf16[192,2048]{1,0:T(8,128)(2,1)S(1)} %add_rows.27), channel_id=1, source_target_pairs={{0,4},{1,3},{2,6},{3,1},{4,0},{5,7},{6,2},{7,5},{8,12},{9,11},{10,... | collective-permute-start | bytes 2359304 | tf_op jit(solution)/shard_map/ppermute | solution.py:107
  82.4 16.8 %collective-permute-start.36 = (bf16[192,2048]{1,0:T(8,128)(2,1)S(1)}, bf16[192,2048]{1,0:T(8,128)(2,1)S(1)}, u32[]{:S(2)}, u32[]{:S(2)}) collective-permute-start(bf16[192,2048]{1,0:T(8,128)(2,1)S(1)} %get-tuple-element.625), channel_id=1, source_target_pairs={{0,1},{1,0},{2,3},{3,2},{4,5},{5,4},{6,7},{7,6},{8,9},{9,8},{10,11... | collective-permute-start | bytes 2359304 | tf_op jit(solution)/shard_map/ppermute | solution.py:107
  100.6 20.1 %collective-permute-start.39 = (bf16[192,2048]{1,0:T(8,128)(2,1)S(1)}, bf16[192,2048]{1,0:T(8,128)(2,1)S(1)}, u32[]{:S(2)}, u32[]{:S(2)}) collective-permute-start(bf16[192,2048]{1,0:T(8,128)(2,1)S(1)} %get-tuple-element.720.refs_0_), channel_id=1, source_target_pairs={{0,2},{1,5},{2,0},{3,7},{4,6},{5,1},{6,4},{7,3},{8,10},{9,13},{10,... | collective-permute-start | bytes 2359304 | tf_op jit(solution)/shard_map/ppermute | solution.py:107
  101.9 18.8 %collective-permute-start.40 = (bf16[192,2048]{1,0:T(8,128)(2,1)S(1)}, bf16[192,2048]{1,0:T(8,128)(2,1)S(1)}, u32[]{:S(2)}, u32[]{:S(2)}) collective-permute-start(bf16[192,2048]{1,0:T(8,128)(2,1)S(1)} %get-tuple-element.720.refs_0_), channel_id=1, source_target_pairs={{0,4},{1,3},{2,6},{3,1},{4,0},{5,7},{6,2},{7,5},{8,12},{9,11},{10,... | collective-permute-start | bytes 2359304 | tf_op jit(solution)/shard_map/ppermute | solution.py:107
  121.2 13.2 %collective-permute-start.42 = (bf16[192,2048]{1,0:T(8,128)(2,1)S(1)}, bf16[192,2048]{1,0:T(8,128)(2,1)S(1)}, u32[]{:S(2)}, u32[]{:S(2)}) collective-permute-start(bf16[192,2048]{1,0:T(8,128)(2,1)S(1)} %collective-permute-done.39.refs_0_.refs_2_), channel_id=1, source_target_pairs={{0,4},{1,3},{2,6},{3,1},{4,0},{5,7},{6,2},{7,5},{8,12},{9,11},{10,... | collective-permute-start | bytes 2359304 | tf_op jit(solution)/shard_map/ppermute | solution.py:107
  153.3 50.5 %collective-permute-start.53 = (bf16[528,2048]{1,0:T(8,128)(2,1)S(1)}, bf16[528,2048]{1,0:T(8,128)(2,1)}, u32[]{:S(2)}, u32[]{:S(2)}) collective-permute-start(bf16[528,2048]{1,0:T(8,128)(2,1)S(1)} %get-tuple-element.683.refs_0_), channel_id=1, source_target_pairs={{0,8},{24,16},{1,9},{25,17},{2,10},{26,18},{3,11},{27,19},{4,12},{... | collective-permute-start | bytes 6488072 | tf_op jit(solution)/shard_map/ppermute | solution.py:161
  177.2 19.7 %collective-permute-start.50 = (bf16[192,2048]{1,0:T(8,128)(2,1)S(1)}, bf16[192,2048]{1,0:T(8,128)(2,1)S(1)}, u32[]{:S(2)}, u32[]{:S(2)}) collective-permute-start(bf16[192,2048]{1,0:T(8,128)(2,1)S(1)} %add_rows.29), channel_id=1, source_target_pairs={{0,2},{1,5},{2,0},{3,7},{4,6},{5,1},{6,4},{7,3},{8,10},{9,13},{10,... | collective-permute-start | bytes 2359304 | tf_op jit(solution)/shard_map/ppermute | solution.py:107
  178.7 18.2 %collective-permute-start.51 = (bf16[192,2048]{1,0:T(8,128)(2,1)S(1)}, bf16[192,2048]{1,0:T(8,128)(2,1)S(1)}, u32[]{:S(2)}, u32[]{:S(2)}) collective-permute-start(bf16[192,2048]{1,0:T(8,128)(2,1)S(1)} %add_rows.30), channel_id=1, source_target_pairs={{0,4},{1,3},{2,6},{3,1},{4,0},{5,7},{6,2},{7,5},{8,12},{9,11},{10,... | collective-permute-start | bytes 2359304 | tf_op jit(solution)/shard_map/ppermute | solution.py:107
  180.1 16.8 %collective-permute-start.52 = (bf16[192,2048]{1,0:T(8,128)(2,1)}, bf16[192,2048]{1,0:T(8,128)(2,1)S(1)}, u32[]{:S(2)}, u32[]{:S(2)}) collective-permute-start(bf16[192,2048]{1,0:T(8,128)(2,1)} %get-tuple-element.719), channel_id=1, source_target_pairs={{0,1},{1,0},{2,3},{3,2},{4,5},{5,4},{6,7},{7,6},{8,9},{9,8},{10,11... | collective-permute-start | bytes 2359304 | tf_op jit(solution)/shard_map/ppermute | solution.py:107
  207.3 51.8 %collective-permute-start.61 = (bf16[528,2048]{1,0:T(8,128)(2,1)}, bf16[528,2048]{1,0:T(8,128)(2,1)}, u32[]{:S(2)}, u32[]{:S(2)}) collective-permute-start(bf16[528,2048]{1,0:T(8,128)(2,1)} %add_rows.31.own), channel_id=1, source_target_pairs={{8,16},{16,8},{9,17},{17,9},{10,18},{18,10},{11,19},{19,11},{12,20... | collective-permute-start | bytes 6488072 | tf_op jit(solution)/shard_map/ppermute | solution.py:161
  209.3 54.1 %collective-permute-start.60 = (bf16[528,2048]{1,0:T(8,128)(2,1)}, bf16[528,2048]{1,0:T(8,128)(2,1)}, u32[]{:S(2)}, u32[]{:S(2)}) collective-permute-start(bf16[528,2048]{1,0:T(8,128)(2,1)} %get-tuple-element.728.refs_0_), channel_id=1, source_target_pairs={{0,8},{24,16},{1,9},{25,17},{2,10},{26,18},{3,11},{27,19},{4,12},{... | collective-permute-start | bytes 6488072 | tf_op jit(solution)/shard_map/ppermute | solution.py:161
  221.0 20.1 %collective-permute-start.55 = (bf16[192,2048]{1,0:T(8,128)(2,1)S(1)}, bf16[192,2048]{1,0:T(8,128)(2,1)}, u32[]{:S(2)}, u32[]{:S(2)}) collective-permute-start(bf16[192,2048]{1,0:T(8,128)(2,1)S(1)} %get-tuple-element.811.refs_0_), channel_id=1, source_target_pairs={{0,2},{1,5},{2,0},{3,7},{4,6},{5,1},{6,4},{7,3},{8,10},{9,13},{10,... | collective-permute-start | bytes 2359304 | tf_op jit(solution)/shard_map/ppermute | solution.py:107
  222.5 18.6 %collective-permute-start.56 = (bf16[192,2048]{1,0:T(8,128)(2,1)S(1)}, bf16[192,2048]{1,0:T(8,128)(2,1)}, u32[]{:S(2)}, u32[]{:S(2)}) collective-permute-start(bf16[192,2048]{1,0:T(8,128)(2,1)S(1)} %get-tuple-element.811.refs_0_), channel_id=1, source_target_pairs={{0,4},{1,3},{2,6},{3,1},{4,0},{5,7},{6,2},{7,5},{8,12},{9,11},{10,... | collective-permute-start | bytes 2359304 | tf_op jit(solution)/shard_map/ppermute | solution.py:107
  241.6 12.3 %collective-permute-start.59 = (bf16[192,2048]{1,0:T(8,128)(2,1)}, bf16[192,2048]{1,0:T(8,128)(2,1)}, u32[]{:S(2)}, u32[]{:S(2)}) collective-permute-start(bf16[192,2048]{1,0:T(8,128)(2,1)} %collective-permute-done.55.refs_0_.refs_2_), channel_id=1, source_target_pairs={{0,4},{1,3},{2,6},{3,1},{4,0},{5,7},{6,2},{7,5},{8,12},{9,11},{10,... | collective-permute-start | bytes 2359304 | tf_op jit(solution)/shard_map/ppermute | solution.py:107
  261.5 52.3 %collective-permute-start.70 = (bf16[528,2048]{1,0:T(8,128)(2,1)S(1)}, bf16[528,2048]{1,0:T(8,128)(2,1)S(1)}, u32[]{:S(2)}, u32[]{:S(2)}) collective-permute-start(bf16[528,2048]{1,0:T(8,128)(2,1)S(1)} %add_or_begin.3.refs_1_), channel_id=1, source_target_pairs={{0,8},{24,16},{8,0},{16,24},{1,9},{25,17},{9,1},{17,25},{2,10},{26... | collective-permute-start | bytes 6488072 | tf_op jit(solution)/shard_map/ppermute | solution.py:161
  266.4 47.9 %collective-permute-start.69 = (bf16[528,2048]{1,0:T(8,128)(2,1)S(1)}, bf16[528,2048]{1,0:T(8,128)(2,1)}, u32[]{:S(2)}, u32[]{:S(2)}) collective-permute-start(bf16[528,2048]{1,0:T(8,128)(2,1)S(1)} %add_rows.32.own), channel_id=1, source_target_pairs={{8,16},{16,8},{9,17},{17,9},{10,18},{18,10},{11,19},{19,11},{12,20... | collective-permute-start | bytes 6488072 | tf_op jit(solution)/shard_map/ppermute | solution.py:161
  294.5 16.1 %collective-permute-start.66 = (bf16[192,1536]{1,0:T(8,128)(2,1)S(1)}, bf16[192,1536]{1,0:T(8,128)(2,1)S(1)}, u32[]{:S(2)}, u32[]{:S(2)}) collective-permute-start(bf16[192,1536]{1,0:T(8,128)(2,1)S(1)} %add_rows.34), channel_id=1, source_target_pairs={{0,2},{1,5},{2,0},{3,7},{4,6},{5,1},{6,4},{7,3},{8,10},{9,13},{10,... | collective-permute-start | bytes 1769480 | tf_op jit(solution)/shard_map/ppermute | solution.py:107
  296.1 14.6 %collective-permute-start.67 = (bf16[192,1536]{1,0:T(8,128)(2,1)S(1)}, bf16[192,1536]{1,0:T(8,128)(2,1)S(1)}, u32[]{:S(2)}, u32[]{:S(2)}) collective-permute-start(bf16[192,1536]{1,0:T(8,128)(2,1)S(1)} %add_rows.35), channel_id=1, source_target_pairs={{0,4},{1,3},{2,6},{3,1},{4,0},{5,7},{6,2},{7,5},{8,12},{9,11},{10,... | collective-permute-start | bytes 1769480 | tf_op jit(solution)/shard_map/ppermute | solution.py:107
  297.8 12.9 %collective-permute-start.68 = (bf16[192,1536]{1,0:T(8,128)(2,1)S(1)}, bf16[192,1536]{1,0:T(8,128)(2,1)S(1)}, u32[]{:S(2)}, u32[]{:S(2)}) collective-permute-start(bf16[192,1536]{1,0:T(8,128)(2,1)S(1)} %get-tuple-element.810), channel_id=1, source_target_pairs={{0,1},{1,0},{2,3},{3,2},{4,5},{5,4},{6,7},{7,6},{8,9},{9,8},{10,11... | collective-permute-start | bytes 1769480 | tf_op jit(solution)/shard_map/ppermute | solution.py:107
  317.5 50.6 %collective-permute-start.76 = (bf16[528,2048]{1,0:T(8,128)(2,1)S(1)}, bf16[528,2048]{1,0:T(8,128)(2,1)S(1)}, u32[]{:S(2)}, u32[]{:S(2)}) collective-permute-start(bf16[528,2048]{1,0:T(8,128)(2,1)S(1)} %add_or_begin.4.refs_1_), channel_id=1, source_target_pairs={{0,8},{24,16},{8,0},{16,24},{1,9},{25,17},{9,1},{17,25},{2,10},{26... | collective-permute-start | bytes 6488072 | tf_op jit(solution)/shard_map/ppermute | solution.py:161
  320.5 51.7 %collective-permute-start.75 = (bf16[528,2048]{1,0:T(8,128)(2,1)S(1)}, bf16[528,2048]{1,0:T(8,128)(2,1)S(1)}, u32[]{:S(2)}, u32[]{:S(2)}) collective-permute-start(bf16[528,2048]{1,0:T(8,128)(2,1)S(1)} %add_rows.36.own), channel_id=1, source_target_pairs={{8,16},{16,8},{9,17},{17,9},{10,18},{18,10},{11,19},{19,11},{12,20... | collective-permute-start | bytes 6488072 | tf_op jit(solution)/shard_map/ppermute | solution.py:161
  334.5 19.8 %collective-permute-start.77 = (bf16[256,1536]{1,0:T(8,128)(2,1)S(1)}, bf16[256,1536]{1,0:T(8,128)(2,1)S(1)}, u32[]{:S(2)}, u32[]{:S(2)}) collective-permute-start(bf16[256,1536]{1,0:T(8,128)(2,1)S(1)} %add_rows.38), channel_id=1, source_target_pairs={{0,2},{1,5},{2,0},{3,7},{4,6},{5,1},{6,4},{7,3},{8,10},{9,13},{10,... | collective-permute-start | bytes 2359304 | tf_op jit(solution)/shard_map/ppermute | solution.py:107
  336.0 18.3 %collective-permute-start.78 = (bf16[256,1536]{1,0:T(8,128)(2,1)S(1)}, bf16[256,1536]{1,0:T(8,128)(2,1)S(1)}, u32[]{:S(2)}, u32[]{:S(2)}) collective-permute-start(bf16[256,1536]{1,0:T(8,128)(2,1)S(1)} %add_rows.39), channel_id=1, source_target_pairs={{0,4},{1,3},{2,6},{3,1},{4,0},{5,7},{6,2},{7,5},{8,12},{9,11},{10,... | collective-permute-start | bytes 2359304 | tf_op jit(solution)/shard_map/ppermute | solution.py:107
  337.4 16.9 %collective-permute-start.79 = (bf16[256,1536]{1,0:T(8,128)(2,1)S(1)}, bf16[256,1536]{1,0:T(8,128)(2,1)S(1)}, u32[]{:S(2)}, u32[]{:S(2)}) collective-permute-start(bf16[256,1536]{1,0:T(8,128)(2,1)S(1)} %get-tuple-element.878), channel_id=1, source_target_pairs={{0,1},{1,0},{2,3},{3,2},{4,5},{5,4},{6,7},{7,6},{8,9},{9,8},{10,11... | collective-permute-start | bytes 2359304 | tf_op jit(solution)/shard_map/ppermute | solution.py:107
  370.0 44.2 %collective-permute-start.81 = (bf16[528,2048]{1,0:T(8,128)(2,1)}, bf16[528,2048]{1,0:T(8,128)(2,1)}, u32[]{:S(2)}, u32[]{:S(2)}) collective-permute-start(bf16[528,2048]{1,0:T(8,128)(2,1)} %add_rows.40.refs_0_), channel_id=1, source_target_pairs={{8,16},{16,8},{9,17},{17,9},{10,18},{18,10},{11,19},{19,11},{12,20... | collective-permute-start | bytes 6488072 | tf_op jit(solution)/shard_map/ppermute | solution.py:161
  373.8 49.5 %collective-permute-start.80 = (bf16[528,2048]{1,0:T(8,128)(2,1)}, bf16[528,2048]{1,0:T(8,128)(2,1)}, u32[]{:S(2)}, u32[]{:S(2)}) collective-permute-start(bf16[528,2048]{1,0:T(8,128)(2,1)} %add_or_begin.5.refs_1_), channel_id=1, source_target_pairs={{0,8},{24,16},{8,0},{16,24},{1,9},{25,17},{9,1},{17,25},{2,10},{26... | collective-permute-start | bytes 6488072 | tf_op jit(solution)/shard_map/ppermute | solution.py:161
  417.1 55.9 %collective-permute-start.84 = (bf16[528,2048]{1,0:T(8,128)(2,1)S(1)}, bf16[528,2048]{1,0:T(8,128)(2,1)S(1)}, u32[]{:S(2)}, u32[]{:S(2)}) collective-permute-start(bf16[528,2048]{1,0:T(8,128)(2,1)S(1)} %add_rows.44.refs_1_), channel_id=1, source_target_pairs={{8,0},{16,24},{9,1},{17,25},{10,2},{18,26},{11,3},{19,27},{12,4},{... | collective-permute-start | bytes 6488072 | tf_op jit(solution)/shard_map/ppermute | solution.py:161
  425.7 47.3 %collective-permute-start.83 = (bf16[528,2048]{1,0:T(8,128)(2,1)S(1)}, bf16[528,2048]{1,0:T(8,128)(2,1)S(1)}, u32[]{:S(2)}, u32[]{:S(2)}) collective-permute-start(bf16[528,2048]{1,0:T(8,128)(2,1)S(1)} %add_rows.45.refs_0_), channel_id=1, source_target_pairs={{8,16},{16,8},{9,17},{17,9},{10,18},{18,10},{11,19},{19,11},{12,20... | collective-permute-start | bytes 6488072 | tf_op jit(solution)/shard_map/ppermute | solution.py:161
  426.5 49.2 %collective-permute-start.82 = (bf16[448,2048]{1,0:T(8,128)(2,1)S(1)}, bf16[448,2048]{1,0:T(8,128)(2,1)S(1)}, u32[]{:S(2)}, u32[]{:S(2)}) collective-permute-start(bf16[448,2048]{1,0:T(8,128)(2,1)S(1)} %copy-done.68), channel_id=1, source_target_pairs={{0,8},{24,16},{1,9},{25,17},{2,10},{26,18},{3,11},{27,19},{4,12},{... | collective-permute-start | bytes 5505032 | tf_op jit(solution)/shard_map/ppermute | solution.py:161
  474.3 52.1 %collective-permute-start.86 = (bf16[528,2048]{1,0:T(8,128)(2,1)S(1)}, bf16[528,2048]{1,0:T(8,128)(2,1)}, u32[]{:S(2)}, u32[]{:S(2)}) collective-permute-start(bf16[528,2048]{1,0:T(8,128)(2,1)S(1)} %add_rows.46.own.refs_1_), channel_id=1, source_target_pairs={{8,0},{16,24},{9,1},{17,25},{10,2},{18,26},{11,3},{19,27},{12,4},{... | collective-permute-start | bytes 6488072 | tf_op jit(solution)/shard_map/ppermute | solution.py:161
  477.3 68.5 %collective-permute-start.85 = (bf16[448,2048]{1,0:T(8,128)(2,1)}, bf16[448,2048]{1,0:T(8,128)(2,1)}, u32[]{:S(2)}, u32[]{:S(2)}) collective-permute-start(bf16[448,2048]{1,0:T(8,128)(2,1)} %add_rows.47.refs_0_), channel_id=1, source_target_pairs={{8,16},{16,8},{9,17},{17,9},{10,18},{18,10},{11,19},{19,11},{12,20... | collective-permute-start | bytes 5505032 | tf_op jit(solution)/shard_map/ppermute | solution.py:161
  479.3 18.7 %collective-permute-start.9 = (bf16[192,2048]{1,0:T(8,128)(2,1)S(1)}, bf16[192,2048]{1,0:T(8,128)(2,1)}, u32[]{:S(2)}, u32[]{:S(2)}) collective-permute-start(bf16[192,2048]{1,0:T(8,128)(2,1)S(1)} %get-tuple-element.122), channel_id=1, source_target_pairs={{0,2},{1,5},{2,0},{3,7},{4,6},{5,1},{6,4},{7,3},{8,10},{9,13},{10,... | collective-permute-start | bytes 2359304 | tf_op jit(solution)/shard_map/cond/branch_1_fun/ppermute | solution.py:107
  480.8 17.2 %collective-permute-start.10 = (bf16[192,2048]{1,0:T(8,128)(2,1)S(1)}, bf16[192,2048]{1,0:T(8,128)(2,1)}, u32[]{:S(2)}, u32[]{:S(2)}) collective-permute-start(bf16[192,2048]{1,0:T(8,128)(2,1)S(1)} %get-tuple-element.123), channel_id=1, source_target_pairs={{0,4},{1,3},{2,6},{3,1},{4,0},{5,7},{6,2},{7,5},{8,12},{9,11},{10,... | collective-permute-start | bytes 2359304 | tf_op jit(solution)/shard_map/cond/branch_1_fun/ppermute | solution.py:107
  482.2 15.8 %collective-permute-start.11 = (bf16[192,2048]{1,0:T(8,128)(2,1)S(1)}, bf16[192,2048]{1,0:T(8,128)(2,1)}, u32[]{:S(2)}, u32[]{:S(2)}) collective-permute-start(bf16[192,2048]{1,0:T(8,128)(2,1)S(1)} %get-tuple-element.124), channel_id=1, source_target_pairs={{0,1},{1,0},{2,3},{3,2},{4,5},{5,4},{6,7},{7,6},{8,9},{9,8},{10,11... | collective-permute-start | bytes 2359304 | tf_op jit(solution)/shard_map/cond/branch_1_fun/ppermute | solution.py:107
  528.0 17.8 %collective-permute-start.12 = (bf16[192,2048]{1,0:T(8,128)(2,1)S(1)}, bf16[192,2048]{1,0:T(8,128)(2,1)}, u32[]{:S(2)}, u32[]{:S(2)}) collective-permute-start(bf16[192,2048]{1,0:T(8,128)(2,1)S(1)} %param.17), channel_id=1, source_target_pairs={{0,2},{1,5},{2,0},{3,7},{4,6},{5,1},{6,4},{7,3},{8,10},{9,13},{10,... | collective-permute-start | bytes 2359304 | tf_op jit(solution)/shard_map/cond/branch_1_fun/ppermute | solution.py:107
  529.6 16.3 %collective-permute-start.13 = (bf16[192,2048]{1,0:T(8,128)(2,1)S(1)}, bf16[192,2048]{1,0:T(8,128)(2,1)}, u32[]{:S(2)}, u32[]{:S(2)}) collective-permute-start(bf16[192,2048]{1,0:T(8,128)(2,1)S(1)} %param.17), channel_id=1, source_target_pairs={{0,4},{1,3},{2,6},{3,1},{4,0},{5,7},{6,2},{7,5},{8,12},{9,11},{10,... | collective-permute-start | bytes 2359304 | tf_op jit(solution)/shard_map/cond/branch_1_fun/ppermute | solution.py:107
  531.0 14.9 %collective-permute-start.14 = (bf16[192,2048]{1,0:T(8,128)(2,1)S(1)}, bf16[192,2048]{1,0:T(8,128)(2,1)}, u32[]{:S(2)}, u32[]{:S(2)}) collective-permute-start(bf16[192,2048]{1,0:T(8,128)(2,1)S(1)} %param.17), channel_id=1, source_target_pairs={{0,1},{1,0},{2,3},{3,2},{4,5},{5,4},{6,7},{7,6},{8,9},{9,8},{10,11... | collective-permute-start | bytes 2359304 | tf_op jit(solution)/shard_map/cond/branch_1_fun/ppermute | solution.py:107
  549.6 41.4 %collective-permute-start.87 = (bf16[448,2048]{1,0:T(8,128)(2,1)}, bf16[448,2048]{1,0:T(8,128)(2,1)}, u32[]{:S(2)}, u32[]{:S(2)}) collective-permute-start(bf16[448,2048]{1,0:T(8,128)(2,1)} %add_rows.49.own.refs_1_), channel_id=1, source_target_pairs={{8,0},{16,24},{9,1},{17,25},{10,2},{18,26},{11,3},{19,27},{12,4},{... | collective-permute-start | bytes 5505032 | tf_op jit(solution)/shard_map/ppermute | solution.py:161
  554.3 12.4 %collective-permute-start.15 = (bf16[192,2048]{1,0:T(8,128)(2,1)}, bf16[192,2048]{1,0:T(8,128)(2,1)}, u32[]{:S(2)}, u32[]{:S(2)}) collective-permute-start(bf16[192,2048]{1,0:T(8,128)(2,1)} %get-tuple-element.137), channel_id=1, source_target_pairs={{0,4},{1,3},{2,6},{3,1},{4,0},{5,7},{6,2},{7,5},{8,12},{9,11},{10,... | collective-permute-start | bytes 2359304 | tf_op jit(solution)/shard_map/cond/branch_1_fun/ppermute | solution.py:107
  (115 other events, 898.2 us)

commit v3 on v2

--- a/solution.py
+++ b/solution.py
@@ -169,12 +169,20 @@
         item["own"] = self.clock(add_rows(item["own"], item["came"]))
         item["came"] = self.move(item["own"], self.middle)
 
+    def meet(self, item):
+        item["came"] = self.clock(item["came"])
+        item["own"] = self.clock(add_rows(item["own"], item["came"]))
+
+    def send(self, item):
+        item["own"] = self.clock(item["own"])
+        item["came"] = self.move(item["own"], self.outward)
+
     def back(self, item, value=None):
+        if value is None:
+            self.meet(item)
+            self.send(item)
+            return None
         item["came"] = self.clock(item["came"])
-        if value is None:
-            item["own"] = self.clock(add_rows(item["own"], item["came"]))
-            item["came"] = self.move(item["own"], self.outward)
-            return None
         both = self.clock(add_or_begin(self.inner, item["own"], item["came"], value))
         came = self.move(both, self.inward + self.outward)
         item["own"], item["came"] = both, came
@@ -669,36 +677,67 @@
     )(*operands)
 
 
-def product_kernel(first, left, right, *refs):
-    outs = refs[first:]
-    total = left_transposed(left[...], right[...]).astype(bf16)
+def product_kernel(count, first, step, left, *refs):
+    pieces = refs[:count]
+    outs, held, sems = refs[count + first : -2], refs[-2], refs[-1]
+    rows = pieces[0].shape[0]
+    here = pl.program_id(0)
+    steps = pl.num_programs(0)
+
+    def copies(j, slot):
+        there = pl.ds(pl.multiple_of(j * step, step), step)
+        return [
+            pltpu.make_async_copy(
+                pieces[r].at[:, there], held.at[slot, pl.ds(r * rows, rows), :], sems.at[slot, r]
+            )
+            for r in range(count)
+        ]
+
+    slot = lax.rem(here, 2)
+
+    @pl.when(here == 0)
+    def _():
+        for copy in copies(0, 0):
+            copy.start()
+
+    @pl.when(here + 1 < steps)
+    def _():
+        for copy in copies(here + 1, 1 - slot):
+            copy.start()
+
+    for copy in copies(here, slot):
+        copy.wait()
+    total = left_transposed(left[...], held[slot]).astype(bf16)
     if first:
-        total = jnp.concatenate([refs[0][...], total], axis=0)
+        total = jnp.concatenate([refs[count][...], total], axis=0)
     low = 0
     for out in outs:
-        rows = out.shape[0]
-        out[...] = total[low : low + rows]
-        low += rows
+        size = out.shape[0]
+        out[...] = total[low : low + size]
+        low += size
 
 
 def weight_product(left, right, rows, above=None, step=512):
+    right = list(right) if isinstance(right, (list, tuple)) else [right]
+    count = len(right)
     tokens, units = left.shape
-    columns = right.shape[1]
+    columns = right[0].shape[1]
     step = min(step, columns)
-    operands = [left, right]
-    specs = [
-        pl.BlockSpec((tokens, units), lambda j: (0, 0)),
-        pl.BlockSpec((tokens, step), lambda j: (0, j)),
-    ]
+    operands = [left, *right]
+    specs = [pl.BlockSpec((tokens, units), lambda j: (0, 0))] + [any_space()] * count
     if above is not None:
         operands.append(above)
         specs.append(pl.BlockSpec((above.shape[0], step), lambda j: (0, j)))
     return pl.pallas_call(
-        functools.partial(product_kernel, len(operands) - 2),
+        functools.partial(product_kernel, count, len(operands) - 1 - count, step),
         grid=(columns // step,),
         out_shape=[shaped((one, columns), bf16) for one in rows],
         in_specs=specs,
         out_specs=[pl.BlockSpec((one, step), lambda j: (0, j)) for one in rows],
+        scratch_shapes=[
+            pltpu.VMEM((2, tokens, step), bf16),
+            pltpu.SemaphoreType.DMA((2, count)),
+        ],
         compiler_params=pltpu.CompilerParams(vmem_limit_bytes=30 << 20),
         cost_estimate=brief(),
         name="weight_product",
@@ -724,17 +763,21 @@
     )
 
 
-def settle_last_kernel(top, inner, own, came, wide, below):
+def settle_last_kernel(top, at, inner, own, came, past, wide, below, whole, buffer, sem):
     rows, columns = wide.shape
     parts = own.shape[1] // columns
     step = rows // parts
 
     def write(source):
+        buffer[...] = source[:top, :].astype(f32)
+        copy = pltpu.make_async_copy(buffer, whole.at[pl.ds(at, top), :], sem)
+        copy.start()
         for j in range(parts):
             wide[j * step : (j + 1) * step, :] = source[
                 top : top + step, j * columns : (j + 1) * columns
             ].astype(f32)
         below[...] = source[top + step :, :].astype(f32)
+        copy.wait()
 
     @pl.when(inner[0] == 1)
     def _():
@@ -745,16 +788,24 @@
         write(came)
 
 
-def settle_last(inner, own, came, top, rows, columns):
+def settle_last(inner, own, came, top, rows, columns, past, at):
     total, dim = own.shape
     left = total - top - rows * columns // dim
-    return call(
-        functools.partial(settle_last_kernel, top),
-        [shaped((rows, columns), f32), shaped((left, dim), f32)],
-        [inner, own, came],
-        "settle_last",
-        scalars=1,
-    )
+    return pl.pallas_call(
+        functools.partial(settle_last_kernel, top, at),
+        out_shape=[
+            shaped((rows, columns), f32),
+            shaped((left, dim), f32),
+            shaped(past.shape, f32),
+        ],
+        in_specs=[smem(), vmem(), vmem(), any_space()],
+        out_specs=[vmem(), vmem(), any_space()],
+        scratch_shapes=[pltpu.VMEM((top, dim), f32), pltpu.SemaphoreType.DMA],
+        input_output_aliases={3: 2},
+        compiler_params=pltpu.CompilerParams(vmem_limit_bytes=24 << 20),
+        cost_estimate=brief(),
+        name="settle_last",
+    )(inner, own, came, past)
 
 
 def pack_kernel(count, *refs):
@@ -1003,10 +1054,9 @@
     )
 
 
-def unpack_kernel(count, parts, packed, table, *refs):
+def unpack_kernel(base, count, parts, packed, table, *refs):
     pieces = refs[:count]
-    outs = refs[count : count + len(parts)]
-    buffers = refs[count + len(parts) : -1]
+    outs, buffers = refs[-1 - 2 * len(parts) : -1 - len(parts)], refs[-1 - len(parts) : -1]
     sems = refs[-1]
     rows = buffers[0].shape[1]
     tall = rows * 3 // 4
@@ -1018,7 +1068,7 @@
         if r >= 2:
             for copy in flying[r - 2]:
                 copy.wait()
-        there = pl.ds(pl.multiple_of(table[r] * rows, rows), rows)
+        there = pl.ds(pl.multiple_of(table[base + r] * rows, rows), rows)
         copies = []
         for k, (low, high) in enumerate(parts):
             if packed:
@@ -1044,22 +1094,26 @@
             copy.wait()
 
 
-def unpack(table, pieces, parts, packed):
+def unpack(table, pieces, parts, packed, first=0, past=None):
     count = len(pieces)
     rows = pieces[0].shape[0]
     if packed:
         rows = rows * 4 // 3
+    past = [] if past is None else list(past)
     return pl.pallas_call(
-        functools.partial(unpack_kernel, count, parts, packed),
-        out_shape=[jax.ShapeDtypeStruct((count * rows, high - low), f32) for low, high in parts],
-        in_specs=[smem()] + [vmem()] * count,
+        functools.partial(unpack_kernel, first, count, parts, packed),
+        out_shape=[
+            jax.ShapeDtypeStruct((table.shape[0] * rows, high - low), f32) for low, high in parts
+        ],
+        in_specs=[smem()] + [vmem()] * count + [any_space()] * len(past),
         out_specs=[any_space()] * len(parts),
         scratch_shapes=[pltpu.VMEM((2, rows, high - low), f32) for low, high in parts]
         + [pltpu.SemaphoreType.DMA((len(parts), 2))],
-        compiler_params=pltpu.CompilerParams(vmem_limit_bytes=36 << 20),
+        input_output_aliases={1 + count + k: k for k in range(len(past))},
+        compiler_params=pltpu.CompilerParams(vmem_limit_bytes=24 << 20),
         cost_estimate=brief(),
         name="unpack",
-    )(table, *pieces)
+    )(table, *pieces, *past)
 
 
 def body(
@@ -1292,29 +1346,41 @@
             )
 
         def near_feed(clock, near):
-            cotangent = clock(join([clock(cot_pieces[0]), *cot_pieces[1:]]))
-            return [cotangent, *feed_group(clock, near, 0, 2, None)]
-
-        def next_feed(clock, near, more):
-            return feed_group(clock, near, 2, 6, more[1:])
-
-        mid_pieces, (cotangent, *_), past = gather(normed_mid_rows, near_feed, next_feed)
-        hidden, gate_grad, upward_grad = feed_group(clock, mid_pieces[6:], 6, 8, past)
+            return feed_group(clock, near, 0, 2, None)
+
+        (a, b, s_o), past = hops(
+            [normed_mid_rows] * 3,
+            [hop_a, hop_b, hop_c],
+            lambda clock, a, b, s_o: near_feed(clock, [normed_mid_rows, clock(s_o)]),
+        )
+
+        def next_feed(clock, c, a_o, b_o):
+            a_o, b_o = clock(a_o, b_o)
+            return [a_o, b_o, *feed_group(clock, [a, a_o], 2, 4, past)]
+
+        (c, a_o, b_o), past = hops([a, a, b], [hop_b, hop_c, hop_c], next_feed)
+        a_o, b_o, *past = past
+        (c_o,), past = hops(
+            [c], [hop_c], lambda clock, c_o: feed_group(clock, [b, b_o], 4, 6, past)
+        )
+        hidden, gate_grad, upward_grad = feed_group(clock, [c, c_o], 6, 8, past)
+        mid_pieces = [normed_mid_rows, s_o, a, a_o, b, b_o, c, c_o]
         chunk = units * 3 // 4
         tall = dim * 3 // (4 * group)
         beside = chunk - tall
-        one, tail = clock(*weight_product(clock(hidden), cotangent, [chunk, units - chunk]))
+        one, tail = clock(*weight_product(clock(hidden), cot_pieces, [chunk, units - chunk]))
         one = belt.begin(one)
         two = []
 
         def middle_filler(clock):
-            normed_mid = clock(join([clock(mid_pieces[0]), *mid_pieces[1:]]))
-            part, rest = clock(*weight_product(gate_grad, normed_mid, [chunk, units - half], tail))
+            part, rest = clock(
+                *weight_product(clock(gate_grad), mid_pieces, [chunk, units - half], tail)
+            )
             two.append(belt.begin(part))
-            return [normed_mid, rest]
+            return [rest]
 
         share = shares([gate_grad, upward_grad], [gate_rows, up_rows], group)
-        parts, (normed_mid, tail) = scatter(share, middle_filler)
+        parts, (tail,) = scatter(share, middle_filler)
         two = two[0]
         belt.cross(one)
         middle_grad, attention_grad, feed_gain_part = clock(
@@ -1323,7 +1389,7 @@
 
         def near_grad(clock, near):
             outer = clock(rows_product([clock(near[0]), near[1]], out_proj, bf16))
-            pair = clock(*weight_product(clock(upward_grad), normed_mid, [chunk, chunk], tail))
+            pair = clock(*weight_product(clock(upward_grad), mid_pieces, [chunk, chunk], tail))
             return [outer, *pair]
 
         def next_grad(clock, near, more):
@@ -1339,8 +1405,9 @@
         query_pre_grad, pair_grads = clock(*attend_back([outer_near, outer_next, clock(outer_last)]))
 
         def latent_filler(clock):
-            whole = clock(join([clock(grad_pieces[0]), *grad_pieces[1:]]))
-            return clock(*weight_product(mixed_there, whole, [beside, size - beside]))
+            return clock(
+                *weight_product(clock(mixed_there), grad_pieces, [beside, size - beside])
+            )
 
         share = latent_shares(plane.table, query_pre_grad, pair_grads, query_up)
         parts, (five, six) = scatter(share, latent_filler)
@@ -1362,8 +1429,8 @@
             lambda clock, low, high: shared_pieces[low:high], shared_filler
         )
         five = clock(pack(parts, five))
+        five = belt.back(three, five)
         belt.cross(four)
-        five = belt.back(three, five)
         fill = -(2 * dim + rank) % (16 * dim)
 
         def gain_rows(clock):
@@ -1378,8 +1445,8 @@
         settled = []
 
         def turn():
+            belt.cross(five)
             belt.back(four)
-            belt.cross(five)
             begun = belt.begin(six)
             belt.land(two)
             down = clock(belt.end(two, units, chunk, down_gradient, 0, units - chunk))
@@ -1397,23 +1464,35 @@
         block_output = clock(add_rows(middle, *parts))
         six, down_gradient, gate_gradient, up_gradient = settled
         up_gradient = clock(belt.end(four, units, chunk - half, up_gradient))
+        belt.meet(six)
         belt.land(five)
+        belt.send(six)
         shared_rows = clock(pick(belt.inner, five["own"], five["came"], tall))
 
-        def between():
-            belt.back(six)
-
-        shared_all, _, _ = gather(shared_rows, apart=True, between=between)
+        def five_end(clock, own):
+            held = dict(five, came=clock(five["came"]))
+            return [clock(belt.end(held, size, 0, None, tall))]
+
+        def near_unpack(clock, near, more):
+            pieces = [shared_rows, s_one, *near]
+            return clock(*unpack(plane.table, pieces, columns, True))
+
+        (a, b, s_one), (proj_gradient,) = hops(
+            [shared_rows] * 3, [hop_a, hop_b, hop_c], lambda clock, *came: five_end(clock, None), True
+        )
+
+        def beside_next(clock, c, a_o, b_o):
+            a_o, b_o = clock(a_o, b_o)
+            return near_unpack(clock, [a, a_o, b, b_o], None)
+
+        (c, a_o, b_o), past = hops([a, a, b], [hop_b, hop_c, hop_c], beside_next, True)
+        (c_o,), _ = hops([c], [hop_c], None, True)
         query_down_gradient, key_proj_gradient, value_proj_gradient = clock(
-            *unpack(plane.table, shared_all, columns, True)
-        )
-        proj_gradient = clock(belt.end(five, size, 0, None, tall))
+            *unpack(plane.table, [c, c_o], columns, True, 6, past)
+        )
         belt.land(six)
-        proj_gradient = clock(
-            belt.end(six, size, beside, proj_gradient, 0, size - beside)
-        )
-        query_up_gradient, gains = settle_last(
-            belt.inner, six["own"], six["came"], size - beside, rank, size
+        query_up_gradient, gains, proj_gradient = settle_last(
+            belt.inner, six["own"], six["came"], size - beside, rank, size, proj_gradient, beside
         )
         gains = gains.reshape(-1)
     return (

time: 609 us -> 587 us (0.964)
  waiting for transfers between devices: 252 us -> 228 us
  starting transfers between devices: 96.7 us -> 108 us
  local copies, waits for them, and re-layouts: 26.8 us -> 19.6 us
    ppermute x15, waiting for transfers between devices: 86.4 us -> 59 us  [move(): return lax.ppermute(value, 'tok', pairs)]
    ppermute x15, starting transfers between devices: 42.3 us -> 54.9 us  [move(): return lax.ppermute(value, 'tok', pairs)]
    unnamed x151 -> x157, local copies, waits for them, and re-layouts: 23.1 us -> 15.9 us
    pallas_call x9 -> x8, Pallas kernels: 42.8 us -> 45.6 us  [the longest x5 32.2 us: weight_product(): pl.pallas_call(functools.partial(product_kernel, count, len(operands) - 1...]
    pallas_call x37 -> x36, Pallas kernels: 58.1 us -> 55.7 us  [call(): pl.pallas_call(kernel, out_shape=shapes, in_specs=[smem()] * scalars + [v...]
    pallas_call x8 -> x7, Pallas kernels: 21.8 us -> 19.4 us  [settle(): pl.pallas_call(functools.partial(settle_kernel, low, at), out_shape=shape...]
    pallas_call x3 -> x4, Pallas kernels: 15.7 us -> 15.7 us  [feed(): pl.pallas_call(functools.partial(feed_kernel, pairs, low // 2), out_shape...]
  transfers between devices with their start and end apart: 88 -> 88, of which waited for: 35 -> 36; matrix products, arithmetic and copies ran while one was open for 1% -> 1% of each run, Pallas kernels for 31% -> 32%
where the time goes in v3:
time: 587 us; the launch traced here: 578 us
  waiting for transfers between devices  228 us (39%)
  Pallas kernels  212 us (36%)
  starting transfers between devices  108 us (18%)
  local copies, waits for them, and re-layouts  19.6 us (3%)
  other arithmetic  6.37 us (1%)
    ppermute x73, waiting for transfers between devices, move(): return lax.ppermute(value, 'head', hop)  169 us
    ppermute x15, waiting for transfers between devices, move(): return lax.ppermute(value, 'tok', pairs)  59 us
    pallas_call x36, Pallas kernels, call(): pl.pallas_call(kernel, out_shape=shapes, in_specs=[smem()] * scalars + [v...  55.7 us
    ppermute x15, starting transfers between devices, move(): return lax.ppermute(value, 'tok', pairs)  54.9 us
    ppermute x73, starting transfers between devices, move(): return lax.ppermute(value, 'head', hop)  53.5 us
    pallas_call x5, Pallas kernels, weight_product(): pl.pallas_call(functools.partial(product_kernel, count, len(operands) - 1...  32.2 us
    pallas_call x9, Pallas kernels, share(): pl.pallas_call(functools.partial(share_kernel, low, size, terms), out_sha...  30 us
    pallas_call x7, Pallas kernels, settle(): pl.pallas_call(functools.partial(settle_kernel, low, at), out_shape=shape...  19.4 us
  transfers between devices with their start and end apart: 88, of which 36 were waited for; matrix products, arithmetic and copies ran while one was open for 1% of the time, Pallas kernels for 32%

profile of v3, /device:TPU:0, one launch (start us, length us, event | category | flops | bytes accessed | tf_op | source)
XLA Modules:
  0.0 577.6 jit_solution(2186152561536681901)
XLA Ops:
  5.5 5.5 enter.1
  12.2 15.3 %conditional.11 = (bf16[192,1536]{1,0:T(8,128)(2,1)}, bf16[192,1536]{1,0:T(8,128)(2,1)}, bf16[192,1536]{1,0:T(8,128)(2,1)}, f32[1536,128]{1,0:T(8,128)}, f32[1536,128]{1,0:T(8,128)}) conditional(s32[]{:T(128)} %bitcast.14, () %tuple.300, (bf16[192,1536]{1,0:T(8,128)(2,1)}, s32[1,1536]{1,0:T(1,128)S(1)}) %tuple.508), branch_computations={%region_0.1_spmd, %region_1.2_spmd} | conditional | flops 198400 | bytes 8682660 | solution.py:1170
  14.4 4.3 multiply_sine_fusion
  18.7 8.8 %collective-permute-done.19 = bf16[192,1536]{1,0:T(8,128)(2,1)} collective-permute-done((bf16[192,1536]{1,0:T(8,128)(2,1)}, bf16[192,1536]{1,0:T(8,128)(2,1)}, u32[]{:S(2)}, u32[]{:S(2)}) %collective-permute-start.19) | collective-permute-done | bytes 589856 | tf_op jit(solution)/shard_map/cond/branch_1_fun/ppermute | solution.py:107
  27.5 10.3 %conditional.12 = (bf16[192,1536]{1,0:T(8,128)(2,1)}, bf16[192,1536]{1,0:T(8,128)(2,1)}, bf16[192,1536]{1,0:T(8,128)(2,1)}) conditional(s32[]{:T(128)} %bitcast.14, () %tuple.299, (bf16[192,1536]{1,0:T(8,128)(2,1)}, bf16[192,1536]{1,0:T(8,128)(2,1)}) %tuple.303), branch_computations={%region_2.3_spmd, %region_3.4_spmd} | conditional | bytes 7078032 | solution.py:1170
  29.7 8.0 %collective-permute-done = bf16[192,1536]{1,0:T(8,128)(2,1)} collective-permute-done((bf16[192,1536]{1,0:T(8,128)(2,1)}, bf16[192,1536]{1,0:T(8,128)(2,1)}, u32[]{:S(2)}, u32[]{:S(2)}) %collective-permute-start) | collective-permute-done | bytes 589856 | tf_op jit(solution)/shard_map/cond/branch_1_fun/ppermute | solution.py:107
  45.1 11.1 %attend_forward.1 = (bf16[1536,1024]{1,0:T(8,128)(2,1)}, bf16[1536,512]{1,0:T(8,128)(2,1)S(1)}, bf16[1536,256]{1,0:T(8,128)(2,1)S(1)}, bf16[1536,256]{1,0:T(8,128)(2,1)S(1)}, bf16[1536,512]{1,0:T(8,128)(2,1)}) custom-call(s32[8]{0:T(128)S(1)} %stack.35.refs_0_.table, bf16[192,1536]{1,0:T(8,128)(2,1)} %get-tuple-element.611.refs_1_, ...), custom_call_target="tpu_custom_call" | custom-call | flops 1024 | bytes 1024 | tf_op jit(solution)/shard_map/attend_forward/pallas_call | solution.py:288
  68.3 9.8 %collective-permute-done.31.refs_2_ = bf16[192,2048]{1,0:T(8,128)(2,1)S(1)} collective-permute-done((bf16[192,2048]{1,0:T(8,128)(2,1)S(1)}, bf16[192,2048]{1,0:T(8,128)(2,1)S(1)}, u32[]{:S(2)}, u32[]{:S(2)}) %collective-permute-start.31) | collective-permute-done | bytes 786464 | tf_op jit(solution)/shard_map/ppermute | solution.py:107
  82.4 7.6 %rows_product.4.refs_2_ = f32[1536,704]{1,0:T(8,128)S(1)} custom-call(bf16[192,2048]{1,0:T(8,128)(2,1)} %bitcast.13.refs_0_.cotangent, bf16[192,2048]{1,0:T(8,128)(2,1)} %collective-permute-done.28.refs_1_, bf16[192,2048]{1,0:T(8,128)(2,1)} %collective-permute-done.25.refs_2_, bf16[192,2048]{1,0:T(8,128)(2,1)} %collective-permute-done.29.refs_3_, ...), custom_call_target="tpu_custom_call" | custom-call | flops 1024 | bytes 1024 | tf_op jit(solution)/shard_map/rows_product/pallas_call | solution.py:390
  90.0 9.2 %collective-permute-done.34.refs_3_ = bf16[192,2048]{1,0:T(8,128)(2,1)S(1)} collective-permute-done((bf16[192,2048]{1,0:T(8,128)(2,1)S(1)}, bf16[192,2048]{1,0:T(8,128)(2,1)S(1)}, u32[]{:S(2)}, u32[]{:S(2)}) %collective-permute-start.34) | collective-permute-done | bytes 786464 | tf_op jit(solution)/shard_map/ppermute | solution.py:107
  108.0 13.7 %collective-permute-done.39.refs_0_.refs_2_ = bf16[192,2048]{1,0:T(8,128)(2,1)S(1)} collective-permute-done((bf16[192,2048]{1,0:T(8,128)(2,1)S(1)}, bf16[192,2048]{1,0:T(8,128)(2,1)S(1)}, u32[]{:S(2)}, u32[]{:S(2)}) %collective-permute-start.39) | collective-permute-done | bytes 786464 | tf_op jit(solution)/shard_map/ppermute | solution.py:107
  125.1 4.0 feed.5
  129.2 5.0 collective-permute-done.42.refs_0_.refs_6_
  142.1 8.6 %weight_product.5 = (bf16[528,2048]{1,0:T(8,128)(2,1)}, bf16[176,2048]{1,0:T(8,128)(2,1)S(1)}) custom-call(bf16[1536,704]{1,0:T(8,128)(2,1)S(1)} %get-tuple-element.925.left.refs_0_, bf16[192,2048]{1,0:T(8,128)(2,1)} %bitcast.13.refs_0_.cotangent, bf16[192,2048]{1,0:T(8,128)(2,1)} %collective-permute-done.28.refs_1_, ...), custom_call_target="tpu_custom_call" | custom-call | flops 1024 | bytes 1024 | tf_op jit(solution)/shard_map/weight_product/pallas_call | solution.py:731
  155.1 5.1 collective-permute-start.53
  160.1 5.9 %share.15 = (bf16[192,2048]{1,0:T(8,128)(2,1)S(1)}, bf16[192,2048]{1,0:T(8,128)(2,1)S(1)}, bf16[192,2048]{1,0:T(8,128)(2,1)S(1)}, bf16[192,2048]{1,0:T(8,128)(2,1)S(1)}) custom-call(bf16[1536,704]{1,0:T(8,128)(2,1)S(1)} %get-tuple-element.759.refs_0_.left, bf16[1536,704]{1,0:T(8,128)(2,1)S(1)} %get-tuple-element.781.refs_1_.left, ...), custom_call_target="tpu_custom_call" | custom-call | flops 1024 | bytes 1024 | tf_op jit(solution)/shard_map/share/pallas_call | solution.py:510
  171.8 6.4 %collective-permute-done.47.refs_2_ = bf16[192,2048]{1,0:T(8,128)(2,1)S(1)} collective-permute-done((bf16[192,2048]{1,0:T(8,128)(2,1)S(1)}, bf16[192,2048]{1,0:T(8,128)(2,1)S(1)}, u32[]{:S(2)}, u32[]{:S(2)}) %collective-permute-start.47) | collective-permute-done | bytes 786464 | tf_op jit(solution)/shard_map/ppermute | solution.py:107
  181.6 7.3 %weight_product.6 = (bf16[528,2048]{1,0:T(8,128)(2,1)}, bf16[352,2048]{1,0:T(8,128)(2,1)S(1)}) custom-call(bf16[1536,704]{1,0:T(8,128)(2,1)S(1)} %get-tuple-element.759.refs_0_.left, bf16[192,2048]{1,0:T(8,128)(2,1)S(1)} %copy-done.28, bf16[192,2048]{1,0:T(8,128)(2,1)S(1)} %copy-done.30, bf16[192,2048]{1,0:T(8,128)(2,1)S(1)} %collective-permute-done.39.refs_0_.refs_2_, ...), custom_call_target="tpu_custom_call" | custom-call | flops 1024 | bytes 1024 | tf_op jit(solution)/shard_map/weight_product/pallas_call | solution.py:731
  188.9 9.3 %collective-permute-done.50.refs_3_ = bf16[192,2048]{1,0:T(8,128)(2,1)S(1)} collective-permute-done((bf16[192,2048]{1,0:T(8,128)(2,1)S(1)}, bf16[192,2048]{1,0:T(8,128)(2,1)S(1)}, u32[]{:S(2)}, u32[]{:S(2)}) %collective-permute-start.50) | collective-permute-done | bytes 786464 | tf_op jit(solution)/shard_map/ppermute | solution.py:107
  198.2 7.3 %collective-permute-done.53.refs_1_ = bf16[528,2048]{1,0:T(8,128)(2,1)} collective-permute-done((bf16[528,2048]{1,0:T(8,128)(2,1)}, bf16[528,2048]{1,0:T(8,128)(2,1)}, u32[]{:S(2)}, u32[]{:S(2)}) %collective-permute-start.53) | collective-permute-done | bytes 2162720 | tf_op jit(solution)/shard_map/ppermute | solution.py:161
  205.5 4.1 add_rows.31.own
  211.6 7.3 %collective-permute-start.60 = (bf16[528,2048]{1,0:T(8,128)(2,1)}, bf16[528,2048]{1,0:T(8,128)(2,1)}, u32[]{:S(2)}, u32[]{:S(2)}) collective-permute-start(bf16[528,2048]{1,0:T(8,128)(2,1)} %get-tuple-element.764.refs_0_), channel_id=1, source_target_pairs={{0,8},{24,16},{1,9},{25,17},{2,10},{26,18},{3,11},{27,19},{4,12},{... | collective-permute-start | bytes 6488072 | tf_op jit(solution)/shard_map/ppermute | solution.py:161
  226.8 7.3 %weight_product.7 = (bf16[528,2048]{1,0:T(8,128)(2,1)S(1)}, bf16[528,2048]{1,0:T(8,128)(2,1)S(1)}) custom-call(bf16[1536,704]{1,0:T(8,128)(2,1)S(1)} %get-tuple-element.781.refs_1_.left, bf16[192,2048]{1,0:T(8,128)(2,1)S(1)} %copy-done.28, bf16[192,2048]{1,0:T(8,128)(2,1)S(1)} %copy-done.30, bf16[192,2048]{1,0:T(8,128)(2,1)S(1)} %collective-permute-done.39.refs_0_.refs_2_, ...), custom_call_target="tpu_custom_call" | custom-call | flops 1024 | bytes 1024 | tf_op jit(solution)/shard_map/weight_product/pallas_call | solution.py:731
  237.0 6.2 %collective-permute-done.55.refs_0_.refs_2_ = bf16[192,2048]{1,0:T(8,128)(2,1)} collective-permute-done((bf16[192,2048]{1,0:T(8,128)(2,1)S(1)}, bf16[192,2048]{1,0:T(8,128)(2,1)}, u32[]{:S(2)}, u32[]{:S(2)}) %collective-permute-start.55) | collective-permute-done | bytes 786464 | tf_op jit(solution)/shard_map/ppermute | solution.py:107
  251.6 4.5 collective-permute-done.59.refs_0_.refs_6_
  270.7 9.0 %attend_backward.1 = (bf16[1536,512]{1,0:T(8,128)(2,1)S(1)}, bf16[1536,512]{1,0:T(8,128)(2,1)S(1)}) custom-call(s32[8]{0:T(128)S(1)} %stack.35.refs_0_.table, bf16[384,512]{1,0:T(8,128)(2,1)S(1)} %rows_product.5.refs_1_, bf16[768,512]{1,0:T(8,128)(2,1)S(1)} %copy-done.42, bf16[384,512]{1,0:T(8,128)(2,1)S(1)} %rows_product.7.refs_3_, ...), custom_call_target="tpu_custom_call" | custom-call | flops 1024 | bytes 1024 | tf_op jit(solution)/shard_map/attend_backward/pallas_call | solution.py:355
  290.4 5.6 collective-permute-done.63.refs_2_
  299.4 6.8 %weight_product.8 = (bf16[336,2048]{1,0:T(8,128)(2,1)S(1)}, bf16[176,2048]{1,0:T(8,128)(2,1)}) custom-call(bf16[1536,512]{1,0:T(8,128)(2,1)S(1)} %copy-done.4, bf16[192,2048]{1,0:T(8,128)(2,1)S(1)} %copy-done.44, bf16[192,2048]{1,0:T(8,128)(2,1)S(1)} %copy-done.46, bf16[192,2048]{1,0:T(8,128)(2,1)} %collective-permute-done.55.refs_0_.refs_2_, ...), custom_call_target="tpu_custom_call" | custom-call | flops 1024 | bytes 1024 | tf_op jit(solution)/shard_map/weight_product/pallas_call | solution.py:731
  306.2 6.3 %collective-permute-done.66.refs_3_ = bf16[192,1536]{1,0:T(8,128)(2,1)S(1)} collective-permute-done((bf16[192,1536]{1,0:T(8,128)(2,1)S(1)}, bf16[192,1536]{1,0:T(8,128)(2,1)S(1)}, u32[]{:S(2)}, u32[]{:S(2)}) %collective-permute-start.66) | collective-permute-done | bytes 589856 | tf_op jit(solution)/shard_map/ppermute | solution.py:107
  320.1 4.8 collective-permute-start.75
  327.2 10.0 %collective-permute-done.72.refs_2_ = bf16[256,1536]{1,0:T(8,128)(2,1)S(1)} collective-permute-done((bf16[256,1536]{1,0:T(8,128)(2,1)S(1)}, bf16[256,1536]{1,0:T(8,128)(2,1)S(1)}, u32[]{:S(2)}, u32[]{:S(2)}) %collective-permute-start.72) | collective-permute-done | bytes 786464 | tf_op jit(solution)/shard_map/ppermute | solution.py:107
  349.0 8.5 %collective-permute-done.77.refs_3_ = bf16[256,1536]{1,0:T(8,128)(2,1)S(1)} collective-permute-done((bf16[256,1536]{1,0:T(8,128)(2,1)S(1)}, bf16[256,1536]{1,0:T(8,128)(2,1)S(1)}, u32[]{:S(2)}, u32[]{:S(2)}) %collective-permute-start.77) | collective-permute-done | bytes 786464 | tf_op jit(solution)/shard_map/ppermute | solution.py:107
  360.0 14.8 %collective-permute-start.81 = (bf16[528,2048]{1,0:T(8,128)(2,1)}, bf16[528,2048]{1,0:T(8,128)(2,1)}, u32[]{:S(2)}, u32[]{:S(2)}) collective-permute-start(bf16[528,2048]{1,0:T(8,128)(2,1)} %add_or_begin.5.refs_1_), channel_id=1, source_target_pairs={{0,8},{24,16},{8,0},{16,24},{1,9},{25,17},{9,1},{17,25},{2,10},{26... | collective-permute-start | bytes 6488072 | tf_op jit(solution)/shard_map/ppermute | solution.py:161
  378.8 11.6 %conditional.15 = (bf16[448,2048]{1,0:T(8,128)(2,1)}) conditional(s32[]{:T(128)} %bitcast.14, () %tuple.344, (f32[1,2048]{1,0:T(1,128)S(1)}, f32[1,1024]{1,0:T(1,128)S(1)}, f32[1,2048]{1,0:T(1,128)S(1)}, bf16[176,2048]{1,0:T(8,128)(2,1)}, bf16[1024,512]{1,0:T(8,128)(2,1)S(1)}) %tuple.507), branch_computations={%region_8.9_spmd, %region_9.10_spmd} | conditional | flops 41984 | bytes 1835018 | solution.py:1170
  390.4 4.9 share.17
  401.0 12.1 %conditional.17 = (bf16[192,2048]{1,0:T(8,128)(2,1)}, bf16[192,2048]{1,0:T(8,128)(2,1)}, bf16[192,2048]{1,0:T(8,128)(2,1)}, bf16[192,2048]{1,0:T(8,128)(2,1)}, bf16[192,2048]{1,0:T(8,128)(2,1)S(1)}) conditional(s32[]{:T(128)} %bitcast.14, () %tuple.327, (bf16[192,2048]{1,0:T(8,128)(2,1)S(1)}, bf16[192,2048]{1,0:T(8,128)(2,1)S(1)}, ...), branch_computations={%region_12.13_spmd, %region_13.14_spmd} | conditional | flops 1024 | bytes 9438368 | solution.py:1170
  403.2 4.2 share.10
  407.4 5.7 collective-permute-done.6
  416.3 5.8 %collective-permute-done.81.refs_1_.refs_2_ = bf16[528,2048]{1,0:T(8,128)(2,1)} collective-permute-done((bf16[528,2048]{1,0:T(8,128)(2,1)}, bf16[528,2048]{1,0:T(8,128)(2,1)}, u32[]{:S(2)}, u32[]{:S(2)}) %collective-permute-start.81) | collective-permute-done | bytes 2162720 | tf_op jit(solution)/shard_map/ppermute | solution.py:161
  429.2 7.7 %collective-permute-start.82 = (bf16[448,2048]{1,0:T(8,128)(2,1)S(1)}, bf16[448,2048]{1,0:T(8,128)(2,1)S(1)}, u32[]{:S(2)}, u32[]{:S(2)}) collective-permute-start(bf16[448,2048]{1,0:T(8,128)(2,1)S(1)} %copy-done.72), channel_id=1, source_target_pairs={{0,8},{24,16},{1,9},{25,17},{2,10},{26,18},{3,11},{27,19},{4,12},{... | collective-permute-start | bytes 5505032 | tf_op jit(solution)/shard_map/ppermute | solution.py:161
  447.8 29.8 %collective-permute-done.84.refs_2_ = bf16[528,2048]{1,0:T(8,128)(2,1)S(1)} collective-permute-done((bf16[528,2048]{1,0:T(8,128)(2,1)S(1)}, bf16[528,2048]{1,0:T(8,128)(2,1)S(1)}, u32[]{:S(2)}, u32[]{:S(2)}) %collective-permute-start.84) | collective-permute-done | bytes 2162720 | tf_op jit(solution)/shard_map/ppermute | solution.py:161
  485.8 19.2 %conditional.18 = (bf16[192,2048]{1,0:T(8,128)(2,1)}, bf16[192,2048]{1,0:T(8,128)(2,1)}, bf16[192,2048]{1,0:T(8,128)(2,1)}) conditional(s32[]{:T(128)} %bitcast.14, () %tuple.442, (bf16[192,2048]{1,0:T(8,128)(2,1)S(1)}, bf16[192,2048]{1,0:T(8,128)(2,1)S(1)}, bf16[192,2048]{1,0:T(8,128)(2,1)S(1)}) %tuple.444), branch_computations={%region_14.15_spmd, %region_15.16_spmd} | conditional | bytes 9437328 | solution.py:1170
  488.8 16.2 %collective-permute-done.9 = bf16[192,2048]{1,0:T(8,128)(2,1)} collective-permute-done((bf16[192,2048]{1,0:T(8,128)(2,1)S(1)}, bf16[192,2048]{1,0:T(8,128)(2,1)}, u32[]{:S(2)}, u32[]{:S(2)}) %collective-permute-start.9) | collective-permute-done | bytes 786464 | tf_op jit(solution)/shard_map/cond/branch_1_fun/ppermute | solution.py:107
  514.6 15.5 %collective-permute-done.86.came = bf16[528,2048]{1,0:T(8,128)(2,1)} collective-permute-done((bf16[528,2048]{1,0:T(8,128)(2,1)}, bf16[528,2048]{1,0:T(8,128)(2,1)}, u32[]{:S(2)}, u32[]{:S(2)}) %collective-permute-start.86) | collective-permute-done | bytes 2162720 | tf_op jit(solution)/shard_map/ppermute | solution.py:161
  533.7 18.3 %conditional.19 = (bf16[192,2048]{1,0:T(8,128)(2,1)}, bf16[192,2048]{1,0:T(8,128)(2,1)}, bf16[192,2048]{1,0:T(8,128)(2,1)}, f32[512,2048]{1,0:T(8,128)}) conditional(s32[]{:T(128)} %bitcast.14, () %tuple.469, (bf16[192,2048]{1,0:T(8,128)(2,1)S(1)}, bf16[528,2048]{1,0:T(8,128)(2,1)}, s32[1]{0:T(128)}, bf16[528,2048]{1,0:T(8,128)(2,1)}) %tuple.471), branch_computations={%region_16.17_spmd, %region_17.18_spmd} | conditional | flops 1024 | bytes 9438360 | solution.py:1170
  540.7 11.3 %collective-permute-done.12 = bf16[192,2048]{1,0:T(8,128)(2,1)} collective-permute-done((bf16[192,2048]{1,0:T(8,128)(2,1)S(1)}, bf16[192,2048]{1,0:T(8,128)(2,1)}, u32[]{:S(2)}, u32[]{:S(2)}) %collective-permute-start.12) | collective-permute-done | bytes 786464 | tf_op jit(solution)/shard_map/cond/branch_1_fun/ppermute | solution.py:107
  552.0 12.9 %conditional.20 = (bf16[192,2048]{1,0:T(8,128)(2,1)}, bf16[192,2048]{1,0:T(8,128)(2,1)}, bf16[192,2048]{1,0:T(8,128)(2,1)}, f32[2048,1024]{1,0:T(8,128)}, f32[2048,256]{1,0:T(8,128)}, /*index=5*/f32[2048,256]{1,0:T(8,128)}) conditional(s32[]{:T(128)} %bitcast.14, () %tuple.468, (bf16[192,2048]{1,0:T(8,128)(2,1)}, bf16[192,2048]{1,0:T(8,128)(2,1)}, ...), branch_computations={%region_18.19_spmd, %region_19.20_spmd} | conditional | flops 1024 | bytes 14942274 | solution.py:1170
  555.8 6.2 %unpack.2 = (f32[2048,1024]{1,0:T(8,128)}, f32[2048,256]{1,0:T(8,128)}, f32[2048,256]{1,0:T(8,128)}) custom-call(s32[8]{0:T(128)S(1)} %get-tuple-element.157.table, bf16[192,2048]{1,0:T(8,128)(2,1)S(1)} %get-tuple-element.158.refs_0_, bf16[192,2048]{1,0:T(8,128)(2,1)} %get-tuple-element.159.refs_1_, bf16[192,2048]{1,0:T(8,128)(2,1)} %get-tuple-element.155.refs_2_, ...), custom_call_target="tpu_custom_call" | custom-call | flops 1024 | bytes 1024 | tf_op jit(solution)/shard_map/cond/branch_1_fun/unpack/pallas_call | solution.py:1103
  (389 shorter events, 246.2 us)
Async XLA Ops:
  0.6 39.5 %collective-permute-start.25 = (bf16[192,2048]{1,0:T(8,128)(2,1)}, bf16[192,2048]{1,0:T(8,128)(2,1)}, u32[]{:S(2)}, u32[]{:S(2)}) collective-permute-start(bf16[192,2048]{1,0:T(8,128)(2,1)} %bitcast.13.refs_0_.cotangent), channel_id=1, source_target_pairs={{0,2},{1,5},{2,0},{3,7},{4,6},{5,1},{6,4},{7,3},{8,10},{9,13},{10,... | collective-permute-start | bytes 2359304 | tf_op jit(solution)/shard_map/ppermute | solution.py:107
  12.2 15.3 %collective-permute-start.19 = (bf16[192,1536]{1,0:T(8,128)(2,1)}, bf16[192,1536]{1,0:T(8,128)(2,1)}, u32[]{:S(2)}, u32[]{:S(2)}) collective-permute-start(bf16[192,1536]{1,0:T(8,128)(2,1)} %get-tuple-element.83), channel_id=1, source_target_pairs={{0,2},{1,5},{2,0},{3,7},{4,6},{5,1},{6,4},{7,3},{8,10},{9,13},{10,... | collective-permute-start | bytes 1769480 | tf_op jit(solution)/shard_map/cond/branch_1_fun/ppermute | solution.py:107
  12.3 15.2 %collective-permute-start.20 = (bf16[192,1536]{1,0:T(8,128)(2,1)}, bf16[192,1536]{1,0:T(8,128)(2,1)}, u32[]{:S(2)}, u32[]{:S(2)}) collective-permute-start(bf16[192,1536]{1,0:T(8,128)(2,1)} %get-tuple-element.83), channel_id=1, source_target_pairs={{0,4},{1,3},{2,6},{3,1},{4,0},{5,7},{6,2},{7,5},{8,12},{9,11},{10,... | collective-permute-start | bytes 1769480 | tf_op jit(solution)/shard_map/cond/branch_1_fun/ppermute | solution.py:107
  14.3 13.2 %collective-permute-start.21 = (bf16[192,1536]{1,0:T(8,128)(2,1)}, bf16[192,1536]{1,0:T(8,128)(2,1)}, u32[]{:S(2)}, u32[]{:S(2)}) collective-permute-start(bf16[192,1536]{1,0:T(8,128)(2,1)} %get-tuple-element.83), channel_id=1, source_target_pairs={{0,1},{1,0},{2,3},{3,2},{4,5},{5,4},{6,7},{7,6},{8,9},{9,8},{10,11... | collective-permute-start | bytes 1769480 | tf_op jit(solution)/shard_map/cond/branch_1_fun/ppermute | solution.py:107
  40.2 23.4 %collective-permute-start.26 = (bf16[192,2048]{1,0:T(8,128)(2,1)}, bf16[192,2048]{1,0:T(8,128)(2,1)}, u32[]{:S(2)}, u32[]{:S(2)}) collective-permute-start(bf16[192,2048]{1,0:T(8,128)(2,1)} %bitcast.13.refs_0_.cotangent), channel_id=1, source_target_pairs={{0,4},{1,3},{2,6},{3,1},{4,0},{5,7},{6,2},{7,5},{8,12},{9,11},{10,... | collective-permute-start | bytes 2359304 | tf_op jit(solution)/shard_map/ppermute | solution.py:107
  41.8 21.7 %collective-permute-start.27 = (bf16[192,2048]{1,0:T(8,128)(2,1)}, bf16[192,2048]{1,0:T(8,128)(2,1)}, u32[]{:S(2)}, u32[]{:S(2)}) collective-permute-start(bf16[192,2048]{1,0:T(8,128)(2,1)} %collective-permute-done.25.refs_2_), channel_id=1, source_target_pairs={{0,4},{1,3},{2,6},{3,1},{4,0},{5,7},{6,2},{7,5},{8,12},{9,11},{10,... | collective-permute-start | bytes 2359304 | tf_op jit(solution)/shard_map/ppermute | solution.py:107
  42.2 21.4 %collective-permute-start.28 = (bf16[192,2048]{1,0:T(8,128)(2,1)}, bf16[192,2048]{1,0:T(8,128)(2,1)}, u32[]{:S(2)}, u32[]{:S(2)}) collective-permute-start(bf16[192,2048]{1,0:T(8,128)(2,1)} %bitcast.13.refs_0_.cotangent), channel_id=1, source_target_pairs={{0,1},{1,0},{2,3},{3,2},{4,5},{5,4},{6,7},{7,6},{8,9},{9,8},{10,11... | collective-permute-start | bytes 2359304 | tf_op jit(solution)/shard_map/ppermute | solution.py:107
  42.2 21.4 %collective-permute-start.29 = (bf16[192,2048]{1,0:T(8,128)(2,1)}, bf16[192,2048]{1,0:T(8,128)(2,1)}, u32[]{:S(2)}, u32[]{:S(2)}) collective-permute-start(bf16[192,2048]{1,0:T(8,128)(2,1)} %collective-permute-done.25.refs_2_), channel_id=1, source_target_pairs={{0,1},{1,0},{2,3},{3,2},{4,5},{5,4},{6,7},{7,6},{8,9},{9,8},{10,11... | collective-permute-start | bytes 2359304 | tf_op jit(solution)/shard_map/ppermute | solution.py:107
  79.3 20.0 %collective-permute-start.34 = (bf16[192,2048]{1,0:T(8,128)(2,1)S(1)}, bf16[192,2048]{1,0:T(8,128)(2,1)S(1)}, u32[]{:S(2)}, u32[]{:S(2)}) collective-permute-start(bf16[192,2048]{1,0:T(8,128)(2,1)S(1)} %add_rows.26), channel_id=1, source_target_pairs={{0,2},{1,5},{2,0},{3,7},{4,6},{5,1},{6,4},{7,3},{8,10},{9,13},{10,... | collective-permute-start | bytes 2359304 | tf_op jit(solution)/shard_map/ppermute | solution.py:107
  80.6 18.7 %collective-permute-start.35 = (bf16[192,2048]{1,0:T(8,128)(2,1)S(1)}, bf16[192,2048]{1,0:T(8,128)(2,1)S(1)}, u32[]{:S(2)}, u32[]{:S(2)}) collective-permute-start(bf16[192,2048]{1,0:T(8,128)(2,1)S(1)} %add_rows.27), channel_id=1, source_target_pairs={{0,4},{1,3},{2,6},{3,1},{4,0},{5,7},{6,2},{7,5},{8,12},{9,11},{10,... | collective-permute-start | bytes 2359304 | tf_op jit(solution)/shard_map/ppermute | solution.py:107
  82.4 16.9 %collective-permute-start.36 = (bf16[192,2048]{1,0:T(8,128)(2,1)S(1)}, bf16[192,2048]{1,0:T(8,128)(2,1)S(1)}, u32[]{:S(2)}, u32[]{:S(2)}) collective-permute-start(bf16[192,2048]{1,0:T(8,128)(2,1)S(1)} %get-tuple-element.659), channel_id=1, source_target_pairs={{0,1},{1,0},{2,3},{3,2},{4,5},{5,4},{6,7},{7,6},{8,9},{9,8},{10,11... | collective-permute-start | bytes 2359304 | tf_op jit(solution)/shard_map/ppermute | solution.py:107
  101.6 20.1 %collective-permute-start.39 = (bf16[192,2048]{1,0:T(8,128)(2,1)S(1)}, bf16[192,2048]{1,0:T(8,128)(2,1)S(1)}, u32[]{:S(2)}, u32[]{:S(2)}) collective-permute-start(bf16[192,2048]{1,0:T(8,128)(2,1)S(1)} %get-tuple-element.678.refs_0_), channel_id=1, source_target_pairs={{0,2},{1,5},{2,0},{3,7},{4,6},{5,1},{6,4},{7,3},{8,10},{9,13},{10,... | collective-permute-start | bytes 2359304 | tf_op jit(solution)/shard_map/ppermute | solution.py:107
  102.9 18.8 %collective-permute-start.40 = (bf16[192,2048]{1,0:T(8,128)(2,1)S(1)}, bf16[192,2048]{1,0:T(8,128)(2,1)S(1)}, u32[]{:S(2)}, u32[]{:S(2)}) collective-permute-start(bf16[192,2048]{1,0:T(8,128)(2,1)S(1)} %get-tuple-element.678.refs_0_), channel_id=1, source_target_pairs={{0,4},{1,3},{2,6},{3,1},{4,0},{5,7},{6,2},{7,5},{8,12},{9,11},{10,... | collective-permute-start | bytes 2359304 | tf_op jit(solution)/shard_map/ppermute | solution.py:107
  155.1 50.4 %collective-permute-start.53 = (bf16[528,2048]{1,0:T(8,128)(2,1)}, bf16[528,2048]{1,0:T(8,128)(2,1)}, u32[]{:S(2)}, u32[]{:S(2)}) collective-permute-start(bf16[528,2048]{1,0:T(8,128)(2,1)} %get-tuple-element.722.refs_0_), channel_id=1, source_target_pairs={{0,8},{24,16},{1,9},{25,17},{2,10},{26,18},{3,11},{27,19},{4,12},{... | collective-permute-start | bytes 6488072 | tf_op jit(solution)/shard_map/ppermute | solution.py:161
  178.8 19.4 %collective-permute-start.50 = (bf16[192,2048]{1,0:T(8,128)(2,1)S(1)}, bf16[192,2048]{1,0:T(8,128)(2,1)S(1)}, u32[]{:S(2)}, u32[]{:S(2)}) collective-permute-start(bf16[192,2048]{1,0:T(8,128)(2,1)S(1)} %add_rows.29), channel_id=1, source_target_pairs={{0,2},{1,5},{2,0},{3,7},{4,6},{5,1},{6,4},{7,3},{8,10},{9,13},{10,... | collective-permute-start | bytes 2359304 | tf_op jit(solution)/shard_map/ppermute | solution.py:107
  180.4 17.8 %collective-permute-start.51 = (bf16[192,2048]{1,0:T(8,128)(2,1)S(1)}, bf16[192,2048]{1,0:T(8,128)(2,1)S(1)}, u32[]{:S(2)}, u32[]{:S(2)}) collective-permute-start(bf16[192,2048]{1,0:T(8,128)(2,1)S(1)} %add_rows.30), channel_id=1, source_target_pairs={{0,4},{1,3},{2,6},{3,1},{4,0},{5,7},{6,2},{7,5},{8,12},{9,11},{10,... | collective-permute-start | bytes 2359304 | tf_op jit(solution)/shard_map/ppermute | solution.py:107
  181.5 16.7 %collective-permute-start.52 = (bf16[192,2048]{1,0:T(8,128)(2,1)}, bf16[192,2048]{1,0:T(8,128)(2,1)S(1)}, u32[]{:S(2)}, u32[]{:S(2)}) collective-permute-start(bf16[192,2048]{1,0:T(8,128)(2,1)} %get-tuple-element.758), channel_id=1, source_target_pairs={{0,1},{1,0},{2,3},{3,2},{4,5},{5,4},{6,7},{7,6},{8,9},{9,8},{10,11... | collective-permute-start | bytes 2359304 | tf_op jit(solution)/shard_map/ppermute | solution.py:107
  209.6 51.7 %collective-permute-start.61 = (bf16[528,2048]{1,0:T(8,128)(2,1)}, bf16[528,2048]{1,0:T(8,128)(2,1)}, u32[]{:S(2)}, u32[]{:S(2)}) collective-permute-start(bf16[528,2048]{1,0:T(8,128)(2,1)} %add_rows.31.own), channel_id=1, source_target_pairs={{8,16},{16,8},{9,17},{17,9},{10,18},{18,10},{11,19},{19,11},{12,20... | collective-permute-start | bytes 6488072 | tf_op jit(solution)/shard_map/ppermute | solution.py:161
  211.6 53.7 %collective-permute-start.60 = (bf16[528,2048]{1,0:T(8,128)(2,1)}, bf16[528,2048]{1,0:T(8,128)(2,1)}, u32[]{:S(2)}, u32[]{:S(2)}) collective-permute-start(bf16[528,2048]{1,0:T(8,128)(2,1)} %get-tuple-element.764.refs_0_), channel_id=1, source_target_pairs={{0,8},{24,16},{1,9},{25,17},{2,10},{26,18},{3,11},{27,19},{4,12},{... | collective-permute-start | bytes 6488072 | tf_op jit(solution)/shard_map/ppermute | solution.py:161
  223.2 20.1 %collective-permute-start.55 = (bf16[192,2048]{1,0:T(8,128)(2,1)S(1)}, bf16[192,2048]{1,0:T(8,128)(2,1)}, u32[]{:S(2)}, u32[]{:S(2)}) collective-permute-start(bf16[192,2048]{1,0:T(8,128)(2,1)S(1)} %get-tuple-element.780.refs_0_), channel_id=1, source_target_pairs={{0,2},{1,5},{2,0},{3,7},{4,6},{5,1},{6,4},{7,3},{8,10},{9,13},{10,... | collective-permute-start | bytes 2359304 | tf_op jit(solution)/shard_map/ppermute | solution.py:107
  224.7 18.5 %collective-permute-start.56 = (bf16[192,2048]{1,0:T(8,128)(2,1)S(1)}, bf16[192,2048]{1,0:T(8,128)(2,1)}, u32[]{:S(2)}, u32[]{:S(2)}) collective-permute-start(bf16[192,2048]{1,0:T(8,128)(2,1)S(1)} %get-tuple-element.780.refs_0_), channel_id=1, source_target_pairs={{0,4},{1,3},{2,6},{3,1},{4,0},{5,7},{6,2},{7,5},{8,12},{9,11},{10,... | collective-permute-start | bytes 2359304 | tf_op jit(solution)/shard_map/ppermute | solution.py:107
  243.7 12.3 %collective-permute-start.59 = (bf16[192,2048]{1,0:T(8,128)(2,1)}, bf16[192,2048]{1,0:T(8,128)(2,1)}, u32[]{:S(2)}, u32[]{:S(2)}) collective-permute-start(bf16[192,2048]{1,0:T(8,128)(2,1)} %collective-permute-done.55.refs_0_.refs_2_), channel_id=1, source_target_pairs={{0,4},{1,3},{2,6},{3,1},{4,0},{5,7},{6,2},{7,5},{8,12},{9,11},{10,... | collective-permute-start | bytes 2359304 | tf_op jit(solution)/shard_map/ppermute | solution.py:107
  263.7 52.0 %collective-permute-start.70 = (bf16[528,2048]{1,0:T(8,128)(2,1)S(1)}, bf16[528,2048]{1,0:T(8,128)(2,1)S(1)}, u32[]{:S(2)}, u32[]{:S(2)}) collective-permute-start(bf16[528,2048]{1,0:T(8,128)(2,1)S(1)} %add_or_begin.3.refs_1_), channel_id=1, source_target_pairs={{0,8},{24,16},{8,0},{16,24},{1,9},{25,17},{9,1},{17,25},{2,10},{26... | collective-permute-start | bytes 6488072 | tf_op jit(solution)/shard_map/ppermute | solution.py:161
  268.6 47.6 %collective-permute-start.69 = (bf16[528,2048]{1,0:T(8,128)(2,1)S(1)}, bf16[528,2048]{1,0:T(8,128)(2,1)}, u32[]{:S(2)}, u32[]{:S(2)}) collective-permute-start(bf16[528,2048]{1,0:T(8,128)(2,1)S(1)} %add_rows.32.own), channel_id=1, source_target_pairs={{8,16},{16,8},{9,17},{17,9},{10,18},{18,10},{11,19},{19,11},{12,20... | collective-permute-start | bytes 6488072 | tf_op jit(solution)/shard_map/ppermute | solution.py:161
  296.4 16.1 %collective-permute-start.66 = (bf16[192,1536]{1,0:T(8,128)(2,1)S(1)}, bf16[192,1536]{1,0:T(8,128)(2,1)S(1)}, u32[]{:S(2)}, u32[]{:S(2)}) collective-permute-start(bf16[192,1536]{1,0:T(8,128)(2,1)S(1)} %add_rows.34), channel_id=1, source_target_pairs={{0,2},{1,5},{2,0},{3,7},{4,6},{5,1},{6,4},{7,3},{8,10},{9,13},{10,... | collective-permute-start | bytes 1769480 | tf_op jit(solution)/shard_map/ppermute | solution.py:107
  298.2 14.4 %collective-permute-start.67 = (bf16[192,1536]{1,0:T(8,128)(2,1)S(1)}, bf16[192,1536]{1,0:T(8,128)(2,1)S(1)}, u32[]{:S(2)}, u32[]{:S(2)}) collective-permute-start(bf16[192,1536]{1,0:T(8,128)(2,1)S(1)} %add_rows.35), channel_id=1, source_target_pairs={{0,4},{1,3},{2,6},{3,1},{4,0},{5,7},{6,2},{7,5},{8,12},{9,11},{10,... | collective-permute-start | bytes 1769480 | tf_op jit(solution)/shard_map/ppermute | solution.py:107
  299.4 13.2 %collective-permute-start.68 = (bf16[192,1536]{1,0:T(8,128)(2,1)S(1)}, bf16[192,1536]{1,0:T(8,128)(2,1)S(1)}, u32[]{:S(2)}, u32[]{:S(2)}) collective-permute-start(bf16[192,1536]{1,0:T(8,128)(2,1)S(1)} %get-tuple-element.846), channel_id=1, source_target_pairs={{0,1},{1,0},{2,3},{3,2},{4,5},{5,4},{6,7},{7,6},{8,9},{9,8},{10,11... | collective-permute-start | bytes 1769480 | tf_op jit(solution)/shard_map/ppermute | solution.py:107
  319.3 38.7 %collective-permute-start.76 = (bf16[528,2048]{1,0:T(8,128)(2,1)S(1)}, bf16[528,2048]{1,0:T(8,128)(2,1)S(1)}, u32[]{:S(2)}, u32[]{:S(2)}) collective-permute-start(bf16[528,2048]{1,0:T(8,128)(2,1)S(1)} %add_rows.36.own), channel_id=1, source_target_pairs={{8,16},{16,8},{9,17},{17,9},{10,18},{18,10},{11,19},{19,11},{12,20... | collective-permute-start | bytes 6488072 | tf_op jit(solution)/shard_map/ppermute | solution.py:161
  320.1 54.8 %collective-permute-start.75 = (bf16[528,2048]{1,0:T(8,128)(2,1)S(1)}, bf16[528,2048]{1,0:T(8,128)(2,1)S(1)}, u32[]{:S(2)}, u32[]{:S(2)}) collective-permute-start(bf16[528,2048]{1,0:T(8,128)(2,1)S(1)} %add_or_begin.4.refs_1_), channel_id=1, source_target_pairs={{0,8},{24,16},{8,0},{16,24},{1,9},{25,17},{9,1},{17,25},{2,10},{26... | collective-permute-start | bytes 6488072 | tf_op jit(solution)/shard_map/ppermute | solution.py:161
  337.7 19.8 %collective-permute-start.77 = (bf16[256,1536]{1,0:T(8,128)(2,1)S(1)}, bf16[256,1536]{1,0:T(8,128)(2,1)S(1)}, u32[]{:S(2)}, u32[]{:S(2)}) collective-permute-start(bf16[256,1536]{1,0:T(8,128)(2,1)S(1)} %add_rows.38), channel_id=1, source_target_pairs={{0,2},{1,5},{2,0},{3,7},{4,6},{5,1},{6,4},{7,3},{8,10},{9,13},{10,... | collective-permute-start | bytes 2359304 | tf_op jit(solution)/shard_map/ppermute | solution.py:107
  339.5 18.0 %collective-permute-start.78 = (bf16[256,1536]{1,0:T(8,128)(2,1)S(1)}, bf16[256,1536]{1,0:T(8,128)(2,1)S(1)}, u32[]{:S(2)}, u32[]{:S(2)}) collective-permute-start(bf16[256,1536]{1,0:T(8,128)(2,1)S(1)} %add_rows.39), channel_id=1, source_target_pairs={{0,4},{1,3},{2,6},{3,1},{4,0},{5,7},{6,2},{7,5},{8,12},{9,11},{10,... | collective-permute-start | bytes 2359304 | tf_op jit(solution)/shard_map/ppermute | solution.py:107
  340.7 16.8 %collective-permute-start.79 = (bf16[256,1536]{1,0:T(8,128)(2,1)S(1)}, bf16[256,1536]{1,0:T(8,128)(2,1)S(1)}, u32[]{:S(2)}, u32[]{:S(2)}) collective-permute-start(bf16[256,1536]{1,0:T(8,128)(2,1)S(1)} %get-tuple-element.913), channel_id=1, source_target_pairs={{0,1},{1,0},{2,3},{3,2},{4,5},{5,4},{6,7},{7,6},{8,9},{9,8},{10,11... | collective-permute-start | bytes 2359304 | tf_op jit(solution)/shard_map/ppermute | solution.py:107
  360.0 62.0 %collective-permute-start.81 = (bf16[528,2048]{1,0:T(8,128)(2,1)}, bf16[528,2048]{1,0:T(8,128)(2,1)}, u32[]{:S(2)}, u32[]{:S(2)}) collective-permute-start(bf16[528,2048]{1,0:T(8,128)(2,1)} %add_or_begin.5.refs_1_), channel_id=1, source_target_pairs={{0,8},{24,16},{8,0},{16,24},{1,9},{25,17},{9,1},{17,25},{2,10},{26... | collective-permute-start | bytes 6488072 | tf_op jit(solution)/shard_map/ppermute | solution.py:161
  376.7 47.5 %collective-permute-start.80 = (bf16[528,2048]{1,0:T(8,128)(2,1)}, bf16[528,2048]{1,0:T(8,128)(2,1)}, u32[]{:S(2)}, u32[]{:S(2)}) collective-permute-start(bf16[528,2048]{1,0:T(8,128)(2,1)} %add_rows.40.refs_0_), channel_id=1, source_target_pairs={{8,16},{16,8},{9,17},{17,9},{10,18},{18,10},{11,19},{19,11},{12,20... | collective-permute-start | bytes 6488072 | tf_op jit(solution)/shard_map/ppermute | solution.py:161
  401.0 12.1 %collective-permute-start.6 = (bf16[192,2048]{1,0:T(8,128)(2,1)S(1)}, bf16[192,2048]{1,0:T(8,128)(2,1)}, u32[]{:S(2)}, u32[]{:S(2)}) collective-permute-start(bf16[192,2048]{1,0:T(8,128)(2,1)S(1)} %get-tuple-element.121), channel_id=1, source_target_pairs={{0,4},{1,3},{2,6},{3,1},{4,0},{5,7},{6,2},{7,5},{8,12},{9,11},{10,... | collective-permute-start | bytes 2359304 | tf_op jit(solution)/shard_map/cond/branch_1_fun/ppermute | solution.py:107
  427.1 50.5 %collective-permute-start.84 = (bf16[528,2048]{1,0:T(8,128)(2,1)S(1)}, bf16[528,2048]{1,0:T(8,128)(2,1)S(1)}, u32[]{:S(2)}, u32[]{:S(2)}) collective-permute-start(bf16[528,2048]{1,0:T(8,128)(2,1)S(1)} %add_rows.45.refs_1_), channel_id=1, source_target_pairs={{8,0},{16,24},{9,1},{17,25},{10,2},{18,26},{11,3},{19,27},{12,4},{... | collective-permute-start | bytes 6488072 | tf_op jit(solution)/shard_map/ppermute | solution.py:161
  428.4 50.5 %collective-permute-start.83 = (bf16[528,2048]{1,0:T(8,128)(2,1)S(1)}, bf16[528,2048]{1,0:T(8,128)(2,1)S(1)}, u32[]{:S(2)}, u32[]{:S(2)}) collective-permute-start(bf16[528,2048]{1,0:T(8,128)(2,1)S(1)} %add_rows.44.refs_0_), channel_id=1, source_target_pairs={{8,16},{16,8},{9,17},{17,9},{10,18},{18,10},{11,19},{19,11},{12,20... | collective-permute-start | bytes 6488072 | tf_op jit(solution)/shard_map/ppermute | solution.py:161
  429.2 52.8 %collective-permute-start.82 = (bf16[448,2048]{1,0:T(8,128)(2,1)S(1)}, bf16[448,2048]{1,0:T(8,128)(2,1)S(1)}, u32[]{:S(2)}, u32[]{:S(2)}) collective-permute-start(bf16[448,2048]{1,0:T(8,128)(2,1)S(1)} %copy-done.72), channel_id=1, source_target_pairs={{0,8},{24,16},{1,9},{25,17},{2,10},{26,18},{3,11},{27,19},{4,12},{... | collective-permute-start | bytes 5505032 | tf_op jit(solution)/shard_map/ppermute | solution.py:161
  480.8 49.3 %collective-permute-start.86 = (bf16[528,2048]{1,0:T(8,128)(2,1)}, bf16[528,2048]{1,0:T(8,128)(2,1)}, u32[]{:S(2)}, u32[]{:S(2)}) collective-permute-start(bf16[528,2048]{1,0:T(8,128)(2,1)} %add_rows.46.own), channel_id=1, source_target_pairs={{8,0},{16,24},{9,1},{17,25},{10,2},{18,26},{11,3},{19,27},{12,4},{... | collective-permute-start | bytes 6488072 | tf_op jit(solution)/shard_map/ppermute | solution.py:161
  483.7 28.4 %collective-permute-start.85 = (bf16[448,2048]{1,0:T(8,128)(2,1)}, bf16[448,2048]{1,0:T(8,128)(2,1)}, u32[]{:S(2)}, u32[]{:S(2)}) collective-permute-start(bf16[448,2048]{1,0:T(8,128)(2,1)} %add_rows.47.refs_0_), channel_id=1, source_target_pairs={{8,16},{16,8},{9,17},{17,9},{10,18},{18,10},{11,19},{19,11},{12,20... | collective-permute-start | bytes 5505032 | tf_op jit(solution)/shard_map/ppermute | solution.py:161
  485.8 19.1 %collective-permute-start.9 = (bf16[192,2048]{1,0:T(8,128)(2,1)S(1)}, bf16[192,2048]{1,0:T(8,128)(2,1)}, u32[]{:S(2)}, u32[]{:S(2)}) collective-permute-start(bf16[192,2048]{1,0:T(8,128)(2,1)S(1)} %get-tuple-element.134), channel_id=1, source_target_pairs={{0,2},{1,5},{2,0},{3,7},{4,6},{5,1},{6,4},{7,3},{8,10},{9,13},{10,... | collective-permute-start | bytes 2359304 | tf_op jit(solution)/shard_map/cond/branch_1_fun/ppermute | solution.py:107
  487.5 17.4 %collective-permute-start.10 = (bf16[192,2048]{1,0:T(8,128)(2,1)S(1)}, bf16[192,2048]{1,0:T(8,128)(2,1)}, u32[]{:S(2)}, u32[]{:S(2)}) collective-permute-start(bf16[192,2048]{1,0:T(8,128)(2,1)S(1)} %get-tuple-element.135), channel_id=1, source_target_pairs={{0,4},{1,3},{2,6},{3,1},{4,0},{5,7},{6,2},{7,5},{8,12},{9,11},{10,... | collective-permute-start | bytes 2359304 | tf_op jit(solution)/shard_map/cond/branch_1_fun/ppermute | solution.py:107
  488.8 16.2 %collective-permute-start.11 = (bf16[192,2048]{1,0:T(8,128)(2,1)S(1)}, bf16[192,2048]{1,0:T(8,128)(2,1)}, u32[]{:S(2)}, u32[]{:S(2)}) collective-permute-start(bf16[192,2048]{1,0:T(8,128)(2,1)S(1)} %get-tuple-element.136), channel_id=1, source_target_pairs={{0,1},{1,0},{2,3},{3,2},{4,5},{5,4},{6,7},{7,6},{8,9},{9,8},{10,11... | collective-permute-start | bytes 2359304 | tf_op jit(solution)/shard_map/cond/branch_1_fun/ppermute | solution.py:107
  530.1 41.2 %collective-permute-start.87 = (bf16[448,2048]{1,0:T(8,128)(2,1)S(1)}, bf16[448,2048]{1,0:T(8,128)(2,1)}, u32[]{:S(2)}, u32[]{:S(2)}) collective-permute-start(bf16[448,2048]{1,0:T(8,128)(2,1)S(1)} %add_rows.49.own), channel_id=1, source_target_pairs={{8,0},{16,24},{9,1},{17,25},{10,2},{18,26},{11,3},{19,27},{12,4},{... | collective-permute-start | bytes 5505032 | tf_op jit(solution)/shard_map/ppermute | solution.py:161
  533.7 18.3 %collective-permute-start.12 = (bf16[192,2048]{1,0:T(8,128)(2,1)S(1)}, bf16[192,2048]{1,0:T(8,128)(2,1)}, u32[]{:S(2)}, u32[]{:S(2)}) collective-permute-start(bf16[192,2048]{1,0:T(8,128)(2,1)S(1)} %get-tuple-element.143), channel_id=1, source_target_pairs={{0,2},{1,5},{2,0},{3,7},{4,6},{5,1},{6,4},{7,3},{8,10},{9,13},{10,... | collective-permute-start | bytes 2359304 | tf_op jit(solution)/shard_map/cond/branch_1_fun/ppermute | solution.py:107
  535.5 16.5 %collective-permute-start.13 = (bf16[192,2048]{1,0:T(8,128)(2,1)S(1)}, bf16[192,2048]{1,0:T(8,128)(2,1)}, u32[]{:S(2)}, u32[]{:S(2)}) collective-permute-start(bf16[192,2048]{1,0:T(8,128)(2,1)S(1)} %get-tuple-element.143), channel_id=1, source_target_pairs={{0,4},{1,3},{2,6},{3,1},{4,0},{5,7},{6,2},{7,5},{8,12},{9,11},{10,... | collective-permute-start | bytes 2359304 | tf_op jit(solution)/shard_map/cond/branch_1_fun/ppermute | solution.py:107
  536.7 15.3 %collective-permute-start.14 = (bf16[192,2048]{1,0:T(8,128)(2,1)S(1)}, bf16[192,2048]{1,0:T(8,128)(2,1)}, u32[]{:S(2)}, u32[]{:S(2)}) collective-permute-start(bf16[192,2048]{1,0:T(8,128)(2,1)S(1)} %get-tuple-element.143), channel_id=1, source_target_pairs={{0,1},{1,0},{2,3},{3,2},{4,5},{5,4},{6,7},{7,6},{8,9},{9,8},{10,11... | collective-permute-start | bytes 2359304 | tf_op jit(solution)/shard_map/cond/branch_1_fun/ppermute | solution.py:107
  552.6 12.3 %collective-permute-start.15 = (bf16[192,2048]{1,0:T(8,128)(2,1)}, bf16[192,2048]{1,0:T(8,128)(2,1)}, u32[]{:S(2)}, u32[]{:S(2)}) collective-permute-start(bf16[192,2048]{1,0:T(8,128)(2,1)} %get-tuple-element.155.refs_2_), channel_id=1, source_target_pairs={{0,4},{1,3},{2,6},{3,1},{4,0},{5,7},{6,2},{7,5},{8,12},{9,11},{10,... | collective-permute-start | bytes 2359304 | tf_op jit(solution)/shard_map/cond/branch_1_fun/ppermute | solution.py:107
  (118 other events, 906.6 us)

commit v4 on v3

--- a/solution.py
+++ b/solution.py
@@ -229,13 +229,21 @@
     table = refs[0]
     pieces = refs[1 : 1 + count]
     weight, cosine, sine, seg_column, seg_row = refs[1 + count : 6 + count]
-    latents, queries, keys, values, mixed_there, mixed = refs[6 + count :]
+    latents, queries_out, keys_out, values_out, mixed_there = refs[6 + count : 11 + count]
+    queries, keys, values, mixed, sems = refs[11 + count :]
     length = queries.shape[0]
+    leaving = []
+
+    def leave_now(source, target):
+        copy = pltpu.make_async_copy(source, target, sems.at[len(leaving)])
+        copy.start()
+        leaving.append(copy)
+
     rows = length // count
     half = width // 2
     for r in range(count):
         there = pl.ds(pl.multiple_of(table[r] * rows, rows), rows)
-        latents[there, :] = pieces[r][:, :rank]
+        leave_now(pieces[r].at[:, :rank], latents.at[there, :])
         keys[there, :] = pieces[r][:, rank : rank + width]
         values[there, :] = pieces[r][:, rank + width :]
         flat = dot(pieces[r][:, :rank], weight[...])
@@ -248,6 +256,9 @@
             queries[there, h * width + half : (h + 1) * width] = (
                 second * cos + first * sin
             ).astype(bf16)
+    leave_now(queries, queries_out)
+    leave_now(keys, keys_out)
+    leave_now(values, values_out)
     for start, size, low in query_blocks(length):
         high = start + size
         stacked = stack_heads(queries, start, size, heads, width)
@@ -260,6 +271,8 @@
     for r in range(count):
         there = pl.ds(pl.multiple_of(table[r] * rows, rows), rows)
         mixed_there[r * rows : (r + 1) * rows, :] = mixed[there, :]
+    for copy in leaving:
+        copy.wait()
 
 
 def brief():
@@ -289,8 +302,14 @@
         functools.partial(attend_forward_kernel, count, heads, width, rank, scale),
         out_shape=shapes,
         in_specs=[smem()] + [vmem()] * (count + 5),
-        out_specs=[vmem()] * 5,
-        scratch_shapes=[pltpu.VMEM((length, heads * width), bf16)],
+        out_specs=[any_space()] * 4 + [vmem()],
+        scratch_shapes=[
+            pltpu.VMEM((length, heads * width), bf16),
+            pltpu.VMEM((length, width), bf16),
+            pltpu.VMEM((length, width), bf16),
+            pltpu.VMEM((length, heads * width), bf16),
+            pltpu.SemaphoreType.DMA((count + 3,)),
+        ],
         compiler_params=pltpu.CompilerParams(vmem_limit_bytes=48 << 20),
         cost_estimate=brief(),
         name="attend_forward",
@@ -717,7 +736,7 @@
         low += size
 
 
-def weight_product(left, right, rows, above=None, step=512):
+def weight_product(left, right, rows, above=None, step=1024):
     right = list(right) if isinstance(right, (list, tuple)) else [right]
     count = len(right)
     tokens, units = left.shape
@@ -1200,10 +1219,10 @@
         (c_o,), _ = hops([c], [hop_c], None, apart or last)
         return [rows, s_o, a, a_o, b, b_o, c, c_o], more, later
 
-    def scatter(share, filler=None, apart=False, between=None):
+    def scatter(share, filler=None, apart=False, between=None, head=False):
         c, c_send = clock(*share(clock, 6, 8))
         (c_came,), near = hops(
-            [c_send], [hop_c], lambda clock, came: clock(*share(clock, 2, 6)), apart
+            [c_send], [hop_c], lambda clock, came: clock(*share(clock, 2, 6)), apart or head
         )
         a, a_send, b, b_send = near
         c = clock(add_rows(c, c_came))
@@ -1356,13 +1375,12 @@
 
         def next_feed(clock, c, a_o, b_o):
             a_o, b_o = clock(a_o, b_o)
-            return [a_o, b_o, *feed_group(clock, [a, a_o], 2, 4, past)]
+            more = feed_group(clock, [a, a_o], 2, 4, past)
+            return [a_o, b_o, *feed_group(clock, [b, b_o], 4, 6, more)]
 
         (c, a_o, b_o), past = hops([a, a, b], [hop_b, hop_c, hop_c], next_feed)
         a_o, b_o, *past = past
-        (c_o,), past = hops(
-            [c], [hop_c], lambda clock, c_o: feed_group(clock, [b, b_o], 4, 6, past)
-        )
+        (c_o,), _ = hops([c], [hop_c])
         hidden, gate_grad, upward_grad = feed_group(clock, [c, c_o], 6, 8, past)
         mid_pieces = [normed_mid_rows, s_o, a, a_o, b, b_o, c, c_o]
         chunk = units * 3 // 4
@@ -1377,12 +1395,12 @@
                 *weight_product(clock(gate_grad), mid_pieces, [chunk, units - half], tail)
             )
             two.append(belt.begin(part))
+            belt.cross(one)
             return [rest]
 
         share = shares([gate_grad, upward_grad], [gate_rows, up_rows], group)
-        parts, (tail,) = scatter(share, middle_filler)
+        parts, (tail,) = scatter(share, middle_filler, head=True)
         two = two[0]
-        belt.cross(one)
         middle_grad, attention_grad, feed_gain_part = clock(
             *middle_back(middle, feed_gain, cotangent_rows, parts)
         )

time: 587 us -> 582 us (level)
  waiting for transfers between devices: 228 us -> 220 us
    ppermute x73, waiting for transfers between devices: 169 us -> 157 us  [move(): return lax.ppermute(value, 'head', hop)]
    unnamed x157 -> x181, local copies, waits for them, and re-layouts: 15.9 us -> 18.8 us
  transfers between devices with their start and end apart: 88 -> 88, of which waited for: 36 -> 36; matrix products, arithmetic and copies ran while one was open for 1% -> 1% of each run, Pallas kernels for 32% -> 33%
where the time goes in v4:
time: 582 us; the launch traced here: 573 us
  waiting for transfers between devices  220 us (38%)
  Pallas kernels  215 us (37%)
  starting transfers between devices  105 us (18%)
  local copies, waits for them, and re-layouts  22.5 us (4%)
  other arithmetic  6.36 us (1%)
    ppermute x73, waiting for transfers between devices, move(): return lax.ppermute(value, 'head', hop)  157 us
    ppermute x15, waiting for transfers between devices, move(): return lax.ppermute(value, 'tok', pairs)  63 us
    pallas_call x36, Pallas kernels, call(): pl.pallas_call(kernel, out_shape=shapes, in_specs=[smem()] * scalars + [v...  57.2 us
    ppermute x15, starting transfers between devices, move(): return lax.ppermute(value, 'tok', pairs)  55.6 us
    ppermute x73, starting transfers between devices, move(): return lax.ppermute(value, 'head', hop)  49.8 us
    pallas_call x9, Pallas kernels, share(): pl.pallas_call(functools.partial(share_kernel, low, size, terms), out_sha...  33.5 us
    pallas_call x5, Pallas kernels, weight_product(): pl.pallas_call(functools.partial(product_kernel, count, len(operands) - 1...  30.7 us
    pallas_call x7, Pallas kernels, settle(): pl.pallas_call(functools.partial(settle_kernel, low, at), out_shape=shape...  19.4 us
  transfers between devices with their start and end apart: 88, of which 36 were waited for; matrix products, arithmetic and copies ran while one was open for 1% of the time, Pallas kernels for 33%

profile of v4, /device:TPU:0, one launch (start us, length us, event | category | flops | bytes accessed | tf_op | source)
XLA Modules:
  0.0 573.1 jit_solution(8001932139865535177)
XLA Ops:
  5.5 5.5 enter.1
  12.2 15.3 %conditional.12 = (bf16[192,1536]{1,0:T(8,128)(2,1)}, bf16[192,1536]{1,0:T(8,128)(2,1)}, bf16[192,1536]{1,0:T(8,128)(2,1)}, f32[1536,128]{1,0:T(8,128)}, f32[1536,128]{1,0:T(8,128)}) conditional(s32[]{:T(128)} %bitcast.14, () %tuple.309, (bf16[192,1536]{1,0:T(8,128)(2,1)}, s32[1,1536]{1,0:T(1,128)S(1)}) %tuple.520), branch_computations={%region_0.1_spmd, %region_1.2_spmd} | conditional | flops 198400 | bytes 8682660 | solution.py:1189
  14.3 4.3 multiply_sine_fusion
  18.7 8.8 %collective-permute-done.20 = bf16[192,1536]{1,0:T(8,128)(2,1)} collective-permute-done((bf16[192,1536]{1,0:T(8,128)(2,1)}, bf16[192,1536]{1,0:T(8,128)(2,1)}, u32[]{:S(2)}, u32[]{:S(2)}) %collective-permute-start.20) | collective-permute-done | bytes 589856 | tf_op jit(solution)/shard_map/cond/branch_1_fun/ppermute | solution.py:107
  27.5 10.3 %conditional.13 = (bf16[192,1536]{1,0:T(8,128)(2,1)}, bf16[192,1536]{1,0:T(8,128)(2,1)}, bf16[192,1536]{1,0:T(8,128)(2,1)}) conditional(s32[]{:T(128)} %bitcast.14, () %tuple.308, (bf16[192,1536]{1,0:T(8,128)(2,1)}, bf16[192,1536]{1,0:T(8,128)(2,1)}) %tuple.312), branch_computations={%region_2.3_spmd, %region_3.4_spmd} | conditional | bytes 7078032 | solution.py:1189
  29.7 8.0 %collective-permute-done = bf16[192,1536]{1,0:T(8,128)(2,1)} collective-permute-done((bf16[192,1536]{1,0:T(8,128)(2,1)}, bf16[192,1536]{1,0:T(8,128)(2,1)}, u32[]{:S(2)}, u32[]{:S(2)}) %collective-permute-start) | collective-permute-done | bytes 589856 | tf_op jit(solution)/shard_map/cond/branch_1_fun/ppermute | solution.py:107
  45.1 10.6 %attend_forward.1 = (bf16[1536,1024]{1,0:T(8,128)(2,1)}, bf16[1536,512]{1,0:T(8,128)(2,1)S(1)}, bf16[1536,256]{1,0:T(8,128)(2,1)S(1)}, bf16[1536,256]{1,0:T(8,128)(2,1)S(1)}, bf16[1536,512]{1,0:T(8,128)(2,1)}) custom-call(s32[8]{0:T(128)S(1)} %stack.35.refs_0_.table, bf16[192,1536]{1,0:T(8,128)(2,1)} %get-tuple-element.636.refs_1_, ...), custom_call_target="tpu_custom_call" | custom-call | flops 1024 | bytes 1024 | tf_op jit(solution)/shard_map/attend_forward/pallas_call | solution.py:301
  67.6 9.8 %collective-permute-done.32.refs_2_ = bf16[192,2048]{1,0:T(8,128)(2,1)S(1)} collective-permute-done((bf16[192,2048]{1,0:T(8,128)(2,1)S(1)}, bf16[192,2048]{1,0:T(8,128)(2,1)S(1)}, u32[]{:S(2)}, u32[]{:S(2)}) %collective-permute-start.32) | collective-permute-done | bytes 786464 | tf_op jit(solution)/shard_map/ppermute | solution.py:107
  81.7 7.5 %rows_product.4.refs_2_ = f32[1536,704]{1,0:T(8,128)S(1)} custom-call(bf16[192,2048]{1,0:T(8,128)(2,1)} %bitcast.13.refs_0_.cotangent, bf16[192,2048]{1,0:T(8,128)(2,1)} %collective-permute-done.29.refs_1_, bf16[192,2048]{1,0:T(8,128)(2,1)} %collective-permute-done.26.refs_2_, bf16[192,2048]{1,0:T(8,128)(2,1)} %collective-permute-done.30.refs_3_, ...), custom_call_target="tpu_custom_call" | custom-call | flops 1024 | bytes 1024 | tf_op jit(solution)/shard_map/rows_product/pallas_call | solution.py:409
  89.3 9.3 %collective-permute-done.35.refs_3_ = bf16[192,2048]{1,0:T(8,128)(2,1)S(1)} collective-permute-done((bf16[192,2048]{1,0:T(8,128)(2,1)S(1)}, bf16[192,2048]{1,0:T(8,128)(2,1)S(1)}, u32[]{:S(2)}, u32[]{:S(2)}) %collective-permute-start.35) | collective-permute-done | bytes 786464 | tf_op jit(solution)/shard_map/ppermute | solution.py:107
  107.3 13.7 %collective-permute-done.40.refs_0_.refs_2_ = bf16[192,2048]{1,0:T(8,128)(2,1)S(1)} collective-permute-done((bf16[192,2048]{1,0:T(8,128)(2,1)S(1)}, bf16[192,2048]{1,0:T(8,128)(2,1)S(1)}, u32[]{:S(2)}, u32[]{:S(2)}) %collective-permute-start.40) | collective-permute-done | bytes 786464 | tf_op jit(solution)/shard_map/ppermute | solution.py:107
  124.5 4.3 feed.5
  139.8 9.4 %weight_product.5 = (bf16[528,2048]{1,0:T(8,128)(2,1)}, bf16[176,2048]{1,0:T(8,128)(2,1)S(1)}) custom-call(bf16[1536,704]{1,0:T(8,128)(2,1)S(1)} %get-tuple-element.948.left.refs_0_, bf16[192,2048]{1,0:T(8,128)(2,1)} %bitcast.13.refs_0_.cotangent, bf16[192,2048]{1,0:T(8,128)(2,1)} %collective-permute-done.29.refs_1_, ...), custom_call_target="tpu_custom_call" | custom-call | flops 1024 | bytes 1024 | tf_op jit(solution)/shard_map/weight_product/pallas_call | solution.py:750
  150.0 5.1 collective-permute-start.53
  159.0 6.7 %conditional.15 = (bf16[192,2048]{1,0:T(8,128)(2,1)}, bf16[192,2048]{1,0:T(8,128)(2,1)}, bf16[192,2048]{1,0:T(8,128)(2,1)}, bf16[192,2048]{1,0:T(8,128)(2,1)}, bf16[192,2048]{1,0:T(8,128)(2,1)}) conditional(s32[]{:T(128)} %bitcast.14, () %tuple.358, (bf16[192,2048]{1,0:T(8,128)(2,1)S(1)}, bf16[1536,704]{1,0:T(8,128)(2,1)S(1)}, ...), branch_computations={%region_6.7_spmd, %region_7.8_spmd} | conditional | flops 1024 | bytes 3932210 | solution.py:1189
  159.0 6.7 %share.9 = (bf16[192,2048]{1,0:T(8,128)(2,1)}, bf16[192,2048]{1,0:T(8,128)(2,1)}, bf16[192,2048]{1,0:T(8,128)(2,1)}, bf16[192,2048]{1,0:T(8,128)(2,1)}) custom-call(bf16[1536,704]{1,0:T(8,128)(2,1)S(1)} %get-tuple-element.113.refs_0_, bf16[1536,704]{1,0:T(8,128)(2,1)S(1)} %get-tuple-element.114.refs_1_, bf16[704,2048]{1,0:T(8,128)(2,1)S(1)} %get-tuple-element.115.refs_2_, ...), custom_call_target="tpu_custom_call" | custom-call | flops 1024 | bytes 1024 | tf_op jit(solution)/shard_map/cond/branch_1_fun/share/pallas_call | solution.py:529
  170.1 6.6 %share.16 = (bf16[192,2048]{1,0:T(8,128)(2,1)S(1)}, bf16[192,2048]{1,0:T(8,128)(2,1)S(1)}) custom-call(bf16[1536,704]{1,0:T(8,128)(2,1)S(1)} %copy-done.74, bf16[1536,704]{1,0:T(8,128)(2,1)} %copy-done.75, bf16[704,2048]{1,0:T(8,128)(2,1)} %bitcast.37, bf16[704,2048]{1,0:T(8,128)(2,1)} %bitcast.44), custom_call_target="tpu_custom_call" | custom-call | flops 1024 | bytes 1024 | tf_op jit(solution)/shard_map/share/pallas_call | solution.py:529
  183.7 6.7 %weight_product.6 = (bf16[528,2048]{1,0:T(8,128)(2,1)}, bf16[352,2048]{1,0:T(8,128)(2,1)S(1)}) custom-call(bf16[1536,704]{1,0:T(8,128)(2,1)S(1)} %copy-done.74, bf16[192,2048]{1,0:T(8,128)(2,1)S(1)} %copy-done.30, bf16[192,2048]{1,0:T(8,128)(2,1)S(1)} %copy-done.32, bf16[192,2048]{1,0:T(8,128)(2,1)S(1)} %copy-done.18, bf16[192,2048]{1,0:T(8,128)(2,1)S(1)} %copy-done.22, ...), custom_call_target="tpu_custom_call" | custom-call | flops 1024 | bytes 1024 | tf_op jit(solution)/shard_map/weight_product/pallas_call | solution.py:750
  190.4 10.2 %collective-permute-done.53.refs_1_ = bf16[528,2048]{1,0:T(8,128)(2,1)} collective-permute-done((bf16[528,2048]{1,0:T(8,128)(2,1)}, bf16[528,2048]{1,0:T(8,128)(2,1)}, u32[]{:S(2)}, u32[]{:S(2)}) %collective-permute-start.53) | collective-permute-done | bytes 2162720 | tf_op jit(solution)/shard_map/ppermute | solution.py:161
  200.6 4.1 add_rows.31.own
  206.8 7.5 %collective-permute-start.60 = (bf16[528,2048]{1,0:T(8,128)(2,1)}, bf16[528,2048]{1,0:T(8,128)(2,1)}, u32[]{:S(2)}, u32[]{:S(2)}) collective-permute-start(bf16[528,2048]{1,0:T(8,128)(2,1)} %get-tuple-element.787.refs_0_), channel_id=1, source_target_pairs={{0,8},{24,16},{1,9},{25,17},{2,10},{26,18},{3,11},{27,19},{4,12},{... | collective-permute-start | bytes 6488072 | tf_op jit(solution)/shard_map/ppermute | solution.py:161
  223.1 6.1 %weight_product.7 = (bf16[528,2048]{1,0:T(8,128)(2,1)S(1)}, bf16[528,2048]{1,0:T(8,128)(2,1)S(1)}) custom-call(bf16[1536,704]{1,0:T(8,128)(2,1)S(1)} %copy-done.76, bf16[192,2048]{1,0:T(8,128)(2,1)S(1)} %copy-done.30, bf16[192,2048]{1,0:T(8,128)(2,1)S(1)} %copy-done.32, bf16[192,2048]{1,0:T(8,128)(2,1)S(1)} %copy-done.18, bf16[192,2048]{1,0:T(8,128)(2,1)S(1)} %copy-done.22, ...), custom_call_target="tpu_custom_call" | custom-call | flops 1024 | bytes 1024 | tf_op jit(solution)/shard_map/weight_product/pallas_call | solution.py:750
  231.9 6.9 %collective-permute-done.55.refs_0_.refs_2_ = bf16[192,2048]{1,0:T(8,128)(2,1)} collective-permute-done((bf16[192,2048]{1,0:T(8,128)(2,1)S(1)}, bf16[192,2048]{1,0:T(8,128)(2,1)}, u32[]{:S(2)}, u32[]{:S(2)}) %collective-permute-start.55) | collective-permute-done | bytes 786464 | tf_op jit(solution)/shard_map/ppermute | solution.py:107
  247.1 4.5 collective-permute-done.59.refs_0_.refs_6_
  266.6 9.0 %attend_backward.1 = (bf16[1536,512]{1,0:T(8,128)(2,1)S(1)}, bf16[1536,512]{1,0:T(8,128)(2,1)S(1)}) custom-call(s32[8]{0:T(128)S(1)} %stack.35.refs_0_.table, bf16[384,512]{1,0:T(8,128)(2,1)S(1)} %rows_product.5.refs_1_, bf16[768,512]{1,0:T(8,128)(2,1)S(1)} %copy-done.44, bf16[384,512]{1,0:T(8,128)(2,1)S(1)} %rows_product.7.refs_3_, ...), custom_call_target="tpu_custom_call" | custom-call | flops 1024 | bytes 1024 | tf_op jit(solution)/shard_map/attend_backward/pallas_call | solution.py:374
  286.0 5.9 %collective-permute-done.63.refs_2_ = bf16[192,1536]{1,0:T(8,128)(2,1)S(1)} collective-permute-done((bf16[192,1536]{1,0:T(8,128)(2,1)S(1)}, bf16[192,1536]{1,0:T(8,128)(2,1)S(1)}, u32[]{:S(2)}, u32[]{:S(2)}) %collective-permute-start.63) | collective-permute-done | bytes 589856 | tf_op jit(solution)/shard_map/ppermute | solution.py:107
  295.0 6.4 %weight_product.8 = (bf16[336,2048]{1,0:T(8,128)(2,1)S(1)}, bf16[176,2048]{1,0:T(8,128)(2,1)}) custom-call(bf16[1536,512]{1,0:T(8,128)(2,1)S(1)} %copy-done.2, bf16[192,2048]{1,0:T(8,128)(2,1)S(1)} %copy-done.46, bf16[192,2048]{1,0:T(8,128)(2,1)S(1)} %copy-done.48, bf16[192,2048]{1,0:T(8,128)(2,1)} %collective-permute-done.55.refs_0_.refs_2_, ...), custom_call_target="tpu_custom_call" | custom-call | flops 1024 | bytes 1024 | tf_op jit(solution)/shard_map/weight_product/pallas_call | solution.py:750
  301.4 6.7 %collective-permute-done.66.refs_3_ = bf16[192,1536]{1,0:T(8,128)(2,1)S(1)} collective-permute-done((bf16[192,1536]{1,0:T(8,128)(2,1)S(1)}, bf16[192,1536]{1,0:T(8,128)(2,1)S(1)}, u32[]{:S(2)}, u32[]{:S(2)}) %collective-permute-start.66) | collective-permute-done | bytes 589856 | tf_op jit(solution)/shard_map/ppermute | solution.py:107
  315.6 4.8 collective-permute-start.75
  322.4 10.3 %collective-permute-done.72.refs_2_ = bf16[256,1536]{1,0:T(8,128)(2,1)S(1)} collective-permute-done((bf16[256,1536]{1,0:T(8,128)(2,1)S(1)}, bf16[256,1536]{1,0:T(8,128)(2,1)S(1)}, u32[]{:S(2)}, u32[]{:S(2)}) %collective-permute-start.72) | collective-permute-done | bytes 786464 | tf_op jit(solution)/shard_map/ppermute | solution.py:107
  344.3 8.4 %collective-permute-done.77.refs_3_ = bf16[256,1536]{1,0:T(8,128)(2,1)S(1)} collective-permute-done((bf16[256,1536]{1,0:T(8,128)(2,1)S(1)}, bf16[256,1536]{1,0:T(8,128)(2,1)S(1)}, u32[]{:S(2)}, u32[]{:S(2)}) %collective-permute-start.77) | collective-permute-done | bytes 786464 | tf_op jit(solution)/shard_map/ppermute | solution.py:107
  355.2 15.2 %collective-permute-start.81 = (bf16[528,2048]{1,0:T(8,128)(2,1)}, bf16[528,2048]{1,0:T(8,128)(2,1)}, u32[]{:S(2)}, u32[]{:S(2)}) collective-permute-start(bf16[528,2048]{1,0:T(8,128)(2,1)} %add_or_begin.5.refs_1_), channel_id=1, source_target_pairs={{0,8},{24,16},{8,0},{16,24},{1,9},{25,17},{9,1},{17,25},{2,10},{26... | collective-permute-start | bytes 6488072 | tf_op jit(solution)/shard_map/ppermute | solution.py:161
  374.3 11.6 %conditional.17 = (bf16[448,2048]{1,0:T(8,128)(2,1)}) conditional(s32[]{:T(128)} %bitcast.14, () %tuple.353, (f32[1,2048]{1,0:T(1,128)S(1)}, f32[1,1024]{1,0:T(1,128)S(1)}, f32[1,2048]{1,0:T(1,128)S(1)}, bf16[176,2048]{1,0:T(8,128)(2,1)}, bf16[1024,512]{1,0:T(8,128)(2,1)S(1)}) %tuple.519), branch_computations={%region_10.11_spmd, %region_11.12_spmd} | conditional | flops 41984 | bytes 1835018 | solution.py:1189
  385.9 4.9 share.17
  396.5 12.1 %conditional.19 = (bf16[192,2048]{1,0:T(8,128)(2,1)}, bf16[192,2048]{1,0:T(8,128)(2,1)}, bf16[192,2048]{1,0:T(8,128)(2,1)}, bf16[192,2048]{1,0:T(8,128)(2,1)}, bf16[192,2048]{1,0:T(8,128)(2,1)S(1)}) conditional(s32[]{:T(128)} %bitcast.14, () %tuple.336, (bf16[192,2048]{1,0:T(8,128)(2,1)S(1)}, bf16[192,2048]{1,0:T(8,128)(2,1)S(1)}, ...), branch_computations={%region_14.15_spmd, %region_15.16_spmd} | conditional | flops 1024 | bytes 9438368 | solution.py:1189
  398.2 4.2 share.11
  402.4 6.2 %collective-permute-done.7 = bf16[192,2048]{1,0:T(8,128)(2,1)} collective-permute-done((bf16[192,2048]{1,0:T(8,128)(2,1)S(1)}, bf16[192,2048]{1,0:T(8,128)(2,1)}, u32[]{:S(2)}, u32[]{:S(2)}) %collective-permute-start.7) | collective-permute-done | bytes 786464 | tf_op jit(solution)/shard_map/cond/branch_1_fun/ppermute | solution.py:107
  411.8 5.8 %collective-permute-done.81.refs_1_.refs_2_ = bf16[528,2048]{1,0:T(8,128)(2,1)} collective-permute-done((bf16[528,2048]{1,0:T(8,128)(2,1)}, bf16[528,2048]{1,0:T(8,128)(2,1)}, u32[]{:S(2)}, u32[]{:S(2)}) %collective-permute-start.81) | collective-permute-done | bytes 2162720 | tf_op jit(solution)/shard_map/ppermute | solution.py:161
  424.8 7.7 %collective-permute-start.82 = (bf16[448,2048]{1,0:T(8,128)(2,1)S(1)}, bf16[448,2048]{1,0:T(8,128)(2,1)S(1)}, u32[]{:S(2)}, u32[]{:S(2)}) collective-permute-start(bf16[448,2048]{1,0:T(8,128)(2,1)S(1)} %copy-done.82), channel_id=1, source_target_pairs={{0,8},{24,16},{1,9},{25,17},{2,10},{26,18},{3,11},{27,19},{4,12},{... | collective-permute-start | bytes 5505032 | tf_op jit(solution)/shard_map/ppermute | solution.py:161
  435.5 4.0 settle.12
  443.3 29.8 %collective-permute-done.84.refs_2_ = bf16[528,2048]{1,0:T(8,128)(2,1)S(1)} collective-permute-done((bf16[528,2048]{1,0:T(8,128)(2,1)S(1)}, bf16[528,2048]{1,0:T(8,128)(2,1)S(1)}, u32[]{:S(2)}, u32[]{:S(2)}) %collective-permute-start.84) | collective-permute-done | bytes 2162720 | tf_op jit(solution)/shard_map/ppermute | solution.py:161
  481.4 18.6 %conditional.20 = (bf16[192,2048]{1,0:T(8,128)(2,1)}, bf16[192,2048]{1,0:T(8,128)(2,1)}, bf16[192,2048]{1,0:T(8,128)(2,1)}) conditional(s32[]{:T(128)} %bitcast.14, () %tuple.450, (bf16[192,2048]{1,0:T(8,128)(2,1)S(1)}, bf16[192,2048]{1,0:T(8,128)(2,1)S(1)}, bf16[192,2048]{1,0:T(8,128)(2,1)S(1)}) %tuple.452), branch_computations={%region_16.17_spmd, %region_17.18_spmd} | conditional | bytes 9437328 | solution.py:1189
  484.1 16.0 %collective-permute-done.10 = bf16[192,2048]{1,0:T(8,128)(2,1)} collective-permute-done((bf16[192,2048]{1,0:T(8,128)(2,1)S(1)}, bf16[192,2048]{1,0:T(8,128)(2,1)}, u32[]{:S(2)}, u32[]{:S(2)}) %collective-permute-start.10) | collective-permute-done | bytes 786464 | tf_op jit(solution)/shard_map/cond/branch_1_fun/ppermute | solution.py:107
  509.7 16.0 %collective-permute-done.86.came = bf16[528,2048]{1,0:T(8,128)(2,1)} collective-permute-done((bf16[528,2048]{1,0:T(8,128)(2,1)}, bf16[528,2048]{1,0:T(8,128)(2,1)}, u32[]{:S(2)}, u32[]{:S(2)}) %collective-permute-start.86) | collective-permute-done | bytes 2162720 | tf_op jit(solution)/shard_map/ppermute | solution.py:161
  529.2 17.8 %conditional.21 = (bf16[192,2048]{1,0:T(8,128)(2,1)}, bf16[192,2048]{1,0:T(8,128)(2,1)}, bf16[192,2048]{1,0:T(8,128)(2,1)}, f32[512,2048]{1,0:T(8,128)}) conditional(s32[]{:T(128)} %bitcast.14, () %tuple.477, (bf16[192,2048]{1,0:T(8,128)(2,1)S(1)}, bf16[528,2048]{1,0:T(8,128)(2,1)}, s32[1]{0:T(128)}, bf16[528,2048]{1,0:T(8,128)(2,1)}) %tuple.479), branch_computations={%region_18.19_spmd, %region_19.20_spmd} | conditional | flops 1024 | bytes 9438360 | solution.py:1189
  536.0 11.0 %collective-permute-done.13 = bf16[192,2048]{1,0:T(8,128)(2,1)} collective-permute-done((bf16[192,2048]{1,0:T(8,128)(2,1)S(1)}, bf16[192,2048]{1,0:T(8,128)(2,1)}, u32[]{:S(2)}, u32[]{:S(2)}) %collective-permute-start.13) | collective-permute-done | bytes 786464 | tf_op jit(solution)/shard_map/cond/branch_1_fun/ppermute | solution.py:107
  547.0 12.9 %conditional.22 = (bf16[192,2048]{1,0:T(8,128)(2,1)}, bf16[192,2048]{1,0:T(8,128)(2,1)}, bf16[192,2048]{1,0:T(8,128)(2,1)}, f32[2048,1024]{1,0:T(8,128)}, f32[2048,256]{1,0:T(8,128)}, /*index=5*/f32[2048,256]{1,0:T(8,128)}) conditional(s32[]{:T(128)} %bitcast.14, () %tuple.476, (bf16[192,2048]{1,0:T(8,128)(2,1)}, bf16[192,2048]{1,0:T(8,128)(2,1)}, ...), branch_computations={%region_20.21_spmd, %region_21.22_spmd} | conditional | flops 1024 | bytes 14942274 | solution.py:1189
  550.8 6.2 %unpack.2 = (f32[2048,1024]{1,0:T(8,128)}, f32[2048,256]{1,0:T(8,128)}, f32[2048,256]{1,0:T(8,128)}) custom-call(s32[8]{0:T(128)S(1)} %get-tuple-element.184.table, bf16[192,2048]{1,0:T(8,128)(2,1)S(1)} %get-tuple-element.185.refs_0_, bf16[192,2048]{1,0:T(8,128)(2,1)} %get-tuple-element.186.refs_1_, bf16[192,2048]{1,0:T(8,128)(2,1)} %get-tuple-element.182.refs_2_, ...), custom_call_target="tpu_custom_call" | custom-call | flops 1024 | bytes 1024 | tf_op jit(solution)/shard_map/cond/branch_1_fun/unpack/pallas_call | solution.py:1122
  (414 shorter events, 247.0 us)
Async XLA Ops:
  0.6 39.5 %collective-permute-start.26 = (bf16[192,2048]{1,0:T(8,128)(2,1)}, bf16[192,2048]{1,0:T(8,128)(2,1)}, u32[]{:S(2)}, u32[]{:S(2)}) collective-permute-start(bf16[192,2048]{1,0:T(8,128)(2,1)} %bitcast.13.refs_0_.cotangent), channel_id=1, source_target_pairs={{0,2},{1,5},{2,0},{3,7},{4,6},{5,1},{6,4},{7,3},{8,10},{9,13},{10,... | collective-permute-start | bytes 2359304 | tf_op jit(solution)/shard_map/ppermute | solution.py:107
  12.2 15.3 %collective-permute-start.20 = (bf16[192,1536]{1,0:T(8,128)(2,1)}, bf16[192,1536]{1,0:T(8,128)(2,1)}, u32[]{:S(2)}, u32[]{:S(2)}) collective-permute-start(bf16[192,1536]{1,0:T(8,128)(2,1)} %get-tuple-element.94), channel_id=1, source_target_pairs={{0,2},{1,5},{2,0},{3,7},{4,6},{5,1},{6,4},{7,3},{8,10},{9,13},{10,... | collective-permute-start | bytes 1769480 | tf_op jit(solution)/shard_map/cond/branch_1_fun/ppermute | solution.py:107
  12.3 15.2 %collective-permute-start.21 = (bf16[192,1536]{1,0:T(8,128)(2,1)}, bf16[192,1536]{1,0:T(8,128)(2,1)}, u32[]{:S(2)}, u32[]{:S(2)}) collective-permute-start(bf16[192,1536]{1,0:T(8,128)(2,1)} %get-tuple-element.94), channel_id=1, source_target_pairs={{0,4},{1,3},{2,6},{3,1},{4,0},{5,7},{6,2},{7,5},{8,12},{9,11},{10,... | collective-permute-start | bytes 1769480 | tf_op jit(solution)/shard_map/cond/branch_1_fun/ppermute | solution.py:107
  14.3 13.2 %collective-permute-start.22 = (bf16[192,1536]{1,0:T(8,128)(2,1)}, bf16[192,1536]{1,0:T(8,128)(2,1)}, u32[]{:S(2)}, u32[]{:S(2)}) collective-permute-start(bf16[192,1536]{1,0:T(8,128)(2,1)} %get-tuple-element.94), channel_id=1, source_target_pairs={{0,1},{1,0},{2,3},{3,2},{4,5},{5,4},{6,7},{7,6},{8,9},{9,8},{10,11... | collective-permute-start | bytes 1769480 | tf_op jit(solution)/shard_map/cond/branch_1_fun/ppermute | solution.py:107
  40.2 22.7 %collective-permute-start.27 = (bf16[192,2048]{1,0:T(8,128)(2,1)}, bf16[192,2048]{1,0:T(8,128)(2,1)}, u32[]{:S(2)}, u32[]{:S(2)}) collective-permute-start(bf16[192,2048]{1,0:T(8,128)(2,1)} %bitcast.13.refs_0_.cotangent), channel_id=1, source_target_pairs={{0,4},{1,3},{2,6},{3,1},{4,0},{5,7},{6,2},{7,5},{8,12},{9,11},{10,... | collective-permute-start | bytes 2359304 | tf_op jit(solution)/shard_map/ppermute | solution.py:107
  41.8 21.0 %collective-permute-start.28 = (bf16[192,2048]{1,0:T(8,128)(2,1)}, bf16[192,2048]{1,0:T(8,128)(2,1)}, u32[]{:S(2)}, u32[]{:S(2)}) collective-permute-start(bf16[192,2048]{1,0:T(8,128)(2,1)} %collective-permute-done.26.refs_2_), channel_id=1, source_target_pairs={{0,4},{1,3},{2,6},{3,1},{4,0},{5,7},{6,2},{7,5},{8,12},{9,11},{10,... | collective-permute-start | bytes 2359304 | tf_op jit(solution)/shard_map/ppermute | solution.py:107
  42.2 20.7 %collective-permute-start.29 = (bf16[192,2048]{1,0:T(8,128)(2,1)}, bf16[192,2048]{1,0:T(8,128)(2,1)}, u32[]{:S(2)}, u32[]{:S(2)}) collective-permute-start(bf16[192,2048]{1,0:T(8,128)(2,1)} %bitcast.13.refs_0_.cotangent), channel_id=1, source_target_pairs={{0,1},{1,0},{2,3},{3,2},{4,5},{5,4},{6,7},{7,6},{8,9},{9,8},{10,11... | collective-permute-start | bytes 2359304 | tf_op jit(solution)/shard_map/ppermute | solution.py:107
  42.2 20.7 %collective-permute-start.30 = (bf16[192,2048]{1,0:T(8,128)(2,1)}, bf16[192,2048]{1,0:T(8,128)(2,1)}, u32[]{:S(2)}, u32[]{:S(2)}) collective-permute-start(bf16[192,2048]{1,0:T(8,128)(2,1)} %collective-permute-done.26.refs_2_), channel_id=1, source_target_pairs={{0,1},{1,0},{2,3},{3,2},{4,5},{5,4},{6,7},{7,6},{8,9},{9,8},{10,11... | collective-permute-start | bytes 2359304 | tf_op jit(solution)/shard_map/ppermute | solution.py:107
  78.6 20.0 %collective-permute-start.35 = (bf16[192,2048]{1,0:T(8,128)(2,1)S(1)}, bf16[192,2048]{1,0:T(8,128)(2,1)S(1)}, u32[]{:S(2)}, u32[]{:S(2)}) collective-permute-start(bf16[192,2048]{1,0:T(8,128)(2,1)S(1)} %add_rows.26), channel_id=1, source_target_pairs={{0,2},{1,5},{2,0},{3,7},{4,6},{5,1},{6,4},{7,3},{8,10},{9,13},{10,... | collective-permute-start | bytes 2359304 | tf_op jit(solution)/shard_map/ppermute | solution.py:107
  79.9 18.7 %collective-permute-start.36 = (bf16[192,2048]{1,0:T(8,128)(2,1)S(1)}, bf16[192,2048]{1,0:T(8,128)(2,1)S(1)}, u32[]{:S(2)}, u32[]{:S(2)}) collective-permute-start(bf16[192,2048]{1,0:T(8,128)(2,1)S(1)} %add_rows.27), channel_id=1, source_target_pairs={{0,4},{1,3},{2,6},{3,1},{4,0},{5,7},{6,2},{7,5},{8,12},{9,11},{10,... | collective-permute-start | bytes 2359304 | tf_op jit(solution)/shard_map/ppermute | solution.py:107
  81.7 16.8 %collective-permute-start.37 = (bf16[192,2048]{1,0:T(8,128)(2,1)S(1)}, bf16[192,2048]{1,0:T(8,128)(2,1)S(1)}, u32[]{:S(2)}, u32[]{:S(2)}) collective-permute-start(bf16[192,2048]{1,0:T(8,128)(2,1)S(1)} %get-tuple-element.684), channel_id=1, source_target_pairs={{0,1},{1,0},{2,3},{3,2},{4,5},{5,4},{6,7},{7,6},{8,9},{9,8},{10,11... | collective-permute-start | bytes 2359304 | tf_op jit(solution)/shard_map/ppermute | solution.py:107
  100.9 20.1 %collective-permute-start.40 = (bf16[192,2048]{1,0:T(8,128)(2,1)S(1)}, bf16[192,2048]{1,0:T(8,128)(2,1)S(1)}, u32[]{:S(2)}, u32[]{:S(2)}) collective-permute-start(bf16[192,2048]{1,0:T(8,128)(2,1)S(1)} %get-tuple-element.703.refs_0_), channel_id=1, source_target_pairs={{0,2},{1,5},{2,0},{3,7},{4,6},{5,1},{6,4},{7,3},{8,10},{9,13},{10,... | collective-permute-start | bytes 2359304 | tf_op jit(solution)/shard_map/ppermute | solution.py:107
  102.2 18.8 %collective-permute-start.41 = (bf16[192,2048]{1,0:T(8,128)(2,1)S(1)}, bf16[192,2048]{1,0:T(8,128)(2,1)S(1)}, u32[]{:S(2)}, u32[]{:S(2)}) collective-permute-start(bf16[192,2048]{1,0:T(8,128)(2,1)S(1)} %get-tuple-element.703.refs_0_), channel_id=1, source_target_pairs={{0,4},{1,3},{2,6},{3,1},{4,0},{5,7},{6,2},{7,5},{8,12},{9,11},{10,... | collective-permute-start | bytes 2359304 | tf_op jit(solution)/shard_map/ppermute | solution.py:107
  150.0 50.6 %collective-permute-start.53 = (bf16[528,2048]{1,0:T(8,128)(2,1)}, bf16[528,2048]{1,0:T(8,128)(2,1)}, u32[]{:S(2)}, u32[]{:S(2)}) collective-permute-start(bf16[528,2048]{1,0:T(8,128)(2,1)} %get-tuple-element.747.refs_0_), channel_id=1, source_target_pairs={{0,8},{24,16},{1,9},{25,17},{2,10},{26,18},{3,11},{27,19},{4,12},{... | collective-permute-start | bytes 6488072 | tf_op jit(solution)/shard_map/ppermute | solution.py:161
  180.9 33.3 %collective-permute-start.50 = (bf16[192,2048]{1,0:T(8,128)(2,1)S(1)}, bf16[192,2048]{1,0:T(8,128)(2,1)S(1)}, u32[]{:S(2)}, u32[]{:S(2)}) collective-permute-start(bf16[192,2048]{1,0:T(8,128)(2,1)S(1)} %add_rows.29), channel_id=1, source_target_pairs={{0,2},{1,5},{2,0},{3,7},{4,6},{5,1},{6,4},{7,3},{8,10},{9,13},{10,... | collective-permute-start | bytes 2359304 | tf_op jit(solution)/shard_map/ppermute | solution.py:107
  182.5 31.8 %collective-permute-start.51 = (bf16[192,2048]{1,0:T(8,128)(2,1)S(1)}, bf16[192,2048]{1,0:T(8,128)(2,1)S(1)}, u32[]{:S(2)}, u32[]{:S(2)}) collective-permute-start(bf16[192,2048]{1,0:T(8,128)(2,1)S(1)} %add_rows.30), channel_id=1, source_target_pairs={{0,4},{1,3},{2,6},{3,1},{4,0},{5,7},{6,2},{7,5},{8,12},{9,11},{10,... | collective-permute-start | bytes 2359304 | tf_op jit(solution)/shard_map/ppermute | solution.py:107
  183.6 30.6 %collective-permute-start.52 = (bf16[192,2048]{1,0:T(8,128)(2,1)S(1)}, bf16[192,2048]{1,0:T(8,128)(2,1)S(1)}, u32[]{:S(2)}, u32[]{:S(2)}) collective-permute-start(bf16[192,2048]{1,0:T(8,128)(2,1)S(1)} %get-tuple-element.781), channel_id=1, source_target_pairs={{0,1},{1,0},{2,3},{3,2},{4,5},{5,4},{6,7},{7,6},{8,9},{9,8},{10,11... | collective-permute-start | bytes 2359304 | tf_op jit(solution)/shard_map/ppermute | solution.py:107
  204.7 52.0 %collective-permute-start.61 = (bf16[528,2048]{1,0:T(8,128)(2,1)}, bf16[528,2048]{1,0:T(8,128)(2,1)}, u32[]{:S(2)}, u32[]{:S(2)}) collective-permute-start(bf16[528,2048]{1,0:T(8,128)(2,1)} %add_rows.31.own), channel_id=1, source_target_pairs={{8,16},{16,8},{9,17},{17,9},{10,18},{18,10},{11,19},{19,11},{12,20... | collective-permute-start | bytes 6488072 | tf_op jit(solution)/shard_map/ppermute | solution.py:161
  206.8 53.8 %collective-permute-start.60 = (bf16[528,2048]{1,0:T(8,128)(2,1)}, bf16[528,2048]{1,0:T(8,128)(2,1)}, u32[]{:S(2)}, u32[]{:S(2)}) collective-permute-start(bf16[528,2048]{1,0:T(8,128)(2,1)} %get-tuple-element.787.refs_0_), channel_id=1, source_target_pairs={{0,8},{24,16},{1,9},{25,17},{2,10},{26,18},{3,11},{27,19},{4,12},{... | collective-permute-start | bytes 6488072 | tf_op jit(solution)/shard_map/ppermute | solution.py:161
  218.5 20.3 %collective-permute-start.55 = (bf16[192,2048]{1,0:T(8,128)(2,1)S(1)}, bf16[192,2048]{1,0:T(8,128)(2,1)}, u32[]{:S(2)}, u32[]{:S(2)}) collective-permute-start(bf16[192,2048]{1,0:T(8,128)(2,1)S(1)} %get-tuple-element.803.refs_0_), channel_id=1, source_target_pairs={{0,2},{1,5},{2,0},{3,7},{4,6},{5,1},{6,4},{7,3},{8,10},{9,13},{10,... | collective-permute-start | bytes 2359304 | tf_op jit(solution)/shard_map/ppermute | solution.py:107
  220.0 18.8 %collective-permute-start.56 = (bf16[192,2048]{1,0:T(8,128)(2,1)S(1)}, bf16[192,2048]{1,0:T(8,128)(2,1)}, u32[]{:S(2)}, u32[]{:S(2)}) collective-permute-start(bf16[192,2048]{1,0:T(8,128)(2,1)S(1)} %get-tuple-element.803.refs_0_), channel_id=1, source_target_pairs={{0,4},{1,3},{2,6},{3,1},{4,0},{5,7},{6,2},{7,5},{8,12},{9,11},{10,... | collective-permute-start | bytes 2359304 | tf_op jit(solution)/shard_map/ppermute | solution.py:107
  239.3 12.3 %collective-permute-start.59 = (bf16[192,2048]{1,0:T(8,128)(2,1)}, bf16[192,2048]{1,0:T(8,128)(2,1)}, u32[]{:S(2)}, u32[]{:S(2)}) collective-permute-start(bf16[192,2048]{1,0:T(8,128)(2,1)} %collective-permute-done.55.refs_0_.refs_2_), channel_id=1, source_target_pairs={{0,4},{1,3},{2,6},{3,1},{4,0},{5,7},{6,2},{7,5},{8,12},{9,11},{10,... | collective-permute-start | bytes 2359304 | tf_op jit(solution)/shard_map/ppermute | solution.py:107
  259.2 52.0 %collective-permute-start.70 = (bf16[528,2048]{1,0:T(8,128)(2,1)S(1)}, bf16[528,2048]{1,0:T(8,128)(2,1)S(1)}, u32[]{:S(2)}, u32[]{:S(2)}) collective-permute-start(bf16[528,2048]{1,0:T(8,128)(2,1)S(1)} %add_or_begin.3.refs_1_), channel_id=1, source_target_pairs={{0,8},{24,16},{8,0},{16,24},{1,9},{25,17},{9,1},{17,25},{2,10},{26... | collective-permute-start | bytes 6488072 | tf_op jit(solution)/shard_map/ppermute | solution.py:161
  264.1 47.7 %collective-permute-start.69 = (bf16[528,2048]{1,0:T(8,128)(2,1)S(1)}, bf16[528,2048]{1,0:T(8,128)(2,1)}, u32[]{:S(2)}, u32[]{:S(2)}) collective-permute-start(bf16[528,2048]{1,0:T(8,128)(2,1)S(1)} %add_rows.32.own), channel_id=1, source_target_pairs={{8,16},{16,8},{9,17},{17,9},{10,18},{18,10},{11,19},{19,11},{12,20... | collective-permute-start | bytes 6488072 | tf_op jit(solution)/shard_map/ppermute | solution.py:161
  292.4 15.7 %collective-permute-start.66 = (bf16[192,1536]{1,0:T(8,128)(2,1)S(1)}, bf16[192,1536]{1,0:T(8,128)(2,1)S(1)}, u32[]{:S(2)}, u32[]{:S(2)}) collective-permute-start(bf16[192,1536]{1,0:T(8,128)(2,1)S(1)} %add_rows.34), channel_id=1, source_target_pairs={{0,2},{1,5},{2,0},{3,7},{4,6},{5,1},{6,4},{7,3},{8,10},{9,13},{10,... | collective-permute-start | bytes 1769480 | tf_op jit(solution)/shard_map/ppermute | solution.py:107
  293.9 14.2 %collective-permute-start.67 = (bf16[192,1536]{1,0:T(8,128)(2,1)S(1)}, bf16[192,1536]{1,0:T(8,128)(2,1)S(1)}, u32[]{:S(2)}, u32[]{:S(2)}) collective-permute-start(bf16[192,1536]{1,0:T(8,128)(2,1)S(1)} %add_rows.35), channel_id=1, source_target_pairs={{0,4},{1,3},{2,6},{3,1},{4,0},{5,7},{6,2},{7,5},{8,12},{9,11},{10,... | collective-permute-start | bytes 1769480 | tf_op jit(solution)/shard_map/ppermute | solution.py:107
  295.0 13.1 %collective-permute-start.68 = (bf16[192,1536]{1,0:T(8,128)(2,1)S(1)}, bf16[192,1536]{1,0:T(8,128)(2,1)S(1)}, u32[]{:S(2)}, u32[]{:S(2)}) collective-permute-start(bf16[192,1536]{1,0:T(8,128)(2,1)S(1)} %get-tuple-element.869), channel_id=1, source_target_pairs={{0,1},{1,0},{2,3},{3,2},{4,5},{5,4},{6,7},{7,6},{8,9},{9,8},{10,11... | collective-permute-start | bytes 1769480 | tf_op jit(solution)/shard_map/ppermute | solution.py:107
  314.8 38.3 %collective-permute-start.76 = (bf16[528,2048]{1,0:T(8,128)(2,1)S(1)}, bf16[528,2048]{1,0:T(8,128)(2,1)S(1)}, u32[]{:S(2)}, u32[]{:S(2)}) collective-permute-start(bf16[528,2048]{1,0:T(8,128)(2,1)S(1)} %add_rows.36.own), channel_id=1, source_target_pairs={{8,16},{16,8},{9,17},{17,9},{10,18},{18,10},{11,19},{19,11},{12,20... | collective-permute-start | bytes 6488072 | tf_op jit(solution)/shard_map/ppermute | solution.py:161
  315.6 54.7 %collective-permute-start.75 = (bf16[528,2048]{1,0:T(8,128)(2,1)S(1)}, bf16[528,2048]{1,0:T(8,128)(2,1)S(1)}, u32[]{:S(2)}, u32[]{:S(2)}) collective-permute-start(bf16[528,2048]{1,0:T(8,128)(2,1)S(1)} %add_or_begin.4.refs_1_), channel_id=1, source_target_pairs={{0,8},{24,16},{8,0},{16,24},{1,9},{25,17},{9,1},{17,25},{2,10},{26... | collective-permute-start | bytes 6488072 | tf_op jit(solution)/shard_map/ppermute | solution.py:161
  333.2 19.5 %collective-permute-start.77 = (bf16[256,1536]{1,0:T(8,128)(2,1)S(1)}, bf16[256,1536]{1,0:T(8,128)(2,1)S(1)}, u32[]{:S(2)}, u32[]{:S(2)}) collective-permute-start(bf16[256,1536]{1,0:T(8,128)(2,1)S(1)} %add_rows.38), channel_id=1, source_target_pairs={{0,2},{1,5},{2,0},{3,7},{4,6},{5,1},{6,4},{7,3},{8,10},{9,13},{10,... | collective-permute-start | bytes 2359304 | tf_op jit(solution)/shard_map/ppermute | solution.py:107
  334.7 18.0 %collective-permute-start.78 = (bf16[256,1536]{1,0:T(8,128)(2,1)S(1)}, bf16[256,1536]{1,0:T(8,128)(2,1)S(1)}, u32[]{:S(2)}, u32[]{:S(2)}) collective-permute-start(bf16[256,1536]{1,0:T(8,128)(2,1)S(1)} %add_rows.39), channel_id=1, source_target_pairs={{0,4},{1,3},{2,6},{3,1},{4,0},{5,7},{6,2},{7,5},{8,12},{9,11},{10,... | collective-permute-start | bytes 2359304 | tf_op jit(solution)/shard_map/ppermute | solution.py:107
  336.0 16.7 %collective-permute-start.79 = (bf16[256,1536]{1,0:T(8,128)(2,1)S(1)}, bf16[256,1536]{1,0:T(8,128)(2,1)S(1)}, u32[]{:S(2)}, u32[]{:S(2)}) collective-permute-start(bf16[256,1536]{1,0:T(8,128)(2,1)S(1)} %get-tuple-element.936), channel_id=1, source_target_pairs={{0,1},{1,0},{2,3},{3,2},{4,5},{5,4},{6,7},{7,6},{8,9},{9,8},{10,11... | collective-permute-start | bytes 2359304 | tf_op jit(solution)/shard_map/ppermute | solution.py:107
  355.2 62.4 %collective-permute-start.81 = (bf16[528,2048]{1,0:T(8,128)(2,1)}, bf16[528,2048]{1,0:T(8,128)(2,1)}, u32[]{:S(2)}, u32[]{:S(2)}) collective-permute-start(bf16[528,2048]{1,0:T(8,128)(2,1)} %add_or_begin.5.refs_1_), channel_id=1, source_target_pairs={{0,8},{24,16},{8,0},{16,24},{1,9},{25,17},{9,1},{17,25},{2,10},{26... | collective-permute-start | bytes 6488072 | tf_op jit(solution)/shard_map/ppermute | solution.py:161
  372.2 47.5 %collective-permute-start.80 = (bf16[528,2048]{1,0:T(8,128)(2,1)}, bf16[528,2048]{1,0:T(8,128)(2,1)}, u32[]{:S(2)}, u32[]{:S(2)}) collective-permute-start(bf16[528,2048]{1,0:T(8,128)(2,1)} %add_rows.40.refs_0_), channel_id=1, source_target_pairs={{8,16},{16,8},{9,17},{17,9},{10,18},{18,10},{11,19},{19,11},{12,20... | collective-permute-start | bytes 6488072 | tf_op jit(solution)/shard_map/ppermute | solution.py:161
  396.5 12.1 %collective-permute-start.7 = (bf16[192,2048]{1,0:T(8,128)(2,1)S(1)}, bf16[192,2048]{1,0:T(8,128)(2,1)}, u32[]{:S(2)}, u32[]{:S(2)}) collective-permute-start(bf16[192,2048]{1,0:T(8,128)(2,1)S(1)} %get-tuple-element.148), channel_id=1, source_target_pairs={{0,4},{1,3},{2,6},{3,1},{4,0},{5,7},{6,2},{7,5},{8,12},{9,11},{10,... | collective-permute-start | bytes 2359304 | tf_op jit(solution)/shard_map/cond/branch_1_fun/ppermute | solution.py:107
  422.7 50.5 %collective-permute-start.84 = (bf16[528,2048]{1,0:T(8,128)(2,1)S(1)}, bf16[528,2048]{1,0:T(8,128)(2,1)S(1)}, u32[]{:S(2)}, u32[]{:S(2)}) collective-permute-start(bf16[528,2048]{1,0:T(8,128)(2,1)S(1)} %add_rows.45.refs_1_), channel_id=1, source_target_pairs={{8,0},{16,24},{9,1},{17,25},{10,2},{18,26},{11,3},{19,27},{12,4},{... | collective-permute-start | bytes 6488072 | tf_op jit(solution)/shard_map/ppermute | solution.py:161
  424.0 50.5 %collective-permute-start.83 = (bf16[528,2048]{1,0:T(8,128)(2,1)S(1)}, bf16[528,2048]{1,0:T(8,128)(2,1)S(1)}, u32[]{:S(2)}, u32[]{:S(2)}) collective-permute-start(bf16[528,2048]{1,0:T(8,128)(2,1)S(1)} %add_rows.44.refs_0_), channel_id=1, source_target_pairs={{8,16},{16,8},{9,17},{17,9},{10,18},{18,10},{11,19},{19,11},{12,20... | collective-permute-start | bytes 6488072 | tf_op jit(solution)/shard_map/ppermute | solution.py:161
  424.8 52.8 %collective-permute-start.82 = (bf16[448,2048]{1,0:T(8,128)(2,1)S(1)}, bf16[448,2048]{1,0:T(8,128)(2,1)S(1)}, u32[]{:S(2)}, u32[]{:S(2)}) collective-permute-start(bf16[448,2048]{1,0:T(8,128)(2,1)S(1)} %copy-done.82), channel_id=1, source_target_pairs={{0,8},{24,16},{1,9},{25,17},{2,10},{26,18},{3,11},{27,19},{4,12},{... | collective-permute-start | bytes 5505032 | tf_op jit(solution)/shard_map/ppermute | solution.py:161
  476.3 49.3 %collective-permute-start.86 = (bf16[528,2048]{1,0:T(8,128)(2,1)}, bf16[528,2048]{1,0:T(8,128)(2,1)}, u32[]{:S(2)}, u32[]{:S(2)}) collective-permute-start(bf16[528,2048]{1,0:T(8,128)(2,1)} %add_rows.46.own), channel_id=1, source_target_pairs={{8,0},{16,24},{9,1},{17,25},{10,2},{18,26},{11,3},{19,27},{12,4},{... | collective-permute-start | bytes 6488072 | tf_op jit(solution)/shard_map/ppermute | solution.py:161
  479.3 27.9 %collective-permute-start.85 = (bf16[448,2048]{1,0:T(8,128)(2,1)}, bf16[448,2048]{1,0:T(8,128)(2,1)}, u32[]{:S(2)}, u32[]{:S(2)}) collective-permute-start(bf16[448,2048]{1,0:T(8,128)(2,1)} %add_rows.47.refs_0_), channel_id=1, source_target_pairs={{8,16},{16,8},{9,17},{17,9},{10,18},{18,10},{11,19},{19,11},{12,20... | collective-permute-start | bytes 5505032 | tf_op jit(solution)/shard_map/ppermute | solution.py:161
  481.4 18.6 %collective-permute-start.10 = (bf16[192,2048]{1,0:T(8,128)(2,1)S(1)}, bf16[192,2048]{1,0:T(8,128)(2,1)}, u32[]{:S(2)}, u32[]{:S(2)}) collective-permute-start(bf16[192,2048]{1,0:T(8,128)(2,1)S(1)} %get-tuple-element.161), channel_id=1, source_target_pairs={{0,2},{1,5},{2,0},{3,7},{4,6},{5,1},{6,4},{7,3},{8,10},{9,13},{10,... | collective-permute-start | bytes 2359304 | tf_op jit(solution)/shard_map/cond/branch_1_fun/ppermute | solution.py:107
  482.9 17.1 %collective-permute-start.11 = (bf16[192,2048]{1,0:T(8,128)(2,1)S(1)}, bf16[192,2048]{1,0:T(8,128)(2,1)}, u32[]{:S(2)}, u32[]{:S(2)}) collective-permute-start(bf16[192,2048]{1,0:T(8,128)(2,1)S(1)} %get-tuple-element.162), channel_id=1, source_target_pairs={{0,4},{1,3},{2,6},{3,1},{4,0},{5,7},{6,2},{7,5},{8,12},{9,11},{10,... | collective-permute-start | bytes 2359304 | tf_op jit(solution)/shard_map/cond/branch_1_fun/ppermute | solution.py:107
  484.1 16.0 %collective-permute-start.12 = (bf16[192,2048]{1,0:T(8,128)(2,1)S(1)}, bf16[192,2048]{1,0:T(8,128)(2,1)}, u32[]{:S(2)}, u32[]{:S(2)}) collective-permute-start(bf16[192,2048]{1,0:T(8,128)(2,1)S(1)} %get-tuple-element.163), channel_id=1, source_target_pairs={{0,1},{1,0},{2,3},{3,2},{4,5},{5,4},{6,7},{7,6},{8,9},{9,8},{10,11... | collective-permute-start | bytes 2359304 | tf_op jit(solution)/shard_map/cond/branch_1_fun/ppermute | solution.py:107
  525.6 41.2 %collective-permute-start.87 = (bf16[448,2048]{1,0:T(8,128)(2,1)S(1)}, bf16[448,2048]{1,0:T(8,128)(2,1)}, u32[]{:S(2)}, u32[]{:S(2)}) collective-permute-start(bf16[448,2048]{1,0:T(8,128)(2,1)S(1)} %add_rows.49.own), channel_id=1, source_target_pairs={{8,0},{16,24},{9,1},{17,25},{10,2},{18,26},{11,3},{19,27},{12,4},{... | collective-permute-start | bytes 5505032 | tf_op jit(solution)/shard_map/ppermute | solution.py:161
  529.2 17.8 %collective-permute-start.13 = (bf16[192,2048]{1,0:T(8,128)(2,1)S(1)}, bf16[192,2048]{1,0:T(8,128)(2,1)}, u32[]{:S(2)}, u32[]{:S(2)}) collective-permute-start(bf16[192,2048]{1,0:T(8,128)(2,1)S(1)} %get-tuple-element.170), channel_id=1, source_target_pairs={{0,2},{1,5},{2,0},{3,7},{4,6},{5,1},{6,4},{7,3},{8,10},{9,13},{10,... | collective-permute-start | bytes 2359304 | tf_op jit(solution)/shard_map/cond/branch_1_fun/ppermute | solution.py:107
  530.8 16.2 %collective-permute-start.14 = (bf16[192,2048]{1,0:T(8,128)(2,1)S(1)}, bf16[192,2048]{1,0:T(8,128)(2,1)}, u32[]{:S(2)}, u32[]{:S(2)}) collective-permute-start(bf16[192,2048]{1,0:T(8,128)(2,1)S(1)} %get-tuple-element.170), channel_id=1, source_target_pairs={{0,4},{1,3},{2,6},{3,1},{4,0},{5,7},{6,2},{7,5},{8,12},{9,11},{10,... | collective-permute-start | bytes 2359304 | tf_op jit(solution)/shard_map/cond/branch_1_fun/ppermute | solution.py:107
  532.0 15.0 %collective-permute-start.15 = (bf16[192,2048]{1,0:T(8,128)(2,1)S(1)}, bf16[192,2048]{1,0:T(8,128)(2,1)}, u32[]{:S(2)}, u32[]{:S(2)}) collective-permute-start(bf16[192,2048]{1,0:T(8,128)(2,1)S(1)} %get-tuple-element.170), channel_id=1, source_target_pairs={{0,1},{1,0},{2,3},{3,2},{4,5},{5,4},{6,7},{7,6},{8,9},{9,8},{10,11... | collective-permute-start | bytes 2359304 | tf_op jit(solution)/shard_map/cond/branch_1_fun/ppermute | solution.py:107
  547.6 12.3 %collective-permute-start.16 = (bf16[192,2048]{1,0:T(8,128)(2,1)}, bf16[192,2048]{1,0:T(8,128)(2,1)}, u32[]{:S(2)}, u32[]{:S(2)}) collective-permute-start(bf16[192,2048]{1,0:T(8,128)(2,1)} %get-tuple-element.182.refs_2_), channel_id=1, source_target_pairs={{0,4},{1,3},{2,6},{3,1},{4,0},{5,7},{6,2},{7,5},{8,12},{9,11},{10,... | collective-permute-start | bytes 2359304 | tf_op jit(solution)/shard_map/cond/branch_1_fun/ppermute | solution.py:107
  (130 other events, 996.8 us)

commit v5 on v4

--- a/solution.py
+++ b/solution.py
@@ -1338,10 +1338,14 @@
         latents, queries, keys, values, mixed_there = clock(*attend(pieces, cosine, sine))
         share = shares([mixed_there], [out_proj], group)
         c, c_send = clock(*share(clock, 6, 8))
-        a, a_send, b, b_send = clock(*share(clock, 2, 6))
-        own, own_send = clock(*share(clock, 0, 2))
+
+        def other_shares(clock, came):
+            return [*clock(*share(clock, 2, 6)), *clock(*share(clock, 0, 2))]
+
+        (c_came,), (a, a_send, b, b_send, own, own_send) = hops(
+            [c_send], [hop_c], other_shares, True
+        )
         cot_b, cot_c, cot_o, cot_ao = clock(cot_b, cot_c, cot_o, cot_ao)
-        (c_came,), _ = hops([c_send], [hop_c])
         c = clock(add_rows(c, c_came))
         (c_in, a_came, b_came), _ = hops([c, a_send, b_send], [hop_b, hop_c, hop_c])
         a, b = clock(add_rows(a, a_came, c_in), add_rows(b, b_came))

time: 582 us -> 579 us (level)
  local copies, waits for them, and re-layouts: 22.5 us -> 16.4 us
  Pallas kernels: 215 us -> 221 us
    unnamed x181 -> x193, local copies, waits for them, and re-layouts: 18.8 us -> 13.7 us
  transfers between devices with their start and end apart: 88 -> 88, of which waited for: 36 -> 35; matrix products, arithmetic and copies ran while one was open for 1% -> 1% of each run, Pallas kernels for 33% -> 34%
where the time goes in v5:
time: 579 us; the launch traced here: 573 us
  Pallas kernels  221 us (38%)
  waiting for transfers between devices  218 us (38%)
  starting transfers between devices  108 us (19%)
  local copies, waits for them, and re-layouts  16.4 us (3%)
  other arithmetic  6.39 us (1%)
    ppermute x73, waiting for transfers between devices, move(): return lax.ppermute(value, 'head', hop)  153 us
    ppermute x15, waiting for transfers between devices, move(): return lax.ppermute(value, 'tok', pairs)  64.5 us
    pallas_call x36, Pallas kernels, call(): pl.pallas_call(kernel, out_shape=shapes, in_specs=[smem()] * scalars + [v...  58.7 us
    ppermute x15, starting transfers between devices, move(): return lax.ppermute(value, 'tok', pairs)  57 us
    ppermute x73, starting transfers between devices, move(): return lax.ppermute(value, 'head', hop)  51.5 us
    pallas_call x9, Pallas kernels, share(): pl.pallas_call(functools.partial(share_kernel, low, size, terms), out_sha...  36.1 us
    pallas_call x5, Pallas kernels, weight_product(): pl.pallas_call(functools.partial(product_kernel, count, len(operands) - 1...  31.3 us
    pallas_call x7, Pallas kernels, settle(): pl.pallas_call(functools.partial(settle_kernel, low, at), out_shape=shape...  19.4 us
  transfers between devices with their start and end apart: 88, of which 35 were waited for; matrix products, arithmetic and copies ran while one was open for 1% of the time, Pallas kernels for 34%

profile of v5, /device:TPU:0, one launch (start us, length us, event | category | flops | bytes accessed | tf_op | source)
XLA Modules:
  0.0 573.4 jit_solution(8133274009819146104)
XLA Ops:
  5.5 5.5 enter.1
  12.2 15.3 %conditional.13 = (bf16[192,1536]{1,0:T(8,128)(2,1)}, bf16[192,1536]{1,0:T(8,128)(2,1)}, bf16[192,1536]{1,0:T(8,128)(2,1)}, f32[1536,128]{1,0:T(8,128)}, f32[1536,128]{1,0:T(8,128)}) conditional(s32[]{:T(128)} %bitcast.2, () %tuple.319, (bf16[192,1536]{1,0:T(8,128)(2,1)}, s32[1,1536]{1,0:T(1,128)S(1)}) %tuple.528), branch_computations={%region_0.1_spmd, %region_1.2_spmd} | conditional | flops 198400 | bytes 8682660 | solution.py:1189
  14.3 4.4 multiply_sine_fusion
  18.7 8.8 %collective-permute-done.21 = bf16[192,1536]{1,0:T(8,128)(2,1)} collective-permute-done((bf16[192,1536]{1,0:T(8,128)(2,1)}, bf16[192,1536]{1,0:T(8,128)(2,1)}, u32[]{:S(2)}, u32[]{:S(2)}) %collective-permute-start.21) | collective-permute-done | bytes 589856 | tf_op jit(solution)/shard_map/cond/branch_1_fun/ppermute | solution.py:107
  27.5 10.3 %conditional.14 = (bf16[192,1536]{1,0:T(8,128)(2,1)}, bf16[192,1536]{1,0:T(8,128)(2,1)}, bf16[192,1536]{1,0:T(8,128)(2,1)}) conditional(s32[]{:T(128)} %bitcast.2, () %tuple.318, (bf16[192,1536]{1,0:T(8,128)(2,1)}, bf16[192,1536]{1,0:T(8,128)(2,1)}) %tuple.322), branch_computations={%region_2.3_spmd, %region_3.4_spmd} | conditional | bytes 7078032 | solution.py:1189
  29.7 8.0 %collective-permute-done = bf16[192,1536]{1,0:T(8,128)(2,1)} collective-permute-done((bf16[192,1536]{1,0:T(8,128)(2,1)}, bf16[192,1536]{1,0:T(8,128)(2,1)}, u32[]{:S(2)}, u32[]{:S(2)}) %collective-permute-start) | collective-permute-done | bytes 589856 | tf_op jit(solution)/shard_map/cond/branch_1_fun/ppermute | solution.py:107
  43.2 10.9 %attend_forward.1 = (bf16[1536,1024]{1,0:T(8,128)(2,1)}, bf16[1536,512]{1,0:T(8,128)(2,1)S(1)}, bf16[1536,256]{1,0:T(8,128)(2,1)S(1)}, bf16[1536,256]{1,0:T(8,128)(2,1)S(1)}, bf16[1536,512]{1,0:T(8,128)(2,1)}) custom-call(s32[8]{0:T(128)S(1)} %stack.35.refs_0_.table, bf16[192,1536]{1,0:T(8,128)(2,1)} %get-tuple-element.659.refs_1_, ...), custom_call_target="tpu_custom_call" | custom-call | flops 1024 | bytes 1024 | tf_op jit(solution)/shard_map/attend_forward/pallas_call | solution.py:301
  56.5 6.1 %conditional.16 = (bf16[192,2048]{1,0:T(8,128)(2,1)}, bf16[192,2048]{1,0:T(8,128)(2,1)}, bf16[192,2048]{1,0:T(8,128)(2,1)S(1)}, bf16[192,2048]{1,0:T(8,128)(2,1)...) conditional(s32[]{:T(128)} %bitcast.2, () %tuple.316, ...), branch_computations={%region_6.7_spmd, %region_7.8_spmd} | conditional | flops 2048 | bytes 5505094 | solution.py:1189
  66.3 9.8 %collective-permute-done.32.refs_2_ = bf16[192,2048]{1,0:T(8,128)(2,1)S(1)} collective-permute-done((bf16[192,2048]{1,0:T(8,128)(2,1)S(1)}, bf16[192,2048]{1,0:T(8,128)(2,1)S(1)}, u32[]{:S(2)}, u32[]{:S(2)}) %collective-permute-start.32) | collective-permute-done | bytes 786464 | tf_op jit(solution)/shard_map/ppermute | solution.py:107
  80.5 7.1 %rows_product.4.refs_2_ = f32[1536,704]{1,0:T(8,128)S(1)} custom-call(bf16[192,2048]{1,0:T(8,128)(2,1)S(1)} %bitcast.29, bf16[192,2048]{1,0:T(8,128)(2,1)} %collective-permute-done.30.refs_1_, bf16[192,2048]{1,0:T(8,128)(2,1)S(1)} %collective-permute-done.27.refs_2_, bf16[192,2048]{1,0:T(8,128)(2,1)} %collective-permute-done.31.refs_3_, ...), custom_call_target="tpu_custom_call" | custom-call | flops 1024 | bytes 1024 | tf_op jit(solution)/shard_map/rows_product/pallas_call | solution.py:409
  87.5 9.7 %collective-permute-done.35.refs_3_ = bf16[192,2048]{1,0:T(8,128)(2,1)S(1)} collective-permute-done((bf16[192,2048]{1,0:T(8,128)(2,1)S(1)}, bf16[192,2048]{1,0:T(8,128)(2,1)S(1)}, u32[]{:S(2)}, u32[]{:S(2)}) %collective-permute-start.35) | collective-permute-done | bytes 786464 | tf_op jit(solution)/shard_map/ppermute | solution.py:107
  106.4 13.7 %collective-permute-done.40.refs_0_.refs_2_ = bf16[192,2048]{1,0:T(8,128)(2,1)S(1)} collective-permute-done((bf16[192,2048]{1,0:T(8,128)(2,1)S(1)}, bf16[192,2048]{1,0:T(8,128)(2,1)S(1)}, u32[]{:S(2)}, u32[]{:S(2)}) %collective-permute-start.40) | collective-permute-done | bytes 786464 | tf_op jit(solution)/shard_map/ppermute | solution.py:107
  138.9 8.6 %weight_product.5 = (bf16[528,2048]{1,0:T(8,128)(2,1)}, bf16[176,2048]{1,0:T(8,128)(2,1)S(1)}) custom-call(bf16[1536,704]{1,0:T(8,128)(2,1)S(1)} %get-tuple-element.969.left.refs_0_, bf16[192,2048]{1,0:T(8,128)(2,1)S(1)} %bitcast.30, bf16[192,2048]{1,0:T(8,128)(2,1)} %collective-permute-done.30.refs_1_, bf16[192,2048]{1,0:T(8,128)(2,1)S(1)} %copy-done.44, ...), custom_call_target="tpu_custom_call" | custom-call | flops 1024 | bytes 1024 | tf_op jit(solution)/shard_map/weight_product/pallas_call | solution.py:750
  148.4 5.0 collective-permute-start.53
  157.3 5.5 conditional.17
  157.3 5.5 share.11
  167.3 6.5 %share.16 = (bf16[192,2048]{1,0:T(8,128)(2,1)S(1)}, bf16[192,2048]{1,0:T(8,128)(2,1)S(1)}) custom-call(bf16[1536,704]{1,0:T(8,128)(2,1)S(1)} %copy-done.78, bf16[1536,704]{1,0:T(8,128)(2,1)} %copy-done.79, bf16[704,2048]{1,0:T(8,128)(2,1)} %bitcast.43, bf16[704,2048]{1,0:T(8,128)(2,1)} %bitcast.50), custom_call_target="tpu_custom_call" | custom-call | flops 1024 | bytes 1024 | tf_op jit(solution)/shard_map/share/pallas_call | solution.py:529
  180.8 6.7 %weight_product.6 = (bf16[528,2048]{1,0:T(8,128)(2,1)}, bf16[352,2048]{1,0:T(8,128)(2,1)S(1)}) custom-call(bf16[1536,704]{1,0:T(8,128)(2,1)S(1)} %copy-done.78, bf16[192,2048]{1,0:T(8,128)(2,1)S(1)} %copy-done.27, bf16[192,2048]{1,0:T(8,128)(2,1)S(1)} %copy-done.29, bf16[192,2048]{1,0:T(8,128)(2,1)S(1)} %collective-permute-done.40.refs_0_.refs_2_, ...), custom_call_target="tpu_custom_call" | custom-call | flops 1024 | bytes 1024 | tf_op jit(solution)/shard_map/weight_product/pallas_call | solution.py:750
  187.5 11.4 %collective-permute-done.53.refs_1_ = bf16[528,2048]{1,0:T(8,128)(2,1)} collective-permute-done((bf16[528,2048]{1,0:T(8,128)(2,1)}, bf16[528,2048]{1,0:T(8,128)(2,1)}, u32[]{:S(2)}, u32[]{:S(2)}) %collective-permute-start.53) | collective-permute-done | bytes 2162720 | tf_op jit(solution)/shard_map/ppermute | solution.py:161
  198.9 4.1 add_rows.31.own
  205.3 7.3 %collective-permute-start.60 = (bf16[528,2048]{1,0:T(8,128)(2,1)}, bf16[528,2048]{1,0:T(8,128)(2,1)}, u32[]{:S(2)}, u32[]{:S(2)}) collective-permute-start(bf16[528,2048]{1,0:T(8,128)(2,1)} %get-tuple-element.808.refs_0_), channel_id=1, source_target_pairs={{0,8},{24,16},{1,9},{25,17},{2,10},{26,18},{3,11},{27,19},{4,12},{... | collective-permute-start | bytes 6488072 | tf_op jit(solution)/shard_map/ppermute | solution.py:161
  220.9 6.1 %weight_product.7 = (bf16[528,2048]{1,0:T(8,128)(2,1)S(1)}, bf16[528,2048]{1,0:T(8,128)(2,1)S(1)}) custom-call(bf16[1536,704]{1,0:T(8,128)(2,1)S(1)} %copy-done.80, bf16[192,2048]{1,0:T(8,128)(2,1)S(1)} %copy-done.27, bf16[192,2048]{1,0:T(8,128)(2,1)S(1)} %copy-done.29, bf16[192,2048]{1,0:T(8,128)(2,1)S(1)} %copy-done.15, bf16[192,2048]{1,0:T(8,128)(2,1)S(1)} %copy-done.19, ...), custom_call_target="tpu_custom_call" | custom-call | flops 1024 | bytes 1024 | tf_op jit(solution)/shard_map/weight_product/pallas_call | solution.py:750
  228.4 7.3 %collective-permute-done.55.refs_0_.refs_2_ = bf16[192,2048]{1,0:T(8,128)(2,1)} collective-permute-done((bf16[192,2048]{1,0:T(8,128)(2,1)S(1)}, bf16[192,2048]{1,0:T(8,128)(2,1)}, u32[]{:S(2)}, u32[]{:S(2)}) %collective-permute-start.55) | collective-permute-done | bytes 786464 | tf_op jit(solution)/shard_map/ppermute | solution.py:107
  239.5 4.4 rows_product.6.refs_2_
  259.0 4.3 add_rows.32.own
  265.8 9.0 %attend_backward.1 = (bf16[1536,512]{1,0:T(8,128)(2,1)S(1)}, bf16[1536,512]{1,0:T(8,128)(2,1)S(1)}) custom-call(s32[8]{0:T(128)S(1)} %stack.35.refs_0_.table, bf16[384,512]{1,0:T(8,128)(2,1)S(1)} %copy-done.58, bf16[768,512]{1,0:T(8,128)(2,1)S(1)} %copy-done.46, bf16[384,512]{1,0:T(8,128)(2,1)S(1)} %rows_product.7.refs_3_, bf16[1536,512]{1,0:T(8,128)(2,1)S(1)} %copy-done.54, ...), custom_call_target="tpu_custom_call" | custom-call | flops 1024 | bytes 1024 | tf_op jit(solution)/shard_map/attend_backward/pallas_call | solution.py:374
  285.6 5.5 collective-permute-done.63.refs_2_
  294.5 7.8 %weight_product.8 = (bf16[336,2048]{1,0:T(8,128)(2,1)S(1)}, bf16[176,2048]{1,0:T(8,128)(2,1)}) custom-call(bf16[1536,512]{1,0:T(8,128)(2,1)} %get-tuple-element.891.refs_0_.left, bf16[192,2048]{1,0:T(8,128)(2,1)S(1)} %copy-done.48, bf16[192,2048]{1,0:T(8,128)(2,1)S(1)} %copy-done.50, bf16[192,2048]{1,0:T(8,128)(2,1)} %collective-permute-done.55.refs_0_.refs_2_, ...), custom_call_target="tpu_custom_call" | custom-call | flops 1024 | bytes 1024 | tf_op jit(solution)/shard_map/weight_product/pallas_call | solution.py:750
  302.3 5.4 collective-permute-done.66.refs_3_
  314.9 5.8 %collective-permute-start.75 = (bf16[528,2048]{1,0:T(8,128)(2,1)S(1)}, bf16[528,2048]{1,0:T(8,128)(2,1)S(1)}, u32[]{:S(2)}, u32[]{:S(2)}) collective-permute-start(bf16[528,2048]{1,0:T(8,128)(2,1)S(1)} %add_or_begin.4.refs_1_), channel_id=1, source_target_pairs={{0,8},{24,16},{8,0},{16,24},{1,9},{25,17},{9,1},{17,25},{2,10},{26... | collective-permute-start | bytes 6488072 | tf_op jit(solution)/shard_map/ppermute | solution.py:161
  322.8 10.2 %collective-permute-done.72.refs_2_ = bf16[256,1536]{1,0:T(8,128)(2,1)S(1)} collective-permute-done((bf16[256,1536]{1,0:T(8,128)(2,1)S(1)}, bf16[256,1536]{1,0:T(8,128)(2,1)S(1)}, u32[]{:S(2)}, u32[]{:S(2)}) %collective-permute-start.72) | collective-permute-done | bytes 786464 | tf_op jit(solution)/shard_map/ppermute | solution.py:107
  344.6 8.5 %collective-permute-done.77.refs_3_ = bf16[256,1536]{1,0:T(8,128)(2,1)S(1)} collective-permute-done((bf16[256,1536]{1,0:T(8,128)(2,1)S(1)}, bf16[256,1536]{1,0:T(8,128)(2,1)S(1)}, u32[]{:S(2)}, u32[]{:S(2)}) %collective-permute-start.77) | collective-permute-done | bytes 786464 | tf_op jit(solution)/shard_map/ppermute | solution.py:107
  355.8 15.2 %collective-permute-start.81 = (bf16[528,2048]{1,0:T(8,128)(2,1)}, bf16[528,2048]{1,0:T(8,128)(2,1)}, u32[]{:S(2)}, u32[]{:S(2)}) collective-permute-start(bf16[528,2048]{1,0:T(8,128)(2,1)} %add_or_begin.5.refs_1_), channel_id=1, source_target_pairs={{0,8},{24,16},{8,0},{16,24},{1,9},{25,17},{9,1},{17,25},{2,10},{26... | collective-permute-start | bytes 6488072 | tf_op jit(solution)/shard_map/ppermute | solution.py:161
  374.8 11.6 %conditional.19 = (bf16[448,2048]{1,0:T(8,128)(2,1)}) conditional(s32[]{:T(128)} %bitcast.2, () %tuple.359, (f32[1,2048]{1,0:T(1,128)S(1)}, f32[1,1024]{1,0:T(1,128)S(1)}, f32[1,2048]{1,0:T(1,128)S(1)}, bf16[176,2048]{1,0:T(8,128)(2,1)}, bf16[1024,512]{1,0:T(8,128)(2,1)S(1)}) %tuple.438), branch_computations={%region_12.13_spmd, %region_13.14_spmd} | conditional | flops 41984 | bytes 1835018 | solution.py:1189
  386.5 4.9 share.17
  397.1 12.1 %conditional.21 = (bf16[192,2048]{1,0:T(8,128)(2,1)}, bf16[192,2048]{1,0:T(8,128)(2,1)}, bf16[192,2048]{1,0:T(8,128)(2,1)}, bf16[192,2048]{1,0:T(8,128)(2,1)}, bf16[192,2048]{1,0:T(8,128)(2,1)S(1)}) conditional(s32[]{:T(128)} %bitcast.2, () %tuple.342, (bf16[192,2048]{1,0:T(8,128)(2,1)S(1)}, bf16[192,2048]{1,0:T(8,128)(2,1)S(1)}, ...), branch_computations={%region_16.17_spmd, %region_17.18_spmd} | conditional | flops 1024 | bytes 9438368 | solution.py:1189
  398.8 4.2 share.13
  403.1 6.1 %collective-permute-done.8 = bf16[192,2048]{1,0:T(8,128)(2,1)} collective-permute-done((bf16[192,2048]{1,0:T(8,128)(2,1)S(1)}, bf16[192,2048]{1,0:T(8,128)(2,1)}, u32[]{:S(2)}, u32[]{:S(2)}) %collective-permute-start.8) | collective-permute-done | bytes 786464 | tf_op jit(solution)/shard_map/cond/branch_1_fun/ppermute | solution.py:107
  412.3 5.8 %collective-permute-done.81.refs_1_.refs_2_ = bf16[528,2048]{1,0:T(8,128)(2,1)} collective-permute-done((bf16[528,2048]{1,0:T(8,128)(2,1)}, bf16[528,2048]{1,0:T(8,128)(2,1)}, u32[]{:S(2)}, u32[]{:S(2)}) %collective-permute-start.81) | collective-permute-done | bytes 2162720 | tf_op jit(solution)/shard_map/ppermute | solution.py:161
  425.3 7.4 %collective-permute-start.82 = (bf16[448,2048]{1,0:T(8,128)(2,1)S(1)}, bf16[448,2048]{1,0:T(8,128)(2,1)S(1)}, u32[]{:S(2)}, u32[]{:S(2)}) collective-permute-start(bf16[448,2048]{1,0:T(8,128)(2,1)S(1)} %copy-done.88), channel_id=1, source_target_pairs={{0,8},{24,16},{1,9},{25,17},{2,10},{26,18},{3,11},{27,19},{4,12},{... | collective-permute-start | bytes 5505032 | tf_op jit(solution)/shard_map/ppermute | solution.py:161
  443.6 30.1 %collective-permute-done.84.refs_2_ = bf16[528,2048]{1,0:T(8,128)(2,1)S(1)} collective-permute-done((bf16[528,2048]{1,0:T(8,128)(2,1)S(1)}, bf16[528,2048]{1,0:T(8,128)(2,1)S(1)}, u32[]{:S(2)}, u32[]{:S(2)}) %collective-permute-start.84) | collective-permute-done | bytes 2162720 | tf_op jit(solution)/shard_map/ppermute | solution.py:161
  481.9 18.6 %conditional.22 = (bf16[192,2048]{1,0:T(8,128)(2,1)}, bf16[192,2048]{1,0:T(8,128)(2,1)}, bf16[192,2048]{1,0:T(8,128)(2,1)}) conditional(s32[]{:T(128)} %bitcast.2, () %tuple.456, (bf16[192,2048]{1,0:T(8,128)(2,1)S(1)}, bf16[192,2048]{1,0:T(8,128)(2,1)S(1)}, bf16[192,2048]{1,0:T(8,128)(2,1)S(1)}) %tuple.458), branch_computations={%region_18.19_spmd, %region_19.20_spmd} | conditional | bytes 9437328 | solution.py:1189
  484.6 15.9 %collective-permute-done.11 = bf16[192,2048]{1,0:T(8,128)(2,1)} collective-permute-done((bf16[192,2048]{1,0:T(8,128)(2,1)S(1)}, bf16[192,2048]{1,0:T(8,128)(2,1)}, u32[]{:S(2)}, u32[]{:S(2)}) %collective-permute-start.11) | collective-permute-done | bytes 786464 | tf_op jit(solution)/shard_map/cond/branch_1_fun/ppermute | solution.py:107
  510.1 16.0 %collective-permute-done.86.came = bf16[528,2048]{1,0:T(8,128)(2,1)} collective-permute-done((bf16[528,2048]{1,0:T(8,128)(2,1)}, bf16[528,2048]{1,0:T(8,128)(2,1)}, u32[]{:S(2)}, u32[]{:S(2)}) %collective-permute-start.86) | collective-permute-done | bytes 2162720 | tf_op jit(solution)/shard_map/ppermute | solution.py:161
  529.8 17.7 %conditional.23 = (bf16[192,2048]{1,0:T(8,128)(2,1)}, bf16[192,2048]{1,0:T(8,128)(2,1)}, bf16[192,2048]{1,0:T(8,128)(2,1)}, f32[512,2048]{1,0:T(8,128)}) conditional(s32[]{:T(128)} %bitcast.2, () %tuple.483, (bf16[192,2048]{1,0:T(8,128)(2,1)S(1)}, bf16[528,2048]{1,0:T(8,128)(2,1)}, s32[1]{0:T(128)}, bf16[528,2048]{1,0:T(8,128)(2,1)}) %tuple.485), branch_computations={%region_20.21_spmd, %region_21.22_spmd} | conditional | flops 1024 | bytes 9438360 | solution.py:1189
  536.5 11.0 %collective-permute-done.14 = bf16[192,2048]{1,0:T(8,128)(2,1)} collective-permute-done((bf16[192,2048]{1,0:T(8,128)(2,1)S(1)}, bf16[192,2048]{1,0:T(8,128)(2,1)}, u32[]{:S(2)}, u32[]{:S(2)}) %collective-permute-start.14) | collective-permute-done | bytes 786464 | tf_op jit(solution)/shard_map/cond/branch_1_fun/ppermute | solution.py:107
  547.5 12.9 %conditional.24 = (bf16[192,2048]{1,0:T(8,128)(2,1)}, bf16[192,2048]{1,0:T(8,128)(2,1)}, bf16[192,2048]{1,0:T(8,128)(2,1)}, f32[2048,1024]{1,0:T(8,128)}, f32[2048,256]{1,0:T(8,128)}, /*index=5*/f32[2048,256]{1,0:T(8,128)}) conditional(s32[]{:T(128)} %bitcast.2, () %tuple.482, (bf16[192,2048]{1,0:T(8,128)(2,1)}, bf16[192,2048]{1,0:T(8,128)(2,1)}, ...), branch_computations={%region_22.23_spmd, %region_23.24_spmd} | conditional | flops 1024 | bytes 14942274 | solution.py:1189
  551.3 6.2 %unpack.2 = (f32[2048,1024]{1,0:T(8,128)}, f32[2048,256]{1,0:T(8,128)}, f32[2048,256]{1,0:T(8,128)}) custom-call(s32[8]{0:T(128)S(1)} %get-tuple-element.209.table, bf16[192,2048]{1,0:T(8,128)(2,1)S(1)} %get-tuple-element.210.refs_0_, bf16[192,2048]{1,0:T(8,128)(2,1)} %get-tuple-element.211.refs_1_, bf16[192,2048]{1,0:T(8,128)(2,1)} %get-tuple-element.207.refs_2_, ...), custom_call_target="tpu_custom_call" | custom-call | flops 1024 | bytes 1024 | tf_op jit(solution)/shard_map/cond/branch_1_fun/unpack/pallas_call | solution.py:1122
  (427 shorter events, 251.2 us)
Async XLA Ops:
  0.6 39.5 %collective-permute-start.27 = (bf16[192,2048]{1,0:T(8,128)(2,1)}, bf16[192,2048]{1,0:T(8,128)(2,1)S(1)}, u32[]{:S(2)}, u32[]{:S(2)}) collective-permute-start(bf16[192,2048]{1,0:T(8,128)(2,1)} %bitcast.26), channel_id=1, source_target_pairs={{0,2},{1,5},{2,0},{3,7},{4,6},{5,1},{6,4},{7,3},{8,10},{9,13},{10,... | collective-permute-start | bytes 2359304 | tf_op jit(solution)/shard_map/ppermute | solution.py:107
  12.2 15.3 %collective-permute-start.21 = (bf16[192,1536]{1,0:T(8,128)(2,1)}, bf16[192,1536]{1,0:T(8,128)(2,1)}, u32[]{:S(2)}, u32[]{:S(2)}) collective-permute-start(bf16[192,1536]{1,0:T(8,128)(2,1)} %get-tuple-element.101), channel_id=1, source_target_pairs={{0,2},{1,5},{2,0},{3,7},{4,6},{5,1},{6,4},{7,3},{8,10},{9,13},{10,... | collective-permute-start | bytes 1769480 | tf_op jit(solution)/shard_map/cond/branch_1_fun/ppermute | solution.py:107
  12.3 15.2 %collective-permute-start.22 = (bf16[192,1536]{1,0:T(8,128)(2,1)}, bf16[192,1536]{1,0:T(8,128)(2,1)}, u32[]{:S(2)}, u32[]{:S(2)}) collective-permute-start(bf16[192,1536]{1,0:T(8,128)(2,1)} %get-tuple-element.101), channel_id=1, source_target_pairs={{0,4},{1,3},{2,6},{3,1},{4,0},{5,7},{6,2},{7,5},{8,12},{9,11},{10,... | collective-permute-start | bytes 1769480 | tf_op jit(solution)/shard_map/cond/branch_1_fun/ppermute | solution.py:107
  14.3 13.2 %collective-permute-start.23 = (bf16[192,1536]{1,0:T(8,128)(2,1)}, bf16[192,1536]{1,0:T(8,128)(2,1)}, u32[]{:S(2)}, u32[]{:S(2)}) collective-permute-start(bf16[192,1536]{1,0:T(8,128)(2,1)} %get-tuple-element.101), channel_id=1, source_target_pairs={{0,1},{1,0},{2,3},{3,2},{4,5},{5,4},{6,7},{7,6},{8,9},{9,8},{10,11... | collective-permute-start | bytes 1769480 | tf_op jit(solution)/shard_map/cond/branch_1_fun/ppermute | solution.py:107
  40.2 23.9 %collective-permute-start.28 = (bf16[192,2048]{1,0:T(8,128)(2,1)S(1)}, bf16[192,2048]{1,0:T(8,128)(2,1)}, u32[]{:S(2)}, u32[]{:S(2)}) collective-permute-start(bf16[192,2048]{1,0:T(8,128)(2,1)S(1)} %bitcast.27), channel_id=1, source_target_pairs={{0,4},{1,3},{2,6},{3,1},{4,0},{5,7},{6,2},{7,5},{8,12},{9,11},{10,... | collective-permute-start | bytes 2359304 | tf_op jit(solution)/shard_map/ppermute | solution.py:107
  41.9 22.1 %collective-permute-start.29 = (bf16[192,2048]{1,0:T(8,128)(2,1)S(1)}, bf16[192,2048]{1,0:T(8,128)(2,1)}, u32[]{:S(2)}, u32[]{:S(2)}) collective-permute-start(bf16[192,2048]{1,0:T(8,128)(2,1)S(1)} %collective-permute-done.27.refs_2_), channel_id=1, source_target_pairs={{0,4},{1,3},{2,6},{3,1},{4,0},{5,7},{6,2},{7,5},{8,12},{9,11},{10,... | collective-permute-start | bytes 2359304 | tf_op jit(solution)/shard_map/ppermute | solution.py:107
  42.3 21.8 %collective-permute-start.30 = (bf16[192,2048]{1,0:T(8,128)(2,1)S(1)}, bf16[192,2048]{1,0:T(8,128)(2,1)}, u32[]{:S(2)}, u32[]{:S(2)}) collective-permute-start(bf16[192,2048]{1,0:T(8,128)(2,1)S(1)} %bitcast.28), channel_id=1, source_target_pairs={{0,1},{1,0},{2,3},{3,2},{4,5},{5,4},{6,7},{7,6},{8,9},{9,8},{10,11... | collective-permute-start | bytes 2359304 | tf_op jit(solution)/shard_map/ppermute | solution.py:107
  42.3 21.8 %collective-permute-start.31 = (bf16[192,2048]{1,0:T(8,128)(2,1)S(1)}, bf16[192,2048]{1,0:T(8,128)(2,1)}, u32[]{:S(2)}, u32[]{:S(2)}) collective-permute-start(bf16[192,2048]{1,0:T(8,128)(2,1)S(1)} %collective-permute-done.27.refs_2_), channel_id=1, source_target_pairs={{0,1},{1,0},{2,3},{3,2},{4,5},{5,4},{6,7},{7,6},{8,9},{9,8},{10,11... | collective-permute-start | bytes 2359304 | tf_op jit(solution)/shard_map/ppermute | solution.py:107
  77.2 20.0 %collective-permute-start.35 = (bf16[192,2048]{1,0:T(8,128)(2,1)S(1)}, bf16[192,2048]{1,0:T(8,128)(2,1)S(1)}, u32[]{:S(2)}, u32[]{:S(2)}) collective-permute-start(bf16[192,2048]{1,0:T(8,128)(2,1)S(1)} %add_rows.26), channel_id=1, source_target_pairs={{0,2},{1,5},{2,0},{3,7},{4,6},{5,1},{6,4},{7,3},{8,10},{9,13},{10,... | collective-permute-start | bytes 2359304 | tf_op jit(solution)/shard_map/ppermute | solution.py:107
  78.6 18.6 %collective-permute-start.36 = (bf16[192,2048]{1,0:T(8,128)(2,1)S(1)}, bf16[192,2048]{1,0:T(8,128)(2,1)S(1)}, u32[]{:S(2)}, u32[]{:S(2)}) collective-permute-start(bf16[192,2048]{1,0:T(8,128)(2,1)S(1)} %add_rows.27), channel_id=1, source_target_pairs={{0,4},{1,3},{2,6},{3,1},{4,0},{5,7},{6,2},{7,5},{8,12},{9,11},{10,... | collective-permute-start | bytes 2359304 | tf_op jit(solution)/shard_map/ppermute | solution.py:107
  80.4 16.8 %collective-permute-start.37 = (bf16[192,2048]{1,0:T(8,128)(2,1)S(1)}, bf16[192,2048]{1,0:T(8,128)(2,1)S(1)}, u32[]{:S(2)}, u32[]{:S(2)}) collective-permute-start(bf16[192,2048]{1,0:T(8,128)(2,1)S(1)} %copy-done.94), channel_id=1, source_target_pairs={{0,1},{1,0},{2,3},{3,2},{4,5},{5,4},{6,7},{7,6},{8,9},{9,8},{10,11... | collective-permute-start | bytes 2359304 | tf_op jit(solution)/shard_map/ppermute | solution.py:107
  100.0 20.1 %collective-permute-start.40 = (bf16[192,2048]{1,0:T(8,128)(2,1)S(1)}, bf16[192,2048]{1,0:T(8,128)(2,1)S(1)}, u32[]{:S(2)}, u32[]{:S(2)}) collective-permute-start(bf16[192,2048]{1,0:T(8,128)(2,1)S(1)} %get-tuple-element.724.refs_0_), channel_id=1, source_target_pairs={{0,2},{1,5},{2,0},{3,7},{4,6},{5,1},{6,4},{7,3},{8,10},{9,13},{10,... | collective-permute-start | bytes 2359304 | tf_op jit(solution)/shard_map/ppermute | solution.py:107
  101.4 18.7 %collective-permute-start.41 = (bf16[192,2048]{1,0:T(8,128)(2,1)S(1)}, bf16[192,2048]{1,0:T(8,128)(2,1)S(1)}, u32[]{:S(2)}, u32[]{:S(2)}) collective-permute-start(bf16[192,2048]{1,0:T(8,128)(2,1)S(1)} %get-tuple-element.724.refs_0_), channel_id=1, source_target_pairs={{0,4},{1,3},{2,6},{3,1},{4,0},{5,7},{6,2},{7,5},{8,12},{9,11},{10,... | collective-permute-start | bytes 2359304 | tf_op jit(solution)/shard_map/ppermute | solution.py:107
  148.4 50.6 %collective-permute-start.53 = (bf16[528,2048]{1,0:T(8,128)(2,1)}, bf16[528,2048]{1,0:T(8,128)(2,1)}, u32[]{:S(2)}, u32[]{:S(2)}) collective-permute-start(bf16[528,2048]{1,0:T(8,128)(2,1)} %get-tuple-element.768.refs_0_), channel_id=1, source_target_pairs={{0,8},{24,16},{1,9},{25,17},{2,10},{26,18},{3,11},{27,19},{4,12},{... | collective-permute-start | bytes 6488072 | tf_op jit(solution)/shard_map/ppermute | solution.py:161
  178.0 34.5 %collective-permute-start.50 = (bf16[192,2048]{1,0:T(8,128)(2,1)S(1)}, bf16[192,2048]{1,0:T(8,128)(2,1)S(1)}, u32[]{:S(2)}, u32[]{:S(2)}) collective-permute-start(bf16[192,2048]{1,0:T(8,128)(2,1)S(1)} %add_rows.29), channel_id=1, source_target_pairs={{0,2},{1,5},{2,0},{3,7},{4,6},{5,1},{6,4},{7,3},{8,10},{9,13},{10,... | collective-permute-start | bytes 2359304 | tf_op jit(solution)/shard_map/ppermute | solution.py:107
  179.6 32.9 %collective-permute-start.51 = (bf16[192,2048]{1,0:T(8,128)(2,1)S(1)}, bf16[192,2048]{1,0:T(8,128)(2,1)S(1)}, u32[]{:S(2)}, u32[]{:S(2)}) collective-permute-start(bf16[192,2048]{1,0:T(8,128)(2,1)S(1)} %add_rows.30), channel_id=1, source_target_pairs={{0,4},{1,3},{2,6},{3,1},{4,0},{5,7},{6,2},{7,5},{8,12},{9,11},{10,... | collective-permute-start | bytes 2359304 | tf_op jit(solution)/shard_map/ppermute | solution.py:107
  180.7 31.8 %collective-permute-start.52 = (bf16[192,2048]{1,0:T(8,128)(2,1)S(1)}, bf16[192,2048]{1,0:T(8,128)(2,1)S(1)}, u32[]{:S(2)}, u32[]{:S(2)}) collective-permute-start(bf16[192,2048]{1,0:T(8,128)(2,1)S(1)} %get-tuple-element.802), channel_id=1, source_target_pairs={{0,1},{1,0},{2,3},{3,2},{4,5},{5,4},{6,7},{7,6},{8,9},{9,8},{10,11... | collective-permute-start | bytes 2359304 | tf_op jit(solution)/shard_map/ppermute | solution.py:107
  203.1 51.4 %collective-permute-start.61 = (bf16[528,2048]{1,0:T(8,128)(2,1)}, bf16[528,2048]{1,0:T(8,128)(2,1)}, u32[]{:S(2)}, u32[]{:S(2)}) collective-permute-start(bf16[528,2048]{1,0:T(8,128)(2,1)} %add_rows.31.own), channel_id=1, source_target_pairs={{8,16},{16,8},{9,17},{17,9},{10,18},{18,10},{11,19},{19,11},{12,20... | collective-permute-start | bytes 6488072 | tf_op jit(solution)/shard_map/ppermute | solution.py:161
  205.3 53.8 %collective-permute-start.60 = (bf16[528,2048]{1,0:T(8,128)(2,1)}, bf16[528,2048]{1,0:T(8,128)(2,1)}, u32[]{:S(2)}, u32[]{:S(2)}) collective-permute-start(bf16[528,2048]{1,0:T(8,128)(2,1)} %get-tuple-element.808.refs_0_), channel_id=1, source_target_pairs={{0,8},{24,16},{1,9},{25,17},{2,10},{26,18},{3,11},{27,19},{4,12},{... | collective-permute-start | bytes 6488072 | tf_op jit(solution)/shard_map/ppermute | solution.py:161
  215.5 20.2 %collective-permute-start.55 = (bf16[192,2048]{1,0:T(8,128)(2,1)S(1)}, bf16[192,2048]{1,0:T(8,128)(2,1)}, u32[]{:S(2)}, u32[]{:S(2)}) collective-permute-start(bf16[192,2048]{1,0:T(8,128)(2,1)S(1)} %get-tuple-element.824.refs_0_), channel_id=1, source_target_pairs={{0,2},{1,5},{2,0},{3,7},{4,6},{5,1},{6,4},{7,3},{8,10},{9,13},{10,... | collective-permute-start | bytes 2359304 | tf_op jit(solution)/shard_map/ppermute | solution.py:107
  217.2 18.6 %collective-permute-start.56 = (bf16[192,2048]{1,0:T(8,128)(2,1)S(1)}, bf16[192,2048]{1,0:T(8,128)(2,1)}, u32[]{:S(2)}, u32[]{:S(2)}) collective-permute-start(bf16[192,2048]{1,0:T(8,128)(2,1)S(1)} %get-tuple-element.824.refs_0_), channel_id=1, source_target_pairs={{0,4},{1,3},{2,6},{3,1},{4,0},{5,7},{6,2},{7,5},{8,12},{9,11},{10,... | collective-permute-start | bytes 2359304 | tf_op jit(solution)/shard_map/ppermute | solution.py:107
  236.3 12.3 %collective-permute-start.59 = (bf16[192,2048]{1,0:T(8,128)(2,1)}, bf16[192,2048]{1,0:T(8,128)(2,1)}, u32[]{:S(2)}, u32[]{:S(2)}) collective-permute-start(bf16[192,2048]{1,0:T(8,128)(2,1)} %collective-permute-done.55.refs_0_.refs_2_), channel_id=1, source_target_pairs={{0,4},{1,3},{2,6},{3,1},{4,0},{5,7},{6,2},{7,5},{8,12},{9,11},{10,... | collective-permute-start | bytes 2359304 | tf_op jit(solution)/shard_map/ppermute | solution.py:107
  257.0 54.0 %collective-permute-start.70 = (bf16[528,2048]{1,0:T(8,128)(2,1)S(1)}, bf16[528,2048]{1,0:T(8,128)(2,1)S(1)}, u32[]{:S(2)}, u32[]{:S(2)}) collective-permute-start(bf16[528,2048]{1,0:T(8,128)(2,1)S(1)} %add_or_begin.3.refs_1_), channel_id=1, source_target_pairs={{0,8},{24,16},{8,0},{16,24},{1,9},{25,17},{9,1},{17,25},{2,10},{26... | collective-permute-start | bytes 6488072 | tf_op jit(solution)/shard_map/ppermute | solution.py:161
  263.3 48.1 %collective-permute-start.69 = (bf16[528,2048]{1,0:T(8,128)(2,1)}, bf16[528,2048]{1,0:T(8,128)(2,1)}, u32[]{:S(2)}, u32[]{:S(2)}) collective-permute-start(bf16[528,2048]{1,0:T(8,128)(2,1)} %add_rows.32.own), channel_id=1, source_target_pairs={{8,16},{16,8},{9,17},{17,9},{10,18},{18,10},{11,19},{19,11},{12,20... | collective-permute-start | bytes 6488072 | tf_op jit(solution)/shard_map/ppermute | solution.py:161
  291.5 16.2 %collective-permute-start.66 = (bf16[192,1536]{1,0:T(8,128)(2,1)S(1)}, bf16[192,1536]{1,0:T(8,128)(2,1)S(1)}, u32[]{:S(2)}, u32[]{:S(2)}) collective-permute-start(bf16[192,1536]{1,0:T(8,128)(2,1)S(1)} %add_rows.34), channel_id=1, source_target_pairs={{0,2},{1,5},{2,0},{3,7},{4,6},{5,1},{6,4},{7,3},{8,10},{9,13},{10,... | collective-permute-start | bytes 1769480 | tf_op jit(solution)/shard_map/ppermute | solution.py:107
  293.2 14.5 %collective-permute-start.67 = (bf16[192,1536]{1,0:T(8,128)(2,1)S(1)}, bf16[192,1536]{1,0:T(8,128)(2,1)S(1)}, u32[]{:S(2)}, u32[]{:S(2)}) collective-permute-start(bf16[192,1536]{1,0:T(8,128)(2,1)S(1)} %add_rows.35), channel_id=1, source_target_pairs={{0,4},{1,3},{2,6},{3,1},{4,0},{5,7},{6,2},{7,5},{8,12},{9,11},{10,... | collective-permute-start | bytes 1769480 | tf_op jit(solution)/shard_map/ppermute | solution.py:107
  294.5 13.3 %collective-permute-start.68 = (bf16[192,1536]{1,0:T(8,128)(2,1)S(1)}, bf16[192,1536]{1,0:T(8,128)(2,1)S(1)}, u32[]{:S(2)}, u32[]{:S(2)}) collective-permute-start(bf16[192,1536]{1,0:T(8,128)(2,1)S(1)} %get-tuple-element.890), channel_id=1, source_target_pairs={{0,1},{1,0},{2,3},{3,2},{4,5},{5,4},{6,7},{7,6},{8,9},{9,8},{10,11... | collective-permute-start | bytes 1769480 | tf_op jit(solution)/shard_map/ppermute | solution.py:107
  314.1 39.5 %collective-permute-start.76 = (bf16[528,2048]{1,0:T(8,128)(2,1)S(1)}, bf16[528,2048]{1,0:T(8,128)(2,1)S(1)}, u32[]{:S(2)}, u32[]{:S(2)}) collective-permute-start(bf16[528,2048]{1,0:T(8,128)(2,1)S(1)} %add_rows.36.own), channel_id=1, source_target_pairs={{8,16},{16,8},{9,17},{17,9},{10,18},{18,10},{11,19},{19,11},{12,20... | collective-permute-start | bytes 6488072 | tf_op jit(solution)/shard_map/ppermute | solution.py:161
  314.9 56.0 %collective-permute-start.75 = (bf16[528,2048]{1,0:T(8,128)(2,1)S(1)}, bf16[528,2048]{1,0:T(8,128)(2,1)S(1)}, u32[]{:S(2)}, u32[]{:S(2)}) collective-permute-start(bf16[528,2048]{1,0:T(8,128)(2,1)S(1)} %add_or_begin.4.refs_1_), channel_id=1, source_target_pairs={{0,8},{24,16},{8,0},{16,24},{1,9},{25,17},{9,1},{17,25},{2,10},{26... | collective-permute-start | bytes 6488072 | tf_op jit(solution)/shard_map/ppermute | solution.py:161
  333.5 19.6 %collective-permute-start.77 = (bf16[256,1536]{1,0:T(8,128)(2,1)S(1)}, bf16[256,1536]{1,0:T(8,128)(2,1)S(1)}, u32[]{:S(2)}, u32[]{:S(2)}) collective-permute-start(bf16[256,1536]{1,0:T(8,128)(2,1)S(1)} %add_rows.38), channel_id=1, source_target_pairs={{0,2},{1,5},{2,0},{3,7},{4,6},{5,1},{6,4},{7,3},{8,10},{9,13},{10,... | collective-permute-start | bytes 2359304 | tf_op jit(solution)/shard_map/ppermute | solution.py:107
  335.1 18.0 %collective-permute-start.78 = (bf16[256,1536]{1,0:T(8,128)(2,1)S(1)}, bf16[256,1536]{1,0:T(8,128)(2,1)S(1)}, u32[]{:S(2)}, u32[]{:S(2)}) collective-permute-start(bf16[256,1536]{1,0:T(8,128)(2,1)S(1)} %add_rows.39), channel_id=1, source_target_pairs={{0,4},{1,3},{2,6},{3,1},{4,0},{5,7},{6,2},{7,5},{8,12},{9,11},{10,... | collective-permute-start | bytes 2359304 | tf_op jit(solution)/shard_map/ppermute | solution.py:107
  336.3 16.8 %collective-permute-start.79 = (bf16[256,1536]{1,0:T(8,128)(2,1)S(1)}, bf16[256,1536]{1,0:T(8,128)(2,1)S(1)}, u32[]{:S(2)}, u32[]{:S(2)}) collective-permute-start(bf16[256,1536]{1,0:T(8,128)(2,1)S(1)} %get-tuple-element.957), channel_id=1, source_target_pairs={{0,1},{1,0},{2,3},{3,2},{4,5},{5,4},{6,7},{7,6},{8,9},{9,8},{10,11... | collective-permute-start | bytes 2359304 | tf_op jit(solution)/shard_map/ppermute | solution.py:107
  355.8 62.4 %collective-permute-start.81 = (bf16[528,2048]{1,0:T(8,128)(2,1)}, bf16[528,2048]{1,0:T(8,128)(2,1)}, u32[]{:S(2)}, u32[]{:S(2)}) collective-permute-start(bf16[528,2048]{1,0:T(8,128)(2,1)} %add_or_begin.5.refs_1_), channel_id=1, source_target_pairs={{0,8},{24,16},{8,0},{16,24},{1,9},{25,17},{9,1},{17,25},{2,10},{26... | collective-permute-start | bytes 6488072 | tf_op jit(solution)/shard_map/ppermute | solution.py:161
  372.8 47.5 %collective-permute-start.80 = (bf16[528,2048]{1,0:T(8,128)(2,1)}, bf16[528,2048]{1,0:T(8,128)(2,1)}, u32[]{:S(2)}, u32[]{:S(2)}) collective-permute-start(bf16[528,2048]{1,0:T(8,128)(2,1)} %add_rows.40.refs_0_), channel_id=1, source_target_pairs={{8,16},{16,8},{9,17},{17,9},{10,18},{18,10},{11,19},{19,11},{12,20... | collective-permute-start | bytes 6488072 | tf_op jit(solution)/shard_map/ppermute | solution.py:161
  397.1 12.1 %collective-permute-start.8 = (bf16[192,2048]{1,0:T(8,128)(2,1)S(1)}, bf16[192,2048]{1,0:T(8,128)(2,1)}, u32[]{:S(2)}, u32[]{:S(2)}) collective-permute-start(bf16[192,2048]{1,0:T(8,128)(2,1)S(1)} %get-tuple-element.173), channel_id=1, source_target_pairs={{0,4},{1,3},{2,6},{3,1},{4,0},{5,7},{6,2},{7,5},{8,12},{9,11},{10,... | collective-permute-start | bytes 2359304 | tf_op jit(solution)/shard_map/cond/branch_1_fun/ppermute | solution.py:107
  423.2 50.5 %collective-permute-start.84 = (bf16[528,2048]{1,0:T(8,128)(2,1)S(1)}, bf16[528,2048]{1,0:T(8,128)(2,1)S(1)}, u32[]{:S(2)}, u32[]{:S(2)}) collective-permute-start(bf16[528,2048]{1,0:T(8,128)(2,1)S(1)} %add_rows.45.refs_1_), channel_id=1, source_target_pairs={{8,0},{16,24},{9,1},{17,25},{10,2},{18,26},{11,3},{19,27},{12,4},{... | collective-permute-start | bytes 6488072 | tf_op jit(solution)/shard_map/ppermute | solution.py:161
  424.5 50.5 %collective-permute-start.83 = (bf16[528,2048]{1,0:T(8,128)(2,1)S(1)}, bf16[528,2048]{1,0:T(8,128)(2,1)S(1)}, u32[]{:S(2)}, u32[]{:S(2)}) collective-permute-start(bf16[528,2048]{1,0:T(8,128)(2,1)S(1)} %add_rows.44.refs_0_), channel_id=1, source_target_pairs={{8,16},{16,8},{9,17},{17,9},{10,18},{18,10},{11,19},{19,11},{12,20... | collective-permute-start | bytes 6488072 | tf_op jit(solution)/shard_map/ppermute | solution.py:161
  425.3 52.8 %collective-permute-start.82 = (bf16[448,2048]{1,0:T(8,128)(2,1)S(1)}, bf16[448,2048]{1,0:T(8,128)(2,1)S(1)}, u32[]{:S(2)}, u32[]{:S(2)}) collective-permute-start(bf16[448,2048]{1,0:T(8,128)(2,1)S(1)} %copy-done.88), channel_id=1, source_target_pairs={{0,8},{24,16},{1,9},{25,17},{2,10},{26,18},{3,11},{27,19},{4,12},{... | collective-permute-start | bytes 5505032 | tf_op jit(solution)/shard_map/ppermute | solution.py:161
  476.9 49.3 %collective-permute-start.86 = (bf16[528,2048]{1,0:T(8,128)(2,1)}, bf16[528,2048]{1,0:T(8,128)(2,1)}, u32[]{:S(2)}, u32[]{:S(2)}) collective-permute-start(bf16[528,2048]{1,0:T(8,128)(2,1)} %add_rows.46.own), channel_id=1, source_target_pairs={{8,0},{16,24},{9,1},{17,25},{10,2},{18,26},{11,3},{19,27},{12,4},{... | collective-permute-start | bytes 6488072 | tf_op jit(solution)/shard_map/ppermute | solution.py:161
  479.8 27.9 %collective-permute-start.85 = (bf16[448,2048]{1,0:T(8,128)(2,1)}, bf16[448,2048]{1,0:T(8,128)(2,1)}, u32[]{:S(2)}, u32[]{:S(2)}) collective-permute-start(bf16[448,2048]{1,0:T(8,128)(2,1)} %add_rows.47.refs_0_), channel_id=1, source_target_pairs={{8,16},{16,8},{9,17},{17,9},{10,18},{18,10},{11,19},{19,11},{12,20... | collective-permute-start | bytes 5505032 | tf_op jit(solution)/shard_map/ppermute | solution.py:161
  481.9 18.6 %collective-permute-start.11 = (bf16[192,2048]{1,0:T(8,128)(2,1)S(1)}, bf16[192,2048]{1,0:T(8,128)(2,1)}, u32[]{:S(2)}, u32[]{:S(2)}) collective-permute-start(bf16[192,2048]{1,0:T(8,128)(2,1)S(1)} %get-tuple-element.186), channel_id=1, source_target_pairs={{0,2},{1,5},{2,0},{3,7},{4,6},{5,1},{6,4},{7,3},{8,10},{9,13},{10,... | collective-permute-start | bytes 2359304 | tf_op jit(solution)/shard_map/cond/branch_1_fun/ppermute | solution.py:107
  483.5 17.0 %collective-permute-start.12 = (bf16[192,2048]{1,0:T(8,128)(2,1)S(1)}, bf16[192,2048]{1,0:T(8,128)(2,1)}, u32[]{:S(2)}, u32[]{:S(2)}) collective-permute-start(bf16[192,2048]{1,0:T(8,128)(2,1)S(1)} %get-tuple-element.187), channel_id=1, source_target_pairs={{0,4},{1,3},{2,6},{3,1},{4,0},{5,7},{6,2},{7,5},{8,12},{9,11},{10,... | collective-permute-start | bytes 2359304 | tf_op jit(solution)/shard_map/cond/branch_1_fun/ppermute | solution.py:107
  484.5 16.0 %collective-permute-start.13 = (bf16[192,2048]{1,0:T(8,128)(2,1)S(1)}, bf16[192,2048]{1,0:T(8,128)(2,1)}, u32[]{:S(2)}, u32[]{:S(2)}) collective-permute-start(bf16[192,2048]{1,0:T(8,128)(2,1)S(1)} %get-tuple-element.188), channel_id=1, source_target_pairs={{0,1},{1,0},{2,3},{3,2},{4,5},{5,4},{6,7},{7,6},{8,9},{9,8},{10,11... | collective-permute-start | bytes 2359304 | tf_op jit(solution)/shard_map/cond/branch_1_fun/ppermute | solution.py:107
  526.2 41.2 %collective-permute-start.87 = (bf16[448,2048]{1,0:T(8,128)(2,1)S(1)}, bf16[448,2048]{1,0:T(8,128)(2,1)}, u32[]{:S(2)}, u32[]{:S(2)}) collective-permute-start(bf16[448,2048]{1,0:T(8,128)(2,1)S(1)} %add_rows.49.own), channel_id=1, source_target_pairs={{8,0},{16,24},{9,1},{17,25},{10,2},{18,26},{11,3},{19,27},{12,4},{... | collective-permute-start | bytes 5505032 | tf_op jit(solution)/shard_map/ppermute | solution.py:161
  529.8 17.7 %collective-permute-start.14 = (bf16[192,2048]{1,0:T(8,128)(2,1)S(1)}, bf16[192,2048]{1,0:T(8,128)(2,1)}, u32[]{:S(2)}, u32[]{:S(2)}) collective-permute-start(bf16[192,2048]{1,0:T(8,128)(2,1)S(1)} %get-tuple-element.195), channel_id=1, source_target_pairs={{0,2},{1,5},{2,0},{3,7},{4,6},{5,1},{6,4},{7,3},{8,10},{9,13},{10,... | collective-permute-start | bytes 2359304 | tf_op jit(solution)/shard_map/cond/branch_1_fun/ppermute | solution.py:107
  531.4 16.1 %collective-permute-start.15 = (bf16[192,2048]{1,0:T(8,128)(2,1)S(1)}, bf16[192,2048]{1,0:T(8,128)(2,1)}, u32[]{:S(2)}, u32[]{:S(2)}) collective-permute-start(bf16[192,2048]{1,0:T(8,128)(2,1)S(1)} %get-tuple-element.195), channel_id=1, source_target_pairs={{0,4},{1,3},{2,6},{3,1},{4,0},{5,7},{6,2},{7,5},{8,12},{9,11},{10,... | collective-permute-start | bytes 2359304 | tf_op jit(solution)/shard_map/cond/branch_1_fun/ppermute | solution.py:107
  532.5 15.0 %collective-permute-start.16 = (bf16[192,2048]{1,0:T(8,128)(2,1)S(1)}, bf16[192,2048]{1,0:T(8,128)(2,1)}, u32[]{:S(2)}, u32[]{:S(2)}) collective-permute-start(bf16[192,2048]{1,0:T(8,128)(2,1)S(1)} %get-tuple-element.195), channel_id=1, source_target_pairs={{0,1},{1,0},{2,3},{3,2},{4,5},{5,4},{6,7},{7,6},{8,9},{9,8},{10,11... | collective-permute-start | bytes 2359304 | tf_op jit(solution)/shard_map/cond/branch_1_fun/ppermute | solution.py:107
  548.1 12.3 %collective-permute-start.17 = (bf16[192,2048]{1,0:T(8,128)(2,1)}, bf16[192,2048]{1,0:T(8,128)(2,1)}, u32[]{:S(2)}, u32[]{:S(2)}) collective-permute-start(bf16[192,2048]{1,0:T(8,128)(2,1)} %get-tuple-element.207.refs_2_), channel_id=1, source_target_pairs={{0,4},{1,3},{2,6},{3,1},{4,0},{5,7},{6,2},{7,5},{8,12},{9,11},{10,... | collective-permute-start | bytes 2359304 | tf_op jit(solution)/shard_map/cond/branch_1_fun/ppermute | solution.py:107
  (136 other events, 1361.7 us)

commit v6 on v5

--- a/solution.py
+++ b/solution.py
@@ -562,7 +562,7 @@
         gate = right_transposed(here, gate_weight[...])
         upward = right_transposed(here, up_weight[...])
         loads[p].wait()
-        hidden_grad = held[p]
+        hidden_grad = held[p].astype(f32)
         sigmoid = jax.nn.sigmoid(gate)
         swish = gate * sigmoid
         results = (
@@ -596,7 +596,7 @@
         out_shape=[jax.ShapeDtypeStruct((count * rows, units), bf16)] * 3,
         in_specs=specs,
         out_specs=[any_space()] * 3,
-        scratch_shapes=[pltpu.VMEM((pairs, 2 * rows, units), f32)]
+        scratch_shapes=[pltpu.VMEM((pairs, 2 * rows, units), bf16)]
         + [pltpu.VMEM((pairs, 2 * rows, units), bf16)] * 3
         + [pltpu.SemaphoreType.DMA((4, pairs))],
         input_output_aliases=aliases,
@@ -1283,7 +1283,7 @@
         parts = [plane.scatter(share(clock, 0, group))]
         middle, normed_mid_rows = middle_rows(x, feed_gain, parts)
         cot_pieces = plane.gather(cotangent_rows)
-        hidden_grad = rows_product(cot_pieces, down_weight, f32)
+        hidden_grad = rows_product(cot_pieces, down_weight, bf16)
         mid_pieces = plane.gather(normed_mid_rows)
         hidden, gate_grad, upward_grad = feed(
             mid_pieces, 0, group, hidden_grad, gate_rows, up_rows, group, None
@@ -1353,7 +1353,7 @@
         def beside_last(clock, a_in, b_in, own_came, cot_bo, cot_co):
             cot_bo, cot_co = clock(cot_bo, cot_co)
             cot_pieces = [cotangent_rows, cot_o, cot_a, cot_ao, cot_b, cot_bo, cot_c, cot_co]
-            hidden_grad = clock(rows_product(cot_pieces, down_weight, f32))
+            hidden_grad = clock(rows_product(cot_pieces, down_weight, bf16))
             return [hidden_grad]
 
         (a_in, b_in, own_came, cot_bo, cot_co), (hidden_grad,) = hops(

time: 579 us -> 578 us (level)
    unnamed x193 -> x189, local copies, waits for them, and re-layouts: 13.7 us -> 14.1 us
where the time goes in v6:
time: 578 us; the launch traced here: 572 us
  Pallas kernels  219 us (38%)
  waiting for transfers between devices  219 us (38%)
  starting transfers between devices  108 us (19%)
  local copies, waits for them, and re-layouts  16.8 us (3%)
  other arithmetic  6.39 us (1%)
    ppermute x73, waiting for transfers between devices, move(): return lax.ppermute(value, 'head', hop)  155 us
    ppermute x15, waiting for transfers between devices, move(): return lax.ppermute(value, 'tok', pairs)  64.6 us
    pallas_call x36, Pallas kernels, call(): pl.pallas_call(kernel, out_shape=shapes, in_specs=[smem()] * scalars + [v...  58.4 us
    ppermute x15, starting transfers between devices, move(): return lax.ppermute(value, 'tok', pairs)  57.2 us
    ppermute x73, starting transfers between devices, move(): return lax.ppermute(value, 'head', hop)  50.4 us
    pallas_call x9, Pallas kernels, share(): pl.pallas_call(functools.partial(share_kernel, low, size, terms), out_sha...  35 us
    pallas_call x5, Pallas kernels, weight_product(): pl.pallas_call(functools.partial(product_kernel, count, len(operands) - 1...  31.3 us
    pallas_call x7, Pallas kernels, settle(): pl.pallas_call(functools.partial(settle_kernel, low, at), out_shape=shape...  19.4 us
  transfers between devices with their start and end apart: 88, of which 35 were waited for; matrix products, arithmetic and copies ran while one was open for 1% of the time, Pallas kernels for 34%

profile of v6, /device:TPU:0, one launch (start us, length us, event | category | flops | bytes accessed | tf_op | source)
XLA Modules:
  0.0 572.2 jit_solution(7716356856451530406)
XLA Ops:
  5.5 5.5 enter.1
  12.2 15.3 %conditional.13 = (bf16[192,1536]{1,0:T(8,128)(2,1)}, bf16[192,1536]{1,0:T(8,128)(2,1)}, bf16[192,1536]{1,0:T(8,128)(2,1)}, f32[1536,128]{1,0:T(8,128)}, f32[1536,128]{1,0:T(8,128)}) conditional(s32[]{:T(128)} %bitcast.2, () %tuple.319, (bf16[192,1536]{1,0:T(8,128)(2,1)}, s32[1,1536]{1,0:T(1,128)S(1)}) %tuple.528), branch_computations={%region_0.1_spmd, %region_1.2_spmd} | conditional | flops 198400 | bytes 8682660 | solution.py:1189
  14.4 4.3 multiply_sine_fusion
  18.7 8.8 %collective-permute-done.21 = bf16[192,1536]{1,0:T(8,128)(2,1)} collective-permute-done((bf16[192,1536]{1,0:T(8,128)(2,1)}, bf16[192,1536]{1,0:T(8,128)(2,1)}, u32[]{:S(2)}, u32[]{:S(2)}) %collective-permute-start.21) | collective-permute-done | bytes 589856 | tf_op jit(solution)/shard_map/cond/branch_1_fun/ppermute | solution.py:107
  27.5 10.3 %conditional.14 = (bf16[192,1536]{1,0:T(8,128)(2,1)}, bf16[192,1536]{1,0:T(8,128)(2,1)}, bf16[192,1536]{1,0:T(8,128)(2,1)}) conditional(s32[]{:T(128)} %bitcast.2, () %tuple.318, (bf16[192,1536]{1,0:T(8,128)(2,1)}, bf16[192,1536]{1,0:T(8,128)(2,1)}) %tuple.322), branch_computations={%region_2.3_spmd, %region_3.4_spmd} | conditional | bytes 7078032 | solution.py:1189
  29.7 8.0 %collective-permute-done = bf16[192,1536]{1,0:T(8,128)(2,1)} collective-permute-done((bf16[192,1536]{1,0:T(8,128)(2,1)}, bf16[192,1536]{1,0:T(8,128)(2,1)}, u32[]{:S(2)}, u32[]{:S(2)}) %collective-permute-start) | collective-permute-done | bytes 589856 | tf_op jit(solution)/shard_map/cond/branch_1_fun/ppermute | solution.py:107
  43.2 10.9 %attend_forward.1 = (bf16[1536,1024]{1,0:T(8,128)(2,1)}, bf16[1536,512]{1,0:T(8,128)(2,1)S(1)}, bf16[1536,256]{1,0:T(8,128)(2,1)S(1)}, bf16[1536,256]{1,0:T(8,128)(2,1)S(1)}, bf16[1536,512]{1,0:T(8,128)(2,1)}) custom-call(s32[8]{0:T(128)S(1)} %stack.35.refs_0_.table, bf16[192,1536]{1,0:T(8,128)(2,1)} %get-tuple-element.659.refs_1_, ...), custom_call_target="tpu_custom_call" | custom-call | flops 1024 | bytes 1024 | tf_op jit(solution)/shard_map/attend_forward/pallas_call | solution.py:301
  56.5 5.1 conditional.16
  65.2 9.8 %collective-permute-done.32.refs_2_ = bf16[192,2048]{1,0:T(8,128)(2,1)S(1)} collective-permute-done((bf16[192,2048]{1,0:T(8,128)(2,1)S(1)}, bf16[192,2048]{1,0:T(8,128)(2,1)S(1)}, u32[]{:S(2)}, u32[]{:S(2)}) %collective-permute-start.32) | collective-permute-done | bytes 786464 | tf_op jit(solution)/shard_map/ppermute | solution.py:107
  79.3 7.1 %rows_product.4.refs_2_ = bf16[1536,704]{1,0:T(8,128)(2,1)S(1)} custom-call(bf16[192,2048]{1,0:T(8,128)(2,1)S(1)} %bitcast.29, bf16[192,2048]{1,0:T(8,128)(2,1)} %collective-permute-done.30.refs_1_, bf16[192,2048]{1,0:T(8,128)(2,1)S(1)} %collective-permute-done.27.refs_2_, bf16[192,2048]{1,0:T(8,128)(2,1)} %collective-permute-done.31.refs_3_, ...), custom_call_target="tpu_custom_call" | custom-call | flops 1024 | bytes 1024 | tf_op jit(solution)/shard_map/rows_product/pallas_call | solution.py:409
  86.4 9.7 %collective-permute-done.35.refs_3_ = bf16[192,2048]{1,0:T(8,128)(2,1)S(1)} collective-permute-done((bf16[192,2048]{1,0:T(8,128)(2,1)S(1)}, bf16[192,2048]{1,0:T(8,128)(2,1)S(1)}, u32[]{:S(2)}, u32[]{:S(2)}) %collective-permute-start.35) | collective-permute-done | bytes 786464 | tf_op jit(solution)/shard_map/ppermute | solution.py:107
  105.1 13.8 %collective-permute-done.40.refs_0_.refs_2_ = bf16[192,2048]{1,0:T(8,128)(2,1)S(1)} collective-permute-done((bf16[192,2048]{1,0:T(8,128)(2,1)S(1)}, bf16[192,2048]{1,0:T(8,128)(2,1)S(1)}, u32[]{:S(2)}, u32[]{:S(2)}) %collective-permute-start.40) | collective-permute-done | bytes 786464 | tf_op jit(solution)/shard_map/ppermute | solution.py:107
  137.7 8.6 %weight_product.5 = (bf16[528,2048]{1,0:T(8,128)(2,1)}, bf16[176,2048]{1,0:T(8,128)(2,1)S(1)}) custom-call(bf16[1536,704]{1,0:T(8,128)(2,1)S(1)} %get-tuple-element.969.left.refs_0_, bf16[192,2048]{1,0:T(8,128)(2,1)S(1)} %bitcast.30, bf16[192,2048]{1,0:T(8,128)(2,1)} %collective-permute-done.30.refs_1_, bf16[192,2048]{1,0:T(8,128)(2,1)S(1)} %copy-done.43, ...), custom_call_target="tpu_custom_call" | custom-call | flops 1024 | bytes 1024 | tf_op jit(solution)/shard_map/weight_product/pallas_call | solution.py:750
  147.2 5.0 collective-permute-start.53
  156.1 5.5 conditional.17
  156.1 5.5 share.11
  166.0 6.5 %share.16 = (bf16[192,2048]{1,0:T(8,128)(2,1)S(1)}, bf16[192,2048]{1,0:T(8,128)(2,1)S(1)}) custom-call(bf16[1536,704]{1,0:T(8,128)(2,1)S(1)} %copy-done.78, bf16[1536,704]{1,0:T(8,128)(2,1)} %copy-done.79, bf16[704,2048]{1,0:T(8,128)(2,1)} %bitcast.43, bf16[704,2048]{1,0:T(8,128)(2,1)} %bitcast.50), custom_call_target="tpu_custom_call" | custom-call | flops 1024 | bytes 1024 | tf_op jit(solution)/shard_map/share/pallas_call | solution.py:529
  179.6 6.7 %weight_product.6 = (bf16[528,2048]{1,0:T(8,128)(2,1)}, bf16[352,2048]{1,0:T(8,128)(2,1)S(1)}) custom-call(bf16[1536,704]{1,0:T(8,128)(2,1)S(1)} %copy-done.78, bf16[192,2048]{1,0:T(8,128)(2,1)S(1)} %copy-done.27, bf16[192,2048]{1,0:T(8,128)(2,1)S(1)} %copy-done.29, bf16[192,2048]{1,0:T(8,128)(2,1)S(1)} %collective-permute-done.40.refs_0_.refs_2_, ...), custom_call_target="tpu_custom_call" | custom-call | flops 1024 | bytes 1024 | tf_op jit(solution)/shard_map/weight_product/pallas_call | solution.py:750
  186.3 11.4 %collective-permute-done.53.refs_1_ = bf16[528,2048]{1,0:T(8,128)(2,1)} collective-permute-done((bf16[528,2048]{1,0:T(8,128)(2,1)}, bf16[528,2048]{1,0:T(8,128)(2,1)}, u32[]{:S(2)}, u32[]{:S(2)}) %collective-permute-start.53) | collective-permute-done | bytes 2162720 | tf_op jit(solution)/shard_map/ppermute | solution.py:161
  197.7 4.1 add_rows.31.own
  204.1 7.3 %collective-permute-start.60 = (bf16[528,2048]{1,0:T(8,128)(2,1)}, bf16[528,2048]{1,0:T(8,128)(2,1)}, u32[]{:S(2)}, u32[]{:S(2)}) collective-permute-start(bf16[528,2048]{1,0:T(8,128)(2,1)} %get-tuple-element.808.refs_0_), channel_id=1, source_target_pairs={{0,8},{24,16},{1,9},{25,17},{2,10},{26,18},{3,11},{27,19},{4,12},{... | collective-permute-start | bytes 6488072 | tf_op jit(solution)/shard_map/ppermute | solution.py:161
  219.7 6.1 %weight_product.7 = (bf16[528,2048]{1,0:T(8,128)(2,1)S(1)}, bf16[528,2048]{1,0:T(8,128)(2,1)S(1)}) custom-call(bf16[1536,704]{1,0:T(8,128)(2,1)S(1)} %copy-done.80, bf16[192,2048]{1,0:T(8,128)(2,1)S(1)} %copy-done.27, bf16[192,2048]{1,0:T(8,128)(2,1)S(1)} %copy-done.29, bf16[192,2048]{1,0:T(8,128)(2,1)S(1)} %copy-done.15, bf16[192,2048]{1,0:T(8,128)(2,1)S(1)} %copy-done.19, ...), custom_call_target="tpu_custom_call" | custom-call | flops 1024 | bytes 1024 | tf_op jit(solution)/shard_map/weight_product/pallas_call | solution.py:750
  227.2 7.5 %collective-permute-done.55.refs_0_.refs_2_ = bf16[192,2048]{1,0:T(8,128)(2,1)} collective-permute-done((bf16[192,2048]{1,0:T(8,128)(2,1)S(1)}, bf16[192,2048]{1,0:T(8,128)(2,1)}, u32[]{:S(2)}, u32[]{:S(2)}) %collective-permute-start.55) | collective-permute-done | bytes 786464 | tf_op jit(solution)/shard_map/ppermute | solution.py:107
  238.4 4.4 rows_product.6.refs_2_
  257.8 4.4 add_rows.32.own
  264.7 9.0 %attend_backward.1 = (bf16[1536,512]{1,0:T(8,128)(2,1)S(1)}, bf16[1536,512]{1,0:T(8,128)(2,1)S(1)}) custom-call(s32[8]{0:T(128)S(1)} %stack.35.refs_0_.table, bf16[384,512]{1,0:T(8,128)(2,1)S(1)} %copy-done.58, bf16[768,512]{1,0:T(8,128)(2,1)S(1)} %copy-done.46, bf16[384,512]{1,0:T(8,128)(2,1)S(1)} %rows_product.7.refs_3_, bf16[1536,512]{1,0:T(8,128)(2,1)S(1)} %copy-done.54, ...), custom_call_target="tpu_custom_call" | custom-call | flops 1024 | bytes 1024 | tf_op jit(solution)/shard_map/attend_backward/pallas_call | solution.py:374
  284.2 5.8 %collective-permute-done.63.refs_2_ = bf16[192,1536]{1,0:T(8,128)(2,1)S(1)} collective-permute-done((bf16[192,1536]{1,0:T(8,128)(2,1)S(1)}, bf16[192,1536]{1,0:T(8,128)(2,1)S(1)}, u32[]{:S(2)}, u32[]{:S(2)}) %collective-permute-start.63) | collective-permute-done | bytes 589856 | tf_op jit(solution)/shard_map/ppermute | solution.py:107
  293.3 7.8 %weight_product.8 = (bf16[336,2048]{1,0:T(8,128)(2,1)S(1)}, bf16[176,2048]{1,0:T(8,128)(2,1)}) custom-call(bf16[1536,512]{1,0:T(8,128)(2,1)} %get-tuple-element.891.refs_0_.left, bf16[192,2048]{1,0:T(8,128)(2,1)S(1)} %copy-done.48, bf16[192,2048]{1,0:T(8,128)(2,1)S(1)} %copy-done.50, bf16[192,2048]{1,0:T(8,128)(2,1)} %collective-permute-done.55.refs_0_.refs_2_, ...), custom_call_target="tpu_custom_call" | custom-call | flops 1024 | bytes 1024 | tf_op jit(solution)/shard_map/weight_product/pallas_call | solution.py:750
  301.1 5.3 collective-permute-done.66.refs_3_
  313.5 6.1 %collective-permute-start.75 = (bf16[528,2048]{1,0:T(8,128)(2,1)S(1)}, bf16[528,2048]{1,0:T(8,128)(2,1)S(1)}, u32[]{:S(2)}, u32[]{:S(2)}) collective-permute-start(bf16[528,2048]{1,0:T(8,128)(2,1)S(1)} %add_or_begin.4.refs_1_), channel_id=1, source_target_pairs={{0,8},{24,16},{8,0},{16,24},{1,9},{25,17},{9,1},{17,25},{2,10},{26... | collective-permute-start | bytes 6488072 | tf_op jit(solution)/shard_map/ppermute | solution.py:161
  321.6 10.3 %collective-permute-done.72.refs_2_ = bf16[256,1536]{1,0:T(8,128)(2,1)S(1)} collective-permute-done((bf16[256,1536]{1,0:T(8,128)(2,1)S(1)}, bf16[256,1536]{1,0:T(8,128)(2,1)S(1)}, u32[]{:S(2)}, u32[]{:S(2)}) %collective-permute-start.72) | collective-permute-done | bytes 786464 | tf_op jit(solution)/shard_map/ppermute | solution.py:107
  343.4 8.4 %collective-permute-done.77.refs_3_ = bf16[256,1536]{1,0:T(8,128)(2,1)S(1)} collective-permute-done((bf16[256,1536]{1,0:T(8,128)(2,1)S(1)}, bf16[256,1536]{1,0:T(8,128)(2,1)S(1)}, u32[]{:S(2)}, u32[]{:S(2)}) %collective-permute-start.77) | collective-permute-done | bytes 786464 | tf_op jit(solution)/shard_map/ppermute | solution.py:107
  354.5 15.3 %collective-permute-start.81 = (bf16[528,2048]{1,0:T(8,128)(2,1)}, bf16[528,2048]{1,0:T(8,128)(2,1)}, u32[]{:S(2)}, u32[]{:S(2)}) collective-permute-start(bf16[528,2048]{1,0:T(8,128)(2,1)} %add_or_begin.5.refs_1_), channel_id=1, source_target_pairs={{0,8},{24,16},{8,0},{16,24},{1,9},{25,17},{9,1},{17,25},{2,10},{26... | collective-permute-start | bytes 6488072 | tf_op jit(solution)/shard_map/ppermute | solution.py:161
  373.6 11.6 %conditional.19 = (bf16[448,2048]{1,0:T(8,128)(2,1)}) conditional(s32[]{:T(128)} %bitcast.2, () %tuple.359, (f32[1,2048]{1,0:T(1,128)S(1)}, f32[1,1024]{1,0:T(1,128)S(1)}, f32[1,2048]{1,0:T(1,128)S(1)}, bf16[176,2048]{1,0:T(8,128)(2,1)}, bf16[1024,512]{1,0:T(8,128)(2,1)S(1)}) %tuple.438), branch_computations={%region_12.13_spmd, %region_13.14_spmd} | conditional | flops 41984 | bytes 1835018 | solution.py:1189
  385.3 4.9 share.17
  395.9 12.1 %conditional.21 = (bf16[192,2048]{1,0:T(8,128)(2,1)}, bf16[192,2048]{1,0:T(8,128)(2,1)}, bf16[192,2048]{1,0:T(8,128)(2,1)}, bf16[192,2048]{1,0:T(8,128)(2,1)}, bf16[192,2048]{1,0:T(8,128)(2,1)S(1)}) conditional(s32[]{:T(128)} %bitcast.2, () %tuple.342, (bf16[192,2048]{1,0:T(8,128)(2,1)S(1)}, bf16[192,2048]{1,0:T(8,128)(2,1)S(1)}, ...), branch_computations={%region_16.17_spmd, %region_17.18_spmd} | conditional | flops 1024 | bytes 9438368 | solution.py:1189
  397.6 4.2 share.13
  401.8 6.2 %collective-permute-done.8 = bf16[192,2048]{1,0:T(8,128)(2,1)} collective-permute-done((bf16[192,2048]{1,0:T(8,128)(2,1)S(1)}, bf16[192,2048]{1,0:T(8,128)(2,1)}, u32[]{:S(2)}, u32[]{:S(2)}) %collective-permute-start.8) | collective-permute-done | bytes 786464 | tf_op jit(solution)/shard_map/cond/branch_1_fun/ppermute | solution.py:107
  411.1 5.8 %collective-permute-done.81.refs_1_.refs_2_ = bf16[528,2048]{1,0:T(8,128)(2,1)} collective-permute-done((bf16[528,2048]{1,0:T(8,128)(2,1)}, bf16[528,2048]{1,0:T(8,128)(2,1)}, u32[]{:S(2)}, u32[]{:S(2)}) %collective-permute-start.81) | collective-permute-done | bytes 2162720 | tf_op jit(solution)/shard_map/ppermute | solution.py:161
  424.1 7.4 %collective-permute-start.82 = (bf16[448,2048]{1,0:T(8,128)(2,1)S(1)}, bf16[448,2048]{1,0:T(8,128)(2,1)S(1)}, u32[]{:S(2)}, u32[]{:S(2)}) collective-permute-start(bf16[448,2048]{1,0:T(8,128)(2,1)S(1)} %copy-done.88), channel_id=1, source_target_pairs={{0,8},{24,16},{1,9},{25,17},{2,10},{26,18},{3,11},{27,19},{4,12},{... | collective-permute-start | bytes 5505032 | tf_op jit(solution)/shard_map/ppermute | solution.py:161
  442.4 30.1 %collective-permute-done.84.refs_2_ = bf16[528,2048]{1,0:T(8,128)(2,1)S(1)} collective-permute-done((bf16[528,2048]{1,0:T(8,128)(2,1)S(1)}, bf16[528,2048]{1,0:T(8,128)(2,1)S(1)}, u32[]{:S(2)}, u32[]{:S(2)}) %collective-permute-start.84) | collective-permute-done | bytes 2162720 | tf_op jit(solution)/shard_map/ppermute | solution.py:161
  480.7 18.6 %conditional.22 = (bf16[192,2048]{1,0:T(8,128)(2,1)}, bf16[192,2048]{1,0:T(8,128)(2,1)}, bf16[192,2048]{1,0:T(8,128)(2,1)}) conditional(s32[]{:T(128)} %bitcast.2, () %tuple.456, (bf16[192,2048]{1,0:T(8,128)(2,1)S(1)}, bf16[192,2048]{1,0:T(8,128)(2,1)S(1)}, bf16[192,2048]{1,0:T(8,128)(2,1)S(1)}) %tuple.458), branch_computations={%region_18.19_spmd, %region_19.20_spmd} | conditional | bytes 9437328 | solution.py:1189
  483.3 15.9 %collective-permute-done.11 = bf16[192,2048]{1,0:T(8,128)(2,1)} collective-permute-done((bf16[192,2048]{1,0:T(8,128)(2,1)S(1)}, bf16[192,2048]{1,0:T(8,128)(2,1)}, u32[]{:S(2)}, u32[]{:S(2)}) %collective-permute-start.11) | collective-permute-done | bytes 786464 | tf_op jit(solution)/shard_map/cond/branch_1_fun/ppermute | solution.py:107
  508.9 16.1 %collective-permute-done.86.came = bf16[528,2048]{1,0:T(8,128)(2,1)} collective-permute-done((bf16[528,2048]{1,0:T(8,128)(2,1)}, bf16[528,2048]{1,0:T(8,128)(2,1)}, u32[]{:S(2)}, u32[]{:S(2)}) %collective-permute-start.86) | collective-permute-done | bytes 2162720 | tf_op jit(solution)/shard_map/ppermute | solution.py:161
  528.5 17.7 %conditional.23 = (bf16[192,2048]{1,0:T(8,128)(2,1)}, bf16[192,2048]{1,0:T(8,128)(2,1)}, bf16[192,2048]{1,0:T(8,128)(2,1)}, f32[512,2048]{1,0:T(8,128)}) conditional(s32[]{:T(128)} %bitcast.2, () %tuple.483, (bf16[192,2048]{1,0:T(8,128)(2,1)S(1)}, bf16[528,2048]{1,0:T(8,128)(2,1)}, s32[1]{0:T(128)}, bf16[528,2048]{1,0:T(8,128)(2,1)}) %tuple.485), branch_computations={%region_20.21_spmd, %region_21.22_spmd} | conditional | flops 1024 | bytes 9438360 | solution.py:1189
  535.2 11.0 %collective-permute-done.14 = bf16[192,2048]{1,0:T(8,128)(2,1)} collective-permute-done((bf16[192,2048]{1,0:T(8,128)(2,1)S(1)}, bf16[192,2048]{1,0:T(8,128)(2,1)}, u32[]{:S(2)}, u32[]{:S(2)}) %collective-permute-start.14) | collective-permute-done | bytes 786464 | tf_op jit(solution)/shard_map/cond/branch_1_fun/ppermute | solution.py:107
  546.3 12.9 %conditional.24 = (bf16[192,2048]{1,0:T(8,128)(2,1)}, bf16[192,2048]{1,0:T(8,128)(2,1)}, bf16[192,2048]{1,0:T(8,128)(2,1)}, f32[2048,1024]{1,0:T(8,128)}, f32[2048,256]{1,0:T(8,128)}, /*index=5*/f32[2048,256]{1,0:T(8,128)}) conditional(s32[]{:T(128)} %bitcast.2, () %tuple.482, (bf16[192,2048]{1,0:T(8,128)(2,1)}, bf16[192,2048]{1,0:T(8,128)(2,1)}, ...), branch_computations={%region_22.23_spmd, %region_23.24_spmd} | conditional | flops 1024 | bytes 14942274 | solution.py:1189
  550.1 6.2 %unpack.2 = (f32[2048,1024]{1,0:T(8,128)}, f32[2048,256]{1,0:T(8,128)}, f32[2048,256]{1,0:T(8,128)}) custom-call(s32[8]{0:T(128)S(1)} %get-tuple-element.209.table, bf16[192,2048]{1,0:T(8,128)(2,1)S(1)} %get-tuple-element.210.refs_0_, bf16[192,2048]{1,0:T(8,128)(2,1)} %get-tuple-element.211.refs_1_, bf16[192,2048]{1,0:T(8,128)(2,1)} %get-tuple-element.207.refs_2_, ...), custom_call_target="tpu_custom_call" | custom-call | flops 1024 | bytes 1024 | tf_op jit(solution)/shard_map/cond/branch_1_fun/unpack/pallas_call | solution.py:1122
  (423 shorter events, 249.0 us)
Async XLA Ops:
  0.6 39.5 %collective-permute-start.27 = (bf16[192,2048]{1,0:T(8,128)(2,1)}, bf16[192,2048]{1,0:T(8,128)(2,1)S(1)}, u32[]{:S(2)}, u32[]{:S(2)}) collective-permute-start(bf16[192,2048]{1,0:T(8,128)(2,1)} %bitcast.26), channel_id=1, source_target_pairs={{0,2},{1,5},{2,0},{3,7},{4,6},{5,1},{6,4},{7,3},{8,10},{9,13},{10,... | collective-permute-start | bytes 2359304 | tf_op jit(solution)/shard_map/ppermute | solution.py:107
  12.2 15.3 %collective-permute-start.21 = (bf16[192,1536]{1,0:T(8,128)(2,1)}, bf16[192,1536]{1,0:T(8,128)(2,1)}, u32[]{:S(2)}, u32[]{:S(2)}) collective-permute-start(bf16[192,1536]{1,0:T(8,128)(2,1)} %get-tuple-element.101), channel_id=1, source_target_pairs={{0,2},{1,5},{2,0},{3,7},{4,6},{5,1},{6,4},{7,3},{8,10},{9,13},{10,... | collective-permute-start | bytes 1769480 | tf_op jit(solution)/shard_map/cond/branch_1_fun/ppermute | solution.py:107
  12.3 15.2 %collective-permute-start.22 = (bf16[192,1536]{1,0:T(8,128)(2,1)}, bf16[192,1536]{1,0:T(8,128)(2,1)}, u32[]{:S(2)}, u32[]{:S(2)}) collective-permute-start(bf16[192,1536]{1,0:T(8,128)(2,1)} %get-tuple-element.101), channel_id=1, source_target_pairs={{0,4},{1,3},{2,6},{3,1},{4,0},{5,7},{6,2},{7,5},{8,12},{9,11},{10,... | collective-permute-start | bytes 1769480 | tf_op jit(solution)/shard_map/cond/branch_1_fun/ppermute | solution.py:107
  14.3 13.2 %collective-permute-start.23 = (bf16[192,1536]{1,0:T(8,128)(2,1)}, bf16[192,1536]{1,0:T(8,128)(2,1)}, u32[]{:S(2)}, u32[]{:S(2)}) collective-permute-start(bf16[192,1536]{1,0:T(8,128)(2,1)} %get-tuple-element.101), channel_id=1, source_target_pairs={{0,1},{1,0},{2,3},{3,2},{4,5},{5,4},{6,7},{7,6},{8,9},{9,8},{10,11... | collective-permute-start | bytes 1769480 | tf_op jit(solution)/shard_map/cond/branch_1_fun/ppermute | solution.py:107
  40.2 22.8 %collective-permute-start.28 = (bf16[192,2048]{1,0:T(8,128)(2,1)S(1)}, bf16[192,2048]{1,0:T(8,128)(2,1)}, u32[]{:S(2)}, u32[]{:S(2)}) collective-permute-start(bf16[192,2048]{1,0:T(8,128)(2,1)S(1)} %bitcast.27), channel_id=1, source_target_pairs={{0,4},{1,3},{2,6},{3,1},{4,0},{5,7},{6,2},{7,5},{8,12},{9,11},{10,... | collective-permute-start | bytes 2359304 | tf_op jit(solution)/shard_map/ppermute | solution.py:107
  41.9 21.0 %collective-permute-start.29 = (bf16[192,2048]{1,0:T(8,128)(2,1)S(1)}, bf16[192,2048]{1,0:T(8,128)(2,1)}, u32[]{:S(2)}, u32[]{:S(2)}) collective-permute-start(bf16[192,2048]{1,0:T(8,128)(2,1)S(1)} %collective-permute-done.27.refs_2_), channel_id=1, source_target_pairs={{0,4},{1,3},{2,6},{3,1},{4,0},{5,7},{6,2},{7,5},{8,12},{9,11},{10,... | collective-permute-start | bytes 2359304 | tf_op jit(solution)/shard_map/ppermute | solution.py:107
  42.3 20.7 %collective-permute-start.30 = (bf16[192,2048]{1,0:T(8,128)(2,1)S(1)}, bf16[192,2048]{1,0:T(8,128)(2,1)}, u32[]{:S(2)}, u32[]{:S(2)}) collective-permute-start(bf16[192,2048]{1,0:T(8,128)(2,1)S(1)} %bitcast.28), channel_id=1, source_target_pairs={{0,1},{1,0},{2,3},{3,2},{4,5},{5,4},{6,7},{7,6},{8,9},{9,8},{10,11... | collective-permute-start | bytes 2359304 | tf_op jit(solution)/shard_map/ppermute | solution.py:107
  42.3 20.7 %collective-permute-start.31 = (bf16[192,2048]{1,0:T(8,128)(2,1)S(1)}, bf16[192,2048]{1,0:T(8,128)(2,1)}, u32[]{:S(2)}, u32[]{:S(2)}) collective-permute-start(bf16[192,2048]{1,0:T(8,128)(2,1)S(1)} %collective-permute-done.27.refs_2_), channel_id=1, source_target_pairs={{0,1},{1,0},{2,3},{3,2},{4,5},{5,4},{6,7},{7,6},{8,9},{9,8},{10,11... | collective-permute-start | bytes 2359304 | tf_op jit(solution)/shard_map/ppermute | solution.py:107
  76.1 20.0 %collective-permute-start.35 = (bf16[192,2048]{1,0:T(8,128)(2,1)S(1)}, bf16[192,2048]{1,0:T(8,128)(2,1)S(1)}, u32[]{:S(2)}, u32[]{:S(2)}) collective-permute-start(bf16[192,2048]{1,0:T(8,128)(2,1)S(1)} %add_rows.26), channel_id=1, source_target_pairs={{0,2},{1,5},{2,0},{3,7},{4,6},{5,1},{6,4},{7,3},{8,10},{9,13},{10,... | collective-permute-start | bytes 2359304 | tf_op jit(solution)/shard_map/ppermute | solution.py:107
  77.5 18.6 %collective-permute-start.36 = (bf16[192,2048]{1,0:T(8,128)(2,1)S(1)}, bf16[192,2048]{1,0:T(8,128)(2,1)S(1)}, u32[]{:S(2)}, u32[]{:S(2)}) collective-permute-start(bf16[192,2048]{1,0:T(8,128)(2,1)S(1)} %add_rows.27), channel_id=1, source_target_pairs={{0,4},{1,3},{2,6},{3,1},{4,0},{5,7},{6,2},{7,5},{8,12},{9,11},{10,... | collective-permute-start | bytes 2359304 | tf_op jit(solution)/shard_map/ppermute | solution.py:107
  79.3 16.8 %collective-permute-start.37 = (bf16[192,2048]{1,0:T(8,128)(2,1)S(1)}, bf16[192,2048]{1,0:T(8,128)(2,1)S(1)}, u32[]{:S(2)}, u32[]{:S(2)}) collective-permute-start(bf16[192,2048]{1,0:T(8,128)(2,1)S(1)} %get-tuple-element.705), channel_id=1, source_target_pairs={{0,1},{1,0},{2,3},{3,2},{4,5},{5,4},{6,7},{7,6},{8,9},{9,8},{10,11... | collective-permute-start | bytes 2359304 | tf_op jit(solution)/shard_map/ppermute | solution.py:107
  98.9 20.1 %collective-permute-start.40 = (bf16[192,2048]{1,0:T(8,128)(2,1)S(1)}, bf16[192,2048]{1,0:T(8,128)(2,1)S(1)}, u32[]{:S(2)}, u32[]{:S(2)}) collective-permute-start(bf16[192,2048]{1,0:T(8,128)(2,1)S(1)} %get-tuple-element.724.refs_0_), channel_id=1, source_target_pairs={{0,2},{1,5},{2,0},{3,7},{4,6},{5,1},{6,4},{7,3},{8,10},{9,13},{10,... | collective-permute-start | bytes 2359304 | tf_op jit(solution)/shard_map/ppermute | solution.py:107
  100.3 18.7 %collective-permute-start.41 = (bf16[192,2048]{1,0:T(8,128)(2,1)S(1)}, bf16[192,2048]{1,0:T(8,128)(2,1)S(1)}, u32[]{:S(2)}, u32[]{:S(2)}) collective-permute-start(bf16[192,2048]{1,0:T(8,128)(2,1)S(1)} %get-tuple-element.724.refs_0_), channel_id=1, source_target_pairs={{0,4},{1,3},{2,6},{3,1},{4,0},{5,7},{6,2},{7,5},{8,12},{9,11},{10,... | collective-permute-start | bytes 2359304 | tf_op jit(solution)/shard_map/ppermute | solution.py:107
  147.2 50.6 %collective-permute-start.53 = (bf16[528,2048]{1,0:T(8,128)(2,1)}, bf16[528,2048]{1,0:T(8,128)(2,1)}, u32[]{:S(2)}, u32[]{:S(2)}) collective-permute-start(bf16[528,2048]{1,0:T(8,128)(2,1)} %get-tuple-element.768.refs_0_), channel_id=1, source_target_pairs={{0,8},{24,16},{1,9},{25,17},{2,10},{26,18},{3,11},{27,19},{4,12},{... | collective-permute-start | bytes 6488072 | tf_op jit(solution)/shard_map/ppermute | solution.py:161
  176.8 34.5 %collective-permute-start.50 = (bf16[192,2048]{1,0:T(8,128)(2,1)S(1)}, bf16[192,2048]{1,0:T(8,128)(2,1)S(1)}, u32[]{:S(2)}, u32[]{:S(2)}) collective-permute-start(bf16[192,2048]{1,0:T(8,128)(2,1)S(1)} %add_rows.29), channel_id=1, source_target_pairs={{0,2},{1,5},{2,0},{3,7},{4,6},{5,1},{6,4},{7,3},{8,10},{9,13},{10,... | collective-permute-start | bytes 2359304 | tf_op jit(solution)/shard_map/ppermute | solution.py:107
  178.4 33.0 %collective-permute-start.51 = (bf16[192,2048]{1,0:T(8,128)(2,1)S(1)}, bf16[192,2048]{1,0:T(8,128)(2,1)S(1)}, u32[]{:S(2)}, u32[]{:S(2)}) collective-permute-start(bf16[192,2048]{1,0:T(8,128)(2,1)S(1)} %add_rows.30), channel_id=1, source_target_pairs={{0,4},{1,3},{2,6},{3,1},{4,0},{5,7},{6,2},{7,5},{8,12},{9,11},{10,... | collective-permute-start | bytes 2359304 | tf_op jit(solution)/shard_map/ppermute | solution.py:107
  179.5 31.9 %collective-permute-start.52 = (bf16[192,2048]{1,0:T(8,128)(2,1)S(1)}, bf16[192,2048]{1,0:T(8,128)(2,1)S(1)}, u32[]{:S(2)}, u32[]{:S(2)}) collective-permute-start(bf16[192,2048]{1,0:T(8,128)(2,1)S(1)} %get-tuple-element.802), channel_id=1, source_target_pairs={{0,1},{1,0},{2,3},{3,2},{4,5},{5,4},{6,7},{7,6},{8,9},{9,8},{10,11... | collective-permute-start | bytes 2359304 | tf_op jit(solution)/shard_map/ppermute | solution.py:107
  201.8 51.5 %collective-permute-start.61 = (bf16[528,2048]{1,0:T(8,128)(2,1)}, bf16[528,2048]{1,0:T(8,128)(2,1)}, u32[]{:S(2)}, u32[]{:S(2)}) collective-permute-start(bf16[528,2048]{1,0:T(8,128)(2,1)} %add_rows.31.own), channel_id=1, source_target_pairs={{8,16},{16,8},{9,17},{17,9},{10,18},{18,10},{11,19},{19,11},{12,20... | collective-permute-start | bytes 6488072 | tf_op jit(solution)/shard_map/ppermute | solution.py:161
  204.1 53.8 %collective-permute-start.60 = (bf16[528,2048]{1,0:T(8,128)(2,1)}, bf16[528,2048]{1,0:T(8,128)(2,1)}, u32[]{:S(2)}, u32[]{:S(2)}) collective-permute-start(bf16[528,2048]{1,0:T(8,128)(2,1)} %get-tuple-element.808.refs_0_), channel_id=1, source_target_pairs={{0,8},{24,16},{1,9},{25,17},{2,10},{26,18},{3,11},{27,19},{4,12},{... | collective-permute-start | bytes 6488072 | tf_op jit(solution)/shard_map/ppermute | solution.py:161
  214.4 20.3 %collective-permute-start.55 = (bf16[192,2048]{1,0:T(8,128)(2,1)S(1)}, bf16[192,2048]{1,0:T(8,128)(2,1)}, u32[]{:S(2)}, u32[]{:S(2)}) collective-permute-start(bf16[192,2048]{1,0:T(8,128)(2,1)S(1)} %get-tuple-element.824.refs_0_), channel_id=1, source_target_pairs={{0,2},{1,5},{2,0},{3,7},{4,6},{5,1},{6,4},{7,3},{8,10},{9,13},{10,... | collective-permute-start | bytes 2359304 | tf_op jit(solution)/shard_map/ppermute | solution.py:107
  215.9 18.8 %collective-permute-start.56 = (bf16[192,2048]{1,0:T(8,128)(2,1)S(1)}, bf16[192,2048]{1,0:T(8,128)(2,1)}, u32[]{:S(2)}, u32[]{:S(2)}) collective-permute-start(bf16[192,2048]{1,0:T(8,128)(2,1)S(1)} %get-tuple-element.824.refs_0_), channel_id=1, source_target_pairs={{0,4},{1,3},{2,6},{3,1},{4,0},{5,7},{6,2},{7,5},{8,12},{9,11},{10,... | collective-permute-start | bytes 2359304 | tf_op jit(solution)/shard_map/ppermute | solution.py:107
  235.2 12.3 %collective-permute-start.59 = (bf16[192,2048]{1,0:T(8,128)(2,1)}, bf16[192,2048]{1,0:T(8,128)(2,1)}, u32[]{:S(2)}, u32[]{:S(2)}) collective-permute-start(bf16[192,2048]{1,0:T(8,128)(2,1)} %collective-permute-done.55.refs_0_.refs_2_), channel_id=1, source_target_pairs={{0,4},{1,3},{2,6},{3,1},{4,0},{5,7},{6,2},{7,5},{8,12},{9,11},{10,... | collective-permute-start | bytes 2359304 | tf_op jit(solution)/shard_map/ppermute | solution.py:107
  255.9 53.6 %collective-permute-start.70 = (bf16[528,2048]{1,0:T(8,128)(2,1)S(1)}, bf16[528,2048]{1,0:T(8,128)(2,1)S(1)}, u32[]{:S(2)}, u32[]{:S(2)}) collective-permute-start(bf16[528,2048]{1,0:T(8,128)(2,1)S(1)} %add_or_begin.3.refs_1_), channel_id=1, source_target_pairs={{0,8},{24,16},{8,0},{16,24},{1,9},{25,17},{9,1},{17,25},{2,10},{26... | collective-permute-start | bytes 6488072 | tf_op jit(solution)/shard_map/ppermute | solution.py:161
  262.2 47.8 %collective-permute-start.69 = (bf16[528,2048]{1,0:T(8,128)(2,1)}, bf16[528,2048]{1,0:T(8,128)(2,1)}, u32[]{:S(2)}, u32[]{:S(2)}) collective-permute-start(bf16[528,2048]{1,0:T(8,128)(2,1)} %add_rows.32.own), channel_id=1, source_target_pairs={{8,16},{16,8},{9,17},{17,9},{10,18},{18,10},{11,19},{19,11},{12,20... | collective-permute-start | bytes 6488072 | tf_op jit(solution)/shard_map/ppermute | solution.py:161
  290.4 15.9 %collective-permute-start.66 = (bf16[192,1536]{1,0:T(8,128)(2,1)S(1)}, bf16[192,1536]{1,0:T(8,128)(2,1)S(1)}, u32[]{:S(2)}, u32[]{:S(2)}) collective-permute-start(bf16[192,1536]{1,0:T(8,128)(2,1)S(1)} %add_rows.34), channel_id=1, source_target_pairs={{0,2},{1,5},{2,0},{3,7},{4,6},{5,1},{6,4},{7,3},{8,10},{9,13},{10,... | collective-permute-start | bytes 1769480 | tf_op jit(solution)/shard_map/ppermute | solution.py:107
  292.0 14.4 %collective-permute-start.67 = (bf16[192,1536]{1,0:T(8,128)(2,1)S(1)}, bf16[192,1536]{1,0:T(8,128)(2,1)S(1)}, u32[]{:S(2)}, u32[]{:S(2)}) collective-permute-start(bf16[192,1536]{1,0:T(8,128)(2,1)S(1)} %add_rows.35), channel_id=1, source_target_pairs={{0,4},{1,3},{2,6},{3,1},{4,0},{5,7},{6,2},{7,5},{8,12},{9,11},{10,... | collective-permute-start | bytes 1769480 | tf_op jit(solution)/shard_map/ppermute | solution.py:107
  293.3 13.1 %collective-permute-start.68 = (bf16[192,1536]{1,0:T(8,128)(2,1)S(1)}, bf16[192,1536]{1,0:T(8,128)(2,1)S(1)}, u32[]{:S(2)}, u32[]{:S(2)}) collective-permute-start(bf16[192,1536]{1,0:T(8,128)(2,1)S(1)} %get-tuple-element.890), channel_id=1, source_target_pairs={{0,1},{1,0},{2,3},{3,2},{4,5},{5,4},{6,7},{7,6},{8,9},{9,8},{10,11... | collective-permute-start | bytes 1769480 | tf_op jit(solution)/shard_map/ppermute | solution.py:107
  312.7 39.6 %collective-permute-start.76 = (bf16[528,2048]{1,0:T(8,128)(2,1)S(1)}, bf16[528,2048]{1,0:T(8,128)(2,1)S(1)}, u32[]{:S(2)}, u32[]{:S(2)}) collective-permute-start(bf16[528,2048]{1,0:T(8,128)(2,1)S(1)} %add_rows.36.own), channel_id=1, source_target_pairs={{8,16},{16,8},{9,17},{17,9},{10,18},{18,10},{11,19},{19,11},{12,20... | collective-permute-start | bytes 6488072 | tf_op jit(solution)/shard_map/ppermute | solution.py:161
  313.5 56.2 %collective-permute-start.75 = (bf16[528,2048]{1,0:T(8,128)(2,1)S(1)}, bf16[528,2048]{1,0:T(8,128)(2,1)S(1)}, u32[]{:S(2)}, u32[]{:S(2)}) collective-permute-start(bf16[528,2048]{1,0:T(8,128)(2,1)S(1)} %add_or_begin.4.refs_1_), channel_id=1, source_target_pairs={{0,8},{24,16},{8,0},{16,24},{1,9},{25,17},{9,1},{17,25},{2,10},{26... | collective-permute-start | bytes 6488072 | tf_op jit(solution)/shard_map/ppermute | solution.py:161
  332.3 19.5 %collective-permute-start.77 = (bf16[256,1536]{1,0:T(8,128)(2,1)S(1)}, bf16[256,1536]{1,0:T(8,128)(2,1)S(1)}, u32[]{:S(2)}, u32[]{:S(2)}) collective-permute-start(bf16[256,1536]{1,0:T(8,128)(2,1)S(1)} %add_rows.38), channel_id=1, source_target_pairs={{0,2},{1,5},{2,0},{3,7},{4,6},{5,1},{6,4},{7,3},{8,10},{9,13},{10,... | collective-permute-start | bytes 2359304 | tf_op jit(solution)/shard_map/ppermute | solution.py:107
  333.8 18.0 %collective-permute-start.78 = (bf16[256,1536]{1,0:T(8,128)(2,1)S(1)}, bf16[256,1536]{1,0:T(8,128)(2,1)S(1)}, u32[]{:S(2)}, u32[]{:S(2)}) collective-permute-start(bf16[256,1536]{1,0:T(8,128)(2,1)S(1)} %add_rows.39), channel_id=1, source_target_pairs={{0,4},{1,3},{2,6},{3,1},{4,0},{5,7},{6,2},{7,5},{8,12},{9,11},{10,... | collective-permute-start | bytes 2359304 | tf_op jit(solution)/shard_map/ppermute | solution.py:107
  335.1 16.7 %collective-permute-start.79 = (bf16[256,1536]{1,0:T(8,128)(2,1)S(1)}, bf16[256,1536]{1,0:T(8,128)(2,1)S(1)}, u32[]{:S(2)}, u32[]{:S(2)}) collective-permute-start(bf16[256,1536]{1,0:T(8,128)(2,1)S(1)} %get-tuple-element.957), channel_id=1, source_target_pairs={{0,1},{1,0},{2,3},{3,2},{4,5},{5,4},{6,7},{7,6},{8,9},{9,8},{10,11... | collective-permute-start | bytes 2359304 | tf_op jit(solution)/shard_map/ppermute | solution.py:107
  354.5 62.5 %collective-permute-start.81 = (bf16[528,2048]{1,0:T(8,128)(2,1)}, bf16[528,2048]{1,0:T(8,128)(2,1)}, u32[]{:S(2)}, u32[]{:S(2)}) collective-permute-start(bf16[528,2048]{1,0:T(8,128)(2,1)} %add_or_begin.5.refs_1_), channel_id=1, source_target_pairs={{0,8},{24,16},{8,0},{16,24},{1,9},{25,17},{9,1},{17,25},{2,10},{26... | collective-permute-start | bytes 6488072 | tf_op jit(solution)/shard_map/ppermute | solution.py:161
  371.6 47.5 %collective-permute-start.80 = (bf16[528,2048]{1,0:T(8,128)(2,1)}, bf16[528,2048]{1,0:T(8,128)(2,1)}, u32[]{:S(2)}, u32[]{:S(2)}) collective-permute-start(bf16[528,2048]{1,0:T(8,128)(2,1)} %add_rows.40.refs_0_), channel_id=1, source_target_pairs={{8,16},{16,8},{9,17},{17,9},{10,18},{18,10},{11,19},{19,11},{12,20... | collective-permute-start | bytes 6488072 | tf_op jit(solution)/shard_map/ppermute | solution.py:161
  395.9 12.1 %collective-permute-start.8 = (bf16[192,2048]{1,0:T(8,128)(2,1)S(1)}, bf16[192,2048]{1,0:T(8,128)(2,1)}, u32[]{:S(2)}, u32[]{:S(2)}) collective-permute-start(bf16[192,2048]{1,0:T(8,128)(2,1)S(1)} %get-tuple-element.173), channel_id=1, source_target_pairs={{0,4},{1,3},{2,6},{3,1},{4,0},{5,7},{6,2},{7,5},{8,12},{9,11},{10,... | collective-permute-start | bytes 2359304 | tf_op jit(solution)/shard_map/cond/branch_1_fun/ppermute | solution.py:107
  422.0 50.5 %collective-permute-start.84 = (bf16[528,2048]{1,0:T(8,128)(2,1)S(1)}, bf16[528,2048]{1,0:T(8,128)(2,1)S(1)}, u32[]{:S(2)}, u32[]{:S(2)}) collective-permute-start(bf16[528,2048]{1,0:T(8,128)(2,1)S(1)} %add_rows.45.refs_1_), channel_id=1, source_target_pairs={{8,0},{16,24},{9,1},{17,25},{10,2},{18,26},{11,3},{19,27},{12,4},{... | collective-permute-start | bytes 6488072 | tf_op jit(solution)/shard_map/ppermute | solution.py:161
  423.3 50.5 %collective-permute-start.83 = (bf16[528,2048]{1,0:T(8,128)(2,1)S(1)}, bf16[528,2048]{1,0:T(8,128)(2,1)S(1)}, u32[]{:S(2)}, u32[]{:S(2)}) collective-permute-start(bf16[528,2048]{1,0:T(8,128)(2,1)S(1)} %add_rows.44.refs_0_), channel_id=1, source_target_pairs={{8,16},{16,8},{9,17},{17,9},{10,18},{18,10},{11,19},{19,11},{12,20... | collective-permute-start | bytes 6488072 | tf_op jit(solution)/shard_map/ppermute | solution.py:161
  424.1 52.8 %collective-permute-start.82 = (bf16[448,2048]{1,0:T(8,128)(2,1)S(1)}, bf16[448,2048]{1,0:T(8,128)(2,1)S(1)}, u32[]{:S(2)}, u32[]{:S(2)}) collective-permute-start(bf16[448,2048]{1,0:T(8,128)(2,1)S(1)} %copy-done.88), channel_id=1, source_target_pairs={{0,8},{24,16},{1,9},{25,17},{2,10},{26,18},{3,11},{27,19},{4,12},{... | collective-permute-start | bytes 5505032 | tf_op jit(solution)/shard_map/ppermute | solution.py:161
  475.6 49.3 %collective-permute-start.86 = (bf16[528,2048]{1,0:T(8,128)(2,1)}, bf16[528,2048]{1,0:T(8,128)(2,1)}, u32[]{:S(2)}, u32[]{:S(2)}) collective-permute-start(bf16[528,2048]{1,0:T(8,128)(2,1)} %add_rows.46.own), channel_id=1, source_target_pairs={{8,0},{16,24},{9,1},{17,25},{10,2},{18,26},{11,3},{19,27},{12,4},{... | collective-permute-start | bytes 6488072 | tf_op jit(solution)/shard_map/ppermute | solution.py:161
  478.6 27.8 %collective-permute-start.85 = (bf16[448,2048]{1,0:T(8,128)(2,1)}, bf16[448,2048]{1,0:T(8,128)(2,1)}, u32[]{:S(2)}, u32[]{:S(2)}) collective-permute-start(bf16[448,2048]{1,0:T(8,128)(2,1)} %add_rows.47.refs_0_), channel_id=1, source_target_pairs={{8,16},{16,8},{9,17},{17,9},{10,18},{18,10},{11,19},{19,11},{12,20... | collective-permute-start | bytes 5505032 | tf_op jit(solution)/shard_map/ppermute | solution.py:161
  480.7 18.6 %collective-permute-start.11 = (bf16[192,2048]{1,0:T(8,128)(2,1)S(1)}, bf16[192,2048]{1,0:T(8,128)(2,1)}, u32[]{:S(2)}, u32[]{:S(2)}) collective-permute-start(bf16[192,2048]{1,0:T(8,128)(2,1)S(1)} %get-tuple-element.186), channel_id=1, source_target_pairs={{0,2},{1,5},{2,0},{3,7},{4,6},{5,1},{6,4},{7,3},{8,10},{9,13},{10,... | collective-permute-start | bytes 2359304 | tf_op jit(solution)/shard_map/cond/branch_1_fun/ppermute | solution.py:107
  482.2 17.1 %collective-permute-start.12 = (bf16[192,2048]{1,0:T(8,128)(2,1)S(1)}, bf16[192,2048]{1,0:T(8,128)(2,1)}, u32[]{:S(2)}, u32[]{:S(2)}) collective-permute-start(bf16[192,2048]{1,0:T(8,128)(2,1)S(1)} %get-tuple-element.187), channel_id=1, source_target_pairs={{0,4},{1,3},{2,6},{3,1},{4,0},{5,7},{6,2},{7,5},{8,12},{9,11},{10,... | collective-permute-start | bytes 2359304 | tf_op jit(solution)/shard_map/cond/branch_1_fun/ppermute | solution.py:107
  483.3 16.0 %collective-permute-start.13 = (bf16[192,2048]{1,0:T(8,128)(2,1)S(1)}, bf16[192,2048]{1,0:T(8,128)(2,1)}, u32[]{:S(2)}, u32[]{:S(2)}) collective-permute-start(bf16[192,2048]{1,0:T(8,128)(2,1)S(1)} %get-tuple-element.188), channel_id=1, source_target_pairs={{0,1},{1,0},{2,3},{3,2},{4,5},{5,4},{6,7},{7,6},{8,9},{9,8},{10,11... | collective-permute-start | bytes 2359304 | tf_op jit(solution)/shard_map/cond/branch_1_fun/ppermute | solution.py:107
  524.9 41.2 %collective-permute-start.87 = (bf16[448,2048]{1,0:T(8,128)(2,1)S(1)}, bf16[448,2048]{1,0:T(8,128)(2,1)}, u32[]{:S(2)}, u32[]{:S(2)}) collective-permute-start(bf16[448,2048]{1,0:T(8,128)(2,1)S(1)} %add_rows.49.own), channel_id=1, source_target_pairs={{8,0},{16,24},{9,1},{17,25},{10,2},{18,26},{11,3},{19,27},{12,4},{... | collective-permute-start | bytes 5505032 | tf_op jit(solution)/shard_map/ppermute | solution.py:161
  528.6 17.7 %collective-permute-start.14 = (bf16[192,2048]{1,0:T(8,128)(2,1)S(1)}, bf16[192,2048]{1,0:T(8,128)(2,1)}, u32[]{:S(2)}, u32[]{:S(2)}) collective-permute-start(bf16[192,2048]{1,0:T(8,128)(2,1)S(1)} %get-tuple-element.195), channel_id=1, source_target_pairs={{0,2},{1,5},{2,0},{3,7},{4,6},{5,1},{6,4},{7,3},{8,10},{9,13},{10,... | collective-permute-start | bytes 2359304 | tf_op jit(solution)/shard_map/cond/branch_1_fun/ppermute | solution.py:107
  530.1 16.2 %collective-permute-start.15 = (bf16[192,2048]{1,0:T(8,128)(2,1)S(1)}, bf16[192,2048]{1,0:T(8,128)(2,1)}, u32[]{:S(2)}, u32[]{:S(2)}) collective-permute-start(bf16[192,2048]{1,0:T(8,128)(2,1)S(1)} %get-tuple-element.195), channel_id=1, source_target_pairs={{0,4},{1,3},{2,6},{3,1},{4,0},{5,7},{6,2},{7,5},{8,12},{9,11},{10,... | collective-permute-start | bytes 2359304 | tf_op jit(solution)/shard_map/cond/branch_1_fun/ppermute | solution.py:107
  531.2 15.0 %collective-permute-start.16 = (bf16[192,2048]{1,0:T(8,128)(2,1)S(1)}, bf16[192,2048]{1,0:T(8,128)(2,1)}, u32[]{:S(2)}, u32[]{:S(2)}) collective-permute-start(bf16[192,2048]{1,0:T(8,128)(2,1)S(1)} %get-tuple-element.195), channel_id=1, source_target_pairs={{0,1},{1,0},{2,3},{3,2},{4,5},{5,4},{6,7},{7,6},{8,9},{9,8},{10,11... | collective-permute-start | bytes 2359304 | tf_op jit(solution)/shard_map/cond/branch_1_fun/ppermute | solution.py:107
  546.8 12.3 %collective-permute-start.17 = (bf16[192,2048]{1,0:T(8,128)(2,1)}, bf16[192,2048]{1,0:T(8,128)(2,1)}, u32[]{:S(2)}, u32[]{:S(2)}) collective-permute-start(bf16[192,2048]{1,0:T(8,128)(2,1)} %get-tuple-element.207.refs_2_), channel_id=1, source_target_pairs={{0,4},{1,3},{2,6},{3,1},{4,0},{5,7},{6,2},{7,5},{8,12},{9,11},{10,... | collective-permute-start | bytes 2359304 | tf_op jit(solution)/shard_map/cond/branch_1_fun/ppermute | solution.py:107
  (134 other events, 1333.8 us)
